TPU v7x, 32 devices: a whole 2x2x4 slice. The times are simulated.
32 devices in a mesh: groups: 2 (over x), ctx: 8 (over z, y), exp: 2 (over core).
Axes of the slice: x: 2, y: 2, z: 4, core: 2. Of those that a mesh axis runs over, the one named last changes fastest.
Arguments:
- queries_in: bfloat16 [4096, 24, 128], P(('groups', 'ctx'), 'exp'), parts along dimension 0, may hold values from -42 to 42
- rotated_keys: bfloat16 [4096, 4, 128], P(('groups', 'ctx'), 'exp'), parts along dimension 0, may hold values from -6 to 6
- value_inputs: bfloat16 [4096, 4, 128], P(('groups', 'ctx'), 'exp'), parts along dimension 0, may hold values from -6 to 6
- stream_in: bfloat16 [4096, 3072], P(('groups', 'ctx', 'exp')), parts along dimension 0, may hold values from -6 to 6
- w_out: bfloat16 [24, 128, 3072], P('exp', 'ctx'), may hold values from -0.4375 to 0.4375
- w_router: bfloat16 [3072, 8], replicated, may hold values from -0.109375 to 0.109375
- routes: int32 [4096, 2], P(('groups', 'ctx', 'exp')), parts along dimension 0, may hold values from 0 to 7, all different within a row; in each aligned block of 128 rows (0 to 127, 128 to 255, ...) at most 64 rows name the same one
- expert_out: bfloat16 [16, 8, 2, 64, 3072], P(('groups', 'ctx'), 'exp'), parts along dimension 0, may hold values from -6 to 6
- grad_out: bfloat16 [4096, 3072], P(('groups', 'ctx', 'exp')), parts along dimension 0, may hold values from -6 to 6
Outputs:
- mixed: bfloat16 [4096, 3072], P(('groups', 'ctx', 'exp')), parts along dimension 0
- grad_input: bfloat16 [4096, 3072], P(('groups', 'ctx', 'exp')), parts along dimension 0
- grad_expert: bfloat16 [16, 8, 2, 64, 3072], P(('groups', 'ctx'), 'exp'), parts along dimension 0
- grad_q: bfloat16 [4096, 24, 128], P(('groups', 'ctx'), 'exp'), parts along dimension 0
- grad_k: bfloat16 [4096, 4, 128], P(('groups', 'ctx'), 'exp'), parts along dimension 0
- grad_v: bfloat16 [4096, 4, 128], P(('groups', 'ctx'), 'exp'), parts along dimension 0
There are 2 independent parts, one for each index of `groups`. A program takes and returns all parts, laid end to end along the dimension named above; an argument that names none is the same for every part. Nothing has to cross between parts.
Inputs may be any that keep to these rules, and one draw needn't show every extreme that they name: `routes`: each row names 2 different experts; among the rows of one device no expert is named by more than 64 rows, and in every draw some device's rows name some expert exactly 64 times.
All inputs are finite; a program needn't handle non-finite values.
Results may differ from a plain program's by a relative error of at most 0.012.
The roundings to bfloat16 on the way count: a program that leaves them out, or rounds other values in their place, can miss the bound.
Values may be sent and summed in bfloat16 or wider, within the bound.
No kernel may reach another device: no remote copies, remote signals or barrier semaphores. Data moves between devices by JAX's collectives and lax.ppermute only.
A program may use at most 128 MiB of HBM per device.

v0:
```python
import jax
import jax.numpy as jnp
from jax import lax
from jax.sharding import PartitionSpec as P

BAND_BLOCKS = 4


def passed_along(value, axis, steps):
    count = lax.axis_size(axis)
    initial, last = (max(0, -steps), min(count, count - steps))
    return lax.ppermute(value, axis, [(source, source + steps) for source in range(initial, last)])


def local(
    queries_in, rotated_keys, value_inputs, stream_in, w_out, w_router, routes, expert_out, grad_out
):
    place = lax.axis_index("ctx")
    tok = queries_in.shape[0]
    heads_q = queries_in.shape[1]
    heads_kv = rotated_keys.shape[1]
    head_dim = queries_in.shape[2]
    query_group = heads_q // heads_kv
    rows = stream_in.shape[0]
    width = stream_in.shape[1]
    experts = w_router.shape[1]
    capacity = expert_out.shape[3]
    scale = head_dim ** (-0.5)
    paired = jnp.stack([rotated_keys, value_inputs])
    blocks = [paired]
    for step in range(1, BAND_BLOCKS):
        blocks.append(passed_along(paired, "ctx", step))
    band = jnp.concatenate(blocks[::-1], axis=1)
    keys_band = band[0]
    values_band = band[1]
    qpos = place * tok + jnp.arange(tok, dtype=jnp.int32)
    kpos = (place - BAND_BLOCKS + 1) * tok + jnp.arange(BAND_BLOCKS * tok, dtype=jnp.int32)
    admitted = (kpos[None, :] <= qpos[:, None]) & (kpos[None, :] >= 0)
    query_rows = queries_in.reshape(tok, heads_kv, query_group, head_dim)
    scores = (
        jnp.einsum("tgad,sgd->gats", query_rows, keys_band, preferred_element_type=jnp.float32)
        * scale
    )
    scores = jnp.where(admitted, scores, -1e30)
    top = jnp.max(scores, axis=-1, keepdims=True)
    lse = top + jnp.log(jnp.sum(jnp.exp(scores - top), axis=-1, keepdims=True))
    probs = lax.optimization_barrier(jnp.exp(scores - lse).astype(jnp.bfloat16))
    attention_out = jnp.einsum(
        "gats,sgd->tgad", probs, values_band, preferred_element_type=jnp.float32
    ).astype(jnp.bfloat16)
    attn_flat = attention_out.reshape(tok, heads_q, head_dim)
    wo_full = lax.all_gather(w_out, "ctx", axis=1, tiled=True)
    proj = lax.psum_scatter(
        jnp.einsum("thd,hdj->tj", attn_flat, wo_full, preferred_element_type=jnp.float32),
        "exp",
        scatter_dimension=0,
        tiled=True,
    )
    resid = stream_in.astype(jnp.float32) + proj
    inv_rms = lax.rsqrt(jnp.mean(resid * resid, axis=-1, keepdims=True) + 1e-05)
    normed = (resid * inv_rms).astype(jnp.bfloat16)
    logits = jnp.dot(normed, w_router, preferred_element_type=jnp.float32)
    choose = (routes[:, :, None] == jnp.arange(experts, dtype=jnp.int32)[None, None, :]).astype(
        jnp.int32
    )
    flat_choose = choose.reshape(rows * 2, experts)
    before = jnp.cumsum(flat_choose, axis=0) - flat_choose
    rank = jnp.sum(before * flat_choose, axis=1)
    slots = routes.reshape(-1) * capacity + rank
    returned = lax.all_to_all(expert_out, "exp", split_axis=2, concat_axis=1, tiled=True)
    table = returned.reshape(experts * capacity, width)
    picked = jnp.take(table, slots, axis=0).reshape(rows, 2, width)
    choose_f = choose.astype(jnp.float32)
    chosen = jnp.sum(logits[:, None, :] * choose_f, axis=-1)
    gate_first = 1.0 / (1.0 + jnp.exp(chosen[:, 1] - chosen[:, 0]))
    gates = jnp.stack([gate_first, 1.0 - gate_first], axis=1)
    mixed = (
        resid
        + gates[:, 0:1] * picked[:, 0].astype(jnp.float32)
        + gates[:, 1:2] * picked[:, 1].astype(jnp.float32)
    )
    mixed = mixed.astype(jnp.bfloat16)
    dgate = jnp.einsum("td,tkd->tk", grad_out, picked, preferred_element_type=jnp.float32)
    spread = gates * (dgate - jnp.sum(gates * dgate, axis=1, keepdims=True))
    dlogit = jnp.sum(spread[:, :, None] * choose_f, axis=1)
    dnormed = jnp.dot(dlogit, w_router.astype(jnp.float32).T, precision=lax.Precision.HIGHEST)
    dyf = grad_out.astype(jnp.float32)
    grad_input = (
        dyf
        + inv_rms * dnormed
        - resid * inv_rms**3 * jnp.mean(dnormed * resid, axis=-1, keepdims=True)
    )
    grad_input = grad_input.astype(jnp.bfloat16)
    contrib = (gates[:, :, None] * dyf[:, None, :]).astype(jnp.bfloat16).reshape(rows * 2, width)
    outgoing = jnp.zeros((experts * capacity, width), jnp.bfloat16).at[slots].set(contrib)
    outgoing = outgoing.reshape(1, experts, 1, capacity, width)
    grad_expert = lax.all_to_all(outgoing, "exp", split_axis=1, concat_axis=2, tiled=True)
    block_grad = lax.all_gather(grad_input, "exp", axis=0, tiled=True)
    attention_gradient = jnp.einsum(
        "tj,hdj->thd", block_grad, wo_full, preferred_element_type=jnp.float32
    ).astype(jnp.bfloat16)
    input_gradient = attention_gradient.reshape(tok, heads_kv, query_group, head_dim)
    delta = jnp.einsum(
        "tgad,tgad->gat", input_gradient, attention_out, preferred_element_type=jnp.float32
    )
    dprob = jnp.einsum(
        "tgad,sgd->gats", input_gradient, values_band, preferred_element_type=jnp.float32
    )
    dscore = (probs.astype(jnp.float32) * (dprob - delta[..., None])).astype(jnp.bfloat16)
    grad_q = (
        jnp.einsum("gats,sgd->tgad", dscore, keys_band, preferred_element_type=jnp.float32) * scale
    )
    grad_q = grad_q.astype(jnp.bfloat16).reshape(tok, heads_q, head_dim)
    dkey = (
        jnp.einsum("gats,tgad->sgd", dscore, query_rows, preferred_element_type=jnp.float32) * scale
    )
    dval = jnp.einsum("gats,tgad->sgd", probs, input_gradient, preferred_element_type=jnp.float32)
    parts = jnp.stack([dkey, dval]).reshape(2, BAND_BLOCKS, tok, heads_kv, head_dim)
    total = parts[:, BAND_BLOCKS - 1]
    for step in range(1, BAND_BLOCKS):
        total = total + passed_along(
            parts[:, BAND_BLOCKS - 1 - step].astype(jnp.bfloat16), "ctx", -step
        ).astype(jnp.float32)
    grad_k = total[0].astype(jnp.bfloat16)
    grad_v = total[1].astype(jnp.bfloat16)
    return (mixed, grad_input, grad_expert, grad_q, grad_k, grad_v)


def solution(mesh):
    in_specs = (
        P(("groups", "ctx"), "exp", None),
        P(("groups", "ctx"), "exp", None),
        P(("groups", "ctx"), "exp", None),
        P(("groups", "ctx", "exp"), None),
        P("exp", "ctx", None),
        P(),
        P(("groups", "ctx", "exp"), None),
        P(("groups", "ctx"), "exp", None, None, None),
        P(("groups", "ctx", "exp"), None),
    )
    out_specs = (
        P(("groups", "ctx", "exp"), None),
        P(("groups", "ctx", "exp"), None),
        P(("groups", "ctx"), "exp", None, None, None),
        P(("groups", "ctx"), "exp", None),
        P(("groups", "ctx"), "exp", None),
        P(("groups", "ctx"), "exp", None),
    )
    return jax.shard_map(local, mesh=mesh, in_specs=in_specs, out_specs=out_specs, check_vma=False)
```

profile of v0, /device:TPU:15, one launch (start us, length us, event | category | flops | bytes accessed | tf_op | source)
XLA Modules:
  0.0 309.1 jit_solution(16860542557782152856)
XLA Ops:
  9.0 3.1 %collective-permute-start.2 = (bf16[2,256,2,128]{3,1,2,0:T(8,128)(2,1)S(1)}, bf16[2,256,2,128]{3,1,2,0:T(8,128)(2,1)S(1)}, u32[]{:S(2)}, u32[]{:S(2)}) collective-permute-start(bf16[2,256,2,128]{3,1,2,0:T(8,128)(2,1)S(1)} %pad_maximum_fusion.1), channel_id=1, source_target_pairs={{0,2},{2,4},{4,6},{6,8},{8,10},{10,12},{12,14},{1,3},{3,5},{5,7},{... | collective-permute-start | bytes 786440 | tf_op jit(solution)/shard_map/ppermute | solution.py:12
  12.2 3.2 %collective-permute-start.1 = (bf16[2,256,2,128]{3,1,2,0:T(8,128)(2,1)S(1)}, bf16[2,256,2,128]{3,1,2,0:T(8,128)(2,1)S(1)}, u32[]{:S(2)}, u32[]{:S(2)}) collective-permute-start(bf16[2,256,2,128]{3,1,2,0:T(8,128)(2,1)S(1)} %pad_maximum_fusion.1), channel_id=1, source_target_pairs={{0,4},{2,6},{4,8},{6,10},{8,12},{10,14},{1,5},{3,7},{5,9},{7,11},{... | collective-permute-start | bytes 786440 | tf_op jit(solution)/shard_map/ppermute | solution.py:12
  15.4 2.2 collective-permute-start
  18.1 6.9 %collective-permute-done.1 = bf16[2,256,2,128]{3,1,2,0:T(8,128)(2,1)S(1)} collective-permute-done((bf16[2,256,2,128]{3,1,2,0:T(8,128)(2,1)S(1)}, bf16[2,256,2,128]{3,1,2,0:T(8,128)(2,1)S(1)}, u32[]{:S(2)}, u32[]{:S(2)}) %collective-permute-start.1) | collective-permute-done | bytes 262176 | tf_op jit(solution)/shard_map/ppermute | solution.py:12
  25.0 26.7 %collective-permute-done = bf16[2,256,2,128]{3,1,2,0:T(8,128)(2,1)S(1)} collective-permute-done((bf16[2,256,2,128]{3,1,2,0:T(8,128)(2,1)S(1)}, bf16[2,256,2,128]{3,1,2,0:T(8,128)(2,1)S(1)}, u32[]{:S(2)}, u32[]{:S(2)}) %collective-permute-start) | collective-permute-done | bytes 262176 | tf_op jit(solution)/shard_map/ppermute | solution.py:12
  51.7 2.0 fusion.2
  53.8 2.5 exponential_reduce_fusion
  56.3 2.0 copy-done.1
  58.3 9.9 %exponential_convert_fusion = bf16[2,6,256,1024]{2,3,1,0:T(8,128)(2,1)} fusion(f32[2,1024,256,6]{2,1,3,0:T(8,128)} %copy-done.1, f32[2,6,256]{2,1,0:T(8,128)S(1)} %log_add_fusion, pred[256,1024]{0,1:T(8,128)(4,1)S(1)} %compare_and_fusion), kind=kLoop, calls=%fused_computation.6 | loop fusion | flops 12582912 | bytes 19148800 | tf_op jit(solution)/shard_map/convert_element_type | solution.py:47
  68.2 3.8 %convolution_convert_fusion = bf16[2,128,6,256]{3,1,2,0:T(8,128)(2,1)S(1)} fusion(bf16[2,6,256,1024]{2,3,1,0:T(8,128)(2,1)} %exponential_convert_fusion, bf16[2,1024,2,128]{3,1,2,0:T(8,128)(2,1)S(1)} %maximum_maximum_fusion), kind=kOutput, calls=%fused_computation.37 | convolution fusion | flops 805699584 | bytes 7602176 | tf_op jit(solution)/shard_map/gats,sgd->tgad/dot_general | solution.py:48
  72.0 87.5 %all-gather.3.cloned.1.call-done = bf16[12,128,3072]{2,1,0:T(8,128)(2,1)} async-done(((bf16[12,16,3072]{2,1,0:T(8,128)(2,1)}), bf16[12,128,3072]{2,1,0:T(8,128)(2,1)}) %all-gather.3.cloned.1.call-update) | async-done | bytes 9437200 | tf_op jit(solution)/shard_map/all_gather | solution.py:52
  159.5 8.0 %convolution_bitcast_fusion = f32[256,3072]{1,0:T(8,128)} fusion(bf16[256,12,128]{0,2,1:T(8,128)(2,1)S(1)} %bitcast.160, bf16[12,128,3072]{2,1,0:T(8,128)(2,1)} %all-gather.3.cloned.1.call-done), kind=kOutput, calls=%fused_computation.9 | convolution fusion | flops 2415919104 | bytes 13369344 | tf_op jit(solution)/shard_map/thd,hdj->tj/dot_general | solution.py:54
  167.5 3.8 %copy.124 = bf16[1,4,2,64,3072]{4,3,1,0,2:T(8,128)(2,1)} copy(bf16[1,4,2,64,3072]{4,3,2,1,0:T(8,128)(2,1)} %param.16) | data formatting | bytes 6291456 | tf_op args[7]
  171.3 6.4 %all-to-all-start = ((bf16[1,4,2,64,3072]{4,3,1,0,2:T(8,128)(2,1)}), bf16[1,4,2,64,3072]{4,3,1,0,2:T(8,128)(2,1)}, u32[]{:S(2)}, u32[]{:S(2)}) async-start(bf16[1,4,2,64,3072]{4,3,1,0,2:T(8,128)(2,1)} %copy.124), calls=%async_computation.1 | async-start | bytes 6291456 | tf_op jit(solution)/shard_map/all_to_all | solution.py:70
  181.1 5.4 %gather_fusion = bf16[256,3072]{1,0:T(8,128)(2,1)S(1)} fusion(bf16[512,3072]{1,0:T(8,128)(2,1)} %bitcast.19, s32[1024]{0:T(1024)S(1)} %pad_clamp_fusion), kind=kCustom, calls=%fused_computation | custom fusion | bytes 3146752 | tf_op jit(solution)/shard_map/jit(_take)/gather | solution.py:72
  188.2 2.1 copy_select_fusion
  190.4 6.7 %fusion.12 = f32[128,1,2]{2,1,0:T(1,128)S(1)} fusion(bf16[128,3072,1]{1,0,2:T(8,128)(2,1)S(1)} %bitcast.166, bf16[128,2,3072]{2,0,1:T(8,128)(2,1)S(1)} %copy_select_fusion), kind=kOutput, calls=%fused_computation.33 | convolution fusion | flops 1572864 | bytes 2360320 | tf_op jit(solution)/shard_map/td,tkd->tk/dot_general | solution.py:83
  200.6 2.2 subtract_convert_fusion
  202.8 3.6 %mul.184 = f32[128,2,3072]{2,1,0:T(2,128)} broadcast(bf16[128,3072]{1,0:T(8,128)(2,1)} %param.17), dimensions={0,2} | broadcast | bytes 3932160 | tf_op jit(solution)/shard_map/mul | solution.py:94
  206.5 15.7 %mul.185 = f32[256,3072]{1,0:T(8,128)} reshape(f32[128,2,3072]{2,1,0:T(2,128)} %mul.184) | data formatting | bytes 6291456 | tf_op jit(solution)/shard_map/mul | solution.py:94
  222.5 6.3 %scatter_custom_fusion = bf16[512,3072]{1,0:T(8,128)(2,1)} fusion(s32[256]{0:T(256)S(1)} %bitcast.170, f32[256,3072]{1,0:T(8,128)} %mul.185, f32[256]{0:T(256)S(1)} %mul.182, bf16[]{:T(256)} %constant.58.clone.1), kind=kCustom, calls=%fused_computation.15 | custom fusion | flops 1572864 | bytes 6292482 | tf_op jit(solution)/shard_map/scatter | solution.py:95
  228.8 7.5 %all_to_all.33 = bf16[1,8,1,64,3072]{4,3,2,0,1:T(8,128)(2,1)S(1)} all-to-all(bf16[1,8,1,64,3072]{4,3,2,0,1:T(8,128)(2,1)} %bitcast.157), channel_id=1, replica_groups=mesh['groups'=2,'ctx'=8,'exp'=2] {'exp'}, dimensions={1} | all-to-all | bytes 6291456 | tf_op jit(solution)/shard_map/all_to_all | solution.py:97
  238.2 6.5 %fusion.15 = bf16[256,12,128]{2,0,1:T(8,128)(2,1)} fusion(bf16[12,128,3072]{2,1,0:T(8,128)(2,1)} %all-gather.3.cloned.1.call-done, bf16[256,3072]{1,0:T(8,128)(2,1)} %all-gather.5.cloned.1.call-done), kind=kOutput, calls=%fused_computation.36 | convolution fusion | flops 2416312320 | bytes 11796480 | tf_op jit(solution)/shard_map/tj,hdj->thd/dot_general | solution.py:99
  244.6 2.7 copy.149
  249.2 6.1 %convolution_bitcast_fusion.1 = f32[1024,2,128]{0,2,1:T(8,128)} fusion(bf16[256,2,6,128]{3,0,2,1:T(8,128)(2,1)S(1)} %bitcast.162, bf16[2,6,256,1024]{2,3,1,0:T(8,128)(2,1)} %exponential_convert_fusion), kind=kOutput, calls=%fused_computation.38 | convolution fusion | flops 805306368 | bytes 8126464 | tf_op jit(solution)/shard_map/gats,tgad->sgd/dot_general | solution.py:117
  255.4 4.5 %fusion.1 = bf16[2,6,256,1024]{2,3,1,0:T(8,128)(2,1)} fusion(bf16[2,6,256,1024]{2,3,1,0:T(8,128)(2,1)S(1)} %bitcast.153, f32[2,6,256]{2,1,0:T(8,128)S(1)} %multiply_reduce_fusion, bf16[256,2,6,128]{3,0,2,1:T(8,128)(2,1)S(1)} %bitcast.163, bf16[2,1024,2,128]{3,1,2,0:T(8,128)(2,1)S(1)} %copy-done.8), kind=kOutput, calls=%fused_computation.4 | convolution fusion | flops 817889280 | bytes 13910016 | tf_op jit(solution)/shard_map/tgad,sgd->gats/dot_general | solution.py:106
  259.9 2.4 copy.160
  262.3 4.7 %fusion.18 = f32[2,1024,128]{2,1,0:T(8,128)S(1)} fusion(bf16[2,6,256,1024]{2,3,1,0:T(8,128)(2,1)} %fusion.1, bf16[256,2,6,128]{3,0,2,1:T(8,128)(2,1)S(1)} %bitcast.151), kind=kOutput, calls=%fused_computation.40 | convolution fusion | flops 805568512 | bytes 8126464 | tf_op jit(solution)/shard_map/gats,tgad->sgd/dot_general | solution.py:115
  270.7 5.0 %collective-permute-start.5 = (bf16[2,256,2,128]{3,2,1,0:T(2,128)(2,1)}, bf16[2,256,2,128]{3,2,1,0:T(2,128)(2,1)S(1)}, u32[]{:S(2)}, u32[]{:S(2)}) collective-permute-start(bf16[2,256,2,128]{3,2,1,0:T(2,128)(2,1)} %get-tuple-element.47), channel_id=1, source_target_pairs={{6,0},{8,2},{10,4},{12,6},{14,8},{7,1},{9,3},{11,5},{13,7},{15,9},... | collective-permute-start | bytes 786440 | tf_op jit(solution)/shard_map/ppermute | solution.py:12
  281.6 2.4 copy.135
  284.0 3.4 %collective-permute-done.4 = bf16[2,256,2,128]{3,2,1,0:T(2,128)(2,1)S(1)} collective-permute-done((bf16[2,256,2,128]{3,2,1,0:T(2,128)(2,1)}, bf16[2,256,2,128]{3,2,1,0:T(2,128)(2,1)S(1)}, u32[]{:S(2)}, u32[]{:S(2)}) %collective-permute-start.4) | collective-permute-done | bytes 262176 | tf_op jit(solution)/shard_map/ppermute | solution.py:12
  287.4 12.5 %collective-permute-done.3 = bf16[2,256,2,128]{3,2,1,0:T(2,128)(2,1)} collective-permute-done((bf16[2,256,2,128]{3,2,1,0:T(2,128)(2,1)}, bf16[2,256,2,128]{3,2,1,0:T(2,128)(2,1)}, u32[]{:S(2)}, u32[]{:S(2)}) %collective-permute-start.3) | collective-permute-done | bytes 262176 | tf_op jit(solution)/shard_map/ppermute | solution.py:12
  (102 shorter events, 26.8 us)
Async XLA Ops:
  7.2 44.6 %copy-start = (bf16[256,12,128]{2,0,1:T(8,128)(2,1)S(1)}, bf16[256,12,128]{2,0,1:T(8,128)(2,1)}, u32[]{:S(2)}) copy-start(bf16[256,12,128]{2,0,1:T(8,128)(2,1)} %param.9) | copy-start | bytes 2359300
  7.2 152.3 %all-gather.3.cloned.1.call-start = ((), (), s32[]{:S(2)}) async-start(), calls=%async_computation.3 | async-start | bytes 10616832 | tf_op jit(solution)/shard_map/all_gather | solution.py:52
  7.9 189.2 %reduce-scatter.2.cloned.1.call-start = ((), (), s32[]{:S(2)}) async-start(), calls=%async_computation.4 | async-start | bytes 4718592 | tf_op jit(solution)/shard_map/reduce_scatter | solution.py:53
  9.0 9.1 %collective-permute-start.2 = (bf16[2,256,2,128]{3,1,2,0:T(8,128)(2,1)S(1)}, bf16[2,256,2,128]{3,1,2,0:T(8,128)(2,1)S(1)}, u32[]{:S(2)}, u32[]{:S(2)}) collective-permute-start(bf16[2,256,2,128]{3,1,2,0:T(8,128)(2,1)S(1)} %pad_maximum_fusion.1), channel_id=1, source_target_pairs={{0,2},{2,4},{4,6},{6,8},{8,10},{10,12},{12,14},{1,3},{3,5},{5,7},{... | collective-permute-start | bytes 786440 | tf_op jit(solution)/shard_map/ppermute | solution.py:12
  12.2 12.8 %collective-permute-start.1 = (bf16[2,256,2,128]{3,1,2,0:T(8,128)(2,1)S(1)}, bf16[2,256,2,128]{3,1,2,0:T(8,128)(2,1)S(1)}, u32[]{:S(2)}, u32[]{:S(2)}) collective-permute-start(bf16[2,256,2,128]{3,1,2,0:T(8,128)(2,1)S(1)} %pad_maximum_fusion.1), channel_id=1, source_target_pairs={{0,4},{2,6},{4,8},{6,10},{8,12},{10,14},{1,5},{3,7},{5,9},{7,11},{... | collective-permute-start | bytes 786440 | tf_op jit(solution)/shard_map/ppermute | solution.py:12
  15.4 36.3 %collective-permute-start = (bf16[2,256,2,128]{3,1,2,0:T(8,128)(2,1)S(1)}, bf16[2,256,2,128]{3,1,2,0:T(8,128)(2,1)S(1)}, u32[]{:S(2)}, u32[]{:S(2)}) collective-permute-start(bf16[2,256,2,128]{3,1,2,0:T(8,128)(2,1)S(1)} %pad_maximum_fusion.1), channel_id=1, source_target_pairs={{0,6},{2,8},{4,10},{6,12},{8,14},{1,7},{3,9},{5,11},{7,13},{9,15},... | collective-permute-start | bytes 786440 | tf_op jit(solution)/shard_map/ppermute | solution.py:12
  51.7 16.4 %copy-start.7 = (bf16[2,1024,2,128]{3,1,2,0:T(8,128)(2,1)}, bf16[2,1024,2,128]{3,1,2,0:T(8,128)(2,1)S(1)}, u32[]{:S(2)}) copy-start(bf16[2,1024,2,128]{3,1,2,0:T(8,128)(2,1)S(1)} %maximum_maximum_fusion) | copy-start | bytes 3145732
  53.8 4.5 %copy-start.1 = (f32[2,1024,256,6]{2,1,3,0:T(8,128)}, f32[2,1024,256,6]{2,1,3,0:T(8,128)S(1)}, u32[]{:S(2)}) copy-start(f32[2,1024,256,6]{2,1,3,0:T(8,128)S(1)} %get-tuple-element.56) | copy-start | bytes 37748740
  72.0 95.5 %copy-start.10 = (bf16[2,128,6,256]{3,1,2,0:T(8,128)(2,1)}, bf16[2,128,6,256]{3,1,2,0:T(8,128)(2,1)S(1)}, u32[]{:S(2)}) copy-start(bf16[2,128,6,256]{3,1,2,0:T(8,128)(2,1)S(1)} %convolution_convert_fusion) | copy-start | bytes 2359300
  171.3 6.4 %copy-start.15 = (s32[128,2]{0,1:T(2,128)S(1)}, s32[128,2]{0,1:T(2,128)}, u32[]{:S(2)}) copy-start(s32[128,2]{0,1:T(2,128)} %param.15) | copy-start | bytes 3076
  171.3 9.8 %all-to-all-start = ((bf16[1,4,2,64,3072]{4,3,1,0,2:T(8,128)(2,1)}), bf16[1,4,2,64,3072]{4,3,1,0,2:T(8,128)(2,1)}, u32[]{:S(2)}, u32[]{:S(2)}) async-start(bf16[1,4,2,64,3072]{4,3,1,0,2:T(8,128)(2,1)} %copy.124), calls=%async_computation.1 | async-start | bytes 6291456 | tf_op jit(solution)/shard_map/all_to_all | solution.py:70
  177.7 60.4 %all-gather.5.cloned.1.call-start = ((), (), s32[]{:S(2)}) async-start(), calls=%async_computation.5 | async-start | bytes 2359296 | tf_op jit(solution)/shard_map/all_gather | solution.py:98
  188.2 2.1 copy-start.12
  190.3 6.8 %copy-start.3 = (bf16[128,3072]{1,0:T(8,128)(2,1)S(1)}, bf16[128,3072]{1,0:T(8,128)(2,1)}, u32[]{:S(2)}) copy-start(bf16[128,3072]{1,0:T(8,128)(2,1)} %param.12) | copy-start | bytes 2359300
  197.0 1.9 copy-start.14
  197.1 1.9 copy-start.2
  199.4 1.2 copy-start.13
  244.6 10.8 %slice-start = ((s8[6291456]{0:T(1024)(128)(4,1)}), s8[2097152]{0:T(1024)(128)(4,1)S(1)}, s32[]{:S(2)}) async-start(s8[6291456]{0:T(1024)(128)(4,1)} %bitcast.152), calls=%async_computation.6 | async-start | bytes 4194304
  247.3 1.9 copy-start.11
  249.2 6.2 %slice-start.1 = ((s8[6291456]{0:T(1024)(128)(4,1)}), s8[4194304]{0:T(1024)(128)(4,1)S(1)}, s32[]{:S(2)}) async-start(s8[6291456]{0:T(1024)(128)(4,1)} %bitcast.152), calls=%async_computation.7 | async-start | bytes 8388608
  249.2 6.2 %copy-start.8 = (bf16[2,1024,2,128]{3,1,2,0:T(8,128)(2,1)S(1)}, bf16[2,1024,2,128]{3,1,2,0:T(8,128)(2,1)}, u32[]{:S(2)}) copy-start(bf16[2,1024,2,128]{3,1,2,0:T(8,128)(2,1)} %copy-done.7) | copy-start | bytes 3145732
  259.9 19.7 %slice-start.2 = ((s8[6291456]{0:T(1024)(128)(4,1)}), s8[2097152]{0:T(1024)(128)(4,1)S(1)}, s32[]{:S(2)}) async-start(s8[6291456]{0:T(1024)(128)(4,1)} %bitcast.154), calls=%async_computation.8 | async-start | bytes 4194304
  262.3 17.4 %slice-start.3 = ((s8[6291456]{0:T(1024)(128)(4,1)}), s8[4194304]{0:T(1024)(128)(4,1)S(1)}, s32[]{:S(2)}) async-start(s8[6291456]{0:T(1024)(128)(4,1)} %bitcast.154), calls=%async_computation.9 | async-start | bytes 8388608
  267.0 1.2 copy-start.4
  267.8 2.9 copy-start.6
  268.2 11.4 %copy-start.9 = (bf16[2,1024,2,128]{3,1,2,0:T(8,128)(2,1)S(1)}, bf16[2,1024,2,128]{3,1,2,0:T(8,128)(2,1)}, u32[]{:S(2)}) copy-start(bf16[2,1024,2,128]{3,1,2,0:T(8,128)(2,1)} %copy-done.7) | copy-start | bytes 3145732
  270.7 13.2 %collective-permute-start.5 = (bf16[2,256,2,128]{3,2,1,0:T(2,128)(2,1)}, bf16[2,256,2,128]{3,2,1,0:T(2,128)(2,1)S(1)}, u32[]{:S(2)}, u32[]{:S(2)}) collective-permute-start(bf16[2,256,2,128]{3,2,1,0:T(2,128)(2,1)} %get-tuple-element.47), channel_id=1, source_target_pairs={{6,0},{8,2},{10,4},{12,6},{14,8},{7,1},{9,3},{11,5},{13,7},{15,9},... | collective-permute-start | bytes 786440 | tf_op jit(solution)/shard_map/ppermute | solution.py:12
  275.7 11.7 %collective-permute-start.4 = (bf16[2,256,2,128]{3,2,1,0:T(2,128)(2,1)}, bf16[2,256,2,128]{3,2,1,0:T(2,128)(2,1)S(1)}, u32[]{:S(2)}, u32[]{:S(2)}) collective-permute-start(bf16[2,256,2,128]{3,2,1,0:T(2,128)(2,1)} %get-tuple-element.48), channel_id=1, source_target_pairs={{4,0},{6,2},{8,4},{10,6},{12,8},{14,10},{5,1},{7,3},{9,5},{11,7},{... | collective-permute-start | bytes 786440 | tf_op jit(solution)/shard_map/ppermute | solution.py:12
  277.7 22.2 %collective-permute-start.3 = (bf16[2,256,2,128]{3,2,1,0:T(2,128)(2,1)}, bf16[2,256,2,128]{3,2,1,0:T(2,128)(2,1)}, u32[]{:S(2)}, u32[]{:S(2)}) collective-permute-start(bf16[2,256,2,128]{3,2,1,0:T(2,128)(2,1)} %get-tuple-element.46), channel_id=1, source_target_pairs={{2,0},{4,2},{6,4},{8,6},{10,8},{12,10},{14,12},{3,1},{5,3},{7,5},{... | collective-permute-start | bytes 786440 | tf_op jit(solution)/shard_map/ppermute | solution.py:12
  281.6 18.3 %copy-start.5 = (f32[1024,2,128]{2,1,0:T(2,128)S(1)}, f32[1024,2,128]{2,1,0:T(2,128)}, u32[]{:S(2)}) copy-start(f32[1024,2,128]{2,1,0:T(2,128)} %copy.160) | copy-start | bytes 3145732
Sparse Core Ops, SparseCore 0:
  10.2 149.2 all-gather.2
  167.7 12.9 reduce-scatter.1
  203.0 11.6 all-gather.4
where the time goes:
time: 314 us; the launch traced here: 309 us
  waiting for transfers between devices  139 us (44%)
  local copies, waits for them, and re-layouts  47.4 us (15%)
  matrix products  45.7 us (15%)
  other arithmetic  31 us (10%)
  starting transfers between devices  23.9 us (8%)
  between operations  14.4 us (5%)
  blocking collectives  7.54 us (2%)
    all_gather x1, waiting for transfers between devices, local(): wo_full = lax.all_gather(w_out, 'ctx', axis=1, tiled=True)  87.5 us
    ppermute x6, waiting for transfers between devices, passed_along(): lax.ppermute(value, axis, [(source, source + steps) for source in range(i...  49.6 us
    mul x3, local copies, waits for them, and re-layouts, local(): gates[:, :, None] * dyf[:, None, :]  19.5 us
    ppermute x6, starting transfers between devices, passed_along(): lax.ppermute(value, axis, [(source, source + steps) for source in range(i...  17.4 us
    unnamed x45, local copies, waits for them, and re-layouts  13.3 us
    convert_element_type x1, other arithmetic, local(): probs = lax.optimization_barrier(jnp.exp(scores - lse).astype(jnp.bfloat16))  9.87 us
    dot_general x1, matrix products, local(): jnp.einsum('thd,hdj->tj', attn_flat, wo_full, preferred_element_type=jnp....  8 us
    all_to_all x1, blocking collectives, local(): lax.all_to_all(outgoing, 'exp', split_axis=1, concat_axis=2, tiled=True)  7.54 us
  transfers between devices with their start and end apart: 10, of which 7 were waited for; matrix products, arithmetic and copies ran while one was open for 24% of the time, Pallas kernels for 0%

commit v1 on v0

v1 whole, which is shorter than its diff:
```python
import functools

import jax
import jax.numpy as jnp
from jax import lax
from jax.experimental import pallas as pl
from jax.experimental.pallas import tpu as pltpu
from jax.sharding import PartitionSpec as P

BAND_BLOCKS = 4
F32 = jnp.float32
BF16 = jnp.bfloat16
VMEM_LIMIT = 48 * 1024 * 1024


def params(limit=VMEM_LIMIT):
    return pltpu.CompilerParams(vmem_limit_bytes=limit)


def cost(flops, nbytes, exps=0):
    return pl.CostEstimate(flops=flops, bytes_accessed=nbytes, transcendentals=exps)


def dot_nn(a, b):
    return lax.dot_general(a, b, (((1,), (0,)), ((), ())), preferred_element_type=F32)


def dot_nt(a, b):
    return lax.dot_general(a, b, (((1,), (1,)), ((), ())), preferred_element_type=F32)


def dot_tn(a, b):
    return lax.dot_general(a, b, (((0,), (0,)), ((), ())), preferred_element_type=F32)


def passed_along(value, axis, steps):
    count = lax.axis_size(axis)
    initial, last = (max(0, -steps), min(count, count - steps))
    return lax.ppermute(value, axis, [(source, source + steps) for source in range(initial, last)])


def swapped(value, axis):
    return lax.ppermute(value, axis, [(0, 1), (1, 0)])


def gathered(w_out):
    heads, depth, _ = w_out.shape
    count = lax.axis_size("ctx")
    place = lax.axis_index("ctx")
    if count != 8 or lax.axis_size("groups") != 2 or heads % 3:
        full = lax.all_gather(w_out, "ctx", axis=1, tiled=True)
        return [full], jnp.zeros((1,), jnp.int32), [(0, 0, heads, 0, 0)]
    side = lax.axis_index("groups")
    third = heads // 3
    mine = lax.dynamic_slice_in_dim(w_out, side * third, third, 0)
    ring = [(c, (c + 2) % count) for c in range(count)]
    pairs = [(c, c ^ 1) for c in range(count)]
    held = [jnp.concatenate([mine, w_out[2 * third :]], axis=0)]
    arrays, plan = [w_out], [(0, 0, heads, 0, 4)]
    table = [0, side * third, (1 - side) * third, 2 * third]
    table += [depth * ((place - 2 * k) % count) for k in range(4)]
    table += [depth * (((place - 2 * k) % count) ^ 1) for k in range(4)]

    def add(array, parts, row):
        arrays.append(array)
        for start, size, head in parts:
            plan.append((len(arrays) - 1, start, size, head, row))

    both = [(0, third, 1), (third, third, 3)]
    for k in range(1, 4):
        held.append(lax.ppermute(held[-1], "ctx", ring))
        add(held[k], both, 4 + k)
        add(swapped(held[k][:third], "groups"), [(0, third, 2)], 4 + k)
    for k in range(3):
        across = lax.ppermute(held[k], "ctx", pairs)
        add(across, both, 8 + k)
        add(swapped(across[:third], "groups"), [(0, third, 2)], 8 + k)
    across = lax.ppermute(held[3][:third], "ctx", pairs)
    add(across, [(0, third, 1)], 11)
    add(swapped(across, "groups"), [(0, third, 2)], 11)
    add(lax.ppermute(held[3][third:], "ctx", pairs), [(0, third, 3)], 11)
    return arrays, jnp.stack([jnp.asarray(t, jnp.int32) for t in table]), plan


def piece_copies(plan, table, pieces, buf, sem, chunk, chunk_size):
    copies = []
    columns = pl.ds(pl.multiple_of(chunk * chunk_size, chunk_size), chunk_size)
    depth_of = [p.shape[1] for p in pieces]
    for number, (array, start, size, head, row) in enumerate(plan):
        rows = pl.ds(pl.multiple_of(table[row], depth_of[array]), depth_of[array])
        copies.append(
            pltpu.make_async_copy(
                pieces[array].at[pl.ds(start, size), :, columns],
                buf.at[pl.ds(table[head], size), rows, columns],
                sem.at[number, chunk],
            )
        )
    return copies


CHUNKS = 3


def wait_chunk(plan, table, pieces, buf, sem, width):
    step = pl.program_id(0)
    size = width // CHUNKS

    @pl.when(step == 0)
    def _():
        for chunk in range(CHUNKS):
            for copy in piece_copies(plan, table, pieces, buf, sem, chunk, size):
                copy.start()

    for copy in piece_copies(plan, table, pieces, buf, sem, step, size):
        copy.wait()
    return pl.ds(pl.multiple_of(step * size, size), size)


def project_kernel(plan, count, table, core, attn, *refs):
    pieces, (own, other, buf, sem) = refs[:count], refs[count:]
    heads, head_dim, width = buf.shape
    columns = wait_chunk(plan, table, pieces, buf, sem, width)
    weights = buf[:, :, columns].reshape(heads * head_dim, width // CHUNKS)
    result = dot_nn(attn[...], weights)
    rows = own.shape[0]

    @pl.when(core[0] == 0)
    def _():
        own[...] = result[:rows]
        other[...] = result[rows:]

    @pl.when(core[0] != 0)
    def _():
        own[...] = result[rows:]
        other[...] = result[:rows]


def project(attn, arrays, table, plan, core, heads, head_dim, width, rows):
    tok = attn.shape[0]
    size = width // CHUNKS
    return pl.pallas_call(
        functools.partial(project_kernel, plan, len(arrays)),
        grid_spec=pltpu.PrefetchScalarGridSpec(
            num_scalar_prefetch=2,
            grid=(CHUNKS,),
            in_specs=[pl.BlockSpec((tok, heads * head_dim), lambda i, *_: (0, 0))]
            + [pl.BlockSpec(memory_space=pltpu.HBM)] * len(arrays),
            out_specs=[pl.BlockSpec((rows, size), lambda i, *_: (0, i))] * 2,
            scratch_shapes=[
                pltpu.VMEM((heads, head_dim, width), BF16),
                pltpu.SemaphoreType.DMA((len(plan), CHUNKS)),
            ],
        ),
        out_shape=[jax.ShapeDtypeStruct((rows, width), F32)] * 2,
        compiler_params=params(),
        cost_estimate=cost(2 * tok * heads * head_dim * width, 2 * heads * head_dim * width),
        name="project",
    )(table, core, attn, *arrays)


def dattn_kernel(plan, count, table, core, own, recv, *refs):
    pieces, (out, grad, acc, buf, sem) = refs[:count], refs[count:]
    heads, head_dim, width = buf.shape
    rows = own.shape[0]
    step = pl.program_id(0)

    @pl.when(core[0] == 0)
    def _():
        grad[:rows] = own[...]
        grad[rows:] = recv[...]

    @pl.when(core[0] != 0)
    def _():
        grad[rows:] = own[...]
        grad[:rows] = recv[...]

    columns = wait_chunk(plan, table, pieces, buf, sem, width)
    weights = buf[:, :, columns].reshape(heads * head_dim, width // CHUNKS)
    part = dot_nt(grad[...], weights)

    @pl.when(step == 0)
    def _():
        acc[...] = part

    @pl.when(step > 0)
    def _():
        acc[...] += part

    @pl.when(step == CHUNKS - 1)
    def _():
        out[...] = acc[...].astype(BF16)


def dattention(own, recv, arrays, table, plan, core, heads, head_dim, width):
    rows = own.shape[0]
    size = width // CHUNKS
    return pl.pallas_call(
        functools.partial(dattn_kernel, plan, len(arrays)),
        grid_spec=pltpu.PrefetchScalarGridSpec(
            num_scalar_prefetch=2,
            grid=(CHUNKS,),
            in_specs=[pl.BlockSpec((rows, size), lambda i, *_: (0, i))] * 2
            + [pl.BlockSpec(memory_space=pltpu.HBM)] * len(arrays),
            out_specs=pl.BlockSpec((2 * rows, heads * head_dim), lambda i, *_: (0, 0)),
            scratch_shapes=[
                pltpu.VMEM((2 * rows, size), BF16),
                pltpu.VMEM((2 * rows, heads * head_dim), F32),
                pltpu.VMEM((heads, head_dim, width), BF16),
                pltpu.SemaphoreType.DMA((len(plan), CHUNKS)),
            ],
        ),
        out_shape=jax.ShapeDtypeStruct((2 * rows, heads * head_dim), BF16),
        compiler_params=params(),
        cost_estimate=cost(4 * rows * heads * head_dim * width, 2 * heads * head_dim * width),
        name="dattention",
    )(table, core, own, recv, *arrays)


def band_of(refs):
    return jnp.concatenate([r[...] for r in refs], axis=0)


def attention_kernel(scale, place, q, *refs):
    keys, values, (attn, probs) = refs[:BAND_BLOCKS], refs[BAND_BLOCKS : 2 * BAND_BLOCKS], refs[-2:]
    tok = q.shape[0]
    scores = dot_nt(q[...], band_of(keys)) * scale
    shape = scores.shape
    row = lax.broadcasted_iota(jnp.int32, shape, 0)
    column = lax.broadcasted_iota(jnp.int32, shape, 1)
    offset = column - (BAND_BLOCKS - 1) * tok
    admitted = (offset <= row) & (offset + place[0] * tok >= 0)
    scores = jnp.where(admitted, scores, -1e30)
    top = jnp.max(scores, axis=-1, keepdims=True)
    grown = jnp.exp(scores - top)
    weight = (grown * (1.0 / jnp.sum(grown, axis=-1, keepdims=True))).astype(BF16)
    probs[0] = weight
    attn[...] = dot_nn(weight, band_of(values)).astype(BF16)


def attention(queries, bands, place, heads, heads_kv, head_dim, scale):
    tok = queries.shape[0]
    group = heads // heads_kv
    keys = pl.BlockSpec((tok, head_dim), lambda h, *_: (0, h // group))
    values = pl.BlockSpec((tok, head_dim), lambda h, *_: (0, heads_kv + h // group))
    per_head = pl.BlockSpec((tok, head_dim), lambda h, *_: (0, h))
    span = BAND_BLOCKS * tok
    return pl.pallas_call(
        functools.partial(attention_kernel, scale),
        grid_spec=pltpu.PrefetchScalarGridSpec(
            num_scalar_prefetch=1,
            grid=(heads,),
            in_specs=[per_head] + [keys] * BAND_BLOCKS + [values] * BAND_BLOCKS,
            out_specs=[per_head, pl.BlockSpec((1, tok, span), lambda h, *_: (h, 0, 0))],
        ),
        out_shape=[
            jax.ShapeDtypeStruct((tok, heads * head_dim), BF16),
            jax.ShapeDtypeStruct((heads, tok, span), BF16),
        ],
        compiler_params=params(),
        cost_estimate=cost(4 * tok * span * heads * head_dim, 2 * heads * tok * span, heads * tok * span),
        name="attention",
    )(place, queries, *bands, *bands)


def attention_grad_kernel(scale, group, heads_kv, q, dout, attn, probs, *refs):
    keys, values = refs[:BAND_BLOCKS], refs[BAND_BLOCKS : 2 * BAND_BLOCKS]
    dq, outs, (dk, dv) = refs[2 * BAND_BLOCKS], refs[2 * BAND_BLOCKS + 1 : -2], refs[-2:]
    tok, head_dim = q.shape
    head = pl.program_id(0)
    grad = dout[...]
    weight = probs[0]
    delta = jnp.sum(grad.astype(F32) * attn[...].astype(F32), axis=-1, keepdims=True)
    dprob = dot_nt(grad, band_of(values))
    dscore = (weight.astype(F32) * (dprob - delta)).astype(BF16)
    dq[...] = (dot_nn(dscore, band_of(keys)) * scale).astype(BF16)
    dkey = dot_tn(dscore, q[...])
    dvalue = dot_tn(weight, grad)

    @pl.when(head % group == 0)
    def _():
        dk[...] = dkey
        dv[...] = dvalue

    @pl.when(head % group > 0)
    def _():
        dk[...] += dkey
        dv[...] += dvalue

    @pl.when(head % group == group - 1)
    def _():
        lanes_k = pl.ds(pl.multiple_of(head // group * head_dim, head_dim), head_dim)
        lanes_v = pl.ds(pl.multiple_of((heads_kv + head // group) * head_dim, head_dim), head_dim)
        for block, out in enumerate(outs):
            rows = pl.ds(block * tok, tok)
            out[:, lanes_k] = (dk[rows, :] * scale).astype(out.dtype)
            out[:, lanes_v] = dv[rows, :].astype(out.dtype)


def attention_grad(queries, dout, attn, probs, bands, heads, heads_kv, head_dim, scale):
    tok = queries.shape[0]
    group = heads // heads_kv
    keys = pl.BlockSpec((tok, head_dim), lambda h: (0, h // group))
    values = pl.BlockSpec((tok, head_dim), lambda h: (0, heads_kv + h // group))
    per_head = pl.BlockSpec((tok, head_dim), lambda h: (0, h))
    span = BAND_BLOCKS * tok
    lanes = 2 * heads_kv * head_dim
    whole = pl.BlockSpec((tok, lanes), lambda h: (0, 0))
    return pl.pallas_call(
        functools.partial(attention_grad_kernel, scale, group, heads_kv),
        grid=(heads,),
        in_specs=[per_head] * 3
        + [pl.BlockSpec((1, tok, span), lambda h: (h, 0, 0))]
        + [keys] * BAND_BLOCKS
        + [values] * BAND_BLOCKS,
        out_specs=[per_head] + [whole] * BAND_BLOCKS,
        out_shape=[jax.ShapeDtypeStruct((tok, heads * head_dim), BF16)]
        + [jax.ShapeDtypeStruct((tok, lanes), BF16)] * (BAND_BLOCKS - 1)
        + [jax.ShapeDtypeStruct((tok, lanes), F32)],
        scratch_shapes=[pltpu.VMEM((span, head_dim), F32)] * 2,
        compiler_params=params(),
        cost_estimate=cost(8 * tok * span * heads * head_dim, 2 * heads * tok * span),
        name="attention_grad",
    )(queries, dout, attn, probs, *bands, *bands)


def pick_kernel(slots, here, there, gout, first, second, dgate):
    step = pl.program_id(0)
    rows, width = gout.shape
    room = here.shape[0]
    column = lax.broadcasted_iota(jnp.int32, (rows, room), 1)
    grad = gout[...].astype(F32)
    sums = []
    for i, out in enumerate((first, second)):
        near = (slots[:, i : i + 1] == column).astype(BF16)
        far = (slots[:, i : i + 1] == column + room).astype(BF16)
        row = dot_nn(near, here[...]) + dot_nn(far, there[...])
        out[...] = row.astype(BF16)
        sums.append(jnp.sum(grad * row, axis=-1, keepdims=True))
    lane = lax.broadcasted_iota(jnp.int32, dgate.shape, 1)
    total = jnp.where(lane == 0, sums[0], jnp.where(lane == 1, sums[1], 0.0))

    @pl.when(step == 0)
    def _():
        dgate[...] = total

    @pl.when(step > 0)
    def _():
        dgate[...] += total


def pick(slots, here, there, grad_out):
    rows, width = grad_out.shape
    room = here.shape[0]
    size = width // CHUNKS
    by_column = lambda n: pl.BlockSpec((n, size), lambda i: (0, i))
    return pl.pallas_call(
        pick_kernel,
        grid=(CHUNKS,),
        in_specs=[pl.BlockSpec((rows, 2), lambda i: (0, 0)), by_column(room), by_column(room), by_column(rows)],
        out_specs=[by_column(rows), by_column(rows), pl.BlockSpec((rows, 128), lambda i: (0, 0))],
        out_shape=[jax.ShapeDtypeStruct((rows, width), BF16)] * 2 + [jax.ShapeDtypeStruct((rows, 128), F32)],
        compiler_params=params(),
        cost_estimate=cost(8 * rows * room * width, 8 * rows * width + 4 * room * width),
        name="pick",
    )(slots, here, there, grad_out)


def middle_kernel(routes, own, recv, stream, first, second, gout, dgate, router, router_t, mixed, grad, gates):
    resid = stream[...].astype(F32) + (own[...] + recv[...])
    inverse = lax.rsqrt(jnp.mean(resid * resid, axis=-1, keepdims=True) + 1e-05)
    normed = (resid * inverse).astype(BF16)
    logits = dot_nn(normed, router[...])
    lane = lax.broadcasted_iota(jnp.int32, logits.shape, 1)
    is_first, is_second = lane == routes[:, 0:1], lane == routes[:, 1:2]
    chosen_first = jnp.sum(jnp.where(is_first, logits, 0.0), axis=-1, keepdims=True)
    chosen_second = jnp.sum(jnp.where(is_second, logits, 0.0), axis=-1, keepdims=True)
    gate_first = 1.0 / (1.0 + jnp.exp(chosen_second - chosen_first))
    gate_second = 1.0 - gate_first
    mixed[...] = (
        resid + gate_first * first[...].astype(F32) + gate_second * second[...].astype(F32)
    ).astype(BF16)
    d_first, d_second = dgate[:, 0:1], dgate[:, 1:2]
    common = gate_first * d_first + gate_second * d_second
    dlogit = jnp.where(is_first, gate_first * (d_first - common), 0.0)
    dlogit = dlogit + jnp.where(is_second, gate_second * (d_second - common), 0.0)
    high = dlogit.astype(BF16)
    rest = dlogit - high.astype(F32)
    middle = rest.astype(BF16)
    low = (rest - middle.astype(F32)).astype(BF16)
    weights = router_t[...]
    dnormed = dot_nn(high, weights) + (dot_nn(middle, weights) + dot_nn(low, weights))
    mean = jnp.mean(dnormed * resid, axis=-1, keepdims=True)
    grad[...] = (
        gout[...].astype(F32) + inverse * dnormed - resid * (inverse * inverse * inverse * mean)
    ).astype(BF16)
    gates[...] = jnp.where(lane == 0, gate_first, jnp.where(lane == 1, gate_second, 0.0))


def middle(routes, own, recv, stream, first, second, grad_out, dgate, router, router_t):
    rows, width = stream.shape
    size = 32 if rows % 32 == 0 else rows
    by_row = lambda n: pl.BlockSpec((size, n), lambda i: (i, 0))
    whole = lambda a: pl.BlockSpec(a.shape, lambda i: (0, 0))
    return pl.pallas_call(
        middle_kernel,
        grid=(rows // size,),
        in_specs=[by_row(2)] + [by_row(width)] * 6 + [by_row(128), whole(router), whole(router_t)],
        out_specs=[by_row(width), by_row(width), by_row(128)],
        out_shape=[jax.ShapeDtypeStruct((rows, width), BF16)] * 2 + [jax.ShapeDtypeStruct((rows, 128), F32)],
        compiler_params=params(),
        cost_estimate=cost(2 * rows * 128 * width * 4, 20 * rows * width),
        name="middle",
    )(routes, own, recv, stream, first, second, grad_out, dgate, router, router_t)


def spread_kernel(slots, gates, gout, here, there):
    room = here.shape[0]
    rows = gout.shape[0]
    place = lax.broadcasted_iota(jnp.int32, (room, rows), 0)
    grad = gout[...].astype(F32)
    near, far = 0.0, 0.0
    for i in range(2):
        part = (gates[:, i : i + 1] * grad).astype(BF16)
        near = near + dot_nn((slots[i : i + 1, :] == place).astype(BF16), part)
        far = far + dot_nn((slots[i : i + 1, :] == place + room).astype(BF16), part)
    here[...] = near.astype(BF16)
    there[...] = far.astype(BF16)


def spread(slots_t, gates, grad_out, room):
    rows, width = grad_out.shape
    size = width // CHUNKS
    by_column = lambda n: pl.BlockSpec((n, size), lambda i: (0, i))
    return pl.pallas_call(
        spread_kernel,
        grid=(CHUNKS,),
        in_specs=[
            pl.BlockSpec((2, rows), lambda i: (0, 0)),
            pl.BlockSpec((rows, 128), lambda i: (0, 0)),
            by_column(rows),
        ],
        out_specs=[by_column(room)] * 2,
        out_shape=[jax.ShapeDtypeStruct((room, width), BF16)] * 2,
        compiler_params=params(),
        cost_estimate=cost(8 * rows * room * width, 2 * rows * width + 4 * room * width),
        name="spread",
    )(slots_t, gates, grad_out)


def local(
    queries_in, rotated_keys, value_inputs, stream_in, w_out, w_router, routes, expert_out, grad_out
):
    place = lax.axis_index("ctx")
    core = lax.axis_index("exp")
    tok, heads_q, head_dim = queries_in.shape
    heads_kv = rotated_keys.shape[1]
    rows, width = stream_in.shape
    experts = w_router.shape[1]
    held, capacity = expert_out.shape[1], expert_out.shape[3]
    room = held * capacity
    scale = head_dim ** (-0.5)
    core_arg = core.astype(jnp.int32).reshape(1)
    place_arg = place.astype(jnp.int32).reshape(1)

    arrays, table, plan = gathered(w_out)

    own_band = jnp.concatenate(
        [rotated_keys.reshape(tok, heads_kv * head_dim), value_inputs.reshape(tok, heads_kv * head_dim)], axis=1
    )
    bands = [own_band] + [passed_along(own_band, "ctx", step) for step in range(1, BAND_BLOCKS)]
    bands = bands[::-1]

    sent = lax.dynamic_index_in_dim(expert_out[0], 1 - core, 1, keepdims=False).reshape(room, width)
    kept = lax.dynamic_index_in_dim(expert_out[0], core, 1, keepdims=False).reshape(room, width)
    arrived = swapped(sent, "exp")
    flat = routes.reshape(-1)
    number = jnp.arange(2 * rows, dtype=jnp.int32)
    earlier = (flat[None, :] == flat[:, None]) & (number[None, :] < number[:, None])
    rank = jnp.sum(earlier.astype(jnp.int32), axis=1)
    slots = (flat * capacity + rank - core * room) % (experts * capacity)
    slots = slots.reshape(rows, 2)
    first, second, dgate = pick(slots, kept, arrived, grad_out)

    queries = queries_in.reshape(tok, heads_q * head_dim)
    attn, probs = attention(queries, bands, place_arg, heads_q, heads_kv, head_dim, scale)

    own, other = project(attn, arrays, table, plan, core_arg, heads_q, head_dim, width, rows)
    router = jnp.pad(w_router, ((0, 0), (0, 128 - experts)))
    mixed, grad_input, gates = middle(
        routes, own, swapped(other, "exp"), stream_in, first, second, grad_out, dgate, router, router.T
    )
    grad_other = swapped(grad_input, "exp")
    here, there = spread(slots.T, gates, grad_out, room)
    back = swapped(there, "exp").reshape(held, 1, capacity, width)
    here = here.reshape(held, 1, capacity, width)
    grad_expert = jnp.where(
        core == 0, jnp.concatenate([here, back], axis=1), jnp.concatenate([back, here], axis=1)
    )[None]

    dattn = dattention(grad_input, grad_other, arrays, table, plan, core_arg, heads_q, head_dim, width)
    grads = attention_grad(queries, dattn, attn, probs, bands, heads_q, heads_kv, head_dim, scale)
    grad_q = grads[0].reshape(tok, heads_q, head_dim)
    total = grads[BAND_BLOCKS]
    for step in range(1, BAND_BLOCKS):
        total = total + passed_along(grads[BAND_BLOCKS - step], "ctx", -step).astype(F32)
    total = total.astype(BF16).reshape(tok, 2, heads_kv, head_dim)
    return (mixed, grad_input, grad_expert, grad_q, total[:, 0], total[:, 1])


def solution(mesh):
    in_specs = (
        P(("groups", "ctx"), "exp", None),
        P(("groups", "ctx"), "exp", None),
        P(("groups", "ctx"), "exp", None),
        P(("groups", "ctx", "exp"), None),
        P("exp", "ctx", None),
        P(),
        P(("groups", "ctx", "exp"), None),
        P(("groups", "ctx"), "exp", None, None, None),
        P(("groups", "ctx", "exp"), None),
    )
    out_specs = (
        P(("groups", "ctx", "exp"), None),
        P(("groups", "ctx", "exp"), None),
        P(("groups", "ctx"), "exp", None, None, None),
        P(("groups", "ctx"), "exp", None),
        P(("groups", "ctx"), "exp", None),
        P(("groups", "ctx"), "exp", None),
    )
    return jax.shard_map(local, mesh=mesh, in_specs=in_specs, out_specs=out_specs, check_vma=False)
```

time: 314 us -> 213 us (0.68)
  the two profiles are of different devices: /device:TPU:15 before, /device:TPU:4 now
where the time goes in v1:
time: 213 us; the launch traced here: 212 us
  waiting for transfers between devices  95 us (45%)
  Pallas kernels  53.5 us (25%)
  starting transfers between devices  31.4 us (15%)
  local copies, waits for them, and re-layouts  25.2 us (12%)
  other arithmetic  5.17 us (2%)
    ppermute x3, waiting for transfers between devices, gathered(): held.append(lax.ppermute(held[-1], 'ctx', ring))  45 us
    ppermute x6, waiting for transfers between devices, passed_along(): lax.ppermute(value, axis, [(source, source + steps) for source in range(i...  28.8 us
    ppermute x6, starting transfers between devices, passed_along(): lax.ppermute(value, axis, [(source, source + steps) for source in range(i...  16.4 us
    pallas_call x1, Pallas kernels, attention_grad(): pl.pallas_call(functools.partial(attention_grad_kernel, scale, group, hea...  13.6 us
    pallas_call x1, Pallas kernels, attention(): pl.pallas_call(functools.partial(attention_kernel, scale), grid_spec=pltp...  12.4 us
    ppermute x3, waiting for transfers between devices, gathered(): across = lax.ppermute(held[k], 'ctx', pairs)  11.4 us
    ppermute x11, waiting for transfers between devices, swapped(): return lax.ppermute(value, axis, [(0, 1), (1, 0)])  9.76 us
    unnamed x91, local copies, waits for them, and re-layouts  9.42 us
  transfers between devices with their start and end apart: 25, of which 12 were waited for; matrix products, arithmetic and copies ran while one was open for 10% of the time, Pallas kernels for 22%

profile of v1, /device:TPU:4, one launch (start us, length us, event | category | flops | bytes accessed | tf_op | source)
XLA Modules:
  0.0 211.6 jit_solution(14059809811074596577)
XLA Ops:
  2.0 1.6 collective-permute-start.3
  3.6 19.6 %collective-permute-done.3.refs_1_ = bf16[8,16,3072]{2,1,0:T(8,128)(2,1)S(1)} collective-permute-done((bf16[8,16,3072]{2,1,0:T(8,128)(2,1)S(1)}, bf16[8,16,3072]{2,1,0:T(8,128)(2,1)S(1)}, u32[]{:S(2)}, u32[]{:S(2)}) %collective-permute-start.3) | collective-permute-done | bytes 786464 | tf_op jit(solution)/shard_map/ppermute | solution.py:71
  23.7 19.8 %collective-permute-done.5.refs_3_ = bf16[8,16,3072]{2,1,0:T(8,128)(2,1)S(1)} collective-permute-done((bf16[8,16,3072]{2,1,0:T(8,128)(2,1)S(1)}, bf16[8,16,3072]{2,1,0:T(8,128)(2,1)S(1)}, u32[]{:S(2)}, u32[]{:S(2)}) %collective-permute-start.5) | collective-permute-done | bytes 786464 | tf_op jit(solution)/shard_map/ppermute | solution.py:71
  44.3 3.1 %collective-permute-start = (bf16[256,512]{1,0:T(8,128)(2,1)S(1)}, bf16[256,512]{1,0:T(8,128)(2,1)S(1)}, u32[]{:S(2)}, u32[]{:S(2)}) collective-permute-start(bf16[256,512]{1,0:T(8,128)(2,1)S(1)} %bitcast_dynamic-update-slice_fusion.refs_3_.refs_7_), channel_id=1, source_target_pairs={{0,6},{2,8},{4,10},{6,12},{8,14},{1,7},{3,9},{5,11},{7,13},{9,15},... | collective-permute-start | bytes 786440 | tf_op jit(solution)/shard_map/ppermute | solution.py:39
  47.4 5.9 %collective-permute-start.1 = (bf16[256,512]{1,0:T(8,128)(2,1)S(1)}, bf16[256,512]{1,0:T(8,128)(2,1)S(1)}, u32[]{:S(2)}, u32[]{:S(2)}) collective-permute-start(bf16[256,512]{1,0:T(8,128)(2,1)S(1)} %bitcast_dynamic-update-slice_fusion.refs_3_.refs_7_), channel_id=1, source_target_pairs={{0,4},{2,6},{4,8},{6,10},{8,12},{10,14},{1,5},{3,7},{5,9},{7,11},{... | collective-permute-start | bytes 786440 | tf_op jit(solution)/shard_map/ppermute | solution.py:39
  54.0 1.5 collective-permute-start.4
  57.1 5.7 %collective-permute-done.7.refs_5_ = bf16[8,16,3072]{2,1,0:T(8,128)(2,1)S(1)} collective-permute-done((bf16[8,16,3072]{2,1,0:T(8,128)(2,1)S(1)}, bf16[8,16,3072]{2,1,0:T(8,128)(2,1)S(1)}, u32[]{:S(2)}, u32[]{:S(2)}) %collective-permute-start.7) | collective-permute-done | bytes 786464 | tf_op jit(solution)/shard_map/ppermute | solution.py:71
  64.8 2.3 %collective-permute-done.refs_0_.refs_4_ = bf16[256,512]{1,0:T(8,128)(2,1)S(1)} collective-permute-done((bf16[256,512]{1,0:T(8,128)(2,1)S(1)}, bf16[256,512]{1,0:T(8,128)(2,1)S(1)}, u32[]{:S(2)}, u32[]{:S(2)}) %collective-permute-start) | collective-permute-done | bytes 262176 | tf_op jit(solution)/shard_map/ppermute | solution.py:39
  67.1 1.5 collective-permute-start.10
  70.0 1.5 collective-permute-start.6
  72.0 11.3 %collective-permute-done.13.refs_11_ = bf16[8,16,3072]{2,1,0:T(8,128)(2,1)} collective-permute-done((bf16[8,16,3072]{2,1,0:T(8,128)(2,1)S(1)}, bf16[8,16,3072]{2,1,0:T(8,128)(2,1)}, u32[]{:S(2)}, u32[]{:S(2)}) %collective-permute-start.13) | collective-permute-done | bytes 786464 | tf_op jit(solution)/shard_map/ppermute | solution.py:75
  83.4 3.0 %collective-permute-start.2 = (bf16[256,512]{1,0:T(8,128)(2,1)S(1)}, bf16[256,512]{1,0:T(8,128)(2,1)}, u32[]{:S(2)}, u32[]{:S(2)}) collective-permute-start(bf16[256,512]{1,0:T(8,128)(2,1)S(1)} %bitcast_dynamic-update-slice_fusion.refs_3_.refs_7_), channel_id=1, source_target_pairs={{0,2},{2,4},{4,6},{6,8},{8,10},{10,12},{12,14},{1,3},{3,5},{5,7},{... | collective-permute-start | bytes 786440 | tf_op jit(solution)/shard_map/ppermute | solution.py:39
  86.5 2.3 %copy.42 = bf16[256,12,128]{0,2,1:T(8,128)(2,1)} copy(bf16[256,12,128]{2,0,1:T(8,128)(2,1)} %param.9) | data formatting | bytes 1572864 | tf_op args[0]
  88.8 2.3 %copy.43.q = bf16[256,1536]{1,0:T(8,128)(2,1)} copy(bf16[256,1536]{0,1:T(8,128)(2,1)} %bitcast.43) | data formatting | bytes 1572864 | tf_op jit(solution)/shard_map/reshape | solution.py:484
  93.6 1.5 collective-permute-start.12
  98.4 1.5 collective-permute-start.14
  100.5 3.4 %constant_dynamic-slice_fusion = (bf16[1,4,1,64,3072]{4,3,2,1,0:T(8,128)(2,1)}, bf16[1,4,1,64,3072]{4,3,2,1,0:T(8,128)(2,1)S(1)}) fusion(bf16[1,4,2,64,3072]{4,3,2,1,0:T(8,128)(2,1)} %param.16, s32[]{:T(128)S(6)} %select_n.66, s32[]{:T(128)S(6)} %select_n.65), kind=kLoop, calls=%fused_computation.15 | loop fusion | bytes 6291464 | tf_op jit(solution)/shard_map/jit(dynamic_index_in_dim)/dynamic_slice | solution.py:473
  103.9 12.4 %attention.1 = (bf16[256,1536]{1,0:T(8,128)(2,1)S(1)}, bf16[12,256,1024]{2,1,0:T(8,128)(2,1)}) custom-call(s32[1]{0:T(128)} %bitcast.11.place, bf16[256,1536]{1,0:T(8,128)(2,1)S(1)} %copy-done.20, bf16[256,512]{1,0:T(8,128)(2,1)S(1)} %copy-done.32, bf16[256,512]{1,0:T(8,128)(2,1)S(1)} %copy-done.35, bf16[256,512]{1,0:T(8,128)(2,1)} %collective-permute-done.2.refs_2_.refs_6_, ...), custom_call_target="tpu_custom_call" | custom-call | flops 1610612736 | bytes 6291456 | tf_op jit(solution)/shard_map/attention/pallas_call | solution.py:247
  116.4 5.5 %collective-permute-done.14.refs_12_ = bf16[4,16,3072]{2,1,0:T(8,128)(2,1)S(1)} collective-permute-done((bf16[4,16,3072]{2,1,0:T(8,128)(2,1)S(1)}, bf16[4,16,3072]{2,1,0:T(8,128)(2,1)S(1)}, u32[]{:S(2)}, u32[]{:S(2)}) %collective-permute-start.14) | collective-permute-done | bytes 393248 | tf_op jit(solution)/shard_map/ppermute | solution.py:43
  122.0 4.2 %collective-permute-done.16.refs_14_ = bf16[4,16,3072]{2,1,0:T(8,128)(2,1)S(1)} collective-permute-done((bf16[4,16,3072]{2,1,0:T(8,128)(2,1)}, bf16[4,16,3072]{2,1,0:T(8,128)(2,1)S(1)}, u32[]{:S(2)}, u32[]{:S(2)}) %collective-permute-start.16) | collective-permute-done | bytes 393248 | tf_op jit(solution)/shard_map/ppermute | solution.py:43
  126.2 7.0 %project.1 = (f32[128,3072]{1,0:T(8,128)}, f32[128,3072]{1,0:T(8,128)}) custom-call(s32[12]{0:T(128)S(1)} %stack.43.table, s32[1]{0:T(128)} %bitcast.10.core, bf16[256,1536]{1,0:T(8,128)(2,1)S(1)} %get-tuple-element.23.attn, bf16[12,16,3072]{2,1,0:T(8,128)(2,1)} %refs_0_.3, bf16[8,16,3072]{2,1,0:T(8,128)(2,1)S(1)} %collective-permute-done.3.refs_1_, ...), custom_call_target="tpu_custom_call" | custom-call | flops 2415919104 | bytes 9437184 | tf_op jit(solution)/shard_map/project/pallas_call | solution.py:141
  137.0 3.5 %pick.1 = (bf16[128,3072]{1,0:T(8,128)(2,1)S(1)}, bf16[128,3072]{1,0:T(8,128)(2,1)S(1)}, f32[128,128]{1,0:T(8,128)S(1)}) custom-call(s32[128,2]{1,0:T(8,128)S(1)} %copy-done.27, bf16[256,3072]{1,0:T(8,128)(2,1)S(1)} %bitcast.39, bf16[256,3072]{1,0:T(8,128)(2,1)} %collective-permute-done.19.there, bf16[128,3072]{1,0:T(8,128)(2,1)S(1)} %copy-done.2), custom_call_target="tpu_custom_call" | custom-call | flops 805306368 | bytes 6291456 | tf_op jit(solution)/shard_map/pick/pallas_call | solution.py:356
  140.5 7.0 %middle.1 = (bf16[128,3072]{1,0:T(8,128)(2,1)}, bf16[128,3072]{1,0:T(8,128)(2,1)}, f32[128,128]{1,0:T(8,128)S(1)}) custom-call(s32[128,2]{1,0:T(8,128)S(1)} %copy-done.26, f32[128,3072]{1,0:T(8,128)} %get-tuple-element.24.own, f32[128,3072]{1,0:T(8,128)} %collective-permute-done.18.recv, bf16[128,3072]{1,0:T(8,128)(2,1)S(1)} %copy-done.22, ...), custom_call_target="tpu_custom_call" | custom-call | flops 402653184 | bytes 7864320 | tf_op jit(solution)/shard_map/middle/pallas_call | solution.py:404
  148.1 3.3 %spread.1 = (bf16[256,3072]{1,0:T(8,128)(2,1)S(1)}, bf16[256,3072]{1,0:T(8,128)(2,1)}) custom-call(s32[2,128]{1,0:T(2,128)S(1)} %bitcast.41, f32[128,128]{1,0:T(8,128)S(1)} %get-tuple-element.31.gates, bf16[128,3072]{1,0:T(8,128)(2,1)S(1)} %copy-done.2), custom_call_target="tpu_custom_call" | custom-call | flops 805306368 | bytes 3932160 | tf_op jit(solution)/shard_map/spread/pallas_call | solution.py:434
  152.7 6.7 %dattention.1.dout = bf16[256,1536]{1,0:T(8,128)(2,1)S(1)} custom-call(s32[12]{0:T(128)S(1)} %stack.43.table, s32[1]{0:T(128)} %bitcast.10.core, bf16[128,3072]{1,0:T(8,128)(2,1)S(1)} %copy-done.19, bf16[128,3072]{1,0:T(8,128)(2,1)S(1)} %collective-permute-done.21.recv, bf16[12,16,3072]{2,1,0:T(8,128)(2,1)} %refs_0_.3, bf16[8,16,3072]{2,1,0:T(8,128)(2,1)} %copy-done, ...), custom_call_target="tpu_custom_call" | custom-call | flops 2415919104 | bytes 9437184 | tf_op jit(solution)/shard_map/dattention/pallas_call | solution.py:197
  159.4 13.6 %attention_grad.1 = (bf16[256,1536]{1,0:T(8,128)(2,1)S(1)}, bf16[256,512]{1,0:T(8,128)(2,1)S(1)}, bf16[256,512]{1,0:T(8,128)(2,1)S(1)}, bf16[256,512]{1,0:T(8,128)(2,1)}, f32[256,512]{1,0:T(8,128)S(1)}) custom-call(bf16[256,1536]{1,0:T(8,128)(2,1)S(1)} %copy-done.21, bf16[256,1536]{1,0:T(8,128)(2,1)S(1)} %dattention.1.dout, ...), custom_call_target="tpu_custom_call" | custom-call | flops 3221225472 | bytes 6291456 | tf_op jit(solution)/shard_map/attention_grad/pallas_call | solution.py:308
  173.1 1.9 collective-permute-start.22
  178.8 2.3 %copy.57 = bf16[256,12,128]{2,0,1:T(8,128)(2,1)} copy(bf16[256,12,128]{0,2,1:T(8,128)(2,1)} %bitcast.42) | data formatting | bytes 1572864
  181.1 4.8 %collective-permute-done.22 = bf16[256,512]{1,0:T(8,128)(2,1)} collective-permute-done((bf16[256,512]{1,0:T(8,128)(2,1)}, bf16[256,512]{1,0:T(8,128)(2,1)}, u32[]{:S(2)}, u32[]{:S(2)}) %collective-permute-start.22) | collective-permute-done | bytes 262176 | tf_op jit(solution)/shard_map/ppermute | solution.py:39
  185.9 2.8 %collective-permute-done.23 = bf16[256,512]{1,0:T(8,128)(2,1)} collective-permute-done((bf16[256,512]{1,0:T(8,128)(2,1)S(1)}, bf16[256,512]{1,0:T(8,128)(2,1)}, u32[]{:S(2)}, u32[]{:S(2)}) %collective-permute-start.23) | collective-permute-done | bytes 262176 | tf_op jit(solution)/shard_map/ppermute | solution.py:39
  188.8 17.0 %collective-permute-done.24 = bf16[256,512]{1,0:T(8,128)(2,1)} collective-permute-done((bf16[256,512]{1,0:T(8,128)(2,1)S(1)}, bf16[256,512]{1,0:T(8,128)(2,1)}, u32[]{:S(2)}, u32[]{:S(2)}) %collective-permute-start.24) | collective-permute-done | bytes 262176 | tf_op jit(solution)/shard_map/ppermute | solution.py:39
  208.0 3.6 %maximum_select_fusion = bf16[1,4,2,64,3072]{4,3,2,1,0:T(8,128)(2,1)} fusion(bf16[1,4,1,64,3072]{4,3,2,1,0:T(8,128)(2,1)} %bitcast.20, bf16[1,4,1,64,3072]{4,3,2,1,0:T(8,128)(2,1)S(1)} %bitcast.40, pred[]{:T(512)S(6)} %eq.33), kind=kLoop, calls=%fused_computation | loop fusion | flops 4718592 | bytes 6291457 | tf_op jit(solution)/shard_map/jit(_where)/select_n | solution.py:496
  (141 shorter events, 26.9 us)
Async XLA Ops:
  0.6 42.8 %copy-start.40 = (bf16[256,2,128]{2,1,0:T(2,128)(2,1)S(1)}, bf16[256,2,128]{2,1,0:T(2,128)(2,1)}, u32[]{:S(2)}) copy-start(bf16[256,2,128]{2,1,0:T(2,128)(2,1)} %param.10) | copy-start | bytes 393220
  0.6 43.7 %copy-start.41 = (bf16[256,2,128]{2,1,0:T(2,128)(2,1)S(1)}, bf16[256,2,128]{2,1,0:T(2,128)(2,1)}, u32[]{:S(2)}) copy-start(bf16[256,2,128]{2,1,0:T(2,128)(2,1)} %param.11) | copy-start | bytes 393220
  2.0 21.2 %collective-permute-start.3 = (bf16[8,16,3072]{2,1,0:T(8,128)(2,1)S(1)}, bf16[8,16,3072]{2,1,0:T(8,128)(2,1)S(1)}, u32[]{:S(2)}, u32[]{:S(2)}) collective-permute-start(bf16[8,16,3072]{2,1,0:T(8,128)(2,1)S(1)} %pad_maximum_fusion), channel_id=1, source_target_pairs={{0,4},{2,6},{4,8},{6,10},{8,12},{10,14},{12,0},{14,2},{1,5},{3,7},... | collective-permute-start | bytes 2359304 | tf_op jit(solution)/shard_map/ppermute | solution.py:71
  23.2 103.0 %copy-start = (bf16[8,16,3072]{2,1,0:T(8,128)(2,1)}, bf16[8,16,3072]{2,1,0:T(8,128)(2,1)S(1)}, u32[]{:S(2)}) copy-start(bf16[8,16,3072]{2,1,0:T(8,128)(2,1)S(1)} %collective-permute-done.3.refs_1_) | copy-start | bytes 2359300
  23.2 20.3 %collective-permute-start.5 = (bf16[8,16,3072]{2,1,0:T(8,128)(2,1)S(1)}, bf16[8,16,3072]{2,1,0:T(8,128)(2,1)S(1)}, u32[]{:S(2)}, u32[]{:S(2)}) collective-permute-start(bf16[8,16,3072]{2,1,0:T(8,128)(2,1)S(1)} %collective-permute-done.3.refs_1_), channel_id=1, source_target_pairs={{0,4},{2,6},{4,8},{6,10},{8,12},{10,14},{12,0},{14,2},{1,5},{3,7},... | collective-permute-start | bytes 2359304 | tf_op jit(solution)/shard_map/ppermute | solution.py:71
  23.2 30.9 %collective-permute-start.9 = (bf16[8,16,3072]{2,1,0:T(8,128)(2,1)S(1)}, bf16[8,16,3072]{2,1,0:T(8,128)(2,1)S(1)}, u32[]{:S(2)}, u32[]{:S(2)}) collective-permute-start(bf16[8,16,3072]{2,1,0:T(8,128)(2,1)S(1)} %pad_maximum_fusion), channel_id=1, source_target_pairs={{0,2},{2,0},{4,6},{6,4},{8,10},{10,8},{12,14},{14,12},{1,3},{3,1},... | collective-permute-start | bytes 2359304 | tf_op jit(solution)/shard_map/ppermute | solution.py:75
  43.4 82.7 %copy-start.1 = (bf16[8,16,3072]{2,1,0:T(8,128)(2,1)}, bf16[8,16,3072]{2,1,0:T(8,128)(2,1)S(1)}, u32[]{:S(2)}) copy-start(bf16[8,16,3072]{2,1,0:T(8,128)(2,1)S(1)} %collective-permute-done.5.refs_3_) | copy-start | bytes 2359300
  43.4 19.4 %collective-permute-start.7 = (bf16[8,16,3072]{2,1,0:T(8,128)(2,1)S(1)}, bf16[8,16,3072]{2,1,0:T(8,128)(2,1)S(1)}, u32[]{:S(2)}, u32[]{:S(2)}) collective-permute-start(bf16[8,16,3072]{2,1,0:T(8,128)(2,1)S(1)} %collective-permute-done.5.refs_3_), channel_id=1, source_target_pairs={{0,4},{2,6},{4,8},{6,10},{8,12},{10,14},{12,0},{14,2},{1,5},{3,7},... | collective-permute-start | bytes 2359304 | tf_op jit(solution)/shard_map/ppermute | solution.py:71
  43.5 28.1 %collective-permute-start.11 = (bf16[8,16,3072]{2,1,0:T(8,128)(2,1)S(1)}, bf16[8,16,3072]{2,1,0:T(8,128)(2,1)}, u32[]{:S(2)}, u32[]{:S(2)}) collective-permute-start(bf16[8,16,3072]{2,1,0:T(8,128)(2,1)S(1)} %collective-permute-done.3.refs_1_), channel_id=1, source_target_pairs={{0,2},{2,0},{4,6},{6,4},{8,10},{10,8},{12,14},{14,12},{1,3},{3,1},... | collective-permute-start | bytes 2359304 | tf_op jit(solution)/shard_map/ppermute | solution.py:75
  44.3 39.1 %copy-start.28 = (bf16[256,512]{1,0:T(8,128)(2,1)}, bf16[256,512]{1,0:T(8,128)(2,1)S(1)}, u32[]{:S(2)}) copy-start(bf16[256,512]{1,0:T(8,128)(2,1)S(1)} %bitcast_dynamic-update-slice_fusion.refs_3_.refs_7_) | copy-start | bytes 786436
  44.3 22.7 %collective-permute-start = (bf16[256,512]{1,0:T(8,128)(2,1)S(1)}, bf16[256,512]{1,0:T(8,128)(2,1)S(1)}, u32[]{:S(2)}, u32[]{:S(2)}) collective-permute-start(bf16[256,512]{1,0:T(8,128)(2,1)S(1)} %bitcast_dynamic-update-slice_fusion.refs_3_.refs_7_), channel_id=1, source_target_pairs={{0,6},{2,8},{4,10},{6,12},{8,14},{1,7},{3,9},{5,11},{7,13},{9,15},... | collective-permute-start | bytes 786440 | tf_op jit(solution)/shard_map/ppermute | solution.py:39
  47.4 22.7 %collective-permute-start.1 = (bf16[256,512]{1,0:T(8,128)(2,1)S(1)}, bf16[256,512]{1,0:T(8,128)(2,1)S(1)}, u32[]{:S(2)}, u32[]{:S(2)}) collective-permute-start(bf16[256,512]{1,0:T(8,128)(2,1)S(1)} %bitcast_dynamic-update-slice_fusion.refs_3_.refs_7_), channel_id=1, source_target_pairs={{0,4},{2,6},{4,8},{6,10},{8,12},{10,14},{1,5},{3,7},{5,9},{7,11},{... | collective-permute-start | bytes 786440 | tf_op jit(solution)/shard_map/ppermute | solution.py:39
  54.0 41.1 %collective-permute-start.4 = (bf16[4,16,3072]{2,1,0:T(8,128)(2,1)}, bf16[4,16,3072]{2,1,0:T(8,128)(2,1)S(1)}, u32[]{:S(2)}, u32[]{:S(2)}) collective-permute-start(bf16[4,16,3072]{2,1,0:T(8,128)(2,1)} %slice.41), channel_id=1, source_target_pairs={{0,16},{16,0},{1,17},{17,1},{2,18},{18,2},{3,19},{19,3},{4,20},{20... | collective-permute-start | bytes 1179656 | tf_op jit(solution)/shard_map/ppermute | solution.py:43
  62.8 20.6 %collective-permute-start.13 = (bf16[8,16,3072]{2,1,0:T(8,128)(2,1)S(1)}, bf16[8,16,3072]{2,1,0:T(8,128)(2,1)}, u32[]{:S(2)}, u32[]{:S(2)}) collective-permute-start(bf16[8,16,3072]{2,1,0:T(8,128)(2,1)S(1)} %collective-permute-done.5.refs_3_), channel_id=1, source_target_pairs={{0,2},{2,0},{4,6},{6,4},{8,10},{10,8},{12,14},{14,12},{1,3},{3,1},... | collective-permute-start | bytes 2359304 | tf_op jit(solution)/shard_map/ppermute | solution.py:75
  67.1 24.0 %copy-start.31 = (bf16[256,512]{1,0:T(8,128)(2,1)}, bf16[256,512]{1,0:T(8,128)(2,1)S(1)}, u32[]{:S(2)}) copy-start(bf16[256,512]{1,0:T(8,128)(2,1)S(1)} %collective-permute-done.refs_0_.refs_4_) | copy-start | bytes 786436
  67.1 28.6 %collective-permute-start.10 = (bf16[4,16,3072]{2,1,0:T(8,128)(2,1)}, bf16[4,16,3072]{2,1,0:T(8,128)(2,1)S(1)}, u32[]{:S(2)}, u32[]{:S(2)}) collective-permute-start(bf16[4,16,3072]{2,1,0:T(8,128)(2,1)} %slice.44), channel_id=1, source_target_pairs={{0,16},{16,0},{1,17},{17,1},{2,18},{18,2},{3,19},{19,3},{4,20},{20... | collective-permute-start | bytes 1179656 | tf_op jit(solution)/shard_map/ppermute | solution.py:43
  70.0 27.6 %collective-permute-start.6 = (bf16[4,16,3072]{2,1,0:T(8,128)(2,1)}, bf16[4,16,3072]{2,1,0:T(8,128)(2,1)S(1)}, u32[]{:S(2)}, u32[]{:S(2)}) collective-permute-start(bf16[4,16,3072]{2,1,0:T(8,128)(2,1)} %slice.42), channel_id=1, source_target_pairs={{0,16},{16,0},{1,17},{17,1},{2,18},{18,2},{3,19},{19,3},{4,20},{20... | collective-permute-start | bytes 1179656 | tf_op jit(solution)/shard_map/ppermute | solution.py:43
  71.5 28.4 %collective-permute-start.15 = (bf16[4,16,3072]{2,1,0:T(8,128)(2,1)}, bf16[4,16,3072]{2,1,0:T(8,128)(2,1)}, u32[]{:S(2)}, u32[]{:S(2)}) collective-permute-start(bf16[4,16,3072]{2,1,0:T(8,128)(2,1)} %get-tuple-element.63), channel_id=1, source_target_pairs={{0,2},{2,0},{4,6},{6,4},{8,10},{10,8},{12,14},{14,12},{1,3},{3,1},... | collective-permute-start | bytes 1179656 | tf_op jit(solution)/shard_map/ppermute | solution.py:78
  83.4 10.2 %collective-permute-start.2 = (bf16[256,512]{1,0:T(8,128)(2,1)S(1)}, bf16[256,512]{1,0:T(8,128)(2,1)}, u32[]{:S(2)}, u32[]{:S(2)}) collective-permute-start(bf16[256,512]{1,0:T(8,128)(2,1)S(1)} %bitcast_dynamic-update-slice_fusion.refs_3_.refs_7_), channel_id=1, source_target_pairs={{0,2},{2,4},{4,6},{6,8},{8,10},{10,12},{12,14},{1,3},{3,5},{5,7},{... | collective-permute-start | bytes 786440 | tf_op jit(solution)/shard_map/ppermute | solution.py:39
  93.6 22.7 %collective-permute-start.12 = (bf16[4,16,3072]{2,1,0:T(8,128)(2,1)S(1)}, bf16[4,16,3072]{2,1,0:T(8,128)(2,1)S(1)}, u32[]{:S(2)}, u32[]{:S(2)}) collective-permute-start(bf16[4,16,3072]{2,1,0:T(8,128)(2,1)S(1)} %slice.45), channel_id=1, source_target_pairs={{0,16},{16,0},{1,17},{17,1},{2,18},{18,2},{3,19},{19,3},{4,20},{20... | collective-permute-start | bytes 1179656 | tf_op jit(solution)/shard_map/ppermute | solution.py:43
  95.1 21.3 %collective-permute-start.8 = (bf16[4,16,3072]{2,1,0:T(8,128)(2,1)}, bf16[4,16,3072]{2,1,0:T(8,128)(2,1)S(1)}, u32[]{:S(2)}, u32[]{:S(2)}) collective-permute-start(bf16[4,16,3072]{2,1,0:T(8,128)(2,1)} %get-tuple-element.63), channel_id=1, source_target_pairs={{0,16},{16,0},{1,17},{17,1},{2,18},{18,2},{3,19},{19,3},{4,20},{20... | collective-permute-start | bytes 1179656 | tf_op jit(solution)/shard_map/ppermute | solution.py:43
  96.4 20.0 %collective-permute-start.17 = (bf16[4,16,3072]{2,1,0:T(8,128)(2,1)}, bf16[4,16,3072]{2,1,0:T(8,128)(2,1)S(1)}, u32[]{:S(2)}, u32[]{:S(2)}) collective-permute-start(bf16[4,16,3072]{2,1,0:T(8,128)(2,1)} %get-tuple-element.62), channel_id=1, source_target_pairs={{0,2},{2,0},{4,6},{6,4},{8,10},{10,8},{12,14},{14,12},{1,3},{3,1},... | collective-permute-start | bytes 1179656 | tf_op jit(solution)/shard_map/ppermute | solution.py:81
  98.4 23.5 %collective-permute-start.14 = (bf16[4,16,3072]{2,1,0:T(8,128)(2,1)S(1)}, bf16[4,16,3072]{2,1,0:T(8,128)(2,1)S(1)}, u32[]{:S(2)}, u32[]{:S(2)}) collective-permute-start(bf16[4,16,3072]{2,1,0:T(8,128)(2,1)S(1)} %slice.46), channel_id=1, source_target_pairs={{0,16},{16,0},{1,17},{17,1},{2,18},{18,2},{3,19},{19,3},{4,20},{20... | collective-permute-start | bytes 1179656 | tf_op jit(solution)/shard_map/ppermute | solution.py:43
  99.9 26.2 %collective-permute-start.16 = (bf16[4,16,3072]{2,1,0:T(8,128)(2,1)}, bf16[4,16,3072]{2,1,0:T(8,128)(2,1)S(1)}, u32[]{:S(2)}, u32[]{:S(2)}) collective-permute-start(bf16[4,16,3072]{2,1,0:T(8,128)(2,1)} %collective-permute-done.15.refs_13_), channel_id=1, source_target_pairs={{0,16},{16,0},{1,17},{17,1},{2,18},{18,2},{3,19},{19,3},{4,20},{20... | collective-permute-start | bytes 1179656 | tf_op jit(solution)/shard_map/ppermute | solution.py:43
  103.9 22.3 %copy-start.4 = (bf16[4,16,3072]{2,1,0:T(8,128)(2,1)S(1)}, bf16[4,16,3072]{2,1,0:T(8,128)(2,1)}, u32[]{:S(2)}) copy-start(bf16[4,16,3072]{2,1,0:T(8,128)(2,1)} %copy-done.3) | copy-start | bytes 1179652
  116.3 20.6 %collective-permute-start.19 = (bf16[256,3072]{1,0:T(8,128)(2,1)}, bf16[256,3072]{1,0:T(8,128)(2,1)}, u32[]{:S(2)}, u32[]{:S(2)}) collective-permute-start(bf16[256,3072]{1,0:T(8,128)(2,1)} %bitcast.14), channel_id=1, source_target_pairs={{0,1},{1,0},{2,3},{3,2},{4,5},{5,4},{6,7},{7,6},{8,9},{9,8},{10,11... | collective-permute-start | bytes 4718600 | tf_op jit(solution)/shard_map/ppermute | solution.py:43
  133.2 7.3 %collective-permute-start.18 = (f32[128,3072]{1,0:T(8,128)}, f32[128,3072]{1,0:T(8,128)}, u32[]{:S(2)}, u32[]{:S(2)}) collective-permute-start(f32[128,3072]{1,0:T(8,128)} %get-tuple-element.25), channel_id=1, source_target_pairs={{0,1},{1,0},{2,3},{3,2},{4,5},{5,4},{6,7},{7,6},{8,9},{9,8},{10,11... | collective-permute-start | bytes 4718600 | tf_op jit(solution)/shard_map/ppermute | solution.py:43
  147.6 3.9 %collective-permute-start.21 = (bf16[128,3072]{1,0:T(8,128)(2,1)}, bf16[128,3072]{1,0:T(8,128)(2,1)S(1)}, u32[]{:S(2)}, u32[]{:S(2)}) collective-permute-start(bf16[128,3072]{1,0:T(8,128)(2,1)} %get-tuple-element.53.own), channel_id=1, source_target_pairs={{0,1},{1,0},{2,3},{3,2},{4,5},{5,4},{6,7},{7,6},{8,9},{9,8},{10,11... | collective-permute-start | bytes 2359304 | tf_op jit(solution)/shard_map/ppermute | solution.py:43
  151.5 56.5 %collective-permute-start.20 = (bf16[256,3072]{1,0:T(8,128)(2,1)}, bf16[256,3072]{1,0:T(8,128)(2,1)}, u32[]{:S(2)}, u32[]{:S(2)}) collective-permute-start(bf16[256,3072]{1,0:T(8,128)(2,1)} %get-tuple-element.33), channel_id=1, source_target_pairs={{0,1},{1,0},{2,3},{3,2},{4,5},{5,4},{6,7},{7,6},{8,9},{9,8},{10,11... | collective-permute-start | bytes 4718600 | tf_op jit(solution)/shard_map/ppermute | solution.py:43
  173.1 12.8 %collective-permute-start.22 = (bf16[256,512]{1,0:T(8,128)(2,1)}, bf16[256,512]{1,0:T(8,128)(2,1)}, u32[]{:S(2)}, u32[]{:S(2)}) collective-permute-start(bf16[256,512]{1,0:T(8,128)(2,1)} %get-tuple-element.37), channel_id=1, source_target_pairs={{2,0},{4,2},{6,4},{8,6},{10,8},{12,10},{14,12},{3,1},{5,3},{7,5},{... | collective-permute-start | bytes 786440 | tf_op jit(solution)/shard_map/ppermute | solution.py:39
  175.0 13.8 %collective-permute-start.23 = (bf16[256,512]{1,0:T(8,128)(2,1)S(1)}, bf16[256,512]{1,0:T(8,128)(2,1)}, u32[]{:S(2)}, u32[]{:S(2)}) collective-permute-start(bf16[256,512]{1,0:T(8,128)(2,1)S(1)} %get-tuple-element.38), channel_id=1, source_target_pairs={{4,0},{6,2},{8,4},{10,6},{12,8},{14,10},{5,1},{7,3},{9,5},{11,7},{... | collective-permute-start | bytes 786440 | tf_op jit(solution)/shard_map/ppermute | solution.py:39
  176.3 29.5 %collective-permute-start.24 = (bf16[256,512]{1,0:T(8,128)(2,1)S(1)}, bf16[256,512]{1,0:T(8,128)(2,1)}, u32[]{:S(2)}, u32[]{:S(2)}) collective-permute-start(bf16[256,512]{1,0:T(8,128)(2,1)S(1)} %get-tuple-element.39), channel_id=1, source_target_pairs={{6,0},{8,2},{10,4},{12,6},{14,8},{7,1},{9,3},{11,5},{13,7},{15,9},... | collective-permute-start | bytes 786440 | tf_op jit(solution)/shard_map/ppermute | solution.py:39
  (36 other events, 271.1 us)

commit v2 on v1

--- a/solution.py
+++ b/solution.py
@@ -10,7 +10,7 @@
 BAND_BLOCKS = 4
 F32 = jnp.float32
 BF16 = jnp.bfloat16
-VMEM_LIMIT = 48 * 1024 * 1024
+VMEM_LIMIT = 24 * 1024 * 1024
 
 
 def params(limit=VMEM_LIMIT):
@@ -43,19 +43,24 @@
     return lax.ppermute(value, axis, [(0, 1), (1, 0)])
 
 
-def gathered(w_out):
+def after(values, *others):
+    return lax.optimization_barrier((tuple(values), others))[0]
+
+
+def gathered(w_out, work):
     heads, depth, _ = w_out.shape
     count = lax.axis_size("ctx")
     place = lax.axis_index("ctx")
     if count != 8 or lax.axis_size("groups") != 2 or heads % 3:
         full = lax.all_gather(w_out, "ctx", axis=1, tiled=True)
+        for task in work:
+            task(())
         return [full], jnp.zeros((1,), jnp.int32), [(0, 0, heads, 0, 0)]
     side = lax.axis_index("groups")
     third = heads // 3
     mine = lax.dynamic_slice_in_dim(w_out, side * third, third, 0)
     ring = [(c, (c + 2) % count) for c in range(count)]
     pairs = [(c, c ^ 1) for c in range(count)]
-    held = [jnp.concatenate([mine, w_out[2 * third :]], axis=0)]
     arrays, plan = [w_out], [(0, 0, heads, 0, 4)]
     table = [0, side * third, (1 - side) * third, 2 * third]
     table += [depth * ((place - 2 * k) % count) for k in range(4)]
@@ -67,18 +72,35 @@
             plan.append((len(arrays) - 1, start, size, head, row))
 
     both = [(0, third, 1), (third, third, 3)]
-    for k in range(1, 4):
-        held.append(lax.ppermute(held[-1], "ctx", ring))
-        add(held[k], both, 4 + k)
-        add(swapped(held[k][:third], "groups"), [(0, third, 2)], 4 + k)
+    held, across = jnp.concatenate([mine, w_out[2 * third :]], axis=0), None
     for k in range(3):
-        across = lax.ppermute(held[k], "ctx", pairs)
-        add(across, both, 8 + k)
-        add(swapped(across[:third], "groups"), [(0, third, 2)], 8 + k)
-    across = lax.ppermute(held[3][:third], "ctx", pairs)
-    add(across, [(0, third, 1)], 11)
-    add(swapped(across, "groups"), [(0, third, 2)], 11)
-    add(lax.ppermute(held[3][third:], "ctx", pairs), [(0, third, 3)], 11)
+        moved = lax.ppermute(held, "ctx", ring)
+        paired = lax.ppermute(held, "ctx", pairs)
+        sent = [moved, paired]
+        if k > 0:
+            sent.append(swapped(held[:third], "groups"))
+            sent.append(swapped(across[:third], "groups"))
+        done = work[k]([held])
+        sent = after(sent, *done)
+        add(sent[0], both, 5 + k)
+        add(sent[1], both, 8 + k)
+        if k > 0:
+            add(sent[2], [(0, third, 2)], 4 + k)
+            add(sent[3], [(0, third, 2)], 7 + k)
+        held, across = sent[0], sent[1]
+    first = lax.ppermute(held[:third], "ctx", pairs)
+    last = lax.ppermute(held[third:], "ctx", pairs)
+    beside = swapped(held[:third], "groups")
+    beyond = swapped(across[:third], "groups")
+    done = work[3]([held])
+    first = after([first], *done)[0]
+    final = swapped(first, "groups")
+    work[4]([first])
+    add(first, [(0, third, 1)], 11)
+    add(last, [(0, third, 3)], 11)
+    add(beside, [(0, third, 2)], 7)
+    add(beyond, [(0, third, 2)], 10)
+    add(final, [(0, third, 2)], 11)
     return arrays, jnp.stack([jnp.asarray(t, jnp.int32) for t in table]), plan
 
 
@@ -116,12 +138,14 @@
     return pl.ds(pl.multiple_of(step * size, size), size)
 
 
-def project_kernel(plan, count, table, core, attn, *refs):
+def project_kernel(plan, count, parts, table, core, *refs):
+    attn = jnp.concatenate([r[...] for r in refs[:parts]], axis=1)
+    refs = refs[parts:]
     pieces, (own, other, buf, sem) = refs[:count], refs[count:]
     heads, head_dim, width = buf.shape
     columns = wait_chunk(plan, table, pieces, buf, sem, width)
     weights = buf[:, :, columns].reshape(heads * head_dim, width // CHUNKS)
-    result = dot_nn(attn[...], weights)
+    result = dot_nn(attn, weights)
     rows = own.shape[0]
 
     @pl.when(core[0] == 0)
@@ -136,15 +160,15 @@
 
 
 def project(attn, arrays, table, plan, core, heads, head_dim, width, rows):
-    tok = attn.shape[0]
+    tok = attn[0].shape[0]
     size = width // CHUNKS
     return pl.pallas_call(
-        functools.partial(project_kernel, plan, len(arrays)),
+        functools.partial(project_kernel, plan, len(arrays), len(attn)),
         grid_spec=pltpu.PrefetchScalarGridSpec(
             num_scalar_prefetch=2,
             grid=(CHUNKS,),
-            in_specs=[pl.BlockSpec((tok, heads * head_dim), lambda i, *_: (0, 0))]
-            + [pl.BlockSpec(memory_space=pltpu.HBM)] * len(arrays),
+            in_specs=[pl.BlockSpec(a.shape, lambda i, *_: (0, 0)) for a in attn]
+            + [pl.BlockSpec(memory_space=pl.ANY)] * len(arrays),
             out_specs=[pl.BlockSpec((rows, size), lambda i, *_: (0, i))] * 2,
             scratch_shapes=[
                 pltpu.VMEM((heads, head_dim, width), BF16),
@@ -155,7 +179,7 @@
         compiler_params=params(),
         cost_estimate=cost(2 * tok * heads * head_dim * width, 2 * heads * head_dim * width),
         name="project",
-    )(table, core, attn, *arrays)
+    )(table, core, *attn, *arrays)
 
 
 def dattn_kernel(plan, count, table, core, own, recv, *refs):
@@ -200,7 +224,7 @@
             num_scalar_prefetch=2,
             grid=(CHUNKS,),
             in_specs=[pl.BlockSpec((rows, size), lambda i, *_: (0, i))] * 2
-            + [pl.BlockSpec(memory_space=pltpu.HBM)] * len(arrays),
+            + [pl.BlockSpec(memory_space=pl.ANY)] * len(arrays),
             out_specs=pl.BlockSpec((2 * rows, heads * head_dim), lambda i, *_: (0, 0)),
             scratch_shapes=[
                 pltpu.VMEM((2 * rows, size), BF16),
@@ -237,32 +261,36 @@
     attn[...] = dot_nn(weight, band_of(values)).astype(BF16)
 
 
-def attention(queries, bands, place, heads, heads_kv, head_dim, scale):
+def attention(queries, bands, place, which, heads, heads_kv, head_dim, scale):
     tok = queries.shape[0]
     group = heads // heads_kv
-    keys = pl.BlockSpec((tok, head_dim), lambda h, *_: (0, h // group))
-    values = pl.BlockSpec((tok, head_dim), lambda h, *_: (0, heads_kv + h // group))
-    per_head = pl.BlockSpec((tok, head_dim), lambda h, *_: (0, h))
+    keys = pl.BlockSpec((tok, head_dim), lambda h, *_: (0, which))
+    values = pl.BlockSpec((tok, head_dim), lambda h, *_: (0, heads_kv + which))
     span = BAND_BLOCKS * tok
     return pl.pallas_call(
         functools.partial(attention_kernel, scale),
         grid_spec=pltpu.PrefetchScalarGridSpec(
             num_scalar_prefetch=1,
-            grid=(heads,),
-            in_specs=[per_head] + [keys] * BAND_BLOCKS + [values] * BAND_BLOCKS,
-            out_specs=[per_head, pl.BlockSpec((1, tok, span), lambda h, *_: (h, 0, 0))],
+            grid=(group,),
+            in_specs=[pl.BlockSpec((tok, head_dim), lambda h, *_: (0, which * group + h))]
+            + [keys] * BAND_BLOCKS
+            + [values] * BAND_BLOCKS,
+            out_specs=[
+                pl.BlockSpec((tok, head_dim), lambda h, *_: (0, h)),
+                pl.BlockSpec((1, tok, span), lambda h, *_: (h, 0, 0)),
+            ],
         ),
         out_shape=[
-            jax.ShapeDtypeStruct((tok, heads * head_dim), BF16),
-            jax.ShapeDtypeStruct((heads, tok, span), BF16),
+            jax.ShapeDtypeStruct((tok, group * head_dim), BF16),
+            jax.ShapeDtypeStruct((group, tok, span), BF16),
         ],
         compiler_params=params(),
-        cost_estimate=cost(4 * tok * span * heads * head_dim, 2 * heads * tok * span, heads * tok * span),
+        cost_estimate=cost(4 * tok * span * group * head_dim, 2 * group * tok * span, group * tok * span),
         name="attention",
     )(place, queries, *bands, *bands)
 
 
-def attention_grad_kernel(scale, group, heads_kv, q, dout, attn, probs, *refs):
+def attention_grad_kernel(scale, group, q, dout, attn, probs, *refs):
     keys, values = refs[:BAND_BLOCKS], refs[BAND_BLOCKS : 2 * BAND_BLOCKS]
     dq, outs, (dk, dv) = refs[2 * BAND_BLOCKS], refs[2 * BAND_BLOCKS + 1 : -2], refs[-2:]
     tok, head_dim = q.shape
@@ -276,49 +304,47 @@
     dkey = dot_tn(dscore, q[...])
     dvalue = dot_tn(weight, grad)
 
-    @pl.when(head % group == 0)
+    @pl.when(head == 0)
     def _():
         dk[...] = dkey
         dv[...] = dvalue
 
-    @pl.when(head % group > 0)
+    @pl.when(head > 0)
     def _():
         dk[...] += dkey
         dv[...] += dvalue
 
-    @pl.when(head % group == group - 1)
-    def _():
-        lanes_k = pl.ds(pl.multiple_of(head // group * head_dim, head_dim), head_dim)
-        lanes_v = pl.ds(pl.multiple_of((heads_kv + head // group) * head_dim, head_dim), head_dim)
+    @pl.when(head == group - 1)
+    def _():
         for block, out in enumerate(outs):
             rows = pl.ds(block * tok, tok)
-            out[:, lanes_k] = (dk[rows, :] * scale).astype(out.dtype)
-            out[:, lanes_v] = dv[rows, :].astype(out.dtype)
-
-
-def attention_grad(queries, dout, attn, probs, bands, heads, heads_kv, head_dim, scale):
+            out[:, :head_dim] = (dk[rows, :] * scale).astype(out.dtype)
+            out[:, head_dim:] = dv[rows, :].astype(out.dtype)
+
+
+def attention_grad(queries, dout, attn, probs, bands, which, heads, heads_kv, head_dim, scale):
     tok = queries.shape[0]
     group = heads // heads_kv
-    keys = pl.BlockSpec((tok, head_dim), lambda h: (0, h // group))
-    values = pl.BlockSpec((tok, head_dim), lambda h: (0, heads_kv + h // group))
+    keys = pl.BlockSpec((tok, head_dim), lambda h: (0, which))
+    values = pl.BlockSpec((tok, head_dim), lambda h: (0, heads_kv + which))
     per_head = pl.BlockSpec((tok, head_dim), lambda h: (0, h))
+    of_all = pl.BlockSpec((tok, head_dim), lambda h: (0, which * group + h))
     span = BAND_BLOCKS * tok
-    lanes = 2 * heads_kv * head_dim
-    whole = pl.BlockSpec((tok, lanes), lambda h: (0, 0))
-    return pl.pallas_call(
-        functools.partial(attention_grad_kernel, scale, group, heads_kv),
-        grid=(heads,),
-        in_specs=[per_head] * 3
+    whole = pl.BlockSpec((tok, 2 * head_dim), lambda h: (0, 0))
+    return pl.pallas_call(
+        functools.partial(attention_grad_kernel, scale, group),
+        grid=(group,),
+        in_specs=[of_all, of_all, per_head]
         + [pl.BlockSpec((1, tok, span), lambda h: (h, 0, 0))]
         + [keys] * BAND_BLOCKS
         + [values] * BAND_BLOCKS,
         out_specs=[per_head] + [whole] * BAND_BLOCKS,
-        out_shape=[jax.ShapeDtypeStruct((tok, heads * head_dim), BF16)]
-        + [jax.ShapeDtypeStruct((tok, lanes), BF16)] * (BAND_BLOCKS - 1)
-        + [jax.ShapeDtypeStruct((tok, lanes), F32)],
+        out_shape=[jax.ShapeDtypeStruct((tok, group * head_dim), BF16)]
+        + [jax.ShapeDtypeStruct((tok, 2 * head_dim), BF16)] * (BAND_BLOCKS - 1)
+        + [jax.ShapeDtypeStruct((tok, 2 * head_dim), F32)],
         scratch_shapes=[pltpu.VMEM((span, head_dim), F32)] * 2,
         compiler_params=params(),
-        cost_estimate=cost(8 * tok * span * heads * head_dim, 2 * heads * tok * span),
+        cost_estimate=cost(8 * tok * span * group * head_dim, 2 * group * tok * span),
         name="attention_grad",
     )(queries, dout, attn, probs, *bands, *bands)
 
@@ -462,27 +488,48 @@
     core_arg = core.astype(jnp.int32).reshape(1)
     place_arg = place.astype(jnp.int32).reshape(1)
 
-    arrays, table, plan = gathered(w_out)
-
     own_band = jnp.concatenate(
         [rotated_keys.reshape(tok, heads_kv * head_dim), value_inputs.reshape(tok, heads_kv * head_dim)], axis=1
     )
-    bands = [own_band] + [passed_along(own_band, "ctx", step) for step in range(1, BAND_BLOCKS)]
-    bands = bands[::-1]
-
+    queries = queries_in.reshape(tok, heads_q * head_dim)
     sent = lax.dynamic_index_in_dim(expert_out[0], 1 - core, 1, keepdims=False).reshape(room, width)
     kept = lax.dynamic_index_in_dim(expert_out[0], core, 1, keepdims=False).reshape(room, width)
-    arrived = swapped(sent, "exp")
     flat = routes.reshape(-1)
     number = jnp.arange(2 * rows, dtype=jnp.int32)
     earlier = (flat[None, :] == flat[:, None]) & (number[None, :] < number[:, None])
     rank = jnp.sum(earlier.astype(jnp.int32), axis=1)
     slots = (flat * capacity + rank - core * room) % (experts * capacity)
     slots = slots.reshape(rows, 2)
-    first, second, dgate = pick(slots, kept, arrived, grad_out)
-
-    queries = queries_in.reshape(tok, heads_q * head_dim)
-    attn, probs = attention(queries, bands, place_arg, heads_q, heads_kv, head_dim, scale)
+    made = {}
+
+    def round_0(ready):
+        made["arrived"] = swapped(sent, "exp")
+        made["queries"] = queries
+        return [made["arrived"], queries, own_band, slots]
+
+    def round_1(ready):
+        band = after([own_band], *ready)[0]
+        bands = [band] + [passed_along(band, "ctx", step) for step in range(1, BAND_BLOCKS)]
+        made["bands"] = bands[::-1]
+        arrived = after([made["arrived"]], *ready)[0]
+        made["picked"] = pick(slots, kept, arrived, grad_out)
+        return [*made["bands"], made["picked"][2]]
+
+    def attend(which):
+        def task(ready):
+            bands = after(made["bands"], *ready)
+            made[which] = attention(queries, bands, place_arg, which, heads_q, heads_kv, head_dim, scale)
+            return [made[which][0]]
+
+        return task
+
+    tasks = [round_0, round_1, attend(0), lambda ready: (), attend(1)]
+    if heads_kv != 2:
+        tasks[4] = lambda ready: [attend(i)(ready) for i in range(1, heads_kv)]
+    arrays, table, plan = gathered(w_out, tasks)
+    first, second, dgate = made["picked"]
+    attn, probs = zip(*[made[i] for i in range(heads_kv)])
+    bands = made["bands"]
 
     own, other = project(attn, arrays, table, plan, core_arg, heads_q, head_dim, width, rows)
     router = jnp.pad(w_router, ((0, 0), (0, 128 - experts)))
@@ -498,13 +545,23 @@
     )[None]
 
     dattn = dattention(grad_input, grad_other, arrays, table, plan, core_arg, heads_q, head_dim, width)
-    grads = attention_grad(queries, dattn, attn, probs, bands, heads_q, heads_kv, head_dim, scale)
-    grad_q = grads[0].reshape(tok, heads_q, head_dim)
-    total = grads[BAND_BLOCKS]
-    for step in range(1, BAND_BLOCKS):
-        total = total + passed_along(grads[BAND_BLOCKS - step], "ctx", -step).astype(F32)
-    total = total.astype(BF16).reshape(tok, 2, heads_kv, head_dim)
-    return (mixed, grad_input, grad_expert, grad_q, total[:, 0], total[:, 1])
+    grads, totals = [], []
+    for i in range(heads_kv):
+        grad = attention_grad(queries, dattn, attn[i], probs[i], bands, i, heads_q, heads_kv, head_dim, scale)
+        passed = [passed_along(grad[BAND_BLOCKS - step], "ctx", -step) for step in range(1, BAND_BLOCKS)]
+        grads.append(grad)
+        totals.append(passed)
+    grad_q = jnp.concatenate([g[0] for g in grads], axis=1).reshape(tok, heads_q, head_dim)
+    totals, grad_q, grad_expert = lax.optimization_barrier((totals, grad_q, grad_expert))
+    sums = []
+    for grad, passed in zip(grads, totals):
+        total = grad[BAND_BLOCKS]
+        for part in passed:
+            total = total + part.astype(F32)
+        sums.append(total.astype(BF16))
+    grad_k = jnp.stack([t[:, :head_dim] for t in sums], axis=1)
+    grad_v = jnp.stack([t[:, head_dim:] for t in sums], axis=1)
+    return (mixed, grad_input, grad_expert, grad_q, grad_k, grad_v)
 
 
 def solution(mesh):

time: 213 us -> 216 us (1.014)
  waiting for transfers between devices: 95 us -> 63.4 us
  local copies, waits for them, and re-layouts: 25.2 us -> 44.7 us
  starting transfers between devices: 31.4 us -> 44.5 us
    ppermute x8, waiting for transfers between devices: 56.4 us -> 23.4 us  [the longest x3 17 us: gathered(): moved = lax.ppermute(held, 'ctx', ring)]
    unnamed x91 -> x77, local copies, waits for them, and re-layouts: 9.42 us -> 25 us
    ppermute x8, starting transfers between devices: 5.75 us -> 12.6 us  [the longest x3 7.56 us: gathered(): moved = lax.ppermute(held, 'ctx', ring)]
    ppermute x6 -> x9, starting transfers between devices: 16.4 us -> 22.9 us  [passed_along(): lax.ppermute(value, axis, [(source, source + steps) for source in range(i...]
    slice x6, local copies, waits for them, and re-layouts: 5.33 us -> 9.92 us  [the longest x2 3.58 us: gathered(): sent.append(swapped(across[:third], 'groups'))]
    ppermute x11, waiting for transfers between devices: 9.76 us -> 12.1 us  [swapped(): return lax.ppermute(value, axis, [(0, 1), (1, 0)])]
    ppermute x6 -> x9, waiting for transfers between devices: 28.8 us -> 27.9 us  [passed_along(): lax.ppermute(value, axis, [(source, source + steps) for source in range(i...]
    pallas_call x1 -> x2, Pallas kernels: 12.4 us -> 11.9 us  [attention(): pl.pallas_call(functools.partial(attention_kernel, scale), grid_spec=pltp...]
  transfers between devices with their start and end apart: 25 -> 28, of which waited for: 12 -> 9; matrix products, arithmetic and copies ran while one was open for 10% -> 12% of each run, Pallas kernels for 22% -> 17%
where the time goes in v2:
time: 216 us; the launch traced here: 215 us
  waiting for transfers between devices  63.4 us (29%)
  Pallas kernels  54.3 us (25%)
  local copies, waits for them, and re-layouts  44.7 us (21%)
  starting transfers between devices  44.5 us (21%)
  other arithmetic  6.83 us (3%)
    ppermute x9, waiting for transfers between devices, passed_along(): lax.ppermute(value, axis, [(source, source + steps) for source in range(i...  27.9 us
    unnamed x77, local copies, waits for them, and re-layouts  25 us
    ppermute x9, starting transfers between devices, passed_along(): lax.ppermute(value, axis, [(source, source + steps) for source in range(i...  22.9 us
    ppermute x3, waiting for transfers between devices, gathered(): moved = lax.ppermute(held, 'ctx', ring)  17 us
    pallas_call x2, Pallas kernels, attention_grad(): pl.pallas_call(functools.partial(attention_grad_kernel, scale, group), gr...  13.7 us
    ppermute x11, waiting for transfers between devices, swapped(): return lax.ppermute(value, axis, [(0, 1), (1, 0)])  12.1 us
    pallas_call x2, Pallas kernels, attention(): pl.pallas_call(functools.partial(attention_kernel, scale), grid_spec=pltp...  11.9 us
    ppermute x11, starting transfers between devices, swapped(): return lax.ppermute(value, axis, [(0, 1), (1, 0)])  9.04 us
  transfers between devices with their start and end apart: 28, of which 9 were waited for; matrix products, arithmetic and copies ran while one was open for 12% of the time, Pallas kernels for 17%

profile of v2, /device:TPU:4, one launch (start us, length us, event | category | flops | bytes accessed | tf_op | source)
XLA Modules:
  0.0 215.0 jit_solution(12762149099192328385)
XLA Ops:
  0.6 3.4 %constant_dynamic-slice_fusion = (bf16[1,4,1,64,3072]{4,3,2,1,0:T(8,128)(2,1)S(1)}, bf16[1,4,1,64,3072]{4,3,2,1,0:T(8,128)(2,1)}) fusion(bf16[1,4,2,64,3072]{4,3,2,1,0:T(8,128)(2,1)} %param.16, s32[]{:T(128)S(6)} %select_n.66, s32[]{:T(128)S(6)} %select_n.64), kind=kLoop, calls=%fused_computation.21 | loop fusion | bytes 6291464 | tf_op jit(solution)/shard_map/jit(dynamic_index_in_dim)/dynamic_slice | solution.py:496
  7.8 2.3 %copy.44 = bf16[256,12,128]{0,2,1:T(8,128)(2,1)} copy(bf16[256,12,128]{2,0,1:T(8,128)(2,1)} %param.9) | data formatting | bytes 1572864 | tf_op args[0]
  10.2 17.0 %collective-permute-done.refs_3_.refs_1_ = bf16[8,16,3072]{2,1,0:T(8,128)(2,1)} collective-permute-done((bf16[8,16,3072]{2,1,0:T(8,128)(2,1)}, bf16[8,16,3072]{2,1,0:T(8,128)(2,1)}, u32[]{:S(2)}, u32[]{:S(2)}) %collective-permute-start) | collective-permute-done | bytes 786464 | tf_op jit(solution)/shard_map/ppermute | solution.py:77
  28.7 4.2 %collective-permute-start.3 = (bf16[256,512]{1,0:T(8,128)(2,1)S(1)}, bf16[256,512]{1,0:T(8,128)(2,1)S(1)}, u32[]{:S(2)}, u32[]{:S(2)}) collective-permute-start(bf16[256,512]{1,0:T(8,128)(2,1)S(1)} %bitcast_dynamic-update-slice_fusion.refs_3_.refs_7_), channel_id=1, source_target_pairs={{0,6},{2,8},{4,10},{6,12},{8,14},{1,7},{3,9},{5,11},{7,13},{9,15},... | collective-permute-start | bytes 786440 | tf_op jit(solution)/shard_map/ppermute | solution.py:39
  32.9 4.0 %collective-permute-start.4 = (bf16[256,512]{1,0:T(8,128)(2,1)S(1)}, bf16[256,512]{1,0:T(8,128)(2,1)S(1)}, u32[]{:S(2)}, u32[]{:S(2)}) collective-permute-start(bf16[256,512]{1,0:T(8,128)(2,1)S(1)} %bitcast_dynamic-update-slice_fusion.refs_3_.refs_7_), channel_id=1, source_target_pairs={{0,4},{2,6},{4,8},{6,10},{8,12},{10,14},{1,5},{3,7},{5,9},{7,11},{... | collective-permute-start | bytes 786440 | tf_op jit(solution)/shard_map/ppermute | solution.py:39
  41.9 10.2 %collective-permute-done.3.refs_0_.refs_4_ = bf16[256,512]{1,0:T(8,128)(2,1)S(1)} collective-permute-done((bf16[256,512]{1,0:T(8,128)(2,1)S(1)}, bf16[256,512]{1,0:T(8,128)(2,1)S(1)}, u32[]{:S(2)}, u32[]{:S(2)}) %collective-permute-start.3) | collective-permute-done | bytes 262176 | tf_op jit(solution)/shard_map/ppermute | solution.py:39
  53.6 2.5 %collective-permute-done.4.refs_1_.refs_5_ = bf16[256,512]{1,0:T(8,128)(2,1)S(1)} collective-permute-done((bf16[256,512]{1,0:T(8,128)(2,1)S(1)}, bf16[256,512]{1,0:T(8,128)(2,1)S(1)}, u32[]{:S(2)}, u32[]{:S(2)}) %collective-permute-start.4) | collective-permute-done | bytes 262176 | tf_op jit(solution)/shard_map/ppermute | solution.py:39
  56.1 4.3 %collective-permute-start.5 = (bf16[256,512]{1,0:T(8,128)(2,1)S(1)}, bf16[256,512]{1,0:T(8,128)(2,1)}, u32[]{:S(2)}, u32[]{:S(2)}) collective-permute-start(bf16[256,512]{1,0:T(8,128)(2,1)S(1)} %bitcast_dynamic-update-slice_fusion.refs_3_.refs_7_), channel_id=1, source_target_pairs={{0,2},{2,4},{4,6},{6,8},{8,10},{10,12},{12,14},{1,3},{3,5},{5,7},{... | collective-permute-start | bytes 786440 | tf_op jit(solution)/shard_map/ppermute | solution.py:39
  63.1 3.4 %pick.1 = (bf16[128,3072]{1,0:T(8,128)(2,1)S(1)}, bf16[128,3072]{1,0:T(8,128)(2,1)S(1)}, f32[128,128]{1,0:T(8,128)S(1)}) custom-call(s32[128,2]{1,0:T(8,128)S(1)} %copy-done.23, bf16[256,3072]{1,0:T(8,128)(2,1)S(1)} %bitcast.39, bf16[256,3072]{1,0:T(8,128)(2,1)} %collective-permute-done.2.there, bf16[128,3072]{1,0:T(8,128)(2,1)S(1)} %copy-done.5), custom_call_target="tpu_custom_call" | custom-call | flops 805306368 | bytes 6291456 | tf_op jit(solution)/shard_map/pick/pallas_call | solution.py:382
  69.0 5.0 %collective-permute-start.10 = (bf16[8,16,3072]{2,1,0:T(8,128)(2,1)}, bf16[8,16,3072]{2,1,0:T(8,128)(2,1)S(1)}, u32[]{:S(2)}, u32[]{:S(2)}) collective-permute-start(bf16[8,16,3072]{2,1,0:T(8,128)(2,1)} %collective-permute-done.6.refs_5_.refs_3_), channel_id=1, source_target_pairs={{0,4},{2,6},{4,8},{6,10},{8,12},{10,14},{12,0},{14,2},{1,5},{3,7},... | collective-permute-start | bytes 2359304 | tf_op jit(solution)/shard_map/ppermute | solution.py:77
  74.0 2.0 collective-permute-start.11
  76.0 1.8 slice.40
  79.3 1.8 slice.41
  83.0 5.9 %attention.2 = (bf16[256,768]{1,0:T(8,128)(2,1)S(1)}, bf16[6,256,1024]{2,1,0:T(8,128)(2,1)S(1)}) custom-call(s32[1]{0:T(128)} %bitcast.11.place, bf16[256,1536]{1,0:T(8,128)(2,1)S(1)} %copy.48.q, bf16[256,512]{1,0:T(8,128)(2,1)S(1)} %collective-permute-done.3.refs_0_.refs_4_, bf16[256,512]{1,0:T(8,128)(2,1)S(1)} %collective-permute-done.4.refs_1_.refs_5_, ...), custom_call_target="tpu_custom_call" | custom-call | flops 805306368 | bytes 3145728 | tf_op jit(solution)/shard_map/attention/pallas_call | solution.py:270
  91.3 3.9 %collective-permute-done.13.refs_12_.refs_10_ = bf16[4,16,3072]{2,1,0:T(8,128)(2,1)} collective-permute-done((bf16[4,16,3072]{2,1,0:T(8,128)(2,1)}, bf16[4,16,3072]{2,1,0:T(8,128)(2,1)}, u32[]{:S(2)}, u32[]{:S(2)}) %collective-permute-start.13) | collective-permute-done | bytes 393248 | tf_op jit(solution)/shard_map/ppermute | solution.py:43
  99.7 1.8 slice.44
  102.0 6.4 %collective-permute-done.14.refs_13_.refs_11_ = bf16[4,16,3072]{2,1,0:T(8,128)(2,1)} collective-permute-done((bf16[4,16,3072]{2,1,0:T(8,128)(2,1)}, bf16[4,16,3072]{2,1,0:T(8,128)(2,1)}, u32[]{:S(2)}, u32[]{:S(2)}) %collective-permute-start.14) | collective-permute-done | bytes 393248 | tf_op jit(solution)/shard_map/ppermute | solution.py:91
  110.0 6.0 %attention.3 = (bf16[256,768]{1,0:T(8,128)(2,1)S(1)}, bf16[6,256,1024]{2,1,0:T(8,128)(2,1)S(1)}) custom-call(s32[1]{0:T(128)} %bitcast.11.place, bf16[256,1536]{1,0:T(8,128)(2,1)S(1)} %copy.48.q, bf16[256,512]{1,0:T(8,128)(2,1)S(1)} %collective-permute-done.3.refs_0_.refs_4_, bf16[256,512]{1,0:T(8,128)(2,1)S(1)} %collective-permute-done.4.refs_1_.refs_5_, ...), custom_call_target="tpu_custom_call" | custom-call | flops 805306368 | bytes 3145728 | tf_op jit(solution)/shard_map/attention/pallas_call | solution.py:270
  117.7 3.7 %collective-permute-done.18.refs_17_.refs_15_ = bf16[4,16,3072]{2,1,0:T(8,128)(2,1)} collective-permute-done((bf16[4,16,3072]{2,1,0:T(8,128)(2,1)}, bf16[4,16,3072]{2,1,0:T(8,128)(2,1)}, u32[]{:S(2)}, u32[]{:S(2)}) %collective-permute-start.18) | collective-permute-done | bytes 393248 | tf_op jit(solution)/shard_map/ppermute | solution.py:43
  121.4 7.3 %project.1 = (f32[128,3072]{1,0:T(8,128)S(1)}, f32[128,3072]{1,0:T(8,128)}) custom-call(s32[12]{0:T(128)S(1)} %stack.61.table, s32[1]{0:T(128)} %bitcast.10.core, bf16[256,768]{1,0:T(8,128)(2,1)S(1)} %copy-done.8, bf16[256,768]{1,0:T(8,128)(2,1)S(1)} %get-tuple-element.75.refs_1_.attn, bf16[12,16,3072]{2,1,0:T(8,128)(2,1)S(1)} %copy-done, ...), custom_call_target="tpu_custom_call" | custom-call | flops 2415919104 | bytes 9437184 | tf_op jit(solution)/shard_map/project/pallas_call | solution.py:165
  129.9 2.0 copy.66
  139.3 6.9 %middle.1 = (bf16[128,3072]{1,0:T(8,128)(2,1)}, bf16[128,3072]{1,0:T(8,128)(2,1)}, f32[128,128]{1,0:T(8,128)S(1)}) custom-call(s32[128,2]{1,0:T(8,128)S(1)} %copy-done.22, f32[128,3072]{1,0:T(8,128)S(1)} %copy-done.15, f32[128,3072]{1,0:T(8,128)} %collective-permute-done.19.recv, bf16[128,3072]{1,0:T(8,128)(2,1)S(1)} %copy-done.16, ...), custom_call_target="tpu_custom_call" | custom-call | flops 402653184 | bytes 7864320 | tf_op jit(solution)/shard_map/middle/pallas_call | solution.py:430
  146.3 3.3 %spread.1 = (bf16[256,3072]{1,0:T(8,128)(2,1)S(1)}, bf16[256,3072]{1,0:T(8,128)(2,1)}) custom-call(s32[2,128]{1,0:T(2,128)S(1)} %bitcast.41, f32[128,128]{1,0:T(8,128)S(1)} %get-tuple-element.97.gates, bf16[128,3072]{1,0:T(8,128)(2,1)S(1)} %copy-done.6), custom_call_target="tpu_custom_call" | custom-call | flops 805306368 | bytes 3932160 | tf_op jit(solution)/shard_map/spread/pallas_call | solution.py:460
  151.4 4.5 %collective-permute-done.20.recv = bf16[128,3072]{1,0:T(8,128)(2,1)} collective-permute-done((bf16[128,3072]{1,0:T(8,128)(2,1)}, bf16[128,3072]{1,0:T(8,128)(2,1)}, u32[]{:S(2)}, u32[]{:S(2)}) %collective-permute-start.20) | collective-permute-done | bytes 786464 | tf_op jit(solution)/shard_map/ppermute | solution.py:43
  155.9 7.7 %dattention.1.dout = bf16[256,1536]{1,0:T(8,128)(2,1)S(1)} custom-call(s32[12]{0:T(128)S(1)} %stack.61.table, s32[1]{0:T(128)} %bitcast.10.core, bf16[128,3072]{1,0:T(8,128)(2,1)} %get-tuple-element.123.own, bf16[128,3072]{1,0:T(8,128)(2,1)} %collective-permute-done.20.recv, bf16[12,16,3072]{2,1,0:T(8,128)(2,1)S(1)} %copy-done, ...), custom_call_target="tpu_custom_call" | custom-call | flops 2415919104 | bytes 9437184 | tf_op jit(solution)/shard_map/dattention/pallas_call | solution.py:221
  163.6 7.2 %attention_grad.3 = (bf16[256,768]{1,0:T(8,128)(2,1)S(1)}, bf16[256,256]{1,0:T(8,128)(2,1)S(1)}, bf16[256,256]{1,0:T(8,128)(2,1)S(1)}, bf16[256,256]{1,0:T(8,128)(2,1)}, f32[256,256]{1,0:T(8,128)S(1)}) custom-call(bf16[256,1536]{1,0:T(8,128)(2,1)S(1)} %copy.48.q, bf16[256,1536]{1,0:T(8,128)(2,1)S(1)} %dattention.1.dout, bf16[256,768]{1,0:T(8,128)(2,1)S(1)} %copy-done.11, ...), custom_call_target="tpu_custom_call" | custom-call | flops 1610612736 | bytes 3145728 | tf_op jit(solution)/shard_map/attention_grad/pallas_call | solution.py:334
  171.5 3.3 %collective-permute-start.24 = (bf16[256,256]{1,0:T(8,128)(2,1)}, bf16[256,256]{1,0:T(8,128)(2,1)}, u32[]{:S(2)}, u32[]{:S(2)}) collective-permute-start(bf16[256,256]{1,0:T(8,128)(2,1)} %get-tuple-element.92), channel_id=1, source_target_pairs={{2,0},{4,2},{6,4},{8,6},{10,8},{12,10},{14,12},{3,1},{5,3},{7,5},{... | collective-permute-start | bytes 393224 | tf_op jit(solution)/shard_map/ppermute | solution.py:39
  174.9 6.4 %attention_grad.2 = (bf16[256,768]{1,0:T(8,128)(2,1)S(1)}, bf16[256,256]{1,0:T(8,128)(2,1)S(1)}, bf16[256,256]{1,0:T(8,128)(2,1)S(1)}, bf16[256,256]{1,0:T(8,128)(2,1)S(1)}, f32[256,256]{1,0:T(8,128)S(1)}) custom-call(bf16[256,1536]{1,0:T(8,128)(2,1)S(1)} %copy.48.q, bf16[256,1536]{1,0:T(8,128)(2,1)S(1)} %dattention.1.dout, bf16[256,768]{1,0:T(8,128)(2,1)S(1)} %copy-done.9, ...), custom_call_target="tpu_custom_call" | custom-call | flops 1610612736 | bytes 3145728 | tf_op jit(solution)/shard_map/attention_grad/pallas_call | solution.py:334
  187.6 1.9 collective-permute-start.21
  192.2 3.7 %maximum_select_fusion = bf16[1,4,2,64,3072]{4,3,2,1,0:T(8,128)(2,1)} fusion(bf16[1,4,1,64,3072]{4,3,2,1,0:T(8,128)(2,1)} %bitcast.21, bf16[1,4,1,64,3072]{4,3,2,1,0:T(8,128)(2,1)S(1)} %bitcast.40, pred[]{:T(512)S(6)} %eq.33), kind=kLoop, calls=%fused_computation | loop fusion | flops 4718592 | bytes 6291457 | tf_op jit(solution)/shard_map/jit(_where)/select_n | solution.py:543
  195.8 4.6 %collective-permute-done.26 = bf16[256,256]{1,0:T(8,128)(2,1)S(1)} collective-permute-done((bf16[256,256]{1,0:T(8,128)(2,1)S(1)}, bf16[256,256]{1,0:T(8,128)(2,1)S(1)}, u32[]{:S(2)}, u32[]{:S(2)}) %collective-permute-start.26) | collective-permute-done | bytes 131104 | tf_op jit(solution)/shard_map/ppermute | solution.py:39
  200.4 10.6 %collective-permute-done.23 = bf16[256,256]{1,0:T(8,128)(2,1)S(1)} collective-permute-done((bf16[256,256]{1,0:T(8,128)(2,1)S(1)}, bf16[256,256]{1,0:T(8,128)(2,1)S(1)}, u32[]{:S(2)}, u32[]{:S(2)}) %collective-permute-start.23) | collective-permute-done | bytes 131104 | tf_op jit(solution)/shard_map/ppermute | solution.py:39
  (138 shorter events, 54.7 us)
Async XLA Ops:
  4.1 23.2 %collective-permute-start.2 = (bf16[256,3072]{1,0:T(8,128)(2,1)}, bf16[256,3072]{1,0:T(8,128)(2,1)}, u32[]{:S(2)}, u32[]{:S(2)}) collective-permute-start(bf16[256,3072]{1,0:T(8,128)(2,1)} %bitcast.13), channel_id=1, source_target_pairs={{0,1},{1,0},{2,3},{3,2},{4,5},{5,4},{6,7},{7,6},{8,9},{9,8},{10,11... | collective-permute-start | bytes 4718600 | tf_op jit(solution)/shard_map/ppermute | solution.py:43
  5.1 22.1 %collective-permute-start = (bf16[8,16,3072]{2,1,0:T(8,128)(2,1)}, bf16[8,16,3072]{2,1,0:T(8,128)(2,1)}, u32[]{:S(2)}, u32[]{:S(2)}) collective-permute-start(bf16[8,16,3072]{2,1,0:T(8,128)(2,1)} %pad_maximum_fusion), channel_id=1, source_target_pairs={{0,4},{2,6},{4,8},{6,10},{8,12},{10,14},{12,0},{14,2},{1,5},{3,7},... | collective-permute-start | bytes 2359304 | tf_op jit(solution)/shard_map/ppermute | solution.py:77
  6.7 20.6 %collective-permute-start.1 = (bf16[8,16,3072]{2,1,0:T(8,128)(2,1)}, bf16[8,16,3072]{2,1,0:T(8,128)(2,1)}, u32[]{:S(2)}, u32[]{:S(2)}) collective-permute-start(bf16[8,16,3072]{2,1,0:T(8,128)(2,1)} %pad_maximum_fusion), channel_id=1, source_target_pairs={{0,2},{2,0},{4,6},{6,4},{8,10},{10,8},{12,14},{14,12},{1,3},{3,1},... | collective-permute-start | bytes 2359304 | tf_op jit(solution)/shard_map/ppermute | solution.py:78
  27.2 41.8 %collective-permute-start.6 = (bf16[8,16,3072]{2,1,0:T(8,128)(2,1)}, bf16[8,16,3072]{2,1,0:T(8,128)(2,1)}, u32[]{:S(2)}, u32[]{:S(2)}) collective-permute-start(bf16[8,16,3072]{2,1,0:T(8,128)(2,1)} %collective-permute-done.refs_3_.refs_1_), channel_id=1, source_target_pairs={{0,4},{2,6},{4,8},{6,10},{8,12},{10,14},{12,0},{14,2},{1,5},{3,7},... | collective-permute-start | bytes 2359304 | tf_op jit(solution)/shard_map/ppermute | solution.py:77
  28.2 40.8 %collective-permute-start.7 = (bf16[8,16,3072]{2,1,0:T(8,128)(2,1)}, bf16[8,16,3072]{2,1,0:T(8,128)(2,1)}, u32[]{:S(2)}, u32[]{:S(2)}) collective-permute-start(bf16[8,16,3072]{2,1,0:T(8,128)(2,1)} %collective-permute-done.refs_3_.refs_1_), channel_id=1, source_target_pairs={{0,2},{2,0},{4,6},{6,4},{8,10},{10,8},{12,14},{14,12},{1,3},{3,1},... | collective-permute-start | bytes 2359304 | tf_op jit(solution)/shard_map/ppermute | solution.py:78
  28.7 23.4 %collective-permute-start.3 = (bf16[256,512]{1,0:T(8,128)(2,1)S(1)}, bf16[256,512]{1,0:T(8,128)(2,1)S(1)}, u32[]{:S(2)}, u32[]{:S(2)}) collective-permute-start(bf16[256,512]{1,0:T(8,128)(2,1)S(1)} %bitcast_dynamic-update-slice_fusion.refs_3_.refs_7_), channel_id=1, source_target_pairs={{0,6},{2,8},{4,10},{6,12},{8,14},{1,7},{3,9},{5,11},{7,13},{9,15},... | collective-permute-start | bytes 786440 | tf_op jit(solution)/shard_map/ppermute | solution.py:39
  32.9 23.2 %collective-permute-start.4 = (bf16[256,512]{1,0:T(8,128)(2,1)S(1)}, bf16[256,512]{1,0:T(8,128)(2,1)S(1)}, u32[]{:S(2)}, u32[]{:S(2)}) collective-permute-start(bf16[256,512]{1,0:T(8,128)(2,1)S(1)} %bitcast_dynamic-update-slice_fusion.refs_3_.refs_7_), channel_id=1, source_target_pairs={{0,4},{2,6},{4,8},{6,10},{8,12},{10,14},{1,5},{3,7},{5,9},{7,11},{... | collective-permute-start | bytes 786440 | tf_op jit(solution)/shard_map/ppermute | solution.py:39
  38.7 30.3 %collective-permute-start.8 = (bf16[4,16,3072]{2,1,0:T(8,128)(2,1)}, bf16[4,16,3072]{2,1,0:T(8,128)(2,1)}, u32[]{:S(2)}, u32[]{:S(2)}) collective-permute-start(bf16[4,16,3072]{2,1,0:T(8,128)(2,1)} %slice.38), channel_id=1, source_target_pairs={{0,16},{16,0},{1,17},{17,1},{2,18},{18,2},{3,19},{19,3},{4,20},{20... | collective-permute-start | bytes 1179656 | tf_op jit(solution)/shard_map/ppermute | solution.py:43
  52.1 16.9 %collective-permute-start.9 = (bf16[4,16,3072]{2,1,0:T(8,128)(2,1)}, bf16[4,16,3072]{2,1,0:T(8,128)(2,1)}, u32[]{:S(2)}, u32[]{:S(2)}) collective-permute-start(bf16[4,16,3072]{2,1,0:T(8,128)(2,1)} %slice.39), channel_id=1, source_target_pairs={{0,16},{16,0},{1,17},{17,1},{2,18},{18,2},{3,19},{19,3},{4,20},{20... | collective-permute-start | bytes 1179656 | tf_op jit(solution)/shard_map/ppermute | solution.py:43
  56.1 12.9 %collective-permute-start.5 = (bf16[256,512]{1,0:T(8,128)(2,1)S(1)}, bf16[256,512]{1,0:T(8,128)(2,1)}, u32[]{:S(2)}, u32[]{:S(2)}) collective-permute-start(bf16[256,512]{1,0:T(8,128)(2,1)S(1)} %bitcast_dynamic-update-slice_fusion.refs_3_.refs_7_), channel_id=1, source_target_pairs={{0,2},{2,4},{4,6},{6,8},{8,10},{10,12},{12,14},{1,3},{3,5},{5,7},{... | collective-permute-start | bytes 786440 | tf_op jit(solution)/shard_map/ppermute | solution.py:39
  69.0 26.2 %collective-permute-start.10 = (bf16[8,16,3072]{2,1,0:T(8,128)(2,1)}, bf16[8,16,3072]{2,1,0:T(8,128)(2,1)S(1)}, u32[]{:S(2)}, u32[]{:S(2)}) collective-permute-start(bf16[8,16,3072]{2,1,0:T(8,128)(2,1)} %collective-permute-done.6.refs_5_.refs_3_), channel_id=1, source_target_pairs={{0,4},{2,6},{4,8},{6,10},{8,12},{10,14},{12,0},{14,2},{1,5},{3,7},... | collective-permute-start | bytes 2359304 | tf_op jit(solution)/shard_map/ppermute | solution.py:77
  74.0 21.2 %collective-permute-start.11 = (bf16[8,16,3072]{2,1,0:T(8,128)(2,1)}, bf16[8,16,3072]{2,1,0:T(8,128)(2,1)}, u32[]{:S(2)}, u32[]{:S(2)}) collective-permute-start(bf16[8,16,3072]{2,1,0:T(8,128)(2,1)} %collective-permute-done.6.refs_5_.refs_3_), channel_id=1, source_target_pairs={{0,2},{2,0},{4,6},{6,4},{8,10},{10,8},{12,14},{14,12},{1,3},{3,1},... | collective-permute-start | bytes 2359304 | tf_op jit(solution)/shard_map/ppermute | solution.py:78
  77.8 13.5 %collective-permute-start.12 = (bf16[4,16,3072]{2,1,0:T(8,128)(2,1)}, bf16[4,16,3072]{2,1,0:T(8,128)(2,1)}, u32[]{:S(2)}, u32[]{:S(2)}) collective-permute-start(bf16[4,16,3072]{2,1,0:T(8,128)(2,1)} %slice.40), channel_id=1, source_target_pairs={{0,16},{16,0},{1,17},{17,1},{2,18},{18,2},{3,19},{19,3},{4,20},{20... | collective-permute-start | bytes 1179656 | tf_op jit(solution)/shard_map/ppermute | solution.py:43
  81.1 14.1 %collective-permute-start.13 = (bf16[4,16,3072]{2,1,0:T(8,128)(2,1)}, bf16[4,16,3072]{2,1,0:T(8,128)(2,1)}, u32[]{:S(2)}, u32[]{:S(2)}) collective-permute-start(bf16[4,16,3072]{2,1,0:T(8,128)(2,1)} %slice.41), channel_id=1, source_target_pairs={{0,16},{16,0},{1,17},{17,1},{2,18},{18,2},{3,19},{19,3},{4,20},{20... | collective-permute-start | bytes 1179656 | tf_op jit(solution)/shard_map/ppermute | solution.py:43
  96.2 12.3 %collective-permute-start.14 = (bf16[4,16,3072]{2,1,0:T(8,128)(2,1)}, bf16[4,16,3072]{2,1,0:T(8,128)(2,1)}, u32[]{:S(2)}, u32[]{:S(2)}) collective-permute-start(bf16[4,16,3072]{2,1,0:T(8,128)(2,1)} %get-tuple-element.133), channel_id=1, source_target_pairs={{0,2},{2,0},{4,6},{6,4},{8,10},{10,8},{12,14},{14,12},{1,3},{3,1},... | collective-permute-start | bytes 1179656 | tf_op jit(solution)/shard_map/ppermute | solution.py:91
  96.5 21.2 %collective-permute-start.16 = (bf16[4,16,3072]{2,1,0:T(8,128)(2,1)}, bf16[4,16,3072]{2,1,0:T(8,128)(2,1)}, u32[]{:S(2)}, u32[]{:S(2)}) collective-permute-start(bf16[4,16,3072]{2,1,0:T(8,128)(2,1)} %get-tuple-element.133), channel_id=1, source_target_pairs={{0,16},{16,0},{1,17},{17,1},{2,18},{18,2},{3,19},{19,3},{4,20},{20... | collective-permute-start | bytes 1179656 | tf_op jit(solution)/shard_map/ppermute | solution.py:43
  98.0 19.7 %collective-permute-start.15 = (bf16[4,16,3072]{2,1,0:T(8,128)(2,1)}, bf16[4,16,3072]{2,1,0:T(8,128)(2,1)}, u32[]{:S(2)}, u32[]{:S(2)}) collective-permute-start(bf16[4,16,3072]{2,1,0:T(8,128)(2,1)} %get-tuple-element.132), channel_id=1, source_target_pairs={{0,2},{2,0},{4,6},{6,4},{8,10},{10,8},{12,14},{14,12},{1,3},{3,1},... | collective-permute-start | bytes 1179656 | tf_op jit(solution)/shard_map/ppermute | solution.py:92
  101.5 16.2 %collective-permute-start.17 = (bf16[4,16,3072]{2,1,0:T(8,128)(2,1)}, bf16[4,16,3072]{2,1,0:T(8,128)(2,1)}, u32[]{:S(2)}, u32[]{:S(2)}) collective-permute-start(bf16[4,16,3072]{2,1,0:T(8,128)(2,1)} %slice.44), channel_id=1, source_target_pairs={{0,16},{16,0},{1,17},{17,1},{2,18},{18,2},{3,19},{19,3},{4,20},{20... | collective-permute-start | bytes 1179656 | tf_op jit(solution)/shard_map/ppermute | solution.py:43
  108.4 13.0 %collective-permute-start.18 = (bf16[4,16,3072]{2,1,0:T(8,128)(2,1)}, bf16[4,16,3072]{2,1,0:T(8,128)(2,1)}, u32[]{:S(2)}, u32[]{:S(2)}) collective-permute-start(bf16[4,16,3072]{2,1,0:T(8,128)(2,1)} %collective-permute-done.14.refs_13_.refs_11_), channel_id=1, source_target_pairs={{0,16},{16,0},{1,17},{17,1},{2,18},{18,2},{3,19},{19,3},{4,20},{20... | collective-permute-start | bytes 1179656 | tf_op jit(solution)/shard_map/ppermute | solution.py:43
  110.0 11.4 %copy-start.8 = (bf16[256,768]{1,0:T(8,128)(2,1)S(1)}, bf16[256,768]{1,0:T(8,128)(2,1)}, u32[]{:S(2)}) copy-start(bf16[256,768]{1,0:T(8,128)(2,1)} %copy-done.7) | copy-start | bytes 1179652
  129.9 4.3 %collective-permute-start.19 = (f32[128,3072]{1,0:T(8,128)}, f32[128,3072]{1,0:T(8,128)}, u32[]{:S(2)}, u32[]{:S(2)}) collective-permute-start(f32[128,3072]{1,0:T(8,128)} %get-tuple-element.82), channel_id=1, source_target_pairs={{0,1},{1,0},{2,3},{3,2},{4,5},{5,4},{6,7},{7,6},{8,9},{9,8},{10,11... | collective-permute-start | bytes 4718600 | tf_op jit(solution)/shard_map/ppermute | solution.py:43
  150.8 40.0 %collective-permute-start.27 = (bf16[256,3072]{1,0:T(8,128)(2,1)}, bf16[256,3072]{1,0:T(8,128)(2,1)}, u32[]{:S(2)}, u32[]{:S(2)}) collective-permute-start(bf16[256,3072]{1,0:T(8,128)(2,1)} %get-tuple-element.99), channel_id=1, source_target_pairs={{0,1},{1,0},{2,3},{3,2},{4,5},{5,4},{6,7},{7,6},{8,9},{9,8},{10,11... | collective-permute-start | bytes 4718600 | tf_op jit(solution)/shard_map/ppermute | solution.py:43
  151.3 4.5 %collective-permute-start.20 = (bf16[128,3072]{1,0:T(8,128)(2,1)}, bf16[128,3072]{1,0:T(8,128)(2,1)}, u32[]{:S(2)}, u32[]{:S(2)}) collective-permute-start(bf16[128,3072]{1,0:T(8,128)(2,1)} %get-tuple-element.123.own), channel_id=1, source_target_pairs={{0,1},{1,0},{2,3},{3,2},{4,5},{5,4},{6,7},{7,6},{8,9},{9,8},{10,11... | collective-permute-start | bytes 2359304 | tf_op jit(solution)/shard_map/ppermute | solution.py:43
  151.4 12.2 %copy-start.4 = (bf16[6,256,1024]{2,1,0:T(8,128)(2,1)S(1)}, bf16[6,256,1024]{2,1,0:T(8,128)(2,1)}, u32[]{:S(2)}) copy-start(bf16[6,256,1024]{2,1,0:T(8,128)(2,1)} %copy-done.3) | copy-start | bytes 9437188
  151.4 12.2 %copy-start.11 = (bf16[256,768]{1,0:T(8,128)(2,1)S(1)}, bf16[256,768]{1,0:T(8,128)(2,1)}, u32[]{:S(2)}) copy-start(bf16[256,768]{1,0:T(8,128)(2,1)} %copy-done.10) | copy-start | bytes 1179652
  163.6 11.3 %copy-start.2 = (bf16[6,256,1024]{2,1,0:T(8,128)(2,1)S(1)}, bf16[6,256,1024]{2,1,0:T(8,128)(2,1)}, u32[]{:S(2)}) copy-start(bf16[6,256,1024]{2,1,0:T(8,128)(2,1)} %copy-done.1) | copy-start | bytes 9437188
  171.5 18.0 %collective-permute-start.24 = (bf16[256,256]{1,0:T(8,128)(2,1)}, bf16[256,256]{1,0:T(8,128)(2,1)}, u32[]{:S(2)}, u32[]{:S(2)}) collective-permute-start(bf16[256,256]{1,0:T(8,128)(2,1)} %get-tuple-element.92), channel_id=1, source_target_pairs={{2,0},{4,2},{6,4},{8,6},{10,8},{12,10},{14,12},{3,1},{5,3},{7,5},{... | collective-permute-start | bytes 393224 | tf_op jit(solution)/shard_map/ppermute | solution.py:39
  185.0 10.8 %collective-permute-start.25 = (bf16[256,256]{1,0:T(8,128)(2,1)S(1)}, bf16[256,256]{1,0:T(8,128)(2,1)S(1)}, u32[]{:S(2)}, u32[]{:S(2)}) collective-permute-start(bf16[256,256]{1,0:T(8,128)(2,1)S(1)} %copy-done.27), channel_id=1, source_target_pairs={{4,0},{6,2},{8,4},{10,6},{12,8},{14,10},{5,1},{7,3},{9,5},{11,7},{... | collective-permute-start | bytes 393224 | tf_op jit(solution)/shard_map/ppermute | solution.py:39
  186.3 14.1 %collective-permute-start.26 = (bf16[256,256]{1,0:T(8,128)(2,1)S(1)}, bf16[256,256]{1,0:T(8,128)(2,1)S(1)}, u32[]{:S(2)}, u32[]{:S(2)}) collective-permute-start(bf16[256,256]{1,0:T(8,128)(2,1)S(1)} %get-tuple-element.94), channel_id=1, source_target_pairs={{6,0},{8,2},{10,4},{12,6},{14,8},{7,1},{9,3},{11,5},{13,7},{15,9},... | collective-permute-start | bytes 393224 | tf_op jit(solution)/shard_map/ppermute | solution.py:39
  187.6 12.8 %collective-permute-start.21 = (bf16[256,256]{1,0:T(8,128)(2,1)S(1)}, bf16[256,256]{1,0:T(8,128)(2,1)S(1)}, u32[]{:S(2)}, u32[]{:S(2)}) collective-permute-start(bf16[256,256]{1,0:T(8,128)(2,1)S(1)} %copy-done.31), channel_id=1, source_target_pairs={{2,0},{4,2},{6,4},{8,6},{10,8},{12,10},{14,12},{3,1},{5,3},{7,5},{... | collective-permute-start | bytes 393224 | tf_op jit(solution)/shard_map/ppermute | solution.py:39
  189.6 10.9 %collective-permute-start.22 = (bf16[256,256]{1,0:T(8,128)(2,1)S(1)}, bf16[256,256]{1,0:T(8,128)(2,1)S(1)}, u32[]{:S(2)}, u32[]{:S(2)}) collective-permute-start(bf16[256,256]{1,0:T(8,128)(2,1)S(1)} %copy-done.29), channel_id=1, source_target_pairs={{4,0},{6,2},{8,4},{10,6},{12,8},{14,10},{5,1},{7,3},{9,5},{11,7},{... | collective-permute-start | bytes 393224 | tf_op jit(solution)/shard_map/ppermute | solution.py:39
  190.9 20.2 %collective-permute-start.23 = (bf16[256,256]{1,0:T(8,128)(2,1)S(1)}, bf16[256,256]{1,0:T(8,128)(2,1)S(1)}, u32[]{:S(2)}, u32[]{:S(2)}) collective-permute-start(bf16[256,256]{1,0:T(8,128)(2,1)S(1)} %get-tuple-element.90), channel_id=1, source_target_pairs={{6,0},{8,2},{10,4},{12,6},{14,8},{7,1},{9,3},{11,5},{13,7},{15,9},... | collective-permute-start | bytes 393224 | tf_op jit(solution)/shard_map/ppermute | solution.py:39
  (31 other events, 88.2 us)

commit v3 on v2

--- a/solution.py
+++ b/solution.py
@@ -10,7 +10,7 @@
 BAND_BLOCKS = 4
 F32 = jnp.float32
 BF16 = jnp.bfloat16
-VMEM_LIMIT = 24 * 1024 * 1024
+VMEM_LIMIT = 56 * 1024 * 1024
 
 
 def params(limit=VMEM_LIMIT):
@@ -47,60 +47,42 @@
     return lax.optimization_barrier((tuple(values), others))[0]
 
 
-def gathered(w_out, work):
+def gathered(w_out, first_task, second_task, last_task):
     heads, depth, _ = w_out.shape
     count = lax.axis_size("ctx")
     place = lax.axis_index("ctx")
-    if count != 8 or lax.axis_size("groups") != 2 or heads % 3:
+    if count != 8 or lax.axis_size("groups") != 2 or heads % 2:
         full = lax.all_gather(w_out, "ctx", axis=1, tiled=True)
-        for task in work:
-            task(())
-        return [full], jnp.zeros((1,), jnp.int32), [(0, 0, heads, 0, 0)]
+        for task in (first_task, second_task, last_task):
+            task()
+        return [full], jnp.zeros((1,), jnp.int32), [(0, heads, 0, 0)]
     side = lax.axis_index("groups")
-    third = heads // 3
-    mine = lax.dynamic_slice_in_dim(w_out, side * third, third, 0)
-    ring = [(c, (c + 2) % count) for c in range(count)]
-    pairs = [(c, c ^ 1) for c in range(count)]
-    arrays, plan = [w_out], [(0, 0, heads, 0, 4)]
-    table = [0, side * third, (1 - side) * third, 2 * third]
+    half = heads // 2
+    ring = lambda value: lax.ppermute(value, "ctx", [(c, (c + 2) % count) for c in range(count)])
+    pair = lambda value: lax.ppermute(value, "ctx", [(c, c ^ 1) for c in range(count)])
+    cross = lambda value: swapped(value, "groups")
+    mine = lax.dynamic_slice_in_dim(w_out, side * half, half, 0)
+
+    z1, y0 = ring(mine), pair(mine)
+    (z1,) = after([z1], *first_task())
+    z2, y1, x1 = ring(z1), pair(z1), cross(z1)
+    z2, y0 = after([z2, y0], *second_task())
+    z3, y2, x2 = ring(z2), pair(z2), cross(y0)
+    z3, x1 = after([z3, x1], y1)
+    z4, y3, x3 = ring(x1), pair(z3), cross(z3)
+    y2, z4 = after([y2, z4], x2, y2)
+    x4 = cross(y2)
+    y3, last = after([y3, x1], x3, z4)
+    y4, x5 = pair(last), cross(y3)
+    last_task(z4, x3)
+
+    table = [0, side * half, (1 - side) * half]
     table += [depth * ((place - 2 * k) % count) for k in range(4)]
     table += [depth * (((place - 2 * k) % count) ^ 1) for k in range(4)]
-
-    def add(array, parts, row):
-        arrays.append(array)
-        for start, size, head in parts:
-            plan.append((len(arrays) - 1, start, size, head, row))
-
-    both = [(0, third, 1), (third, third, 3)]
-    held, across = jnp.concatenate([mine, w_out[2 * third :]], axis=0), None
-    for k in range(3):
-        moved = lax.ppermute(held, "ctx", ring)
-        paired = lax.ppermute(held, "ctx", pairs)
-        sent = [moved, paired]
-        if k > 0:
-            sent.append(swapped(held[:third], "groups"))
-            sent.append(swapped(across[:third], "groups"))
-        done = work[k]([held])
-        sent = after(sent, *done)
-        add(sent[0], both, 5 + k)
-        add(sent[1], both, 8 + k)
-        if k > 0:
-            add(sent[2], [(0, third, 2)], 4 + k)
-            add(sent[3], [(0, third, 2)], 7 + k)
-        held, across = sent[0], sent[1]
-    first = lax.ppermute(held[:third], "ctx", pairs)
-    last = lax.ppermute(held[third:], "ctx", pairs)
-    beside = swapped(held[:third], "groups")
-    beyond = swapped(across[:third], "groups")
-    done = work[3]([held])
-    first = after([first], *done)[0]
-    final = swapped(first, "groups")
-    work[4]([first])
-    add(first, [(0, third, 1)], 11)
-    add(last, [(0, third, 3)], 11)
-    add(beside, [(0, third, 2)], 7)
-    add(beyond, [(0, third, 2)], 10)
-    add(final, [(0, third, 2)], 11)
+    arrays = [w_out, z1, z2, z3, y0, y1, y2, y3, x1, z4, x3, x2, y4, x4, x5]
+    plan = [(0, heads, 0, 3)]
+    plan += [(1 + k, half, 1, 4 + k) for k in range(7)]
+    plan += [(8 + k, half, 2, 4 + k) for k in range(7)]
     return arrays, jnp.stack([jnp.asarray(t, jnp.int32) for t in table]), plan
 
 
@@ -108,11 +90,11 @@
     copies = []
     columns = pl.ds(pl.multiple_of(chunk * chunk_size, chunk_size), chunk_size)
     depth_of = [p.shape[1] for p in pieces]
-    for number, (array, start, size, head, row) in enumerate(plan):
+    for number, (array, size, head, row) in enumerate(plan):
         rows = pl.ds(pl.multiple_of(table[row], depth_of[array]), depth_of[array])
         copies.append(
             pltpu.make_async_copy(
-                pieces[array].at[pl.ds(start, size), :, columns],
+                pieces[array].at[:, :, columns],
                 buf.at[pl.ds(table[head], size), rows, columns],
                 sem.at[number, chunk],
             )
@@ -261,18 +243,18 @@
     attn[...] = dot_nn(weight, band_of(values)).astype(BF16)
 
 
-def attention(queries, bands, place, which, heads, heads_kv, head_dim, scale):
-    tok = queries.shape[0]
+def attention(queries, bands, place, heads, heads_kv, head_dim, scale):
+    tok = queries.shape[1]
     group = heads // heads_kv
-    keys = pl.BlockSpec((tok, head_dim), lambda h, *_: (0, which))
-    values = pl.BlockSpec((tok, head_dim), lambda h, *_: (0, heads_kv + which))
+    keys = pl.BlockSpec((tok, head_dim), lambda h, *_: (0, h // group))
+    values = pl.BlockSpec((tok, head_dim), lambda h, *_: (0, heads_kv + h // group))
     span = BAND_BLOCKS * tok
     return pl.pallas_call(
         functools.partial(attention_kernel, scale),
         grid_spec=pltpu.PrefetchScalarGridSpec(
             num_scalar_prefetch=1,
-            grid=(group,),
-            in_specs=[pl.BlockSpec((tok, head_dim), lambda h, *_: (0, which * group + h))]
+            grid=(heads,),
+            in_specs=[pl.BlockSpec((None, tok, head_dim), lambda h, *_: (h, 0, 0))]
             + [keys] * BAND_BLOCKS
             + [values] * BAND_BLOCKS,
             out_specs=[
@@ -281,16 +263,17 @@
             ],
         ),
         out_shape=[
-            jax.ShapeDtypeStruct((tok, group * head_dim), BF16),
-            jax.ShapeDtypeStruct((group, tok, span), BF16),
+            jax.ShapeDtypeStruct((tok, heads * head_dim), BF16),
+            jax.ShapeDtypeStruct((heads, tok, span), BF16),
         ],
         compiler_params=params(),
-        cost_estimate=cost(4 * tok * span * group * head_dim, 2 * group * tok * span, group * tok * span),
+        cost_estimate=cost(4 * tok * span * heads * head_dim, 2 * heads * tok * span, heads * tok * span),
         name="attention",
     )(place, queries, *bands, *bands)
 
 
-def attention_grad_kernel(scale, group, q, dout, attn, probs, *refs):
+def attention_grad_kernel(scale, group, given, q, dout, attn, probs, *refs):
+    refs = refs[:2 * BAND_BLOCKS] + refs[2 * BAND_BLOCKS + given :]
     keys, values = refs[:BAND_BLOCKS], refs[BAND_BLOCKS : 2 * BAND_BLOCKS]
     dq, outs, (dk, dv) = refs[2 * BAND_BLOCKS], refs[2 * BAND_BLOCKS + 1 : -2], refs[-2:]
     tok, head_dim = q.shape
@@ -322,31 +305,34 @@
             out[:, head_dim:] = dv[rows, :].astype(out.dtype)
 
 
-def attention_grad(queries, dout, attn, probs, bands, which, heads, heads_kv, head_dim, scale):
-    tok = queries.shape[0]
+def attention_grad(queries, dout, attn, probs, bands, which, grad_q, heads_kv, scale):
+    heads, tok, head_dim = queries.shape
     group = heads // heads_kv
     keys = pl.BlockSpec((tok, head_dim), lambda h: (0, which))
     values = pl.BlockSpec((tok, head_dim), lambda h: (0, heads_kv + which))
-    per_head = pl.BlockSpec((tok, head_dim), lambda h: (0, h))
+    by_head = pl.BlockSpec((None, tok, head_dim), lambda h: (which * group + h, 0, 0))
     of_all = pl.BlockSpec((tok, head_dim), lambda h: (0, which * group + h))
     span = BAND_BLOCKS * tok
     whole = pl.BlockSpec((tok, 2 * head_dim), lambda h: (0, 0))
-    return pl.pallas_call(
-        functools.partial(attention_grad_kernel, scale, group),
+    given = [] if grad_q is None else [grad_q]
+    return pl.pallas_call(
+        functools.partial(attention_grad_kernel, scale, group, len(given)),
         grid=(group,),
-        in_specs=[of_all, of_all, per_head]
-        + [pl.BlockSpec((1, tok, span), lambda h: (h, 0, 0))]
+        in_specs=[by_head, of_all, of_all]
+        + [pl.BlockSpec((1, tok, span), lambda h: (which * group + h, 0, 0))]
         + [keys] * BAND_BLOCKS
-        + [values] * BAND_BLOCKS,
-        out_specs=[per_head] + [whole] * BAND_BLOCKS,
-        out_shape=[jax.ShapeDtypeStruct((tok, group * head_dim), BF16)]
+        + [values] * BAND_BLOCKS
+        + [pl.BlockSpec(memory_space=pl.ANY)] * len(given),
+        out_specs=[by_head] + [whole] * BAND_BLOCKS,
+        out_shape=[jax.ShapeDtypeStruct((heads, tok, head_dim), BF16)]
         + [jax.ShapeDtypeStruct((tok, 2 * head_dim), BF16)] * (BAND_BLOCKS - 1)
         + [jax.ShapeDtypeStruct((tok, 2 * head_dim), F32)],
         scratch_shapes=[pltpu.VMEM((span, head_dim), F32)] * 2,
-        compiler_params=params(),
-        cost_estimate=cost(8 * tok * span * group * head_dim, 2 * group * tok * span),
+        input_output_aliases={4 + 2 * BAND_BLOCKS: 0} if given else {},
+        compiler_params=params(),
+        cost_estimate=cost(tok, tok),
         name="attention_grad",
-    )(queries, dout, attn, probs, *bands, *bands)
+    )(queries, dout, attn, probs, *bands, *bands, *given)
 
 
 def pick_kernel(slots, here, there, gout, first, second, dgate):
@@ -491,7 +477,7 @@
     own_band = jnp.concatenate(
         [rotated_keys.reshape(tok, heads_kv * head_dim), value_inputs.reshape(tok, heads_kv * head_dim)], axis=1
     )
-    queries = queries_in.reshape(tok, heads_q * head_dim)
+    queries = jnp.transpose(queries_in, (1, 0, 2))
     sent = lax.dynamic_index_in_dim(expert_out[0], 1 - core, 1, keepdims=False).reshape(room, width)
     kept = lax.dynamic_index_in_dim(expert_out[0], core, 1, keepdims=False).reshape(room, width)
     flat = routes.reshape(-1)
@@ -500,58 +486,51 @@
     rank = jnp.sum(earlier.astype(jnp.int32), axis=1)
     slots = (flat * capacity + rank - core * room) % (experts * capacity)
     slots = slots.reshape(rows, 2)
+    router = jnp.pad(w_router, ((0, 0), (0, 128 - experts)))
+    router_t = jnp.pad(w_router.T, ((0, 128 - experts), (0, 0)))
     made = {}
 
-    def round_0(ready):
+    def exchange_rows():
         made["arrived"] = swapped(sent, "exp")
-        made["queries"] = queries
-        return [made["arrived"], queries, own_band, slots]
-
-    def round_1(ready):
+        return [made["arrived"], slots, own_band, router, router_t]
+
+    def pick_rows():
+        made["picked"] = pick(slots, kept, made["arrived"], grad_out)
+        return [made["picked"][2]]
+
+    def attend(*ready):
         band = after([own_band], *ready)[0]
         bands = [band] + [passed_along(band, "ctx", step) for step in range(1, BAND_BLOCKS)]
         made["bands"] = bands[::-1]
-        arrived = after([made["arrived"]], *ready)[0]
-        made["picked"] = pick(slots, kept, arrived, grad_out)
-        return [*made["bands"], made["picked"][2]]
-
-    def attend(which):
-        def task(ready):
-            bands = after(made["bands"], *ready)
-            made[which] = attention(queries, bands, place_arg, which, heads_q, heads_kv, head_dim, scale)
-            return [made[which][0]]
-
-        return task
-
-    tasks = [round_0, round_1, attend(0), lambda ready: (), attend(1)]
-    if heads_kv != 2:
-        tasks[4] = lambda ready: [attend(i)(ready) for i in range(1, heads_kv)]
-    arrays, table, plan = gathered(w_out, tasks)
+        made["attention"] = attention(
+            queries, made["bands"], place_arg, heads_q, heads_kv, head_dim, scale
+        )
+
+    arrays, table, plan = gathered(w_out, exchange_rows, pick_rows, attend)
     first, second, dgate = made["picked"]
-    attn, probs = zip(*[made[i] for i in range(heads_kv)])
+    attn, probs = made["attention"]
     bands = made["bands"]
 
-    own, other = project(attn, arrays, table, plan, core_arg, heads_q, head_dim, width, rows)
-    router = jnp.pad(w_router, ((0, 0), (0, 128 - experts)))
+    own, other = project([attn], arrays, table, plan, core_arg, heads_q, head_dim, width, rows)
     mixed, grad_input, gates = middle(
-        routes, own, swapped(other, "exp"), stream_in, first, second, grad_out, dgate, router, router.T
+        routes, own, swapped(other, "exp"), stream_in, first, second, grad_out, dgate, router, router_t
     )
     grad_other = swapped(grad_input, "exp")
     here, there = spread(slots.T, gates, grad_out, room)
+    dattn = dattention(grad_input, grad_other, arrays, table, plan, core_arg, heads_q, head_dim, width)
+    there = after([there], dattn)[0]
     back = swapped(there, "exp").reshape(held, 1, capacity, width)
     here = here.reshape(held, 1, capacity, width)
     grad_expert = jnp.where(
         core == 0, jnp.concatenate([here, back], axis=1), jnp.concatenate([back, here], axis=1)
     )[None]
-
-    dattn = dattention(grad_input, grad_other, arrays, table, plan, core_arg, heads_q, head_dim, width)
-    grads, totals = [], []
+    grads, totals, grad_q = [], [], None
     for i in range(heads_kv):
-        grad = attention_grad(queries, dattn, attn[i], probs[i], bands, i, heads_q, heads_kv, head_dim, scale)
-        passed = [passed_along(grad[BAND_BLOCKS - step], "ctx", -step) for step in range(1, BAND_BLOCKS)]
+        grad = attention_grad(queries, dattn, attn, probs, bands, i, grad_q, heads_kv, scale)
+        totals.append([passed_along(grad[BAND_BLOCKS - step], "ctx", -step) for step in range(1, BAND_BLOCKS)])
         grads.append(grad)
-        totals.append(passed)
-    grad_q = jnp.concatenate([g[0] for g in grads], axis=1).reshape(tok, heads_q, head_dim)
+        grad_q = grad[0]
+    grad_q = jnp.transpose(grad_q, (1, 0, 2))
     totals, grad_q, grad_expert = lax.optimization_barrier((totals, grad_q, grad_expert))
     sums = []
     for grad, passed in zip(grads, totals):

time: 216 us -> 193 us (0.89)
  local copies, waits for them, and re-layouts: 44.7 us -> 13.6 us
  waiting for transfers between devices: 63.4 us -> 82.1 us
  starting transfers between devices: 44.5 us -> 29.5 us
  Pallas kernels: 54.3 us -> 62.8 us
  other arithmetic: 6.83 us -> 2.29 us
    ppermute x8 -> x9, waiting for transfers between devices: 23.4 us -> 48.7 us  [the longest x4 48.7 us: gathered(): lax.ppermute(value, 'ctx', [(c, (c + 2) % count) for c in range(count)])]
    unnamed x77 -> x57, local copies, waits for them, and re-layouts: 25 us -> 5.01 us
    slice x6 -> x0, local copies, waits for them, and re-layouts: 9.92 us -> none  [the longest x2 3.58 us: gathered(): sent.append(swapped(across[:third], 'groups'))]
    ppermute x11 -> x9, waiting for transfers between devices: 12.1 us -> 3.63 us  [swapped(): return lax.ppermute(value, axis, [(0, 1), (1, 0)])]
    ppermute x8 -> x9, starting transfers between devices: 12.6 us -> 4.74 us  [the longest x5 3.16 us: gathered(): lax.ppermute(value, 'ctx', [(c, c ^ 1) for c in range(count)])]
    ppermute x9, starting transfers between devices: 22.9 us -> 17.7 us  [passed_along(): lax.ppermute(value, axis, [(source, source + steps) for source in range(i...]
    pallas_call x2, Pallas kernels: 13.7 us -> 16 us  [attention_grad(): pl.pallas_call(functools.partial(attention_grad_kernel, scale, group, len...]
    ppermute x11 -> x9, starting transfers between devices: 9.04 us -> 7.07 us  [swapped(): return lax.ppermute(value, axis, [(0, 1), (1, 0)])]
  transfers between devices with their start and end apart: 28 -> 27, of which waited for: 9 -> 10; matrix products, arithmetic and copies ran while one was open for 12% -> 4% of each run, Pallas kernels for 17% -> 20%
where the time goes in v3:
time: 193 us; the launch traced here: 192 us
  waiting for transfers between devices  82.1 us (43%)
  Pallas kernels  62.8 us (33%)
  starting transfers between devices  29.5 us (15%)
  local copies, waits for them, and re-layouts  13.6 us (7%)
  other arithmetic  2.29 us (1%)
    ppermute x4, waiting for transfers between devices, gathered(): lax.ppermute(value, 'ctx', [(c, (c + 2) % count) for c in range(count)])  48.7 us
    ppermute x9, waiting for transfers between devices, passed_along(): lax.ppermute(value, axis, [(source, source + steps) for source in range(i...  29.7 us
    ppermute x9, starting transfers between devices, passed_along(): lax.ppermute(value, axis, [(source, source + steps) for source in range(i...  17.7 us
    pallas_call x2, Pallas kernels, attention_grad(): pl.pallas_call(functools.partial(attention_grad_kernel, scale, group, len...  16 us
    pallas_call x1, Pallas kernels, attention(): pl.pallas_call(functools.partial(attention_kernel, scale), grid_spec=pltp...  12.1 us
    pallas_call x1, Pallas kernels, dattention(): pl.pallas_call(functools.partial(dattn_kernel, plan, len(arrays)), grid_s...  8.7 us
    pallas_call x1, Pallas kernels, project(): pl.pallas_call(functools.partial(project_kernel, plan, len(arrays), len(a...  8.41 us
    pallas_call x1, Pallas kernels, middle(): pl.pallas_call(middle_kernel, grid=(rows // size,), in_specs=[by_row(2)]...  8.21 us
  transfers between devices with their start and end apart: 27, of which 10 were waited for; matrix products, arithmetic and copies ran while one was open for 4% of the time, Pallas kernels for 20%

profile of v3, /device:TPU:4, one launch (start us, length us, event | category | flops | bytes accessed | tf_op | source)
XLA Modules:
  0.0 191.6 jit_solution(2666518734786020802)
XLA Ops:
  0.7 3.8 %constant_dynamic-slice_fusion = (bf16[1,4,1,64,3072]{4,3,2,1,0:T(8,128)(2,1)}, bf16[1,4,1,64,3072]{4,3,2,1,0:T(8,128)(2,1)}) fusion(bf16[1,4,2,64,3072]{4,3,2,1,0:T(8,128)(2,1)} %param.16, s32[]{:T(128)S(6)} %select_n.66, s32[]{:T(128)S(6)} %select_n.64), kind=kLoop, calls=%fused_computation.18 | loop fusion | bytes 6291464 | tf_op jit(solution)/shard_map/jit(dynamic_index_in_dim)/dynamic_slice | solution.py:482
  5.4 1.6 collective-permute-start
  10.7 12.5 %collective-permute-done.refs_2_.refs_1_ = bf16[6,16,3072]{2,1,0:T(8,128)(2,1)S(1)} collective-permute-done((bf16[6,16,3072]{2,1,0:T(8,128)(2,1)}, bf16[6,16,3072]{2,1,0:T(8,128)(2,1)S(1)}, u32[]{:S(2)}, u32[]{:S(2)}) %collective-permute-start) | collective-permute-done | bytes 589856 | tf_op jit(solution)/shard_map/ppermute | solution.py:61
  24.5 1.5 collective-permute-start.6
  26.0 4.9 %pick.1 = (bf16[128,3072]{1,0:T(8,128)(2,1)}, bf16[128,3072]{1,0:T(8,128)(2,1)}, f32[128,128]{1,0:T(8,128)}) custom-call(s32[128,2]{1,0:T(8,128)} %copy.39.slots, bf16[256,3072]{1,0:T(8,128)(2,1)} %bitcast.38, bf16[256,3072]{1,0:T(8,128)(2,1)} %collective-permute-done.1.there, bf16[128,3072]{1,0:T(8,128)(2,1)} %gout.5), custom_call_target="tpu_custom_call" | custom-call | flops 805306368 | bytes 6291456 | tf_op jit(solution)/shard_map/pick/pallas_call | solution.py:368
  30.9 9.1 %collective-permute-done.2.refs_3_.refs_2_ = bf16[6,16,3072]{2,1,0:T(8,128)(2,1)S(1)} collective-permute-done((bf16[6,16,3072]{2,1,0:T(8,128)(2,1)S(1)}, bf16[6,16,3072]{2,1,0:T(8,128)(2,1)S(1)}, u32[]{:S(2)}, u32[]{:S(2)}) %collective-permute-start.2) | collective-permute-done | bytes 589856 | tf_op jit(solution)/shard_map/ppermute | solution.py:61
  40.7 1.4 collective-permute-start.9
  42.0 13.9 %collective-permute-done.5.refs_4_.refs_3_ = bf16[6,16,3072]{2,1,0:T(8,128)(2,1)S(1)} collective-permute-done((bf16[6,16,3072]{2,1,0:T(8,128)(2,1)S(1)}, bf16[6,16,3072]{2,1,0:T(8,128)(2,1)S(1)}, u32[]{:S(2)}, u32[]{:S(2)}) %collective-permute-start.5) | collective-permute-done | bytes 589856 | tf_op jit(solution)/shard_map/ppermute | solution.py:61
  56.0 1.5 collective-permute-start.10
  58.0 13.2 %collective-permute-done.8.refs_10_.refs_9_ = bf16[6,16,3072]{2,1,0:T(8,128)(2,1)S(1)} collective-permute-done((bf16[6,16,3072]{2,1,0:T(8,128)(2,1)}, bf16[6,16,3072]{2,1,0:T(8,128)(2,1)S(1)}, u32[]{:S(2)}, u32[]{:S(2)}) %collective-permute-start.8) | collective-permute-done | bytes 589856 | tf_op jit(solution)/shard_map/ppermute | solution.py:61
  71.2 1.3 collective-permute-start.11
  75.6 4.1 %collective-permute-start.12 = (bf16[256,512]{1,0:T(8,128)(2,1)S(1)}, bf16[256,512]{1,0:T(8,128)(2,1)S(1)}, u32[]{:S(2)}, u32[]{:S(2)}) collective-permute-start(bf16[256,512]{1,0:T(8,128)(2,1)S(1)} %bitcast_dynamic-update-slice_fusion.refs_3_.refs_7_), channel_id=1, source_target_pairs={{0,4},{2,6},{4,8},{6,10},{8,12},{10,14},{1,5},{3,7},{5,9},{7,11},{... | collective-permute-start | bytes 786440 | tf_op jit(solution)/shard_map/ppermute | solution.py:39
  79.7 3.3 %collective-permute-start.13 = (bf16[256,512]{1,0:T(8,128)(2,1)S(1)}, bf16[256,512]{1,0:T(8,128)(2,1)S(1)}, u32[]{:S(2)}, u32[]{:S(2)}) collective-permute-start(bf16[256,512]{1,0:T(8,128)(2,1)S(1)} %bitcast_dynamic-update-slice_fusion.refs_3_.refs_7_), channel_id=1, source_target_pairs={{0,2},{2,4},{4,6},{6,8},{8,10},{10,12},{12,14},{1,3},{3,5},{5,7},{... | collective-permute-start | bytes 786440 | tf_op jit(solution)/shard_map/ppermute | solution.py:39
  84.9 5.8 %collective-permute-done.13.refs_2_.refs_6_ = bf16[256,512]{1,0:T(8,128)(2,1)S(1)} collective-permute-done((bf16[256,512]{1,0:T(8,128)(2,1)S(1)}, bf16[256,512]{1,0:T(8,128)(2,1)S(1)}, u32[]{:S(2)}, u32[]{:S(2)}) %collective-permute-start.13) | collective-permute-done | bytes 262176 | tf_op jit(solution)/shard_map/ppermute | solution.py:39
  91.5 12.1 %attention.1 = (bf16[256,1536]{1,0:T(8,128)(2,1)}, bf16[12,256,1024]{2,1,0:T(8,128)(2,1)}) custom-call(s32[1]{0:T(128)} %bitcast.11.place, bf16[12,256,128]{2,1,0:T(8,128)(2,1)} %bitcast.39, bf16[256,512]{1,0:T(8,128)(2,1)} %copy-done.2, bf16[256,512]{1,0:T(8,128)(2,1)} %copy-done.3, bf16[256,512]{1,0:T(8,128)(2,1)} %copy-done.4, ...), custom_call_target="tpu_custom_call" | custom-call | flops 1610612736 | bytes 6291456 | tf_op jit(solution)/shard_map/attention/pallas_call | solution.py:252
  103.6 8.4 %project.1 = (f32[128,3072]{1,0:T(8,128)}, f32[128,3072]{1,0:T(8,128)}) custom-call(s32[11]{0:T(128)} %stack.61.table, s32[1]{0:T(128)} %bitcast.10.core, bf16[256,1536]{1,0:T(8,128)(2,1)} %get-tuple-element.55.refs_0_.attn, bf16[12,16,3072]{2,1,0:T(8,128)(2,1)} %refs_0_.1, bf16[6,16,3072]{2,1,0:T(8,128)(2,1)} %copy-done.5, bf16[6,16,3072]{2,1,0:T(8,128)(2,1)} %copy-done.7, ...), custom_call_target="tpu_custom_call" | custom-call | flops 2415919104 | bytes 9437184 | tf_op jit(solution)/shard_map/project/pallas_call | solution.py:147
  112.1 3.6 %collective-permute-done.18.recv = f32[128,3072]{1,0:T(8,128)S(1)} collective-permute-done((f32[128,3072]{1,0:T(8,128)}, f32[128,3072]{1,0:T(8,128)S(1)}, u32[]{:S(2)}, u32[]{:S(2)}) %collective-permute-start.18) | collective-permute-done | bytes 1572896 | tf_op jit(solution)/shard_map/ppermute | solution.py:43
  117.0 8.2 %middle.1 = (bf16[128,3072]{1,0:T(8,128)(2,1)}, bf16[128,3072]{1,0:T(8,128)(2,1)}, f32[128,128]{1,0:T(8,128)}) custom-call(s32[128,2]{1,0:T(8,128)} %copy-done.16, f32[128,3072]{1,0:T(8,128)} %get-tuple-element.59.own, f32[128,3072]{1,0:T(8,128)} %copy-done.14, bf16[128,3072]{1,0:T(8,128)(2,1)} %stream.1, bf16[128,3072]{1,0:T(8,128)(2,1)} %get-tuple-element.61.first, ...), custom_call_target="tpu_custom_call" | custom-call | flops 402653184 | bytes 7864320 | tf_op jit(solution)/shard_map/middle/pallas_call | solution.py:416
  125.4 4.5 %spread.1 = (bf16[256,3072]{1,0:T(8,128)(2,1)}, bf16[256,3072]{1,0:T(8,128)(2,1)}) custom-call(s32[2,128]{1,0:T(2,128)} %bitcast.48, f32[128,128]{1,0:T(8,128)} %get-tuple-element.74.gates, bf16[128,3072]{1,0:T(8,128)(2,1)} %gout.5), custom_call_target="tpu_custom_call" | custom-call | flops 805306368 | bytes 3932160 | tf_op jit(solution)/shard_map/spread/pallas_call | solution.py:446
  130.8 8.7 %dattention.1.dout = bf16[256,1536]{1,0:T(8,128)(2,1)} custom-call(s32[11]{0:T(128)} %stack.61.table, s32[1]{0:T(128)} %bitcast.10.core, bf16[128,3072]{1,0:T(8,128)(2,1)} %get-tuple-element.101.own, bf16[128,3072]{1,0:T(8,128)(2,1)} %copy-done.15, bf16[12,16,3072]{2,1,0:T(8,128)(2,1)} %refs_0_.1, bf16[6,16,3072]{2,1,0:T(8,128)(2,1)} %copy-done.5, ...), custom_call_target="tpu_custom_call" | custom-call | flops 2415919104 | bytes 9437184 | tf_op jit(solution)/shard_map/dattention/pallas_call | solution.py:203
  139.9 7.9 %attention_grad.2 = (bf16[12,256,128]{2,1,0:T(8,128)(2,1)}, bf16[256,256]{1,0:T(8,128)(2,1)}, bf16[256,256]{1,0:T(8,128)(2,1)}, bf16[256,256]{1,0:T(8,128)(2,1)}, f32[256,256]{1,0:T(8,128)}) custom-call(bf16[12,256,128]{2,1,0:T(8,128)(2,1)} %bitcast.40, bf16[256,1536]{1,0:T(8,128)(2,1)} %dattention.1.dout, bf16[256,1536]{1,0:T(8,128)(2,1)} %get-tuple-element.55.refs_0_.attn, ...), custom_call_target="tpu_custom_call" | custom-call | flops 256 | bytes 256 | tf_op jit(solution)/shard_map/attention_grad/pallas_call | solution.py:318
  147.9 8.1 %attention_grad.3 = (bf16[12,256,128]{2,1,0:T(8,128)(2,1)}, bf16[256,256]{1,0:T(8,128)(2,1)}, bf16[256,256]{1,0:T(8,128)(2,1)}, bf16[256,256]{1,0:T(8,128)(2,1)}, f32[256,256]{1,0:T(8,128)}) custom-call(bf16[12,256,128]{2,1,0:T(8,128)(2,1)} %bitcast.41, bf16[256,1536]{1,0:T(8,128)(2,1)} %dattention.1.dout, ...), custom_call_target="tpu_custom_call", output_to_operand_aliasing={{0}: (12, {})} | custom-call | flops 256 | bytes 256 | tf_op jit(solution)/shard_map/attention_grad/pallas_call | solution.py:318
  156.0 1.9 %collective-permute-start.23 = (bf16[256,256]{1,0:T(8,128)(2,1)}, bf16[256,256]{1,0:T(8,128)(2,1)S(1)}, u32[]{:S(2)}, u32[]{:S(2)}) collective-permute-start(bf16[256,256]{1,0:T(8,128)(2,1)} %get-tuple-element.70), channel_id=1, source_target_pairs={{2,0},{4,2},{6,4},{8,6},{10,8},{12,10},{14,12},{3,1},{5,3},{7,5},{... | collective-permute-start | bytes 393224 | tf_op jit(solution)/shard_map/ppermute | solution.py:39
  158.0 1.3 collective-permute-start.24
  159.3 1.3 collective-permute-start.25
  160.6 1.9 %collective-permute-start.20 = (bf16[256,256]{1,0:T(8,128)(2,1)}, bf16[256,256]{1,0:T(8,128)(2,1)S(1)}, u32[]{:S(2)}, u32[]{:S(2)}) collective-permute-start(bf16[256,256]{1,0:T(8,128)(2,1)} %get-tuple-element.66), channel_id=1, source_target_pairs={{2,0},{4,2},{6,4},{8,6},{10,8},{12,10},{14,12},{3,1},{5,3},{7,5},{... | collective-permute-start | bytes 393224 | tf_op jit(solution)/shard_map/ppermute | solution.py:39
  162.5 5.0 %collective-permute-done.23 = bf16[256,256]{1,0:T(8,128)(2,1)S(1)} collective-permute-done((bf16[256,256]{1,0:T(8,128)(2,1)}, bf16[256,256]{1,0:T(8,128)(2,1)S(1)}, u32[]{:S(2)}, u32[]{:S(2)}) %collective-permute-start.23) | collective-permute-done | bytes 131104 | tf_op jit(solution)/shard_map/ppermute | solution.py:39
  167.5 1.3 collective-permute-start.21
  168.8 1.3 collective-permute-start.22
  170.1 1.9 %maximum_select_fusion = bf16[1,4,2,64,3072]{4,3,2,1,0:T(8,128)(2,1)} fusion(bf16[1,4,1,64,3072]{4,3,2,1,0:T(8,128)(2,1)S(1)} %bitcast.43, bf16[1,4,1,64,3072]{4,3,2,1,0:T(8,128)(2,1)S(1)} %bitcast.42, pred[]{:T(512)S(6)} %eq.33), kind=kLoop, calls=%fused_computation | loop fusion | flops 4718592 | bytes 6291457 | tf_op jit(solution)/shard_map/jit(_where)/select_n | solution.py:524
  172.1 7.3 %collective-permute-done.25 = bf16[256,256]{1,0:T(8,128)(2,1)S(1)} collective-permute-done((bf16[256,256]{1,0:T(8,128)(2,1)}, bf16[256,256]{1,0:T(8,128)(2,1)S(1)}, u32[]{:S(2)}, u32[]{:S(2)}) %collective-permute-start.25) | collective-permute-done | bytes 131104 | tf_op jit(solution)/shard_map/ppermute | solution.py:39
  179.3 10.4 %collective-permute-done.22 = bf16[256,256]{1,0:T(8,128)(2,1)S(1)} collective-permute-done((bf16[256,256]{1,0:T(8,128)(2,1)S(1)}, bf16[256,256]{1,0:T(8,128)(2,1)S(1)}, u32[]{:S(2)}, u32[]{:S(2)}) %collective-permute-start.22) | collective-permute-done | bytes 131104 | tf_op jit(solution)/shard_map/ppermute | solution.py:39
  (105 shorter events, 17.3 us)
Async XLA Ops:
  4.5 18.7 %collective-permute-start.1 = (bf16[256,3072]{1,0:T(8,128)(2,1)}, bf16[256,3072]{1,0:T(8,128)(2,1)}, u32[]{:S(2)}, u32[]{:S(2)}) collective-permute-start(bf16[256,3072]{1,0:T(8,128)(2,1)} %bitcast.13), channel_id=1, source_target_pairs={{0,1},{1,0},{2,3},{3,2},{4,5},{5,4},{6,7},{7,6},{8,9},{9,8},{10,11... | collective-permute-start | bytes 4718600 | tf_op jit(solution)/shard_map/ppermute | solution.py:43
  5.4 17.8 %collective-permute-start = (bf16[6,16,3072]{2,1,0:T(8,128)(2,1)}, bf16[6,16,3072]{2,1,0:T(8,128)(2,1)S(1)}, u32[]{:S(2)}, u32[]{:S(2)}) collective-permute-start(bf16[6,16,3072]{2,1,0:T(8,128)(2,1)} %constant_dynamic-slice_fusion.2), channel_id=1, source_target_pairs={{0,4},{2,6},{4,8},{6,10},{8,12},{10,14},{12,0},{14,2},{1,5},{3,7},... | collective-permute-start | bytes 1769480 | tf_op jit(solution)/shard_map/ppermute | solution.py:61
  7.0 23.9 %collective-permute-start.3 = (bf16[6,16,3072]{2,1,0:T(8,128)(2,1)}, bf16[6,16,3072]{2,1,0:T(8,128)(2,1)S(1)}, u32[]{:S(2)}, u32[]{:S(2)}) collective-permute-start(bf16[6,16,3072]{2,1,0:T(8,128)(2,1)} %constant_dynamic-slice_fusion.2), channel_id=1, source_target_pairs={{0,2},{2,0},{4,6},{6,4},{8,10},{10,8},{12,14},{14,12},{1,3},{3,1},... | collective-permute-start | bytes 1769480 | tf_op jit(solution)/shard_map/ppermute | solution.py:62
  10.7 69.0 %copy-start.1 = (bf16[256,512]{1,0:T(8,128)(2,1)}, bf16[256,512]{1,0:T(8,128)(2,1)S(1)}, u32[]{:S(2)}) copy-start(bf16[256,512]{1,0:T(8,128)(2,1)S(1)} %bitcast_dynamic-update-slice_fusion.refs_3_.refs_7_) | copy-start | bytes 786436
  23.2 16.8 %collective-permute-start.2 = (bf16[6,16,3072]{2,1,0:T(8,128)(2,1)S(1)}, bf16[6,16,3072]{2,1,0:T(8,128)(2,1)S(1)}, u32[]{:S(2)}, u32[]{:S(2)}) collective-permute-start(bf16[6,16,3072]{2,1,0:T(8,128)(2,1)S(1)} %collective-permute-done.refs_2_.refs_1_), channel_id=1, source_target_pairs={{0,4},{2,6},{4,8},{6,10},{8,12},{10,14},{12,0},{14,2},{1,5},{3,7},... | collective-permute-start | bytes 1769480 | tf_op jit(solution)/shard_map/ppermute | solution.py:61
  24.0 18.0 %collective-permute-start.7 = (bf16[6,16,3072]{2,1,0:T(8,128)(2,1)S(1)}, bf16[6,16,3072]{2,1,0:T(8,128)(2,1)S(1)}, u32[]{:S(2)}, u32[]{:S(2)}) collective-permute-start(bf16[6,16,3072]{2,1,0:T(8,128)(2,1)S(1)} %collective-permute-done.refs_2_.refs_1_), channel_id=1, source_target_pairs={{0,2},{2,0},{4,6},{6,4},{8,10},{10,8},{12,14},{14,12},{1,3},{3,1},... | collective-permute-start | bytes 1769480 | tf_op jit(solution)/shard_map/ppermute | solution.py:62
  24.5 17.5 %collective-permute-start.6 = (bf16[6,16,3072]{2,1,0:T(8,128)(2,1)S(1)}, bf16[6,16,3072]{2,1,0:T(8,128)(2,1)}, u32[]{:S(2)}, u32[]{:S(2)}) collective-permute-start(bf16[6,16,3072]{2,1,0:T(8,128)(2,1)S(1)} %collective-permute-done.refs_2_.refs_1_), channel_id=1, source_target_pairs={{0,16},{16,0},{1,17},{17,1},{2,18},{18,2},{3,19},{19,3},{4,20},{20... | collective-permute-start | bytes 1769480 | tf_op jit(solution)/shard_map/ppermute | solution.py:43
  30.9 72.7 %copy-start.6 = (bf16[6,16,3072]{2,1,0:T(8,128)(2,1)}, bf16[6,16,3072]{2,1,0:T(8,128)(2,1)S(1)}, u32[]{:S(2)}) copy-start(bf16[6,16,3072]{2,1,0:T(8,128)(2,1)S(1)} %collective-permute-done.3.refs_5_.refs_4_) | copy-start | bytes 1769476
  40.0 63.6 %copy-start.7 = (bf16[6,16,3072]{2,1,0:T(8,128)(2,1)}, bf16[6,16,3072]{2,1,0:T(8,128)(2,1)S(1)}, u32[]{:S(2)}) copy-start(bf16[6,16,3072]{2,1,0:T(8,128)(2,1)S(1)} %collective-permute-done.2.refs_3_.refs_2_) | copy-start | bytes 1769476
  40.0 16.0 %collective-permute-start.5 = (bf16[6,16,3072]{2,1,0:T(8,128)(2,1)S(1)}, bf16[6,16,3072]{2,1,0:T(8,128)(2,1)S(1)}, u32[]{:S(2)}, u32[]{:S(2)}) collective-permute-start(bf16[6,16,3072]{2,1,0:T(8,128)(2,1)S(1)} %collective-permute-done.2.refs_3_.refs_2_), channel_id=1, source_target_pairs={{0,4},{2,6},{4,8},{6,10},{8,12},{10,14},{12,0},{14,2},{1,5},{3,7},... | collective-permute-start | bytes 1769480 | tf_op jit(solution)/shard_map/ppermute | solution.py:61
  40.0 18.0 %collective-permute-start.4 = (bf16[6,16,3072]{2,1,0:T(8,128)(2,1)S(1)}, bf16[6,16,3072]{2,1,0:T(8,128)(2,1)}, u32[]{:S(2)}, u32[]{:S(2)}) collective-permute-start(bf16[6,16,3072]{2,1,0:T(8,128)(2,1)S(1)} %collective-permute-done.2.refs_3_.refs_2_), channel_id=1, source_target_pairs={{0,2},{2,0},{4,6},{6,4},{8,10},{10,8},{12,14},{14,12},{1,3},{3,1},... | collective-permute-start | bytes 1769480 | tf_op jit(solution)/shard_map/ppermute | solution.py:62
  40.7 17.3 %collective-permute-start.9 = (bf16[6,16,3072]{2,1,0:T(8,128)(2,1)S(1)}, bf16[6,16,3072]{2,1,0:T(8,128)(2,1)S(1)}, u32[]{:S(2)}, u32[]{:S(2)}) collective-permute-start(bf16[6,16,3072]{2,1,0:T(8,128)(2,1)S(1)} %collective-permute-done.3.refs_5_.refs_4_), channel_id=1, source_target_pairs={{0,16},{16,0},{1,17},{17,1},{2,18},{18,2},{3,19},{19,3},{4,20},{20... | collective-permute-start | bytes 1769480 | tf_op jit(solution)/shard_map/ppermute | solution.py:43
  42.0 61.6 %copy-start.8 = (bf16[6,16,3072]{2,1,0:T(8,128)(2,1)}, bf16[6,16,3072]{2,1,0:T(8,128)(2,1)S(1)}, u32[]{:S(2)}) copy-start(bf16[6,16,3072]{2,1,0:T(8,128)(2,1)S(1)} %collective-permute-done.7.refs_6_.refs_5_) | copy-start | bytes 1769476
  56.0 15.2 %collective-permute-start.8 = (bf16[6,16,3072]{2,1,0:T(8,128)(2,1)}, bf16[6,16,3072]{2,1,0:T(8,128)(2,1)S(1)}, u32[]{:S(2)}, u32[]{:S(2)}) collective-permute-start(bf16[6,16,3072]{2,1,0:T(8,128)(2,1)} %collective-permute-done.6.refs_9_.refs_8_), channel_id=1, source_target_pairs={{0,4},{2,6},{4,8},{6,10},{8,12},{10,14},{12,0},{14,2},{1,5},{3,7},... | collective-permute-start | bytes 1769480 | tf_op jit(solution)/shard_map/ppermute | solution.py:61
  56.0 15.2 %collective-permute-start.10 = (bf16[6,16,3072]{2,1,0:T(8,128)(2,1)S(1)}, bf16[6,16,3072]{2,1,0:T(8,128)(2,1)S(1)}, u32[]{:S(2)}, u32[]{:S(2)}) collective-permute-start(bf16[6,16,3072]{2,1,0:T(8,128)(2,1)S(1)} %collective-permute-done.5.refs_4_.refs_3_), channel_id=1, source_target_pairs={{0,16},{16,0},{1,17},{17,1},{2,18},{18,2},{3,19},{19,3},{4,20},{20... | collective-permute-start | bytes 1769480 | tf_op jit(solution)/shard_map/ppermute | solution.py:43
  57.5 15.1 %collective-permute-start.14 = (bf16[6,16,3072]{2,1,0:T(8,128)(2,1)S(1)}, bf16[6,16,3072]{2,1,0:T(8,128)(2,1)}, u32[]{:S(2)}, u32[]{:S(2)}) collective-permute-start(bf16[6,16,3072]{2,1,0:T(8,128)(2,1)S(1)} %collective-permute-done.5.refs_4_.refs_3_), channel_id=1, source_target_pairs={{0,2},{2,0},{4,6},{6,4},{8,10},{10,8},{12,14},{14,12},{1,3},{3,1},... | collective-permute-start | bytes 1769480 | tf_op jit(solution)/shard_map/ppermute | solution.py:62
  71.2 32.4 %copy-start.11 = (bf16[6,16,3072]{2,1,0:T(8,128)(2,1)}, bf16[6,16,3072]{2,1,0:T(8,128)(2,1)S(1)}, u32[]{:S(2)}) copy-start(bf16[6,16,3072]{2,1,0:T(8,128)(2,1)S(1)} %collective-permute-done.8.refs_10_.refs_9_) | copy-start | bytes 1769476
  71.2 8.5 %collective-permute-start.11 = (bf16[256,512]{1,0:T(8,128)(2,1)S(1)}, bf16[256,512]{1,0:T(8,128)(2,1)S(1)}, u32[]{:S(2)}, u32[]{:S(2)}) collective-permute-start(bf16[256,512]{1,0:T(8,128)(2,1)S(1)} %bitcast_dynamic-update-slice_fusion.refs_3_.refs_7_), channel_id=1, source_target_pairs={{0,6},{2,8},{4,10},{6,12},{8,14},{1,7},{3,9},{5,11},{7,13},{9,15},... | collective-permute-start | bytes 786440 | tf_op jit(solution)/shard_map/ppermute | solution.py:39
  72.6 31.0 %collective-permute-start.15 = (bf16[6,16,3072]{2,1,0:T(8,128)(2,1)}, bf16[6,16,3072]{2,1,0:T(8,128)(2,1)}, u32[]{:S(2)}, u32[]{:S(2)}) collective-permute-start(bf16[6,16,3072]{2,1,0:T(8,128)(2,1)} %collective-permute-done.6.refs_9_.refs_8_), channel_id=1, source_target_pairs={{0,2},{2,0},{4,6},{6,4},{8,10},{10,8},{12,14},{14,12},{1,3},{3,1},... | collective-permute-start | bytes 1769480 | tf_op jit(solution)/shard_map/ppermute | solution.py:62
  73.6 30.0 %collective-permute-start.17 = (bf16[6,16,3072]{2,1,0:T(8,128)(2,1)}, bf16[6,16,3072]{2,1,0:T(8,128)(2,1)}, u32[]{:S(2)}, u32[]{:S(2)}) collective-permute-start(bf16[6,16,3072]{2,1,0:T(8,128)(2,1)} %collective-permute-done.14.refs_8_.refs_7_), channel_id=1, source_target_pairs={{0,16},{16,0},{1,17},{17,1},{2,18},{18,2},{3,19},{19,3},{4,20},{20... | collective-permute-start | bytes 1769480 | tf_op jit(solution)/shard_map/ppermute | solution.py:43
  74.7 28.9 %collective-permute-start.16 = (bf16[6,16,3072]{2,1,0:T(8,128)(2,1)}, bf16[6,16,3072]{2,1,0:T(8,128)(2,1)}, u32[]{:S(2)}, u32[]{:S(2)}) collective-permute-start(bf16[6,16,3072]{2,1,0:T(8,128)(2,1)} %collective-permute-done.4.refs_7_.refs_6_), channel_id=1, source_target_pairs={{0,16},{16,0},{1,17},{17,1},{2,18},{18,2},{3,19},{19,3},{4,20},{20... | collective-permute-start | bytes 1769480 | tf_op jit(solution)/shard_map/ppermute | solution.py:43
  75.6 9.3 %collective-permute-start.12 = (bf16[256,512]{1,0:T(8,128)(2,1)S(1)}, bf16[256,512]{1,0:T(8,128)(2,1)S(1)}, u32[]{:S(2)}, u32[]{:S(2)}) collective-permute-start(bf16[256,512]{1,0:T(8,128)(2,1)S(1)} %bitcast_dynamic-update-slice_fusion.refs_3_.refs_7_), channel_id=1, source_target_pairs={{0,4},{2,6},{4,8},{6,10},{8,12},{10,14},{1,5},{3,7},{5,9},{7,11},{... | collective-permute-start | bytes 786440 | tf_op jit(solution)/shard_map/ppermute | solution.py:39
  79.7 11.0 %collective-permute-start.13 = (bf16[256,512]{1,0:T(8,128)(2,1)S(1)}, bf16[256,512]{1,0:T(8,128)(2,1)S(1)}, u32[]{:S(2)}, u32[]{:S(2)}) collective-permute-start(bf16[256,512]{1,0:T(8,128)(2,1)S(1)} %bitcast_dynamic-update-slice_fusion.refs_3_.refs_7_), channel_id=1, source_target_pairs={{0,2},{2,4},{4,6},{6,8},{8,10},{10,12},{12,14},{1,3},{3,5},{5,7},{... | collective-permute-start | bytes 786440 | tf_op jit(solution)/shard_map/ppermute | solution.py:39
  112.0 3.7 %collective-permute-start.18 = (f32[128,3072]{1,0:T(8,128)}, f32[128,3072]{1,0:T(8,128)S(1)}, u32[]{:S(2)}, u32[]{:S(2)}) collective-permute-start(f32[128,3072]{1,0:T(8,128)} %get-tuple-element.60), channel_id=1, source_target_pairs={{0,1},{1,0},{2,3},{3,2},{4,5},{5,4},{6,7},{7,6},{8,9},{9,8},{10,11... | collective-permute-start | bytes 4718600 | tf_op jit(solution)/shard_map/ppermute | solution.py:43
  125.2 4.7 %collective-permute-start.19 = (bf16[128,3072]{1,0:T(8,128)(2,1)}, bf16[128,3072]{1,0:T(8,128)(2,1)S(1)}, u32[]{:S(2)}, u32[]{:S(2)}) collective-permute-start(bf16[128,3072]{1,0:T(8,128)(2,1)} %get-tuple-element.101.own), channel_id=1, source_target_pairs={{0,1},{1,0},{2,3},{3,2},{4,5},{5,4},{6,7},{7,6},{8,9},{9,8},{10,11... | collective-permute-start | bytes 2359304 | tf_op jit(solution)/shard_map/ppermute | solution.py:43
  139.5 29.3 %collective-permute-start.26 = (bf16[256,3072]{1,0:T(8,128)(2,1)}, bf16[256,3072]{1,0:T(8,128)(2,1)S(1)}, u32[]{:S(2)}, u32[]{:S(2)}) collective-permute-start(bf16[256,3072]{1,0:T(8,128)(2,1)} %get-tuple-element.77), channel_id=1, source_target_pairs={{0,1},{1,0},{2,3},{3,2},{4,5},{5,4},{6,7},{7,6},{8,9},{9,8},{10,11... | collective-permute-start | bytes 4718600 | tf_op jit(solution)/shard_map/ppermute | solution.py:43
  156.0 11.5 %collective-permute-start.23 = (bf16[256,256]{1,0:T(8,128)(2,1)}, bf16[256,256]{1,0:T(8,128)(2,1)S(1)}, u32[]{:S(2)}, u32[]{:S(2)}) collective-permute-start(bf16[256,256]{1,0:T(8,128)(2,1)} %get-tuple-element.70), channel_id=1, source_target_pairs={{2,0},{4,2},{6,4},{8,6},{10,8},{12,10},{14,12},{3,1},{5,3},{7,5},{... | collective-permute-start | bytes 393224 | tf_op jit(solution)/shard_map/ppermute | solution.py:39
  158.0 14.1 %collective-permute-start.24 = (bf16[256,256]{1,0:T(8,128)(2,1)}, bf16[256,256]{1,0:T(8,128)(2,1)S(1)}, u32[]{:S(2)}, u32[]{:S(2)}) collective-permute-start(bf16[256,256]{1,0:T(8,128)(2,1)} %get-tuple-element.71), channel_id=1, source_target_pairs={{4,0},{6,2},{8,4},{10,6},{12,8},{14,10},{5,1},{7,3},{9,5},{11,7},{... | collective-permute-start | bytes 393224 | tf_op jit(solution)/shard_map/ppermute | solution.py:39
  159.3 20.1 %collective-permute-start.25 = (bf16[256,256]{1,0:T(8,128)(2,1)}, bf16[256,256]{1,0:T(8,128)(2,1)S(1)}, u32[]{:S(2)}, u32[]{:S(2)}) collective-permute-start(bf16[256,256]{1,0:T(8,128)(2,1)} %get-tuple-element.72), channel_id=1, source_target_pairs={{6,0},{8,2},{10,4},{12,6},{14,8},{7,1},{9,3},{11,5},{13,7},{15,9},... | collective-permute-start | bytes 393224 | tf_op jit(solution)/shard_map/ppermute | solution.py:39
  160.6 18.8 %collective-permute-start.20 = (bf16[256,256]{1,0:T(8,128)(2,1)}, bf16[256,256]{1,0:T(8,128)(2,1)S(1)}, u32[]{:S(2)}, u32[]{:S(2)}) collective-permute-start(bf16[256,256]{1,0:T(8,128)(2,1)} %get-tuple-element.66), channel_id=1, source_target_pairs={{2,0},{4,2},{6,4},{8,6},{10,8},{12,10},{14,12},{3,1},{5,3},{7,5},{... | collective-permute-start | bytes 393224 | tf_op jit(solution)/shard_map/ppermute | solution.py:39
  167.5 11.8 %collective-permute-start.21 = (bf16[256,256]{1,0:T(8,128)(2,1)S(1)}, bf16[256,256]{1,0:T(8,128)(2,1)S(1)}, u32[]{:S(2)}, u32[]{:S(2)}) collective-permute-start(bf16[256,256]{1,0:T(8,128)(2,1)S(1)} %copy-done.25), channel_id=1, source_target_pairs={{4,0},{6,2},{8,4},{10,6},{12,8},{14,10},{5,1},{7,3},{9,5},{11,7},{... | collective-permute-start | bytes 393224 | tf_op jit(solution)/shard_map/ppermute | solution.py:39
  168.8 21.0 %collective-permute-start.22 = (bf16[256,256]{1,0:T(8,128)(2,1)S(1)}, bf16[256,256]{1,0:T(8,128)(2,1)S(1)}, u32[]{:S(2)}, u32[]{:S(2)}) collective-permute-start(bf16[256,256]{1,0:T(8,128)(2,1)S(1)} %copy-done.24), channel_id=1, source_target_pairs={{6,0},{8,2},{10,4},{12,6},{14,8},{7,1},{9,3},{11,5},{13,7},{15,9},... | collective-permute-start | bytes 393224 | tf_op jit(solution)/shard_map/ppermute | solution.py:39
  (21 other events, 221.4 us)

commit v4 on v3

--- a/solution.py
+++ b/solution.py
@@ -47,13 +47,13 @@
     return lax.optimization_barrier((tuple(values), others))[0]
 
 
-def gathered(w_out, first_task, second_task, last_task):
+def gathered(w_out, *tasks):
     heads, depth, _ = w_out.shape
     count = lax.axis_size("ctx")
     place = lax.axis_index("ctx")
     if count != 8 or lax.axis_size("groups") != 2 or heads % 2:
         full = lax.all_gather(w_out, "ctx", axis=1, tiled=True)
-        for task in (first_task, second_task, last_task):
+        for task in tasks:
             task()
         return [full], jnp.zeros((1,), jnp.int32), [(0, heads, 0, 0)]
     side = lax.axis_index("groups")
@@ -64,17 +64,17 @@
     mine = lax.dynamic_slice_in_dim(w_out, side * half, half, 0)
 
     z1, y0 = ring(mine), pair(mine)
-    (z1,) = after([z1], *first_task())
+    (z1,) = after([z1], *tasks[0]())
     z2, y1, x1 = ring(z1), pair(z1), cross(z1)
-    z2, y0 = after([z2, y0], *second_task())
+    z2, y0 = after([z2, y0], *tasks[1](z1))
     z3, y2, x2 = ring(z2), pair(z2), cross(y0)
-    z3, x1 = after([z3, x1], y1)
+    z3, x1 = after([z3, x1], y1, *tasks[2](z2))
     z4, y3, x3 = ring(x1), pair(z3), cross(z3)
     y2, z4 = after([y2, z4], x2, y2)
     x4 = cross(y2)
     y3, last = after([y3, x1], x3, z4)
     y4, x5 = pair(last), cross(y3)
-    last_task(z4, x3)
+    tasks[3](z4, x3)
 
     table = [0, side * half, (1 - side) * half]
     table += [depth * ((place - 2 * k) % count) for k in range(4)]
@@ -226,40 +226,56 @@
     return jnp.concatenate([r[...] for r in refs], axis=0)
 
 
+HEADS_FORWARD = 6
+HEADS_BACKWARD = 6
+
+
+def heads_a_step(most, group):
+    return max(n for n in range(1, most + 1) if group % n == 0)
+
+
+def stacked(ref, count):
+    size = ref.shape[1] // count
+    return jnp.concatenate([ref[:, i * size : (i + 1) * size] for i in range(count)], axis=0)
+
+
 def attention_kernel(scale, place, q, *refs):
     keys, values, (attn, probs) = refs[:BAND_BLOCKS], refs[BAND_BLOCKS : 2 * BAND_BLOCKS], refs[-2:]
-    tok = q.shape[0]
-    scores = dot_nt(q[...], band_of(keys)) * scale
-    shape = scores.shape
-    row = lax.broadcasted_iota(jnp.int32, shape, 0)
-    column = lax.broadcasted_iota(jnp.int32, shape, 1)
+    count, tok, head_dim = q.shape
+    scores = dot_nt(q[...].reshape(count * tok, head_dim), band_of(keys)) * scale
+    scores = scores.reshape(count, tok, BAND_BLOCKS * tok)
+    row = lax.broadcasted_iota(jnp.int32, scores.shape, 1)
+    column = lax.broadcasted_iota(jnp.int32, scores.shape, 2)
     offset = column - (BAND_BLOCKS - 1) * tok
     admitted = (offset <= row) & (offset + place[0] * tok >= 0)
     scores = jnp.where(admitted, scores, -1e30)
     top = jnp.max(scores, axis=-1, keepdims=True)
     grown = jnp.exp(scores - top)
     weight = (grown * (1.0 / jnp.sum(grown, axis=-1, keepdims=True))).astype(BF16)
-    probs[0] = weight
-    attn[...] = dot_nn(weight, band_of(values)).astype(BF16)
+    probs[...] = weight
+    result = dot_nn(weight.reshape(count * tok, BAND_BLOCKS * tok), band_of(values)).astype(BF16)
+    for i in range(count):
+        attn[:, i * head_dim : (i + 1) * head_dim] = result[i * tok : (i + 1) * tok]
 
 
 def attention(queries, bands, place, heads, heads_kv, head_dim, scale):
     tok = queries.shape[1]
     group = heads // heads_kv
-    keys = pl.BlockSpec((tok, head_dim), lambda h, *_: (0, h // group))
-    values = pl.BlockSpec((tok, head_dim), lambda h, *_: (0, heads_kv + h // group))
+    count = heads_a_step(HEADS_FORWARD, group)
+    keys = pl.BlockSpec((tok, head_dim), lambda h, *_: (0, h * count // group))
+    values = pl.BlockSpec((tok, head_dim), lambda h, *_: (0, heads_kv + h * count // group))
     span = BAND_BLOCKS * tok
     return pl.pallas_call(
         functools.partial(attention_kernel, scale),
         grid_spec=pltpu.PrefetchScalarGridSpec(
             num_scalar_prefetch=1,
-            grid=(heads,),
-            in_specs=[pl.BlockSpec((None, tok, head_dim), lambda h, *_: (h, 0, 0))]
+            grid=(heads // count,),
+            in_specs=[pl.BlockSpec((count, tok, head_dim), lambda h, *_: (h, 0, 0))]
             + [keys] * BAND_BLOCKS
             + [values] * BAND_BLOCKS,
             out_specs=[
-                pl.BlockSpec((tok, head_dim), lambda h, *_: (0, h)),
-                pl.BlockSpec((1, tok, span), lambda h, *_: (h, 0, 0)),
+                pl.BlockSpec((tok, count * head_dim), lambda h, *_: (0, h)),
+                pl.BlockSpec((count, tok, span), lambda h, *_: (h, 0, 0)),
             ],
         ),
         out_shape=[
@@ -272,63 +288,88 @@
     )(place, queries, *bands, *bands)
 
 
-def attention_grad_kernel(scale, group, given, q, dout, attn, probs, *refs):
-    refs = refs[:2 * BAND_BLOCKS] + refs[2 * BAND_BLOCKS + given :]
+def attention_grad_kernel(scale, steps, last, q, dout, attn, probs, *refs):
+    refs = list(refs)
     keys, values = refs[:BAND_BLOCKS], refs[BAND_BLOCKS : 2 * BAND_BLOCKS]
-    dq, outs, (dk, dv) = refs[2 * BAND_BLOCKS], refs[2 * BAND_BLOCKS + 1 : -2], refs[-2:]
-    tok, head_dim = q.shape
-    head = pl.program_id(0)
-    grad = dout[...]
-    weight = probs[0]
-    delta = jnp.sum(grad.astype(F32) * attn[...].astype(F32), axis=-1, keepdims=True)
+    refs = refs[2 * BAND_BLOCKS :]
+    if last:
+        (_, core, here, back), refs, sem = refs[:4], refs[4:-1], refs[-1]
+        joined = refs.pop(1 + BAND_BLOCKS)
+        copies = [
+            pltpu.make_async_copy(here, joined.at[0, :, core[0]], sem.at[0]),
+            pltpu.make_async_copy(back, joined.at[0, :, 1 - core[0]], sem.at[1]),
+        ]
+
+        @pl.when(pl.program_id(0) == 0)
+        def _():
+            for copy in copies:
+                copy.start()
+
+    dq, outs, (dk, dv) = refs[0], refs[1:-2], refs[-2:]
+    count, tok, head_dim = q.shape
+    step = pl.program_id(0)
+    grad = stacked(dout, count)
+    weight = probs[...].reshape(count * tok, BAND_BLOCKS * tok)
+    delta = jnp.sum(grad.astype(F32) * stacked(attn, count).astype(F32), axis=-1, keepdims=True)
     dprob = dot_nt(grad, band_of(values))
     dscore = (weight.astype(F32) * (dprob - delta)).astype(BF16)
-    dq[...] = (dot_nn(dscore, band_of(keys)) * scale).astype(BF16)
-    dkey = dot_tn(dscore, q[...])
+    dq[...] = (dot_nn(dscore, band_of(keys)) * scale).astype(BF16).reshape(count, tok, head_dim)
+    dkey = dot_tn(dscore, q[...].reshape(count * tok, head_dim))
     dvalue = dot_tn(weight, grad)
 
-    @pl.when(head == 0)
+    @pl.when(step == 0)
     def _():
         dk[...] = dkey
         dv[...] = dvalue
 
-    @pl.when(head > 0)
+    @pl.when(step > 0)
     def _():
         dk[...] += dkey
         dv[...] += dvalue
 
-    @pl.when(head == group - 1)
+    @pl.when(step == steps - 1)
     def _():
         for block, out in enumerate(outs):
             rows = pl.ds(block * tok, tok)
             out[:, :head_dim] = (dk[rows, :] * scale).astype(out.dtype)
             out[:, head_dim:] = dv[rows, :].astype(out.dtype)
-
-
-def attention_grad(queries, dout, attn, probs, bands, which, grad_q, heads_kv, scale):
+        if last:
+            for copy in copies:
+                copy.wait()
+
+
+def attention_grad(queries, dout, attn, probs, bands, which, given, heads_kv, scale):
     heads, tok, head_dim = queries.shape
     group = heads // heads_kv
+    count = heads_a_step(HEADS_BACKWARD, group)
+    steps = group // count
     keys = pl.BlockSpec((tok, head_dim), lambda h: (0, which))
     values = pl.BlockSpec((tok, head_dim), lambda h: (0, heads_kv + which))
-    by_head = pl.BlockSpec((None, tok, head_dim), lambda h: (which * group + h, 0, 0))
-    of_all = pl.BlockSpec((tok, head_dim), lambda h: (0, which * group + h))
+    by_head = pl.BlockSpec((count, tok, head_dim), lambda h: (which * steps + h, 0, 0))
+    of_all = pl.BlockSpec((tok, count * head_dim), lambda h: (0, which * steps + h))
     span = BAND_BLOCKS * tok
     whole = pl.BlockSpec((tok, 2 * head_dim), lambda h: (0, 0))
-    given = [] if grad_q is None else [grad_q]
+    anywhere = pl.BlockSpec(memory_space=pl.ANY)
+    last = bool(given)
+    joined = []
+    if last:
+        held, capacity, width = given[2].shape
+        joined = [jax.ShapeDtypeStruct((1, held, 2, capacity, width), BF16)]
     return pl.pallas_call(
-        functools.partial(attention_grad_kernel, scale, group, len(given)),
-        grid=(group,),
+        functools.partial(attention_grad_kernel, scale, steps, last),
+        grid=(steps,),
         in_specs=[by_head, of_all, of_all]
-        + [pl.BlockSpec((1, tok, span), lambda h: (which * group + h, 0, 0))]
+        + [pl.BlockSpec((count, tok, span), lambda h: (which * steps + h, 0, 0))]
         + [keys] * BAND_BLOCKS
         + [values] * BAND_BLOCKS
-        + [pl.BlockSpec(memory_space=pl.ANY)] * len(given),
-        out_specs=[by_head] + [whole] * BAND_BLOCKS,
+        + ([anywhere, pl.BlockSpec(memory_space=pltpu.SMEM), anywhere, anywhere] if last else []),
+        out_specs=[by_head] + [whole] * BAND_BLOCKS + [anywhere] * len(joined),
         out_shape=[jax.ShapeDtypeStruct((heads, tok, head_dim), BF16)]
         + [jax.ShapeDtypeStruct((tok, 2 * head_dim), BF16)] * (BAND_BLOCKS - 1)
-        + [jax.ShapeDtypeStruct((tok, 2 * head_dim), F32)],
-        scratch_shapes=[pltpu.VMEM((span, head_dim), F32)] * 2,
-        input_output_aliases={4 + 2 * BAND_BLOCKS: 0} if given else {},
+        + [jax.ShapeDtypeStruct((tok, 2 * head_dim), F32)]
+        + joined,
+        scratch_shapes=[pltpu.VMEM((span, head_dim), F32)] * 2 + [pltpu.SemaphoreType.DMA((2,))] * len(joined),
+        input_output_aliases={4 + 2 * BAND_BLOCKS: 0} if last else {},
         compiler_params=params(),
         cost_estimate=cost(tok, tok),
         name="attention_grad",
@@ -377,7 +418,7 @@
     )(slots, here, there, grad_out)
 
 
-def middle_kernel(routes, own, recv, stream, first, second, gout, dgate, router, router_t, mixed, grad, gates):
+def middle_kernel(experts, routes, own, recv, stream, first, second, gout, dgate, router, router_t, mixed, grad, gates):
     resid = stream[...].astype(F32) + (own[...] + recv[...])
     inverse = lax.rsqrt(jnp.mean(resid * resid, axis=-1, keepdims=True) + 1e-05)
     normed = (resid * inverse).astype(BF16)
@@ -393,14 +434,16 @@
     ).astype(BF16)
     d_first, d_second = dgate[:, 0:1], dgate[:, 1:2]
     common = gate_first * d_first + gate_second * d_second
-    dlogit = jnp.where(is_first, gate_first * (d_first - common), 0.0)
-    dlogit = dlogit + jnp.where(is_second, gate_second * (d_second - common), 0.0)
+    expert = lane % experts
+    dlogit = jnp.where(expert == routes[:, 0:1], gate_first * (d_first - common), 0.0)
+    dlogit = dlogit + jnp.where(expert == routes[:, 1:2], gate_second * (d_second - common), 0.0)
     high = dlogit.astype(BF16)
     rest = dlogit - high.astype(F32)
     middle = rest.astype(BF16)
     low = (rest - middle.astype(F32)).astype(BF16)
-    weights = router_t[...]
-    dnormed = dot_nn(high, weights) + (dot_nn(middle, weights) + dot_nn(low, weights))
+    part = lane // experts
+    parts = jnp.where(part == 0, high.astype(F32), jnp.where(part == 1, middle.astype(F32), low.astype(F32)))
+    dnormed = dot_nn(parts.astype(BF16), router_t[...])
     mean = jnp.mean(dnormed * resid, axis=-1, keepdims=True)
     grad[...] = (
         gout[...].astype(F32) + inverse * dnormed - resid * (inverse * inverse * inverse * mean)
@@ -408,13 +451,16 @@
     gates[...] = jnp.where(lane == 0, gate_first, jnp.where(lane == 1, gate_second, 0.0))
 
 
-def middle(routes, own, recv, stream, first, second, grad_out, dgate, router, router_t):
+MIDDLE_ROWS = 64
+
+
+def middle(routes, own, recv, stream, first, second, grad_out, dgate, router, router_t, experts):
     rows, width = stream.shape
-    size = 32 if rows % 32 == 0 else rows
+    size = MIDDLE_ROWS if rows % MIDDLE_ROWS == 0 else rows
     by_row = lambda n: pl.BlockSpec((size, n), lambda i: (i, 0))
     whole = lambda a: pl.BlockSpec(a.shape, lambda i: (0, 0))
     return pl.pallas_call(
-        middle_kernel,
+        functools.partial(middle_kernel, experts),
         grid=(rows // size,),
         in_specs=[by_row(2)] + [by_row(width)] * 6 + [by_row(128), whole(router), whole(router_t)],
         out_specs=[by_row(width), by_row(width), by_row(128)],
@@ -478,8 +524,6 @@
         [rotated_keys.reshape(tok, heads_kv * head_dim), value_inputs.reshape(tok, heads_kv * head_dim)], axis=1
     )
     queries = jnp.transpose(queries_in, (1, 0, 2))
-    sent = lax.dynamic_index_in_dim(expert_out[0], 1 - core, 1, keepdims=False).reshape(room, width)
-    kept = lax.dynamic_index_in_dim(expert_out[0], core, 1, keepdims=False).reshape(room, width)
     flat = routes.reshape(-1)
     number = jnp.arange(2 * rows, dtype=jnp.int32)
     earlier = (flat[None, :] == flat[:, None]) & (number[None, :] < number[:, None])
@@ -487,15 +531,22 @@
     slots = (flat * capacity + rank - core * room) % (experts * capacity)
     slots = slots.reshape(rows, 2)
     router = jnp.pad(w_router, ((0, 0), (0, 128 - experts)))
-    router_t = jnp.pad(w_router.T, ((0, 128 - experts), (0, 0)))
+    router_t = jnp.pad(jnp.concatenate([w_router.T] * 3, axis=0), ((0, 128 - 3 * experts), (0, 0)))
     made = {}
 
-    def exchange_rows():
-        made["arrived"] = swapped(sent, "exp")
-        return [made["arrived"], slots, own_band, router, router_t]
-
-    def pick_rows():
-        made["picked"] = pick(slots, kept, made["arrived"], grad_out)
+    def prepare(*ready):
+        return [slots, own_band, router, router_t]
+
+    def swap_rows(*ready):
+        rows_out = after([expert_out[0]], *ready)[0]
+        sent = lax.dynamic_index_in_dim(rows_out, 1 - core, 1, keepdims=False).reshape(room, width)
+        kept = lax.dynamic_index_in_dim(rows_out, core, 1, keepdims=False).reshape(room, width)
+        made["rows"] = kept, swapped(sent, "exp")
+        return made["rows"]
+
+    def pick_rows(*ready):
+        kept, arrived = after(made["rows"], *ready)
+        made["picked"] = pick(slots, kept, arrived, grad_out)
         return [made["picked"][2]]
 
     def attend(*ready):
@@ -506,32 +557,31 @@
             queries, made["bands"], place_arg, heads_q, heads_kv, head_dim, scale
         )
 
-    arrays, table, plan = gathered(w_out, exchange_rows, pick_rows, attend)
+    arrays, table, plan = gathered(w_out, prepare, swap_rows, pick_rows, attend)
     first, second, dgate = made["picked"]
     attn, probs = made["attention"]
     bands = made["bands"]
 
     own, other = project([attn], arrays, table, plan, core_arg, heads_q, head_dim, width, rows)
     mixed, grad_input, gates = middle(
-        routes, own, swapped(other, "exp"), stream_in, first, second, grad_out, dgate, router, router_t
+        routes, own, swapped(other, "exp"), stream_in, first, second, grad_out, dgate, router, router_t, experts
     )
     grad_other = swapped(grad_input, "exp")
     here, there = spread(slots.T, gates, grad_out, room)
     dattn = dattention(grad_input, grad_other, arrays, table, plan, core_arg, heads_q, head_dim, width)
     there = after([there], dattn)[0]
-    back = swapped(there, "exp").reshape(held, 1, capacity, width)
-    here = here.reshape(held, 1, capacity, width)
-    grad_expert = jnp.where(
-        core == 0, jnp.concatenate([here, back], axis=1), jnp.concatenate([back, here], axis=1)
-    )[None]
-    grads, totals, grad_q = [], [], None
+    back = swapped(there, "exp").reshape(held, capacity, width)
+    here = here.reshape(held, capacity, width)
+    grads, totals, given = [], [], ()
     for i in range(heads_kv):
-        grad = attention_grad(queries, dattn, attn, probs, bands, i, grad_q, heads_kv, scale)
+        if i == heads_kv - 1:
+            given = (grads[-1][0], core_arg, here, back)
+        grad = attention_grad(queries, dattn, attn, probs, bands, i, given, heads_kv, scale)
         totals.append([passed_along(grad[BAND_BLOCKS - step], "ctx", -step) for step in range(1, BAND_BLOCKS)])
         grads.append(grad)
-        grad_q = grad[0]
-    grad_q = jnp.transpose(grad_q, (1, 0, 2))
-    totals, grad_q, grad_expert = lax.optimization_barrier((totals, grad_q, grad_expert))
+    grad_q = jnp.transpose(grads[-1][0], (1, 0, 2))
+    grad_expert = grads[-1][1 + BAND_BLOCKS]
+    totals = lax.optimization_barrier(totals)
     sums = []
     for grad, passed in zip(grads, totals):
         total = grad[BAND_BLOCKS]

time: 193 us -> 284 us (1.47)
  Pallas kernels: 62.8 us -> 150 us
  local copies, waits for them, and re-layouts: 13.6 us -> 18.9 us
  waiting for transfers between devices: 82.1 us -> 78.1 us
  starting transfers between devices: 29.5 us -> 33.3 us
    pallas_call x3, Pallas kernels: 24.3 us -> 112 us  [the longest x2 106 us: attention_grad(): pl.pallas_call(functools.partial(attention_grad_kernel, scale, steps, las...]
    ppermute x4, waiting for transfers between devices: 48.7 us -> 28 us  [gathered(): lax.ppermute(value, 'ctx', [(c, (c + 2) % count) for c in range(count)])]
    ppermute x5, waiting for transfers between devices: 0.01 us -> 17.6 us  [gathered(): lax.ppermute(value, 'ctx', [(c, c ^ 1) for c in range(count)])]
    unnamed x57 -> x53, local copies, waits for them, and re-layouts: 5.01 us -> 10.5 us
    ppermute x5, starting transfers between devices: 3.16 us -> 6.96 us  [gathered(): lax.ppermute(value, 'ctx', [(c, c ^ 1) for c in range(count)])]
  transfers between devices with their start and end apart: 27 -> 27, of which waited for: 10 -> 14; matrix products, arithmetic and copies ran while one was open for 4% -> 2% of each run, Pallas kernels for 20% -> 45%
where the time goes in v4:
time: 284 us
  Pallas kernels  150 us (53%)
  waiting for transfers between devices  78.1 us (27%)
  starting transfers between devices  33.3 us (12%)
  local copies, waits for them, and re-layouts  18.9 us (7%)
    pallas_call x2, Pallas kernels, attention_grad(): pl.pallas_call(functools.partial(attention_grad_kernel, scale, steps, las...  106 us
    ppermute x9, waiting for transfers between devices, passed_along(): lax.ppermute(value, axis, [(source, source + steps) for source in range(i...  28.9 us
    ppermute x4, waiting for transfers between devices, gathered(): lax.ppermute(value, 'ctx', [(c, (c + 2) % count) for c in range(count)])  28 us
    ppermute x9, starting transfers between devices, passed_along(): lax.ppermute(value, axis, [(source, source + steps) for source in range(i...  17.6 us
    ppermute x5, waiting for transfers between devices, gathered(): lax.ppermute(value, 'ctx', [(c, c ^ 1) for c in range(count)])  17.6 us
    pallas_call x1, Pallas kernels, attention(): pl.pallas_call(functools.partial(attention_kernel, scale), grid_spec=pltp...  11 us
    unnamed x53, local copies, waits for them, and re-layouts  10.5 us
    pallas_call x1, Pallas kernels, dattention(): pl.pallas_call(functools.partial(dattn_kernel, plan, len(arrays)), grid_s...  8.67 us
  transfers between devices with their start and end apart: 27, of which 14 were waited for; matrix products, arithmetic and copies ran while one was open for 2% of the time, Pallas kernels for 45%

profile of v4, /device:TPU:4, one launch (start us, length us, event | category | flops | bytes accessed | tf_op | source)
XLA Modules:
  0.0 283.6 jit_solution(2207416657646356034)
XLA Ops:
  0.7 1.9 constant_dynamic-slice_fusion.2
  2.6 1.6 collective-permute-start
  9.0 10.7 %collective-permute-done.refs_2_.refs_1_ = bf16[6,16,3072]{2,1,0:T(8,128)(2,1)S(1)} collective-permute-done((bf16[6,16,3072]{2,1,0:T(8,128)(2,1)}, bf16[6,16,3072]{2,1,0:T(8,128)(2,1)S(1)}, u32[]{:S(2)}, u32[]{:S(2)}) %collective-permute-start) | collective-permute-done | bytes 589856 | tf_op jit(solution)/shard_map/ppermute | solution.py:61
  19.7 3.5 %constant_dynamic-slice_fusion = (bf16[4,1,64,3072]{3,2,1,0:T(8,128)(2,1)S(1)}, bf16[4,1,64,3072]{3,2,1,0:T(8,128)(2,1)}) fusion(bf16[4,2,64,3072]{3,2,1,0:T(8,128)(2,1)} %bitcast.39, s32[]{:T(128)S(6)} %select_n.51, s32[]{:T(128)S(6)} %select_n.50), kind=kLoop, calls=%fused_computation.23 | loop fusion | bytes 6291464 | tf_op jit(solution)/shard_map/jit(dynamic_index_in_dim)/dynamic_slice | solution.py:542
  23.7 1.5 collective-permute-start.7
  25.3 1.5 collective-permute-start.6
  26.7 12.8 %collective-permute-done.2.refs_5_.refs_4_ = bf16[6,16,3072]{2,1,0:T(8,128)(2,1)S(1)} collective-permute-done((bf16[6,16,3072]{2,1,0:T(8,128)(2,1)}, bf16[6,16,3072]{2,1,0:T(8,128)(2,1)S(1)}, u32[]{:S(2)}, u32[]{:S(2)}) %collective-permute-start.2) | collective-permute-done | bytes 589856 | tf_op jit(solution)/shard_map/ppermute | solution.py:62
  42.9 1.5 collective-permute-start.4
  45.9 4.9 %pick.1 = (bf16[128,3072]{1,0:T(8,128)(2,1)}, bf16[128,3072]{1,0:T(8,128)(2,1)}, f32[128,128]{1,0:T(8,128)}) custom-call(s32[128,2]{1,0:T(8,128)} %copy.31.slots, bf16[256,3072]{1,0:T(8,128)(2,1)} %bitcast.35, bf16[256,3072]{1,0:T(8,128)(2,1)} %copy-done.13, bf16[128,3072]{1,0:T(8,128)(2,1)} %gout.5), custom_call_target="tpu_custom_call" | custom-call | flops 805306368 | bytes 6291456 | tf_op jit(solution)/shard_map/pick/pallas_call | solution.py:409
  52.2 6.5 %collective-permute-done.5.refs_4_.refs_3_ = bf16[6,16,3072]{2,1,0:T(8,128)(2,1)} collective-permute-done((bf16[6,16,3072]{2,1,0:T(8,128)(2,1)S(1)}, bf16[6,16,3072]{2,1,0:T(8,128)(2,1)}, u32[]{:S(2)}, u32[]{:S(2)}) %collective-permute-start.5) | collective-permute-done | bytes 589856 | tf_op jit(solution)/shard_map/ppermute | solution.py:61
  58.7 1.5 collective-permute-start.10
  60.2 1.5 collective-permute-start.14
  61.8 3.2 %collective-permute-done.4.refs_7_.refs_6_ = bf16[6,16,3072]{2,1,0:T(8,128)(2,1)} collective-permute-done((bf16[6,16,3072]{2,1,0:T(8,128)(2,1)S(1)}, bf16[6,16,3072]{2,1,0:T(8,128)(2,1)}, u32[]{:S(2)}, u32[]{:S(2)}) %collective-permute-start.4) | collective-permute-done | bytes 589856 | tf_op jit(solution)/shard_map/ppermute | solution.py:62
  64.9 9.3 %collective-permute-done.8.refs_10_.refs_9_ = bf16[6,16,3072]{2,1,0:T(8,128)(2,1)S(1)} collective-permute-done((bf16[6,16,3072]{2,1,0:T(8,128)(2,1)S(1)}, bf16[6,16,3072]{2,1,0:T(8,128)(2,1)S(1)}, u32[]{:S(2)}, u32[]{:S(2)}) %collective-permute-start.8) | collective-permute-done | bytes 589856 | tf_op jit(solution)/shard_map/ppermute | solution.py:61
  75.1 1.9 collective-permute-start.13
  77.2 1.9 collective-permute-start.15
  82.4 3.8 %collective-permute-done.13.refs_2_.refs_6_ = bf16[256,512]{1,0:T(8,128)(2,1)S(1)} collective-permute-done((bf16[256,512]{1,0:T(8,128)(2,1)S(1)}, bf16[256,512]{1,0:T(8,128)(2,1)S(1)}, u32[]{:S(2)}, u32[]{:S(2)}) %collective-permute-start.13) | collective-permute-done | bytes 262176 | tf_op jit(solution)/shard_map/ppermute | solution.py:39
  86.2 3.4 %collective-permute-start.11 = (bf16[256,512]{1,0:T(8,128)(2,1)S(1)}, bf16[256,512]{1,0:T(8,128)(2,1)S(1)}, u32[]{:S(2)}, u32[]{:S(2)}) collective-permute-start(bf16[256,512]{1,0:T(8,128)(2,1)S(1)} %bitcast_dynamic-update-slice_fusion.refs_3_.refs_7_), channel_id=1, source_target_pairs={{0,6},{2,8},{4,10},{6,12},{8,14},{1,7},{3,9},{5,11},{7,13},{9,15},... | collective-permute-start | bytes 786440 | tf_op jit(solution)/shard_map/ppermute | solution.py:39
  90.3 4.0 %collective-permute-done.11.refs_0_.refs_4_ = bf16[256,512]{1,0:T(8,128)(2,1)S(1)} collective-permute-done((bf16[256,512]{1,0:T(8,128)(2,1)S(1)}, bf16[256,512]{1,0:T(8,128)(2,1)S(1)}, u32[]{:S(2)}, u32[]{:S(2)}) %collective-permute-start.11) | collective-permute-done | bytes 262176 | tf_op jit(solution)/shard_map/ppermute | solution.py:39
  95.0 11.0 %attention.1 = (bf16[256,1536]{1,0:T(8,128)(2,1)}, bf16[12,256,1024]{2,1,0:T(8,128)(2,1)}) custom-call(s32[1]{0:T(128)} %bitcast.11.place, bf16[12,256,128]{2,1,0:T(8,128)(2,1)} %bitcast.36, bf16[256,512]{1,0:T(8,128)(2,1)} %copy-done.3, bf16[256,512]{1,0:T(8,128)(2,1)} %copy-done.2, bf16[256,512]{1,0:T(8,128)(2,1)} %copy-done.1, bf16[256,512]{1,0:T(8,128)(2,1)} %copy-done, ...), custom_call_target="tpu_custom_call" | custom-call | flops 1610612736 | bytes 6291456 | tf_op jit(solution)/shard_map/attention/pallas_call | solution.py:268
  106.8 8.4 %project.1 = (f32[128,3072]{1,0:T(8,128)}, f32[128,3072]{1,0:T(8,128)}) custom-call(s32[11]{0:T(128)} %stack.61.table, s32[1]{0:T(128)} %bitcast.10.core.refs_9_, bf16[256,1536]{1,0:T(8,128)(2,1)} %get-tuple-element.60.refs_0_.attn, bf16[12,16,3072]{2,1,0:T(8,128)(2,1)} %refs_0_.1, bf16[6,16,3072]{2,1,0:T(8,128)(2,1)} %copy-done.4, ...), custom_call_target="tpu_custom_call" | custom-call | flops 2415919104 | bytes 9437184 | tf_op jit(solution)/shard_map/project/pallas_call | solution.py:147
  115.3 3.6 %collective-permute-done.18.recv = f32[128,3072]{1,0:T(8,128)S(1)} collective-permute-done((f32[128,3072]{1,0:T(8,128)}, f32[128,3072]{1,0:T(8,128)S(1)}, u32[]{:S(2)}, u32[]{:S(2)}) %collective-permute-start.18) | collective-permute-done | bytes 1572896 | tf_op jit(solution)/shard_map/ppermute | solution.py:43
  120.2 6.3 %middle.1 = (bf16[128,3072]{1,0:T(8,128)(2,1)}, bf16[128,3072]{1,0:T(8,128)(2,1)}, f32[128,128]{1,0:T(8,128)}) custom-call(s32[128,2]{1,0:T(8,128)} %copy-done.17, f32[128,3072]{1,0:T(8,128)} %get-tuple-element.64.own, f32[128,3072]{1,0:T(8,128)} %copy-done.15, bf16[128,3072]{1,0:T(8,128)(2,1)} %stream.1, bf16[128,3072]{1,0:T(8,128)(2,1)} %get-tuple-element.66.first, ...), custom_call_target="tpu_custom_call" | custom-call | flops 402653184 | bytes 7864320 | tf_op jit(solution)/shard_map/middle/pallas_call | solution.py:462
  126.7 4.5 %spread.1 = (bf16[256,3072]{1,0:T(8,128)(2,1)}, bf16[256,3072]{1,0:T(8,128)(2,1)}) custom-call(s32[2,128]{1,0:T(2,128)} %bitcast.47, f32[128,128]{1,0:T(8,128)} %get-tuple-element.72.gates, bf16[128,3072]{1,0:T(8,128)(2,1)} %gout.5), custom_call_target="tpu_custom_call" | custom-call | flops 805306368 | bytes 3932160 | tf_op jit(solution)/shard_map/spread/pallas_call | solution.py:492
  132.0 8.7 %dattention.1.dout = bf16[256,1536]{1,0:T(8,128)(2,1)} custom-call(s32[11]{0:T(128)} %stack.61.table, s32[1]{0:T(128)} %bitcast.10.core.refs_9_, bf16[128,3072]{1,0:T(8,128)(2,1)} %get-tuple-element.105.own, bf16[128,3072]{1,0:T(8,128)(2,1)} %copy-done.16, bf16[12,16,3072]{2,1,0:T(8,128)(2,1)} %refs_0_.1, bf16[6,16,3072]{2,1,0:T(8,128)(2,1)} %copy-done.4, ...), custom_call_target="tpu_custom_call" | custom-call | flops 2415919104 | bytes 9437184 | tf_op jit(solution)/shard_map/dattention/pallas_call | solution.py:203
  141.1 6.5 %attention_grad.2 = (bf16[12,256,128]{2,1,0:T(8,128)(2,1)}, bf16[256,256]{1,0:T(8,128)(2,1)}, bf16[256,256]{1,0:T(8,128)(2,1)}, bf16[256,256]{1,0:T(8,128)(2,1)}, f32[256,256]{1,0:T(8,128)}) custom-call(bf16[12,256,128]{2,1,0:T(8,128)(2,1)} %bitcast.37, bf16[256,1536]{1,0:T(8,128)(2,1)} %dattention.1.dout, bf16[256,1536]{1,0:T(8,128)(2,1)} %get-tuple-element.60.refs_0_.attn, ...), custom_call_target="tpu_custom_call" | custom-call | flops 256 | bytes 256 | tf_op jit(solution)/shard_map/attention_grad/pallas_call | solution.py:358
  147.7 3.9 %collective-permute-start.21 = (bf16[256,256]{1,0:T(8,128)(2,1)}, bf16[256,256]{1,0:T(8,128)(2,1)S(1)}, u32[]{:S(2)}, u32[]{:S(2)}) collective-permute-start(bf16[256,256]{1,0:T(8,128)(2,1)} %get-tuple-element.79), channel_id=1, source_target_pairs={{2,0},{4,2},{6,4},{8,6},{10,8},{12,10},{14,12},{3,1},{5,3},{7,5},{... | collective-permute-start | bytes 393224 | tf_op jit(solution)/shard_map/ppermute | solution.py:39
  155.4 99.7 %attention_grad.3 = (bf16[12,256,128]{2,1,0:T(8,128)(2,1)}, bf16[256,256]{1,0:T(8,128)(2,1)}, bf16[256,256]{1,0:T(8,128)(2,1)}, bf16[256,256]{1,0:T(8,128)(2,1)}...) custom-call(bf16[12,256,128]{2,1,0:T(8,128)(2,1)} %bitcast.38, ...), custom_call_target="tpu_custom_call", output_to_operand_aliasing={{0}: (12, {})} | custom-call | flops 256 | bytes 256 | tf_op jit(solution)/shard_map/attention_grad/pallas_call | solution.py:358
  255.1 1.9 collective-permute-start.24
  259.7 4.8 %collective-permute-done.24 = bf16[256,256]{1,0:T(8,128)(2,1)S(1)} collective-permute-done((bf16[256,256]{1,0:T(8,128)(2,1)}, bf16[256,256]{1,0:T(8,128)(2,1)S(1)}, u32[]{:S(2)}, u32[]{:S(2)}) %collective-permute-start.24) | collective-permute-done | bytes 131104 | tf_op jit(solution)/shard_map/ppermute | solution.py:39
  264.4 8.3 %collective-permute-done.25 = bf16[256,256]{1,0:T(8,128)(2,1)S(1)} collective-permute-done((bf16[256,256]{1,0:T(8,128)(2,1)}, bf16[256,256]{1,0:T(8,128)(2,1)S(1)}, u32[]{:S(2)}, u32[]{:S(2)}) %collective-permute-start.25) | collective-permute-done | bytes 131104 | tf_op jit(solution)/shard_map/ppermute | solution.py:39
  272.8 8.1 %collective-permute-done.26 = bf16[256,256]{1,0:T(8,128)(2,1)S(1)} collective-permute-done((bf16[256,256]{1,0:T(8,128)(2,1)}, bf16[256,256]{1,0:T(8,128)(2,1)S(1)}, u32[]{:S(2)}, u32[]{:S(2)}) %collective-permute-start.26) | collective-permute-done | bytes 131104 | tf_op jit(solution)/shard_map/ppermute | solution.py:39
  (100 shorter events, 29.9 us)
Async XLA Ops:
  2.6 17.1 %collective-permute-start = (bf16[6,16,3072]{2,1,0:T(8,128)(2,1)}, bf16[6,16,3072]{2,1,0:T(8,128)(2,1)S(1)}, u32[]{:S(2)}, u32[]{:S(2)}) collective-permute-start(bf16[6,16,3072]{2,1,0:T(8,128)(2,1)} %constant_dynamic-slice_fusion.2), channel_id=1, source_target_pairs={{0,4},{2,6},{4,8},{6,10},{8,12},{10,14},{12,0},{14,2},{1,5},{3,7},... | collective-permute-start | bytes 1769480 | tf_op jit(solution)/shard_map/ppermute | solution.py:61
  6.5 35.7 %copy-start.22 = (s32[128,2]{0,1:T(2,128)}, s32[128,2]{0,1:T(2,128)S(1)}, u32[]{:S(2)}) copy-start(s32[128,2]{0,1:T(2,128)S(1)} %and_select_fusion) | copy-start | bytes 3076
  8.0 78.2 %copy-start = (bf16[256,512]{1,0:T(8,128)(2,1)}, bf16[256,512]{1,0:T(8,128)(2,1)S(1)}, u32[]{:S(2)}) copy-start(bf16[256,512]{1,0:T(8,128)(2,1)S(1)} %bitcast_dynamic-update-slice_fusion.refs_3_.refs_7_) | copy-start | bytes 786436
  23.2 17.8 %collective-permute-start.3 = (bf16[256,3072]{1,0:T(8,128)(2,1)S(1)}, bf16[256,3072]{1,0:T(8,128)(2,1)S(1)}, u32[]{:S(2)}, u32[]{:S(2)}) collective-permute-start(bf16[256,3072]{1,0:T(8,128)(2,1)S(1)} %bitcast.42), channel_id=1, source_target_pairs={{0,1},{1,0},{2,3},{3,2},{4,5},{5,4},{6,7},{7,6},{8,9},{9,8},{10,11... | collective-permute-start | bytes 4718600 | tf_op jit(solution)/shard_map/ppermute | solution.py:43
  23.2 16.3 %collective-permute-start.2 = (bf16[6,16,3072]{2,1,0:T(8,128)(2,1)}, bf16[6,16,3072]{2,1,0:T(8,128)(2,1)S(1)}, u32[]{:S(2)}, u32[]{:S(2)}) collective-permute-start(bf16[6,16,3072]{2,1,0:T(8,128)(2,1)} %constant_dynamic-slice_fusion.2), channel_id=1, source_target_pairs={{0,2},{2,0},{4,6},{6,4},{8,10},{10,8},{12,14},{14,12},{1,3},{3,1},... | collective-permute-start | bytes 1769480 | tf_op jit(solution)/shard_map/ppermute | solution.py:62
  23.7 17.3 %collective-permute-start.1 = (bf16[6,16,3072]{2,1,0:T(8,128)(2,1)S(1)}, bf16[6,16,3072]{2,1,0:T(8,128)(2,1)S(1)}, u32[]{:S(2)}, u32[]{:S(2)}) collective-permute-start(bf16[6,16,3072]{2,1,0:T(8,128)(2,1)S(1)} %collective-permute-done.refs_2_.refs_1_), channel_id=1, source_target_pairs={{0,4},{2,6},{4,8},{6,10},{8,12},{10,14},{12,0},{14,2},{1,5},{3,7},... | collective-permute-start | bytes 1769480 | tf_op jit(solution)/shard_map/ppermute | solution.py:61
  23.7 28.5 %collective-permute-start.7 = (bf16[6,16,3072]{2,1,0:T(8,128)(2,1)S(1)}, bf16[6,16,3072]{2,1,0:T(8,128)(2,1)S(1)}, u32[]{:S(2)}, u32[]{:S(2)}) collective-permute-start(bf16[6,16,3072]{2,1,0:T(8,128)(2,1)S(1)} %collective-permute-done.refs_2_.refs_1_), channel_id=1, source_target_pairs={{0,2},{2,0},{4,6},{6,4},{8,10},{10,8},{12,14},{14,12},{1,3},{3,1},... | collective-permute-start | bytes 1769480 | tf_op jit(solution)/shard_map/ppermute | solution.py:62
  25.3 26.9 %collective-permute-start.6 = (bf16[6,16,3072]{2,1,0:T(8,128)(2,1)S(1)}, bf16[6,16,3072]{2,1,0:T(8,128)(2,1)S(1)}, u32[]{:S(2)}, u32[]{:S(2)}) collective-permute-start(bf16[6,16,3072]{2,1,0:T(8,128)(2,1)S(1)} %collective-permute-done.refs_2_.refs_1_), channel_id=1, source_target_pairs={{0,16},{16,0},{1,17},{17,1},{2,18},{18,2},{3,19},{19,3},{4,20},{20... | collective-permute-start | bytes 1769480 | tf_op jit(solution)/shard_map/ppermute | solution.py:43
  42.2 16.5 %collective-permute-start.5 = (bf16[6,16,3072]{2,1,0:T(8,128)(2,1)S(1)}, bf16[6,16,3072]{2,1,0:T(8,128)(2,1)}, u32[]{:S(2)}, u32[]{:S(2)}) collective-permute-start(bf16[6,16,3072]{2,1,0:T(8,128)(2,1)S(1)} %collective-permute-done.1.refs_3_.refs_2_), channel_id=1, source_target_pairs={{0,4},{2,6},{4,8},{6,10},{8,12},{10,14},{12,0},{14,2},{1,5},{3,7},... | collective-permute-start | bytes 1769480 | tf_op jit(solution)/shard_map/ppermute | solution.py:61
  42.9 22.0 %collective-permute-start.4 = (bf16[6,16,3072]{2,1,0:T(8,128)(2,1)S(1)}, bf16[6,16,3072]{2,1,0:T(8,128)(2,1)}, u32[]{:S(2)}, u32[]{:S(2)}) collective-permute-start(bf16[6,16,3072]{2,1,0:T(8,128)(2,1)S(1)} %collective-permute-done.1.refs_3_.refs_2_), channel_id=1, source_target_pairs={{0,2},{2,0},{4,6},{6,4},{8,10},{10,8},{12,14},{14,12},{1,3},{3,1},... | collective-permute-start | bytes 1769480 | tf_op jit(solution)/shard_map/ppermute | solution.py:62
  44.5 17.3 %collective-permute-start.9 = (bf16[6,16,3072]{2,1,0:T(8,128)(2,1)S(1)}, bf16[6,16,3072]{2,1,0:T(8,128)(2,1)S(1)}, u32[]{:S(2)}, u32[]{:S(2)}) collective-permute-start(bf16[6,16,3072]{2,1,0:T(8,128)(2,1)S(1)} %collective-permute-done.2.refs_5_.refs_4_), channel_id=1, source_target_pairs={{0,16},{16,0},{1,17},{17,1},{2,18},{18,2},{3,19},{19,3},{4,20},{20... | collective-permute-start | bytes 1769480 | tf_op jit(solution)/shard_map/ppermute | solution.py:43
  52.2 53.8 %copy-start.7 = (bf16[6,16,3072]{2,1,0:T(8,128)(2,1)}, bf16[6,16,3072]{2,1,0:T(8,128)(2,1)S(1)}, u32[]{:S(2)}) copy-start(bf16[6,16,3072]{2,1,0:T(8,128)(2,1)S(1)} %collective-permute-done.7.refs_6_.refs_5_) | copy-start | bytes 1769476
  52.2 53.8 %copy-start.8 = (bf16[6,16,3072]{2,1,0:T(8,128)(2,1)}, bf16[6,16,3072]{2,1,0:T(8,128)(2,1)S(1)}, u32[]{:S(2)}) copy-start(bf16[6,16,3072]{2,1,0:T(8,128)(2,1)S(1)} %collective-permute-done.6.refs_9_.refs_8_) | copy-start | bytes 1769476
  58.7 15.5 %collective-permute-start.8 = (bf16[6,16,3072]{2,1,0:T(8,128)(2,1)S(1)}, bf16[6,16,3072]{2,1,0:T(8,128)(2,1)S(1)}, u32[]{:S(2)}, u32[]{:S(2)}) collective-permute-start(bf16[6,16,3072]{2,1,0:T(8,128)(2,1)S(1)} %collective-permute-done.6.refs_9_.refs_8_), channel_id=1, source_target_pairs={{0,4},{2,6},{4,8},{6,10},{8,12},{10,14},{12,0},{14,2},{1,5},{3,7},... | collective-permute-start | bytes 1769480 | tf_op jit(solution)/shard_map/ppermute | solution.py:61
  58.7 16.3 %collective-permute-start.10 = (bf16[6,16,3072]{2,1,0:T(8,128)(2,1)}, bf16[6,16,3072]{2,1,0:T(8,128)(2,1)S(1)}, u32[]{:S(2)}, u32[]{:S(2)}) collective-permute-start(bf16[6,16,3072]{2,1,0:T(8,128)(2,1)} %collective-permute-done.5.refs_4_.refs_3_), channel_id=1, source_target_pairs={{0,16},{16,0},{1,17},{17,1},{2,18},{18,2},{3,19},{19,3},{4,20},{20... | collective-permute-start | bytes 1769480 | tf_op jit(solution)/shard_map/ppermute | solution.py:43
  60.2 17.0 %collective-permute-start.14 = (bf16[6,16,3072]{2,1,0:T(8,128)(2,1)}, bf16[6,16,3072]{2,1,0:T(8,128)(2,1)}, u32[]{:S(2)}, u32[]{:S(2)}) collective-permute-start(bf16[6,16,3072]{2,1,0:T(8,128)(2,1)} %collective-permute-done.5.refs_4_.refs_3_), channel_id=1, source_target_pairs={{0,2},{2,0},{4,6},{6,4},{8,10},{10,8},{12,14},{14,12},{1,3},{3,1},... | collective-permute-start | bytes 1769480 | tf_op jit(solution)/shard_map/ppermute | solution.py:62
  75.1 11.1 %collective-permute-start.13 = (bf16[256,512]{1,0:T(8,128)(2,1)S(1)}, bf16[256,512]{1,0:T(8,128)(2,1)S(1)}, u32[]{:S(2)}, u32[]{:S(2)}) collective-permute-start(bf16[256,512]{1,0:T(8,128)(2,1)S(1)} %bitcast_dynamic-update-slice_fusion.refs_3_.refs_7_), channel_id=1, source_target_pairs={{0,2},{2,4},{4,6},{6,8},{8,10},{10,12},{12,14},{1,3},{3,5},{5,7},{... | collective-permute-start | bytes 786440 | tf_op jit(solution)/shard_map/ppermute | solution.py:39
  77.2 28.8 %collective-permute-start.15 = (bf16[6,16,3072]{2,1,0:T(8,128)(2,1)S(1)}, bf16[6,16,3072]{2,1,0:T(8,128)(2,1)S(1)}, u32[]{:S(2)}, u32[]{:S(2)}) collective-permute-start(bf16[6,16,3072]{2,1,0:T(8,128)(2,1)S(1)} %collective-permute-done.6.refs_9_.refs_8_), channel_id=1, source_target_pairs={{0,2},{2,0},{4,6},{6,4},{8,10},{10,8},{12,14},{14,12},{1,3},{3,1},... | collective-permute-start | bytes 1769480 | tf_op jit(solution)/shard_map/ppermute | solution.py:62
  79.1 26.9 %collective-permute-start.17 = (bf16[6,16,3072]{2,1,0:T(8,128)(2,1)}, bf16[6,16,3072]{2,1,0:T(8,128)(2,1)}, u32[]{:S(2)}, u32[]{:S(2)}) collective-permute-start(bf16[6,16,3072]{2,1,0:T(8,128)(2,1)} %collective-permute-done.14.refs_8_.refs_7_), channel_id=1, source_target_pairs={{0,16},{16,0},{1,17},{17,1},{2,18},{18,2},{3,19},{19,3},{4,20},{20... | collective-permute-start | bytes 1769480 | tf_op jit(solution)/shard_map/ppermute | solution.py:43
  80.6 25.4 %collective-permute-start.16 = (bf16[6,16,3072]{2,1,0:T(8,128)(2,1)}, bf16[6,16,3072]{2,1,0:T(8,128)(2,1)}, u32[]{:S(2)}, u32[]{:S(2)}) collective-permute-start(bf16[6,16,3072]{2,1,0:T(8,128)(2,1)} %collective-permute-done.4.refs_7_.refs_6_), channel_id=1, source_target_pairs={{0,16},{16,0},{1,17},{17,1},{2,18},{18,2},{3,19},{19,3},{4,20},{20... | collective-permute-start | bytes 1769480 | tf_op jit(solution)/shard_map/ppermute | solution.py:43
  81.1 9.2 %collective-permute-start.12 = (bf16[256,512]{1,0:T(8,128)(2,1)S(1)}, bf16[256,512]{1,0:T(8,128)(2,1)S(1)}, u32[]{:S(2)}, u32[]{:S(2)}) collective-permute-start(bf16[256,512]{1,0:T(8,128)(2,1)S(1)} %bitcast_dynamic-update-slice_fusion.refs_3_.refs_7_), channel_id=1, source_target_pairs={{0,4},{2,6},{4,8},{6,10},{8,12},{10,14},{1,5},{3,7},{5,9},{7,11},{... | collective-permute-start | bytes 786440 | tf_op jit(solution)/shard_map/ppermute | solution.py:39
  86.2 8.1 %collective-permute-start.11 = (bf16[256,512]{1,0:T(8,128)(2,1)S(1)}, bf16[256,512]{1,0:T(8,128)(2,1)S(1)}, u32[]{:S(2)}, u32[]{:S(2)}) collective-permute-start(bf16[256,512]{1,0:T(8,128)(2,1)S(1)} %bitcast_dynamic-update-slice_fusion.refs_3_.refs_7_), channel_id=1, source_target_pairs={{0,6},{2,8},{4,10},{6,12},{8,14},{1,7},{3,9},{5,11},{7,13},{9,15},... | collective-permute-start | bytes 786440 | tf_op jit(solution)/shard_map/ppermute | solution.py:39
  115.3 3.7 %collective-permute-start.18 = (f32[128,3072]{1,0:T(8,128)}, f32[128,3072]{1,0:T(8,128)S(1)}, u32[]{:S(2)}, u32[]{:S(2)}) collective-permute-start(f32[128,3072]{1,0:T(8,128)} %get-tuple-element.65), channel_id=1, source_target_pairs={{0,1},{1,0},{2,3},{3,2},{4,5},{5,4},{6,7},{7,6},{8,9},{9,8},{10,11... | collective-permute-start | bytes 4718600 | tf_op jit(solution)/shard_map/ppermute | solution.py:43
  126.5 4.7 %collective-permute-start.19 = (bf16[128,3072]{1,0:T(8,128)(2,1)}, bf16[128,3072]{1,0:T(8,128)(2,1)S(1)}, u32[]{:S(2)}, u32[]{:S(2)}) collective-permute-start(bf16[128,3072]{1,0:T(8,128)(2,1)} %get-tuple-element.105.own), channel_id=1, source_target_pairs={{0,1},{1,0},{2,3},{3,2},{4,5},{5,4},{6,7},{7,6},{8,9},{9,8},{10,11... | collective-permute-start | bytes 2359304 | tf_op jit(solution)/shard_map/ppermute | solution.py:43
  140.7 13.5 %collective-permute-start.20 = (bf16[256,3072]{1,0:T(8,128)(2,1)S(1)}, bf16[256,3072]{1,0:T(8,128)(2,1)S(1)}, u32[]{:S(2)}, u32[]{:S(2)}) collective-permute-start(bf16[256,3072]{1,0:T(8,128)(2,1)S(1)} %copy-done.23), channel_id=1, source_target_pairs={{0,1},{1,0},{2,3},{3,2},{4,5},{5,4},{6,7},{7,6},{8,9},{9,8},{10,11... | collective-permute-start | bytes 4718600 | tf_op jit(solution)/shard_map/ppermute | solution.py:43
  147.7 110.7 %collective-permute-start.21 = (bf16[256,256]{1,0:T(8,128)(2,1)}, bf16[256,256]{1,0:T(8,128)(2,1)S(1)}, u32[]{:S(2)}, u32[]{:S(2)}) collective-permute-start(bf16[256,256]{1,0:T(8,128)(2,1)} %get-tuple-element.79), channel_id=1, source_target_pairs={{2,0},{4,2},{6,4},{8,6},{10,8},{12,10},{14,12},{3,1},{5,3},{7,5},{... | collective-permute-start | bytes 393224 | tf_op jit(solution)/shard_map/ppermute | solution.py:39
  151.6 108.1 %collective-permute-start.22 = (bf16[256,256]{1,0:T(8,128)(2,1)}, bf16[256,256]{1,0:T(8,128)(2,1)S(1)}, u32[]{:S(2)}, u32[]{:S(2)}) collective-permute-start(bf16[256,256]{1,0:T(8,128)(2,1)} %get-tuple-element.80), channel_id=1, source_target_pairs={{4,0},{6,2},{8,4},{10,6},{12,8},{14,10},{5,1},{7,3},{9,5},{11,7},{... | collective-permute-start | bytes 393224 | tf_op jit(solution)/shard_map/ppermute | solution.py:39
  152.9 106.8 %collective-permute-start.23 = (bf16[256,256]{1,0:T(8,128)(2,1)}, bf16[256,256]{1,0:T(8,128)(2,1)S(1)}, u32[]{:S(2)}, u32[]{:S(2)}) collective-permute-start(bf16[256,256]{1,0:T(8,128)(2,1)} %get-tuple-element.81), channel_id=1, source_target_pairs={{6,0},{8,2},{10,4},{12,6},{14,8},{7,1},{9,3},{11,5},{13,7},{15,9},... | collective-permute-start | bytes 393224 | tf_op jit(solution)/shard_map/ppermute | solution.py:39
  155.4 125.4 %copy-start.18 = (f32[256,256]{1,0:T(8,128)S(1)}, f32[256,256]{1,0:T(8,128)}, u32[]{:S(2)}) copy-start(f32[256,256]{1,0:T(8,128)} %get-tuple-element.78) | copy-start | bytes 786436
  255.1 9.3 %collective-permute-start.24 = (bf16[256,256]{1,0:T(8,128)(2,1)}, bf16[256,256]{1,0:T(8,128)(2,1)S(1)}, u32[]{:S(2)}, u32[]{:S(2)}) collective-permute-start(bf16[256,256]{1,0:T(8,128)(2,1)} %get-tuple-element.82), channel_id=1, source_target_pairs={{2,0},{4,2},{6,4},{8,6},{10,8},{12,10},{14,12},{3,1},{5,3},{7,5},{... | collective-permute-start | bytes 393224 | tf_op jit(solution)/shard_map/ppermute | solution.py:39
  257.1 15.7 %collective-permute-start.25 = (bf16[256,256]{1,0:T(8,128)(2,1)}, bf16[256,256]{1,0:T(8,128)(2,1)S(1)}, u32[]{:S(2)}, u32[]{:S(2)}) collective-permute-start(bf16[256,256]{1,0:T(8,128)(2,1)} %get-tuple-element.83), channel_id=1, source_target_pairs={{4,0},{6,2},{8,4},{10,6},{12,8},{14,10},{5,1},{7,3},{9,5},{11,7},{... | collective-permute-start | bytes 393224 | tf_op jit(solution)/shard_map/ppermute | solution.py:39
  258.4 22.5 %collective-permute-start.26 = (bf16[256,256]{1,0:T(8,128)(2,1)}, bf16[256,256]{1,0:T(8,128)(2,1)S(1)}, u32[]{:S(2)}, u32[]{:S(2)}) collective-permute-start(bf16[256,256]{1,0:T(8,128)(2,1)} %get-tuple-element.84), channel_id=1, source_target_pairs={{6,0},{8,2},{10,4},{12,6},{14,8},{7,1},{9,3},{11,5},{13,7},{15,9},... | collective-permute-start | bytes 393224 | tf_op jit(solution)/shard_map/ppermute | solution.py:39
  (19 other events, 110.9 us)

commit v5 on v4

--- a/solution.py
+++ b/solution.py
@@ -293,16 +293,17 @@
     keys, values = refs[:BAND_BLOCKS], refs[BAND_BLOCKS : 2 * BAND_BLOCKS]
     refs = refs[2 * BAND_BLOCKS :]
     if last:
-        (_, core, here, back), refs, sem = refs[:4], refs[4:-1], refs[-1]
+        (_, core, here, back), refs, (held, sem) = refs[:4], refs[4:-2], refs[-2:]
         joined = refs.pop(1 + BAND_BLOCKS)
-        copies = [
-            pltpu.make_async_copy(here, joined.at[0, :, core[0]], sem.at[0]),
-            pltpu.make_async_copy(back, joined.at[0, :, 1 - core[0]], sem.at[1]),
+        places = core[0], 1 - core[0]
+        inward = [pltpu.make_async_copy(r, held.at[i], sem.at[0, i]) for i, r in enumerate((here, back))]
+        outward = [
+            pltpu.make_async_copy(held.at[i], joined.at[0, :, at], sem.at[1, i]) for i, at in enumerate(places)
         ]
 
         @pl.when(pl.program_id(0) == 0)
         def _():
-            for copy in copies:
+            for copy in inward:
                 copy.start()
 
     dq, outs, (dk, dv) = refs[0], refs[1:-2], refs[-2:]
@@ -314,6 +315,15 @@
     dprob = dot_nt(grad, band_of(values))
     dscore = (weight.astype(F32) * (dprob - delta)).astype(BF16)
     dq[...] = (dot_nn(dscore, band_of(keys)) * scale).astype(BF16).reshape(count, tok, head_dim)
+    if last:
+
+        @pl.when(step == 0)
+        def _():
+            for copy in inward:
+                copy.wait()
+            for copy in outward:
+                copy.start()
+
     dkey = dot_tn(dscore, q[...].reshape(count * tok, head_dim))
     dvalue = dot_tn(weight, grad)
 
@@ -334,7 +344,7 @@
             out[:, :head_dim] = (dk[rows, :] * scale).astype(out.dtype)
             out[:, head_dim:] = dv[rows, :].astype(out.dtype)
         if last:
-            for copy in copies:
+            for copy in outward:
                 copy.wait()
 
 
@@ -351,10 +361,11 @@
     whole = pl.BlockSpec((tok, 2 * head_dim), lambda h: (0, 0))
     anywhere = pl.BlockSpec(memory_space=pl.ANY)
     last = bool(given)
-    joined = []
+    joined, extra = [], []
     if last:
         held, capacity, width = given[2].shape
         joined = [jax.ShapeDtypeStruct((1, held, 2, capacity, width), BF16)]
+        extra = [pltpu.VMEM((2, held, capacity, width), BF16), pltpu.SemaphoreType.DMA((2, 2))]
     return pl.pallas_call(
         functools.partial(attention_grad_kernel, scale, steps, last),
         grid=(steps,),
@@ -368,7 +379,7 @@
         + [jax.ShapeDtypeStruct((tok, 2 * head_dim), BF16)] * (BAND_BLOCKS - 1)
         + [jax.ShapeDtypeStruct((tok, 2 * head_dim), F32)]
         + joined,
-        scratch_shapes=[pltpu.VMEM((span, head_dim), F32)] * 2 + [pltpu.SemaphoreType.DMA((2,))] * len(joined),
+        scratch_shapes=[pltpu.VMEM((span, head_dim), F32)] * 2 + extra,
         input_output_aliases={4 + 2 * BAND_BLOCKS: 0} if last else {},
         compiler_params=params(),
         cost_estimate=cost(tok, tok),

time: 284 us -> 192 us (0.68)
  Pallas kernels: 150 us -> 57.3 us
    pallas_call x2, Pallas kernels: 106 us -> 13.6 us  [attention_grad(): pl.pallas_call(functools.partial(attention_grad_kernel, scale, steps, las...]
  transfers between devices with their start and end apart: 27 -> 27, of which waited for: 14 -> 14; matrix products, arithmetic and copies ran while one was open for 2% -> 3% of each run, Pallas kernels for 45% -> 18%
where the time goes in v5:
time: 192 us; the launch traced here: 191 us
  waiting for transfers between devices  78.1 us (41%)
  Pallas kernels  57.3 us (30%)
  starting transfers between devices  33.3 us (17%)
  local copies, waits for them, and re-layouts  18.9 us (10%)
  other arithmetic  2.25 us (1%)
    ppermute x9, waiting for transfers between devices, passed_along(): lax.ppermute(value, axis, [(source, source + steps) for source in range(i...  28.9 us
    ppermute x4, waiting for transfers between devices, gathered(): lax.ppermute(value, 'ctx', [(c, (c + 2) % count) for c in range(count)])  28 us
    ppermute x9, starting transfers between devices, passed_along(): lax.ppermute(value, axis, [(source, source + steps) for source in range(i...  17.6 us
    ppermute x5, waiting for transfers between devices, gathered(): lax.ppermute(value, 'ctx', [(c, c ^ 1) for c in range(count)])  17.6 us
    pallas_call x2, Pallas kernels, attention_grad(): pl.pallas_call(functools.partial(attention_grad_kernel, scale, steps, las...  13.6 us
    pallas_call x1, Pallas kernels, attention(): pl.pallas_call(functools.partial(attention_kernel, scale), grid_spec=pltp...  11 us
    unnamed x53, local copies, waits for them, and re-layouts  10.5 us
    pallas_call x1, Pallas kernels, dattention(): pl.pallas_call(functools.partial(dattn_kernel, plan, len(arrays)), grid_s...  8.67 us
  transfers between devices with their start and end apart: 27, of which 14 were waited for; matrix products, arithmetic and copies ran while one was open for 3% of the time, Pallas kernels for 18%

profile of v5, /device:TPU:4, one launch (start us, length us, event | category | flops | bytes accessed | tf_op | source)
XLA Modules:
  0.0 191.0 jit_solution(13833899257991343789)
XLA Ops:
  0.7 1.9 %constant_dynamic-slice_fusion.2 = bf16[6,16,3072]{2,1,0:T(8,128)(2,1)} fusion(bf16[12,16,3072]{2,1,0:T(8,128)(2,1)} %refs_0_.1, s32[]{:T(128)S(6)} %select_n.48), kind=kLoop, calls=%fused_computation.25 | loop fusion | bytes 1179652 | tf_op jit(solution)/shard_map/dynamic_slice | solution.py:64
  2.6 1.6 collective-permute-start
  9.0 10.7 %collective-permute-done.refs_2_.refs_1_ = bf16[6,16,3072]{2,1,0:T(8,128)(2,1)S(1)} collective-permute-done((bf16[6,16,3072]{2,1,0:T(8,128)(2,1)}, bf16[6,16,3072]{2,1,0:T(8,128)(2,1)S(1)}, u32[]{:S(2)}, u32[]{:S(2)}) %collective-permute-start) | collective-permute-done | bytes 589856 | tf_op jit(solution)/shard_map/ppermute | solution.py:61
  19.7 3.5 %constant_dynamic-slice_fusion = (bf16[4,1,64,3072]{3,2,1,0:T(8,128)(2,1)S(1)}, bf16[4,1,64,3072]{3,2,1,0:T(8,128)(2,1)}) fusion(bf16[4,2,64,3072]{3,2,1,0:T(8,128)(2,1)} %bitcast.39, s32[]{:T(128)S(6)} %select_n.51, s32[]{:T(128)S(6)} %select_n.50), kind=kLoop, calls=%fused_computation.23 | loop fusion | bytes 6291464 | tf_op jit(solution)/shard_map/jit(dynamic_index_in_dim)/dynamic_slice | solution.py:553
  23.7 1.5 collective-permute-start.7
  25.3 1.5 collective-permute-start.6
  26.7 12.8 %collective-permute-done.2.refs_5_.refs_4_ = bf16[6,16,3072]{2,1,0:T(8,128)(2,1)S(1)} collective-permute-done((bf16[6,16,3072]{2,1,0:T(8,128)(2,1)}, bf16[6,16,3072]{2,1,0:T(8,128)(2,1)S(1)}, u32[]{:S(2)}, u32[]{:S(2)}) %collective-permute-start.2) | collective-permute-done | bytes 589856 | tf_op jit(solution)/shard_map/ppermute | solution.py:62
  42.9 1.5 collective-permute-start.4
  45.9 4.9 %pick.1 = (bf16[128,3072]{1,0:T(8,128)(2,1)}, bf16[128,3072]{1,0:T(8,128)(2,1)}, f32[128,128]{1,0:T(8,128)}) custom-call(s32[128,2]{1,0:T(8,128)} %copy.31.slots, bf16[256,3072]{1,0:T(8,128)(2,1)} %bitcast.35, bf16[256,3072]{1,0:T(8,128)(2,1)} %copy-done.13, bf16[128,3072]{1,0:T(8,128)(2,1)} %gout.5), custom_call_target="tpu_custom_call" | custom-call | flops 805306368 | bytes 6291456 | tf_op jit(solution)/shard_map/pick/pallas_call | solution.py:420
  52.2 6.5 %collective-permute-done.5.refs_4_.refs_3_ = bf16[6,16,3072]{2,1,0:T(8,128)(2,1)} collective-permute-done((bf16[6,16,3072]{2,1,0:T(8,128)(2,1)S(1)}, bf16[6,16,3072]{2,1,0:T(8,128)(2,1)}, u32[]{:S(2)}, u32[]{:S(2)}) %collective-permute-start.5) | collective-permute-done | bytes 589856 | tf_op jit(solution)/shard_map/ppermute | solution.py:61
  58.7 1.5 collective-permute-start.10
  60.2 1.5 collective-permute-start.14
  61.8 3.2 %collective-permute-done.4.refs_7_.refs_6_ = bf16[6,16,3072]{2,1,0:T(8,128)(2,1)} collective-permute-done((bf16[6,16,3072]{2,1,0:T(8,128)(2,1)S(1)}, bf16[6,16,3072]{2,1,0:T(8,128)(2,1)}, u32[]{:S(2)}, u32[]{:S(2)}) %collective-permute-start.4) | collective-permute-done | bytes 589856 | tf_op jit(solution)/shard_map/ppermute | solution.py:62
  64.9 9.3 %collective-permute-done.8.refs_10_.refs_9_ = bf16[6,16,3072]{2,1,0:T(8,128)(2,1)S(1)} collective-permute-done((bf16[6,16,3072]{2,1,0:T(8,128)(2,1)S(1)}, bf16[6,16,3072]{2,1,0:T(8,128)(2,1)S(1)}, u32[]{:S(2)}, u32[]{:S(2)}) %collective-permute-start.8) | collective-permute-done | bytes 589856 | tf_op jit(solution)/shard_map/ppermute | solution.py:61
  75.1 1.9 collective-permute-start.13
  77.2 1.9 collective-permute-start.15
  82.4 3.8 %collective-permute-done.13.refs_2_.refs_6_ = bf16[256,512]{1,0:T(8,128)(2,1)S(1)} collective-permute-done((bf16[256,512]{1,0:T(8,128)(2,1)S(1)}, bf16[256,512]{1,0:T(8,128)(2,1)S(1)}, u32[]{:S(2)}, u32[]{:S(2)}) %collective-permute-start.13) | collective-permute-done | bytes 262176 | tf_op jit(solution)/shard_map/ppermute | solution.py:39
  86.2 3.4 %collective-permute-start.11 = (bf16[256,512]{1,0:T(8,128)(2,1)S(1)}, bf16[256,512]{1,0:T(8,128)(2,1)S(1)}, u32[]{:S(2)}, u32[]{:S(2)}) collective-permute-start(bf16[256,512]{1,0:T(8,128)(2,1)S(1)} %bitcast_dynamic-update-slice_fusion.refs_3_.refs_7_), channel_id=1, source_target_pairs={{0,6},{2,8},{4,10},{6,12},{8,14},{1,7},{3,9},{5,11},{7,13},{9,15},... | collective-permute-start | bytes 786440 | tf_op jit(solution)/shard_map/ppermute | solution.py:39
  90.3 4.0 %collective-permute-done.11.refs_0_.refs_4_ = bf16[256,512]{1,0:T(8,128)(2,1)S(1)} collective-permute-done((bf16[256,512]{1,0:T(8,128)(2,1)S(1)}, bf16[256,512]{1,0:T(8,128)(2,1)S(1)}, u32[]{:S(2)}, u32[]{:S(2)}) %collective-permute-start.11) | collective-permute-done | bytes 262176 | tf_op jit(solution)/shard_map/ppermute | solution.py:39
  95.0 11.0 %attention.1 = (bf16[256,1536]{1,0:T(8,128)(2,1)}, bf16[12,256,1024]{2,1,0:T(8,128)(2,1)}) custom-call(s32[1]{0:T(128)} %bitcast.11.place, bf16[12,256,128]{2,1,0:T(8,128)(2,1)} %bitcast.36, bf16[256,512]{1,0:T(8,128)(2,1)} %copy-done.3, bf16[256,512]{1,0:T(8,128)(2,1)} %copy-done.2, bf16[256,512]{1,0:T(8,128)(2,1)} %copy-done.1, bf16[256,512]{1,0:T(8,128)(2,1)} %copy-done, ...), custom_call_target="tpu_custom_call" | custom-call | flops 1610612736 | bytes 6291456 | tf_op jit(solution)/shard_map/attention/pallas_call | solution.py:268
  106.8 8.4 %project.1 = (f32[128,3072]{1,0:T(8,128)}, f32[128,3072]{1,0:T(8,128)}) custom-call(s32[11]{0:T(128)} %stack.61.table, s32[1]{0:T(128)} %bitcast.10.core.refs_9_, bf16[256,1536]{1,0:T(8,128)(2,1)} %get-tuple-element.60.refs_0_.attn, bf16[12,16,3072]{2,1,0:T(8,128)(2,1)} %refs_0_.1, bf16[6,16,3072]{2,1,0:T(8,128)(2,1)} %copy-done.4, ...), custom_call_target="tpu_custom_call" | custom-call | flops 2415919104 | bytes 9437184 | tf_op jit(solution)/shard_map/project/pallas_call | solution.py:147
  115.3 3.6 %collective-permute-done.18.recv = f32[128,3072]{1,0:T(8,128)S(1)} collective-permute-done((f32[128,3072]{1,0:T(8,128)}, f32[128,3072]{1,0:T(8,128)S(1)}, u32[]{:S(2)}, u32[]{:S(2)}) %collective-permute-start.18) | collective-permute-done | bytes 1572896 | tf_op jit(solution)/shard_map/ppermute | solution.py:43
  120.2 6.3 %middle.1 = (bf16[128,3072]{1,0:T(8,128)(2,1)}, bf16[128,3072]{1,0:T(8,128)(2,1)}, f32[128,128]{1,0:T(8,128)}) custom-call(s32[128,2]{1,0:T(8,128)} %copy-done.17, f32[128,3072]{1,0:T(8,128)} %get-tuple-element.64.own, f32[128,3072]{1,0:T(8,128)} %copy-done.15, bf16[128,3072]{1,0:T(8,128)(2,1)} %stream.1, bf16[128,3072]{1,0:T(8,128)(2,1)} %get-tuple-element.66.first, ...), custom_call_target="tpu_custom_call" | custom-call | flops 402653184 | bytes 7864320 | tf_op jit(solution)/shard_map/middle/pallas_call | solution.py:473
  126.7 4.5 %spread.1 = (bf16[256,3072]{1,0:T(8,128)(2,1)}, bf16[256,3072]{1,0:T(8,128)(2,1)}) custom-call(s32[2,128]{1,0:T(2,128)} %bitcast.47, f32[128,128]{1,0:T(8,128)} %get-tuple-element.72.gates, bf16[128,3072]{1,0:T(8,128)(2,1)} %gout.5), custom_call_target="tpu_custom_call" | custom-call | flops 805306368 | bytes 3932160 | tf_op jit(solution)/shard_map/spread/pallas_call | solution.py:503
  132.0 8.7 %dattention.1.dout = bf16[256,1536]{1,0:T(8,128)(2,1)} custom-call(s32[11]{0:T(128)} %stack.61.table, s32[1]{0:T(128)} %bitcast.10.core.refs_9_, bf16[128,3072]{1,0:T(8,128)(2,1)} %get-tuple-element.105.own, bf16[128,3072]{1,0:T(8,128)(2,1)} %copy-done.16, bf16[12,16,3072]{2,1,0:T(8,128)(2,1)} %refs_0_.1, bf16[6,16,3072]{2,1,0:T(8,128)(2,1)} %copy-done.4, ...), custom_call_target="tpu_custom_call" | custom-call | flops 2415919104 | bytes 9437184 | tf_op jit(solution)/shard_map/dattention/pallas_call | solution.py:203
  141.1 6.5 %attention_grad.2 = (bf16[12,256,128]{2,1,0:T(8,128)(2,1)}, bf16[256,256]{1,0:T(8,128)(2,1)}, bf16[256,256]{1,0:T(8,128)(2,1)}, bf16[256,256]{1,0:T(8,128)(2,1)}, f32[256,256]{1,0:T(8,128)}) custom-call(bf16[12,256,128]{2,1,0:T(8,128)(2,1)} %bitcast.37, bf16[256,1536]{1,0:T(8,128)(2,1)} %dattention.1.dout, bf16[256,1536]{1,0:T(8,128)(2,1)} %get-tuple-element.60.refs_0_.attn, ...), custom_call_target="tpu_custom_call" | custom-call | flops 256 | bytes 256 | tf_op jit(solution)/shard_map/attention_grad/pallas_call | solution.py:369
  147.7 3.9 %collective-permute-start.21 = (bf16[256,256]{1,0:T(8,128)(2,1)}, bf16[256,256]{1,0:T(8,128)(2,1)S(1)}, u32[]{:S(2)}, u32[]{:S(2)}) collective-permute-start(bf16[256,256]{1,0:T(8,128)(2,1)} %get-tuple-element.79), channel_id=1, source_target_pairs={{2,0},{4,2},{6,4},{8,6},{10,8},{12,10},{14,12},{3,1},{5,3},{7,5},{... | collective-permute-start | bytes 393224 | tf_op jit(solution)/shard_map/ppermute | solution.py:39
  155.4 7.1 %attention_grad.3 = (bf16[12,256,128]{2,1,0:T(8,128)(2,1)}, bf16[256,256]{1,0:T(8,128)(2,1)}, bf16[256,256]{1,0:T(8,128)(2,1)}, bf16[256,256]{1,0:T(8,128)(2,1)}...) custom-call(bf16[12,256,128]{2,1,0:T(8,128)(2,1)} %bitcast.38, ...), custom_call_target="tpu_custom_call", output_to_operand_aliasing={{0}: (12, {})} | custom-call | flops 256 | bytes 256 | tf_op jit(solution)/shard_map/attention_grad/pallas_call | solution.py:369
  162.5 1.9 %collective-permute-start.24 = (bf16[256,256]{1,0:T(8,128)(2,1)}, bf16[256,256]{1,0:T(8,128)(2,1)S(1)}, u32[]{:S(2)}, u32[]{:S(2)}) collective-permute-start(bf16[256,256]{1,0:T(8,128)(2,1)} %get-tuple-element.82), channel_id=1, source_target_pairs={{2,0},{4,2},{6,4},{8,6},{10,8},{12,10},{14,12},{3,1},{5,3},{7,5},{... | collective-permute-start | bytes 393224 | tf_op jit(solution)/shard_map/ppermute | solution.py:39
  167.0 7.2 %collective-permute-done.23 = bf16[256,256]{1,0:T(8,128)(2,1)S(1)} collective-permute-done((bf16[256,256]{1,0:T(8,128)(2,1)}, bf16[256,256]{1,0:T(8,128)(2,1)S(1)}, u32[]{:S(2)}, u32[]{:S(2)}) %collective-permute-start.23) | collective-permute-done | bytes 131104 | tf_op jit(solution)/shard_map/ppermute | solution.py:39
  174.3 5.9 %collective-permute-done.25 = bf16[256,256]{1,0:T(8,128)(2,1)S(1)} collective-permute-done((bf16[256,256]{1,0:T(8,128)(2,1)}, bf16[256,256]{1,0:T(8,128)(2,1)S(1)}, u32[]{:S(2)}, u32[]{:S(2)}) %collective-permute-start.25) | collective-permute-done | bytes 131104 | tf_op jit(solution)/shard_map/ppermute | solution.py:39
  180.1 8.1 %collective-permute-done.26 = bf16[256,256]{1,0:T(8,128)(2,1)S(1)} collective-permute-done((bf16[256,256]{1,0:T(8,128)(2,1)}, bf16[256,256]{1,0:T(8,128)(2,1)S(1)}, u32[]{:S(2)}, u32[]{:S(2)}) %collective-permute-start.26) | collective-permute-done | bytes 131104 | tf_op jit(solution)/shard_map/ppermute | solution.py:39
  (100 shorter events, 29.9 us)
Async XLA Ops:
  2.6 17.1 %collective-permute-start = (bf16[6,16,3072]{2,1,0:T(8,128)(2,1)}, bf16[6,16,3072]{2,1,0:T(8,128)(2,1)S(1)}, u32[]{:S(2)}, u32[]{:S(2)}) collective-permute-start(bf16[6,16,3072]{2,1,0:T(8,128)(2,1)} %constant_dynamic-slice_fusion.2), channel_id=1, source_target_pairs={{0,4},{2,6},{4,8},{6,10},{8,12},{10,14},{12,0},{14,2},{1,5},{3,7},... | collective-permute-start | bytes 1769480 | tf_op jit(solution)/shard_map/ppermute | solution.py:61
  6.5 35.7 %copy-start.22 = (s32[128,2]{0,1:T(2,128)}, s32[128,2]{0,1:T(2,128)S(1)}, u32[]{:S(2)}) copy-start(s32[128,2]{0,1:T(2,128)S(1)} %and_select_fusion) | copy-start | bytes 3076
  8.0 78.2 %copy-start = (bf16[256,512]{1,0:T(8,128)(2,1)}, bf16[256,512]{1,0:T(8,128)(2,1)S(1)}, u32[]{:S(2)}) copy-start(bf16[256,512]{1,0:T(8,128)(2,1)S(1)} %bitcast_dynamic-update-slice_fusion.refs_3_.refs_7_) | copy-start | bytes 786436
  23.2 17.8 %collective-permute-start.3 = (bf16[256,3072]{1,0:T(8,128)(2,1)S(1)}, bf16[256,3072]{1,0:T(8,128)(2,1)S(1)}, u32[]{:S(2)}, u32[]{:S(2)}) collective-permute-start(bf16[256,3072]{1,0:T(8,128)(2,1)S(1)} %bitcast.42), channel_id=1, source_target_pairs={{0,1},{1,0},{2,3},{3,2},{4,5},{5,4},{6,7},{7,6},{8,9},{9,8},{10,11... | collective-permute-start | bytes 4718600 | tf_op jit(solution)/shard_map/ppermute | solution.py:43
  23.2 16.3 %collective-permute-start.2 = (bf16[6,16,3072]{2,1,0:T(8,128)(2,1)}, bf16[6,16,3072]{2,1,0:T(8,128)(2,1)S(1)}, u32[]{:S(2)}, u32[]{:S(2)}) collective-permute-start(bf16[6,16,3072]{2,1,0:T(8,128)(2,1)} %constant_dynamic-slice_fusion.2), channel_id=1, source_target_pairs={{0,2},{2,0},{4,6},{6,4},{8,10},{10,8},{12,14},{14,12},{1,3},{3,1},... | collective-permute-start | bytes 1769480 | tf_op jit(solution)/shard_map/ppermute | solution.py:62
  23.7 17.3 %collective-permute-start.1 = (bf16[6,16,3072]{2,1,0:T(8,128)(2,1)S(1)}, bf16[6,16,3072]{2,1,0:T(8,128)(2,1)S(1)}, u32[]{:S(2)}, u32[]{:S(2)}) collective-permute-start(bf16[6,16,3072]{2,1,0:T(8,128)(2,1)S(1)} %collective-permute-done.refs_2_.refs_1_), channel_id=1, source_target_pairs={{0,4},{2,6},{4,8},{6,10},{8,12},{10,14},{12,0},{14,2},{1,5},{3,7},... | collective-permute-start | bytes 1769480 | tf_op jit(solution)/shard_map/ppermute | solution.py:61
  23.7 28.5 %collective-permute-start.7 = (bf16[6,16,3072]{2,1,0:T(8,128)(2,1)S(1)}, bf16[6,16,3072]{2,1,0:T(8,128)(2,1)S(1)}, u32[]{:S(2)}, u32[]{:S(2)}) collective-permute-start(bf16[6,16,3072]{2,1,0:T(8,128)(2,1)S(1)} %collective-permute-done.refs_2_.refs_1_), channel_id=1, source_target_pairs={{0,2},{2,0},{4,6},{6,4},{8,10},{10,8},{12,14},{14,12},{1,3},{3,1},... | collective-permute-start | bytes 1769480 | tf_op jit(solution)/shard_map/ppermute | solution.py:62
  25.3 26.9 %collective-permute-start.6 = (bf16[6,16,3072]{2,1,0:T(8,128)(2,1)S(1)}, bf16[6,16,3072]{2,1,0:T(8,128)(2,1)S(1)}, u32[]{:S(2)}, u32[]{:S(2)}) collective-permute-start(bf16[6,16,3072]{2,1,0:T(8,128)(2,1)S(1)} %collective-permute-done.refs_2_.refs_1_), channel_id=1, source_target_pairs={{0,16},{16,0},{1,17},{17,1},{2,18},{18,2},{3,19},{19,3},{4,20},{20... | collective-permute-start | bytes 1769480 | tf_op jit(solution)/shard_map/ppermute | solution.py:43
  42.2 16.5 %collective-permute-start.5 = (bf16[6,16,3072]{2,1,0:T(8,128)(2,1)S(1)}, bf16[6,16,3072]{2,1,0:T(8,128)(2,1)}, u32[]{:S(2)}, u32[]{:S(2)}) collective-permute-start(bf16[6,16,3072]{2,1,0:T(8,128)(2,1)S(1)} %collective-permute-done.1.refs_3_.refs_2_), channel_id=1, source_target_pairs={{0,4},{2,6},{4,8},{6,10},{8,12},{10,14},{12,0},{14,2},{1,5},{3,7},... | collective-permute-start | bytes 1769480 | tf_op jit(solution)/shard_map/ppermute | solution.py:61
  42.9 22.0 %collective-permute-start.4 = (bf16[6,16,3072]{2,1,0:T(8,128)(2,1)S(1)}, bf16[6,16,3072]{2,1,0:T(8,128)(2,1)}, u32[]{:S(2)}, u32[]{:S(2)}) collective-permute-start(bf16[6,16,3072]{2,1,0:T(8,128)(2,1)S(1)} %collective-permute-done.1.refs_3_.refs_2_), channel_id=1, source_target_pairs={{0,2},{2,0},{4,6},{6,4},{8,10},{10,8},{12,14},{14,12},{1,3},{3,1},... | collective-permute-start | bytes 1769480 | tf_op jit(solution)/shard_map/ppermute | solution.py:62
  44.5 17.3 %collective-permute-start.9 = (bf16[6,16,3072]{2,1,0:T(8,128)(2,1)S(1)}, bf16[6,16,3072]{2,1,0:T(8,128)(2,1)S(1)}, u32[]{:S(2)}, u32[]{:S(2)}) collective-permute-start(bf16[6,16,3072]{2,1,0:T(8,128)(2,1)S(1)} %collective-permute-done.2.refs_5_.refs_4_), channel_id=1, source_target_pairs={{0,16},{16,0},{1,17},{17,1},{2,18},{18,2},{3,19},{19,3},{4,20},{20... | collective-permute-start | bytes 1769480 | tf_op jit(solution)/shard_map/ppermute | solution.py:43
  52.2 53.8 %copy-start.7 = (bf16[6,16,3072]{2,1,0:T(8,128)(2,1)}, bf16[6,16,3072]{2,1,0:T(8,128)(2,1)S(1)}, u32[]{:S(2)}) copy-start(bf16[6,16,3072]{2,1,0:T(8,128)(2,1)S(1)} %collective-permute-done.7.refs_6_.refs_5_) | copy-start | bytes 1769476
  52.2 53.8 %copy-start.8 = (bf16[6,16,3072]{2,1,0:T(8,128)(2,1)}, bf16[6,16,3072]{2,1,0:T(8,128)(2,1)S(1)}, u32[]{:S(2)}) copy-start(bf16[6,16,3072]{2,1,0:T(8,128)(2,1)S(1)} %collective-permute-done.6.refs_9_.refs_8_) | copy-start | bytes 1769476
  58.7 15.5 %collective-permute-start.8 = (bf16[6,16,3072]{2,1,0:T(8,128)(2,1)S(1)}, bf16[6,16,3072]{2,1,0:T(8,128)(2,1)S(1)}, u32[]{:S(2)}, u32[]{:S(2)}) collective-permute-start(bf16[6,16,3072]{2,1,0:T(8,128)(2,1)S(1)} %collective-permute-done.6.refs_9_.refs_8_), channel_id=1, source_target_pairs={{0,4},{2,6},{4,8},{6,10},{8,12},{10,14},{12,0},{14,2},{1,5},{3,7},... | collective-permute-start | bytes 1769480 | tf_op jit(solution)/shard_map/ppermute | solution.py:61
  58.7 16.3 %collective-permute-start.10 = (bf16[6,16,3072]{2,1,0:T(8,128)(2,1)}, bf16[6,16,3072]{2,1,0:T(8,128)(2,1)S(1)}, u32[]{:S(2)}, u32[]{:S(2)}) collective-permute-start(bf16[6,16,3072]{2,1,0:T(8,128)(2,1)} %collective-permute-done.5.refs_4_.refs_3_), channel_id=1, source_target_pairs={{0,16},{16,0},{1,17},{17,1},{2,18},{18,2},{3,19},{19,3},{4,20},{20... | collective-permute-start | bytes 1769480 | tf_op jit(solution)/shard_map/ppermute | solution.py:43
  60.2 17.0 %collective-permute-start.14 = (bf16[6,16,3072]{2,1,0:T(8,128)(2,1)}, bf16[6,16,3072]{2,1,0:T(8,128)(2,1)}, u32[]{:S(2)}, u32[]{:S(2)}) collective-permute-start(bf16[6,16,3072]{2,1,0:T(8,128)(2,1)} %collective-permute-done.5.refs_4_.refs_3_), channel_id=1, source_target_pairs={{0,2},{2,0},{4,6},{6,4},{8,10},{10,8},{12,14},{14,12},{1,3},{3,1},... | collective-permute-start | bytes 1769480 | tf_op jit(solution)/shard_map/ppermute | solution.py:62
  75.1 11.1 %collective-permute-start.13 = (bf16[256,512]{1,0:T(8,128)(2,1)S(1)}, bf16[256,512]{1,0:T(8,128)(2,1)S(1)}, u32[]{:S(2)}, u32[]{:S(2)}) collective-permute-start(bf16[256,512]{1,0:T(8,128)(2,1)S(1)} %bitcast_dynamic-update-slice_fusion.refs_3_.refs_7_), channel_id=1, source_target_pairs={{0,2},{2,4},{4,6},{6,8},{8,10},{10,12},{12,14},{1,3},{3,5},{5,7},{... | collective-permute-start | bytes 786440 | tf_op jit(solution)/shard_map/ppermute | solution.py:39
  77.2 28.8 %collective-permute-start.15 = (bf16[6,16,3072]{2,1,0:T(8,128)(2,1)S(1)}, bf16[6,16,3072]{2,1,0:T(8,128)(2,1)S(1)}, u32[]{:S(2)}, u32[]{:S(2)}) collective-permute-start(bf16[6,16,3072]{2,1,0:T(8,128)(2,1)S(1)} %collective-permute-done.6.refs_9_.refs_8_), channel_id=1, source_target_pairs={{0,2},{2,0},{4,6},{6,4},{8,10},{10,8},{12,14},{14,12},{1,3},{3,1},... | collective-permute-start | bytes 1769480 | tf_op jit(solution)/shard_map/ppermute | solution.py:62
  79.1 26.9 %collective-permute-start.17 = (bf16[6,16,3072]{2,1,0:T(8,128)(2,1)}, bf16[6,16,3072]{2,1,0:T(8,128)(2,1)}, u32[]{:S(2)}, u32[]{:S(2)}) collective-permute-start(bf16[6,16,3072]{2,1,0:T(8,128)(2,1)} %collective-permute-done.14.refs_8_.refs_7_), channel_id=1, source_target_pairs={{0,16},{16,0},{1,17},{17,1},{2,18},{18,2},{3,19},{19,3},{4,20},{20... | collective-permute-start | bytes 1769480 | tf_op jit(solution)/shard_map/ppermute | solution.py:43
  80.6 25.4 %collective-permute-start.16 = (bf16[6,16,3072]{2,1,0:T(8,128)(2,1)}, bf16[6,16,3072]{2,1,0:T(8,128)(2,1)}, u32[]{:S(2)}, u32[]{:S(2)}) collective-permute-start(bf16[6,16,3072]{2,1,0:T(8,128)(2,1)} %collective-permute-done.4.refs_7_.refs_6_), channel_id=1, source_target_pairs={{0,16},{16,0},{1,17},{17,1},{2,18},{18,2},{3,19},{19,3},{4,20},{20... | collective-permute-start | bytes 1769480 | tf_op jit(solution)/shard_map/ppermute | solution.py:43
  81.1 9.2 %collective-permute-start.12 = (bf16[256,512]{1,0:T(8,128)(2,1)S(1)}, bf16[256,512]{1,0:T(8,128)(2,1)S(1)}, u32[]{:S(2)}, u32[]{:S(2)}) collective-permute-start(bf16[256,512]{1,0:T(8,128)(2,1)S(1)} %bitcast_dynamic-update-slice_fusion.refs_3_.refs_7_), channel_id=1, source_target_pairs={{0,4},{2,6},{4,8},{6,10},{8,12},{10,14},{1,5},{3,7},{5,9},{7,11},{... | collective-permute-start | bytes 786440 | tf_op jit(solution)/shard_map/ppermute | solution.py:39
  86.2 8.1 %collective-permute-start.11 = (bf16[256,512]{1,0:T(8,128)(2,1)S(1)}, bf16[256,512]{1,0:T(8,128)(2,1)S(1)}, u32[]{:S(2)}, u32[]{:S(2)}) collective-permute-start(bf16[256,512]{1,0:T(8,128)(2,1)S(1)} %bitcast_dynamic-update-slice_fusion.refs_3_.refs_7_), channel_id=1, source_target_pairs={{0,6},{2,8},{4,10},{6,12},{8,14},{1,7},{3,9},{5,11},{7,13},{9,15},... | collective-permute-start | bytes 786440 | tf_op jit(solution)/shard_map/ppermute | solution.py:39
  115.3 3.7 %collective-permute-start.18 = (f32[128,3072]{1,0:T(8,128)}, f32[128,3072]{1,0:T(8,128)S(1)}, u32[]{:S(2)}, u32[]{:S(2)}) collective-permute-start(f32[128,3072]{1,0:T(8,128)} %get-tuple-element.65), channel_id=1, source_target_pairs={{0,1},{1,0},{2,3},{3,2},{4,5},{5,4},{6,7},{7,6},{8,9},{9,8},{10,11... | collective-permute-start | bytes 4718600 | tf_op jit(solution)/shard_map/ppermute | solution.py:43
  126.5 4.7 %collective-permute-start.19 = (bf16[128,3072]{1,0:T(8,128)(2,1)}, bf16[128,3072]{1,0:T(8,128)(2,1)S(1)}, u32[]{:S(2)}, u32[]{:S(2)}) collective-permute-start(bf16[128,3072]{1,0:T(8,128)(2,1)} %get-tuple-element.105.own), channel_id=1, source_target_pairs={{0,1},{1,0},{2,3},{3,2},{4,5},{5,4},{6,7},{7,6},{8,9},{9,8},{10,11... | collective-permute-start | bytes 2359304 | tf_op jit(solution)/shard_map/ppermute | solution.py:43
  140.7 13.5 %collective-permute-start.20 = (bf16[256,3072]{1,0:T(8,128)(2,1)S(1)}, bf16[256,3072]{1,0:T(8,128)(2,1)S(1)}, u32[]{:S(2)}, u32[]{:S(2)}) collective-permute-start(bf16[256,3072]{1,0:T(8,128)(2,1)S(1)} %copy-done.23), channel_id=1, source_target_pairs={{0,1},{1,0},{2,3},{3,2},{4,5},{5,4},{6,7},{7,6},{8,9},{9,8},{10,11... | collective-permute-start | bytes 4718600 | tf_op jit(solution)/shard_map/ppermute | solution.py:43
  147.7 18.0 %collective-permute-start.21 = (bf16[256,256]{1,0:T(8,128)(2,1)}, bf16[256,256]{1,0:T(8,128)(2,1)S(1)}, u32[]{:S(2)}, u32[]{:S(2)}) collective-permute-start(bf16[256,256]{1,0:T(8,128)(2,1)} %get-tuple-element.79), channel_id=1, source_target_pairs={{2,0},{4,2},{6,4},{8,6},{10,8},{12,10},{14,12},{3,1},{5,3},{7,5},{... | collective-permute-start | bytes 393224 | tf_op jit(solution)/shard_map/ppermute | solution.py:39
  151.6 15.4 %collective-permute-start.22 = (bf16[256,256]{1,0:T(8,128)(2,1)}, bf16[256,256]{1,0:T(8,128)(2,1)S(1)}, u32[]{:S(2)}, u32[]{:S(2)}) collective-permute-start(bf16[256,256]{1,0:T(8,128)(2,1)} %get-tuple-element.80), channel_id=1, source_target_pairs={{4,0},{6,2},{8,4},{10,6},{12,8},{14,10},{5,1},{7,3},{9,5},{11,7},{... | collective-permute-start | bytes 393224 | tf_op jit(solution)/shard_map/ppermute | solution.py:39
  152.9 21.4 %collective-permute-start.23 = (bf16[256,256]{1,0:T(8,128)(2,1)}, bf16[256,256]{1,0:T(8,128)(2,1)S(1)}, u32[]{:S(2)}, u32[]{:S(2)}) collective-permute-start(bf16[256,256]{1,0:T(8,128)(2,1)} %get-tuple-element.81), channel_id=1, source_target_pairs={{6,0},{8,2},{10,4},{12,6},{14,8},{7,1},{9,3},{11,5},{13,7},{15,9},... | collective-permute-start | bytes 393224 | tf_op jit(solution)/shard_map/ppermute | solution.py:39
  155.4 32.8 %copy-start.18 = (f32[256,256]{1,0:T(8,128)S(1)}, f32[256,256]{1,0:T(8,128)}, u32[]{:S(2)}) copy-start(f32[256,256]{1,0:T(8,128)} %get-tuple-element.78) | copy-start | bytes 786436
  162.5 11.8 %collective-permute-start.24 = (bf16[256,256]{1,0:T(8,128)(2,1)}, bf16[256,256]{1,0:T(8,128)(2,1)S(1)}, u32[]{:S(2)}, u32[]{:S(2)}) collective-permute-start(bf16[256,256]{1,0:T(8,128)(2,1)} %get-tuple-element.82), channel_id=1, source_target_pairs={{2,0},{4,2},{6,4},{8,6},{10,8},{12,10},{14,12},{3,1},{5,3},{7,5},{... | collective-permute-start | bytes 393224 | tf_op jit(solution)/shard_map/ppermute | solution.py:39
  164.4 15.7 %collective-permute-start.25 = (bf16[256,256]{1,0:T(8,128)(2,1)}, bf16[256,256]{1,0:T(8,128)(2,1)S(1)}, u32[]{:S(2)}, u32[]{:S(2)}) collective-permute-start(bf16[256,256]{1,0:T(8,128)(2,1)} %get-tuple-element.83), channel_id=1, source_target_pairs={{4,0},{6,2},{8,4},{10,6},{12,8},{14,10},{5,1},{7,3},{9,5},{11,7},{... | collective-permute-start | bytes 393224 | tf_op jit(solution)/shard_map/ppermute | solution.py:39
  165.7 22.5 %collective-permute-start.26 = (bf16[256,256]{1,0:T(8,128)(2,1)}, bf16[256,256]{1,0:T(8,128)(2,1)S(1)}, u32[]{:S(2)}, u32[]{:S(2)}) collective-permute-start(bf16[256,256]{1,0:T(8,128)(2,1)} %get-tuple-element.84), channel_id=1, source_target_pairs={{6,0},{8,2},{10,4},{12,6},{14,8},{7,1},{9,3},{11,5},{13,7},{15,9},... | collective-permute-start | bytes 393224 | tf_op jit(solution)/shard_map/ppermute | solution.py:39
  (19 other events, 110.9 us)

commit v6 on v5

--- a/solution.py
+++ b/solution.py
@@ -41,6 +41,19 @@
 
 def swapped(value, axis):
     return lax.ppermute(value, axis, [(0, 1), (1, 0)])
+
+
+def exchanged(one, three):
+    count = lax.axis_size("ctx")
+    pairs = [(c, c ^ 1) for c in range(count)]
+    others = [(c, c - 1 if c % 2 else c - 3) for c in range(count) if c % 2 or c >= 4]
+    return lax.ppermute(one, "ctx", pairs), lax.ppermute(three, "ctx", others)
+
+
+def combined(two, by_one, by_three):
+    even = lax.axis_index("ctx") % 2 == 0
+    onward = (two.astype(F32) + jnp.where(even, by_three, by_one).astype(F32)).astype(BF16)
+    return passed_along(onward, "ctx", -2), jnp.where(even, by_one, by_three)
 
 
 def after(values, *others):
@@ -64,7 +77,7 @@
     mine = lax.dynamic_slice_in_dim(w_out, side * half, half, 0)
 
     z1, y0 = ring(mine), pair(mine)
-    (z1,) = after([z1], *tasks[0]())
+    z1, y0 = after([z1, y0], *tasks[0]())
     z2, y1, x1 = ring(z1), pair(z1), cross(z1)
     z2, y0 = after([z2, y0], *tasks[1](z1))
     z3, y2, x2 = ring(z2), pair(z2), cross(y0)
@@ -133,12 +146,12 @@
     @pl.when(core[0] == 0)
     def _():
         own[...] = result[:rows]
-        other[...] = result[rows:]
+        other[...] = result[rows:].astype(BF16)
 
     @pl.when(core[0] != 0)
     def _():
         own[...] = result[rows:]
-        other[...] = result[:rows]
+        other[...] = result[:rows].astype(BF16)
 
 
 def project(attn, arrays, table, plan, core, heads, head_dim, width, rows):
@@ -157,7 +170,7 @@
                 pltpu.SemaphoreType.DMA((len(plan), CHUNKS)),
             ],
         ),
-        out_shape=[jax.ShapeDtypeStruct((rows, width), F32)] * 2,
+        out_shape=[jax.ShapeDtypeStruct((rows, width), F32), jax.ShapeDtypeStruct((rows, width), BF16)],
         compiler_params=params(),
         cost_estimate=cost(2 * tok * heads * head_dim * width, 2 * heads * head_dim * width),
         name="project",
@@ -387,17 +400,19 @@
     )(queries, dout, attn, probs, *bands, *bands, *given)
 
 
-def pick_kernel(slots, here, there, gout, first, second, dgate):
+def pick_kernel(core, slots, here_ref, there_ref, gout, first, second, dgate):
     step = pl.program_id(0)
     rows, width = gout.shape
-    room = here.shape[0]
+    held, capacity, size = here_ref.shape
+    room = held * capacity
+    here, there = (r[...].reshape(room, size) for r in (here_ref, there_ref))
     column = lax.broadcasted_iota(jnp.int32, (rows, room), 1)
     grad = gout[...].astype(F32)
     sums = []
     for i, out in enumerate((first, second)):
         near = (slots[:, i : i + 1] == column).astype(BF16)
         far = (slots[:, i : i + 1] == column + room).astype(BF16)
-        row = dot_nn(near, here[...]) + dot_nn(far, there[...])
+        row = dot_nn(near, here) + dot_nn(far, there)
         out[...] = row.astype(BF16)
         sums.append(jnp.sum(grad * row, axis=-1, keepdims=True))
     lane = lax.broadcasted_iota(jnp.int32, dgate.shape, 1)
@@ -412,25 +427,31 @@
         dgate[...] += total
 
 
-def pick(slots, here, there, grad_out):
+def pick(core, slots, here, there, grad_out):
     rows, width = grad_out.shape
-    room = here.shape[0]
+    held, capacity = here.shape[1], here.shape[3]
+    room = held * capacity
     size = width // CHUNKS
-    by_column = lambda n: pl.BlockSpec((n, size), lambda i: (0, i))
+    by_column = lambda n: pl.BlockSpec((n, size), lambda i, core: (0, i))
+    table = pl.BlockSpec((None, held, None, capacity, size), lambda i, core: (0, 0, core[0], 0, i))
+    whole = lambda n: pl.BlockSpec((rows, n), lambda i, core: (0, 0))
     return pl.pallas_call(
         pick_kernel,
-        grid=(CHUNKS,),
-        in_specs=[pl.BlockSpec((rows, 2), lambda i: (0, 0)), by_column(room), by_column(room), by_column(rows)],
-        out_specs=[by_column(rows), by_column(rows), pl.BlockSpec((rows, 128), lambda i: (0, 0))],
+        grid_spec=pltpu.PrefetchScalarGridSpec(
+            num_scalar_prefetch=1,
+            grid=(CHUNKS,),
+            in_specs=[whole(2), table, table, by_column(rows)],
+            out_specs=[by_column(rows), by_column(rows), whole(128)],
+        ),
         out_shape=[jax.ShapeDtypeStruct((rows, width), BF16)] * 2 + [jax.ShapeDtypeStruct((rows, 128), F32)],
         compiler_params=params(),
         cost_estimate=cost(8 * rows * room * width, 8 * rows * width + 4 * room * width),
         name="pick",
-    )(slots, here, there, grad_out)
+    )(core, slots, here, there, grad_out)
 
 
 def middle_kernel(experts, routes, own, recv, stream, first, second, gout, dgate, router, router_t, mixed, grad, gates):
-    resid = stream[...].astype(F32) + (own[...] + recv[...])
+    resid = stream[...].astype(F32) + (own[...] + recv[...].astype(F32))
     inverse = lax.rsqrt(jnp.mean(resid * resid, axis=-1, keepdims=True) + 1e-05)
     normed = (resid * inverse).astype(BF16)
     logits = dot_nn(normed, router[...])
@@ -549,15 +570,13 @@
         return [slots, own_band, router, router_t]
 
     def swap_rows(*ready):
-        rows_out = after([expert_out[0]], *ready)[0]
-        sent = lax.dynamic_index_in_dim(rows_out, 1 - core, 1, keepdims=False).reshape(room, width)
-        kept = lax.dynamic_index_in_dim(rows_out, core, 1, keepdims=False).reshape(room, width)
-        made["rows"] = kept, swapped(sent, "exp")
-        return made["rows"]
+        rows_out = after([expert_out], *ready)[0]
+        made["rows"] = swapped(rows_out, "exp")
+        return [made["rows"]]
 
     def pick_rows(*ready):
-        kept, arrived = after(made["rows"], *ready)
-        made["picked"] = pick(slots, kept, arrived, grad_out)
+        arrived = after([made["rows"]], *ready)[0]
+        made["picked"] = pick(core_arg, slots, expert_out, arrived, grad_out)
         return [made["picked"][2]]
 
     def attend(*ready):
@@ -588,17 +607,17 @@
         if i == heads_kv - 1:
             given = (grads[-1][0], core_arg, here, back)
         grad = attention_grad(queries, dattn, attn, probs, bands, i, given, heads_kv, scale)
-        totals.append([passed_along(grad[BAND_BLOCKS - step], "ctx", -step) for step in range(1, BAND_BLOCKS)])
+        if i > 0:
+            totals[-1] = after(totals[-1], grad[0])
+        totals.append(exchanged(grad[BAND_BLOCKS - 1], grad[BAND_BLOCKS - 3]))
         grads.append(grad)
     grad_q = jnp.transpose(grads[-1][0], (1, 0, 2))
     grad_expert = grads[-1][1 + BAND_BLOCKS]
-    totals = lax.optimization_barrier(totals)
-    sums = []
-    for grad, passed in zip(grads, totals):
-        total = grad[BAND_BLOCKS]
-        for part in passed:
-            total = total + part.astype(F32)
-        sums.append(total.astype(BF16))
+    totals = [combined(grad[BAND_BLOCKS - 2], *pair) for grad, pair in zip(grads, totals)]
+    sums = [
+        (grad[BAND_BLOCKS] + (near.astype(F32) + far.astype(F32))).astype(BF16)
+        for grad, (near, far) in zip(grads, totals)
+    ]
     grad_k = jnp.stack([t[:, :head_dim] for t in sums], axis=1)
     grad_v = jnp.stack([t[:, head_dim:] for t in sums], axis=1)
     return (mixed, grad_input, grad_expert, grad_q, grad_k, grad_v)

time: 192 us -> 180 us (0.938)
  waiting for transfers between devices: 78.1 us -> 71.8 us
  starting transfers between devices: 33.3 us -> 29.2 us
  local copies, waits for them, and re-layouts: 18.9 us -> 16.6 us
    ppermute x9 -> x5, waiting for transfers between devices: 28.9 us -> 16.8 us  [passed_along(): lax.ppermute(value, axis, [(source, source + steps) for source in range(i...]
    ppermute x5, waiting for transfers between devices: 17.6 us -> 5.6 us  [gathered(): lax.ppermute(value, 'ctx', [(c, c ^ 1) for c in range(count)])]
    ppermute x4, waiting for transfers between devices: 28 us -> 38.3 us  [gathered(): lax.ppermute(value, 'ctx', [(c, (c + 2) % count) for c in range(count)])]
    ppermute x9 -> x5, starting transfers between devices: 17.6 us -> 7.33 us  [passed_along(): lax.ppermute(value, axis, [(source, source + steps) for source in range(i...]
    ppermute x0 -> x4, waiting for transfers between devices: none -> 7.75 us  [exchanged(): return (lax.ppermute(one, 'ctx', pairs), lax.ppermute(three, 'ctx', others))]
    ppermute x0 -> x4, starting transfers between devices: none -> 5.9 us  [exchanged(): return (lax.ppermute(one, 'ctx', pairs), lax.ppermute(three, 'ctx', others))]
    dynamic_slice x1 -> x0, local copies, waits for them, and re-layouts: 3.49 us -> none  [swap_rows(): lax.dynamic_index_in_dim(rows_out, 1 - core, 1, keepdims=False)]
    unnamed x53 -> x47, local copies, waits for them, and re-layouts: 10.5 us -> 9.78 us
  transfers between devices with their start and end apart: 27 -> 27, of which waited for: 14 -> 14; matrix products, arithmetic and copies ran while one was open for 3% -> 6% of each run, Pallas kernels for 18% -> 19%
where the time goes in v6:
time: 180 us; the launch traced here: 178 us
  waiting for transfers between devices  71.8 us (40%)
  Pallas kernels  56.9 us (32%)
  starting transfers between devices  29.2 us (16%)
  local copies, waits for them, and re-layouts  16.6 us (9%)
  other arithmetic  2.39 us (1%)
    ppermute x4, waiting for transfers between devices, gathered(): lax.ppermute(value, 'ctx', [(c, (c + 2) % count) for c in range(count)])  38.3 us
    ppermute x5, waiting for transfers between devices, passed_along(): lax.ppermute(value, axis, [(source, source + steps) for source in range(i...  16.8 us
    pallas_call x2, Pallas kernels, attention_grad(): pl.pallas_call(functools.partial(attention_grad_kernel, scale, steps, las...  13.6 us
    pallas_call x1, Pallas kernels, attention(): pl.pallas_call(functools.partial(attention_kernel, scale), grid_spec=pltp...  10.9 us
    unnamed x47, local copies, waits for them, and re-layouts  9.78 us
    pallas_call x1, Pallas kernels, dattention(): pl.pallas_call(functools.partial(dattn_kernel, plan, len(arrays)), grid_s...  8.63 us
    pallas_call x1, Pallas kernels, project(): pl.pallas_call(functools.partial(project_kernel, plan, len(arrays), len(a...  8.31 us
    ppermute x4, waiting for transfers between devices, exchanged(): return (lax.ppermute(one, 'ctx', pairs), lax.ppermute(three, 'ctx', others))  7.75 us
  transfers between devices with their start and end apart: 27, of which 14 were waited for; matrix products, arithmetic and copies ran while one was open for 6% of the time, Pallas kernels for 19%

profile of v6, /device:TPU:4, one launch (start us, length us, event | category | flops | bytes accessed | tf_op | source)
XLA Modules:
  0.0 178.0 jit_solution(6719410227799055325)
XLA Ops:
  0.7 1.9 %constant_dynamic-slice_fusion = bf16[6,16,3072]{2,1,0:T(8,128)(2,1)} fusion(bf16[12,16,3072]{2,1,0:T(8,128)(2,1)} %refs_0_.1, s32[]{:T(128)S(6)} %select_n.67), kind=kLoop, calls=%fused_computation.25 | loop fusion | bytes 1179652 | tf_op jit(solution)/shard_map/dynamic_slice | solution.py:77
  2.6 2.1 %collective-permute-start = (bf16[6,16,3072]{2,1,0:T(8,128)(2,1)}, bf16[6,16,3072]{2,1,0:T(8,128)(2,1)}, u32[]{:S(2)}, u32[]{:S(2)}) collective-permute-start(bf16[6,16,3072]{2,1,0:T(8,128)(2,1)} %constant_dynamic-slice_fusion), channel_id=1, source_target_pairs={{0,4},{2,6},{4,8},{6,10},{8,12},{10,14},{12,0},{14,2},{1,5},{3,7},... | collective-permute-start | bytes 1769480 | tf_op jit(solution)/shard_map/ppermute | solution.py:74
  8.2 2.3 %pad.8.router = bf16[3072,128]{1,0:T(8,128)(2,1)} pad(bf16[3072,8]{1,0:T(8,128)(2,1)} %copy.30, bf16[]{:T(256)} %constant.92.clone.1), padding=0_0x0_120 | pad | bytes 835586 | tf_op jit(solution)/shard_map/jit(_pad)/pad | solution.py:565
  12.4 5.6 %collective-permute-done.1.refs_5_.refs_4_ = bf16[6,16,3072]{2,1,0:T(8,128)(2,1)} collective-permute-done((bf16[6,16,3072]{2,1,0:T(8,128)(2,1)}, bf16[6,16,3072]{2,1,0:T(8,128)(2,1)}, u32[]{:S(2)}, u32[]{:S(2)}) %collective-permute-start.1) | collective-permute-done | bytes 589856 | tf_op jit(solution)/shard_map/ppermute | solution.py:75
  18.0 2.1 %collective-permute-done.refs_2_.refs_1_ = bf16[6,16,3072]{2,1,0:T(8,128)(2,1)} collective-permute-done((bf16[6,16,3072]{2,1,0:T(8,128)(2,1)}, bf16[6,16,3072]{2,1,0:T(8,128)(2,1)}, u32[]{:S(2)}, u32[]{:S(2)}) %collective-permute-start) | collective-permute-done | bytes 589856 | tf_op jit(solution)/shard_map/ppermute | solution.py:74
  20.1 1.6 collective-permute-start.7
  23.2 14.8 %collective-permute-done.2.refs_3_.refs_2_ = bf16[6,16,3072]{2,1,0:T(8,128)(2,1)} collective-permute-done((bf16[6,16,3072]{2,1,0:T(8,128)(2,1)}, bf16[6,16,3072]{2,1,0:T(8,128)(2,1)}, u32[]{:S(2)}, u32[]{:S(2)}) %collective-permute-start.2) | collective-permute-done | bytes 589856 | tf_op jit(solution)/shard_map/ppermute | solution.py:74
  38.0 1.7 copy-done.5
  40.4 1.5 collective-permute-start.4
  41.9 1.5 collective-permute-start.9
  43.4 4.8 %pick.1 = (bf16[128,3072]{1,0:T(8,128)(2,1)}, bf16[128,3072]{1,0:T(8,128)(2,1)}, f32[128,128]{1,0:T(8,128)}) custom-call(s32[1]{0:T(128)} %bitcast.10.core.refs_9_, s32[128,2]{1,0:T(8,128)} %copy.31.slots, bf16[1,4,2,64,3072]{4,3,2,1,0:T(8,128)(2,1)} %here_ref.1, bf16[1,4,2,64,3072]{4,3,2,1,0:T(8,128)(2,1)} %copy-done.5, bf16[128,3072]{1,0:T(8,128)(2,1)} %gout.5), custom_call_target="tpu_custom_call" | custom-call | flops 805306368 | bytes 6291456 | tf_op jit(solution)/shard_map/pick/pallas_call | solution.py:438
  48.2 8.4 %collective-permute-done.5.refs_4_.refs_3_ = bf16[6,16,3072]{2,1,0:T(8,128)(2,1)S(1)} collective-permute-done((bf16[6,16,3072]{2,1,0:T(8,128)(2,1)}, bf16[6,16,3072]{2,1,0:T(8,128)(2,1)S(1)}, u32[]{:S(2)}, u32[]{:S(2)}) %collective-permute-start.5) | collective-permute-done | bytes 589856 | tf_op jit(solution)/shard_map/ppermute | solution.py:74
  56.6 1.5 collective-permute-start.10
  58.1 1.5 collective-permute-start.14
  59.6 13.0 %collective-permute-done.8.refs_10_.refs_9_ = bf16[6,16,3072]{2,1,0:T(8,128)(2,1)S(1)} collective-permute-done((bf16[6,16,3072]{2,1,0:T(8,128)(2,1)}, bf16[6,16,3072]{2,1,0:T(8,128)(2,1)S(1)}, u32[]{:S(2)}, u32[]{:S(2)}) %collective-permute-start.8) | collective-permute-done | bytes 589856 | tf_op jit(solution)/shard_map/ppermute | solution.py:74
  72.7 1.9 %collective-permute-start.13 = (bf16[256,512]{1,0:T(8,128)(2,1)S(1)}, bf16[256,512]{1,0:T(8,128)(2,1)S(1)}, u32[]{:S(2)}, u32[]{:S(2)}) collective-permute-start(bf16[256,512]{1,0:T(8,128)(2,1)S(1)} %bitcast_dynamic-update-slice_fusion.refs_3_.refs_7_), channel_id=1, source_target_pairs={{0,2},{2,4},{4,6},{6,8},{8,10},{10,12},{12,14},{1,3},{3,5},{5,7},{... | collective-permute-start | bytes 786440 | tf_op jit(solution)/shard_map/ppermute | solution.py:39
  74.6 2.1 %collective-permute-start.15 = (bf16[6,16,3072]{2,1,0:T(8,128)(2,1)}, bf16[6,16,3072]{2,1,0:T(8,128)(2,1)}, u32[]{:S(2)}, u32[]{:S(2)}) collective-permute-start(bf16[6,16,3072]{2,1,0:T(8,128)(2,1)} %collective-permute-done.6.refs_9_.refs_8_), channel_id=1, source_target_pairs={{0,2},{2,0},{4,6},{6,4},{8,10},{10,8},{12,14},{14,12},{1,3},{3,1},... | collective-permute-start | bytes 1769480 | tf_op jit(solution)/shard_map/ppermute | solution.py:75
  80.0 3.8 %collective-permute-done.13.refs_2_.refs_6_ = bf16[256,512]{1,0:T(8,128)(2,1)S(1)} collective-permute-done((bf16[256,512]{1,0:T(8,128)(2,1)S(1)}, bf16[256,512]{1,0:T(8,128)(2,1)S(1)}, u32[]{:S(2)}, u32[]{:S(2)}) %collective-permute-start.13) | collective-permute-done | bytes 262176 | tf_op jit(solution)/shard_map/ppermute | solution.py:39
  83.8 1.5 collective-permute-start.11
  86.6 3.2 %collective-permute-done.11.refs_0_.refs_4_ = bf16[256,512]{1,0:T(8,128)(2,1)S(1)} collective-permute-done((bf16[256,512]{1,0:T(8,128)(2,1)S(1)}, bf16[256,512]{1,0:T(8,128)(2,1)S(1)}, u32[]{:S(2)}, u32[]{:S(2)}) %collective-permute-start.11) | collective-permute-done | bytes 262176 | tf_op jit(solution)/shard_map/ppermute | solution.py:39
  90.5 10.9 %attention.1 = (bf16[256,1536]{1,0:T(8,128)(2,1)}, bf16[12,256,1024]{2,1,0:T(8,128)(2,1)}) custom-call(s32[1]{0:T(128)} %bitcast.11.place, bf16[12,256,128]{2,1,0:T(8,128)(2,1)} %bitcast.32, bf16[256,512]{1,0:T(8,128)(2,1)} %copy-done.3, bf16[256,512]{1,0:T(8,128)(2,1)} %copy-done.2, bf16[256,512]{1,0:T(8,128)(2,1)} %copy-done.1, bf16[256,512]{1,0:T(8,128)(2,1)} %copy-done, ...), custom_call_target="tpu_custom_call" | custom-call | flops 1610612736 | bytes 6291456 | tf_op jit(solution)/shard_map/attention/pallas_call | solution.py:281
  102.3 8.3 %project.1 = (f32[128,3072]{1,0:T(8,128)}, bf16[128,3072]{1,0:T(8,128)(2,1)}) custom-call(s32[11]{0:T(128)} %stack.61.table, s32[1]{0:T(128)} %bitcast.10.core.refs_9_, bf16[256,1536]{1,0:T(8,128)(2,1)} %get-tuple-element.56.refs_0_.attn, bf16[12,16,3072]{2,1,0:T(8,128)(2,1)} %refs_0_.1, bf16[6,16,3072]{2,1,0:T(8,128)(2,1)} %collective-permute-done.refs_2_.refs_1_, ...), custom_call_target="tpu_custom_call" | custom-call | flops 2415919104 | bytes 9437184 | tf_op jit(solution)/shard_map/project/pallas_call | solution.py:160
  110.7 2.5 %collective-permute-done.18.recv = bf16[128,3072]{1,0:T(8,128)(2,1)S(1)} collective-permute-done((bf16[128,3072]{1,0:T(8,128)(2,1)}, bf16[128,3072]{1,0:T(8,128)(2,1)S(1)}, u32[]{:S(2)}, u32[]{:S(2)}) %collective-permute-start.18) | collective-permute-done | bytes 786464 | tf_op jit(solution)/shard_map/ppermute | solution.py:43
  114.0 6.2 %middle.1 = (bf16[128,3072]{1,0:T(8,128)(2,1)}, bf16[128,3072]{1,0:T(8,128)(2,1)}, f32[128,128]{1,0:T(8,128)}) custom-call(s32[128,2]{1,0:T(8,128)} %copy-done.13, f32[128,3072]{1,0:T(8,128)} %get-tuple-element.60.own, bf16[128,3072]{1,0:T(8,128)(2,1)} %copy-done.12, bf16[128,3072]{1,0:T(8,128)(2,1)} %stream.1, bf16[128,3072]{1,0:T(8,128)(2,1)} %get-tuple-element.62.first, ...), custom_call_target="tpu_custom_call" | custom-call | flops 402653184 | bytes 7864320 | tf_op jit(solution)/shard_map/middle/pallas_call | solution.py:494
  120.4 4.5 %spread.1 = (bf16[256,3072]{1,0:T(8,128)(2,1)}, bf16[256,3072]{1,0:T(8,128)(2,1)}) custom-call(s32[2,128]{1,0:T(2,128)} %bitcast.41, f32[128,128]{1,0:T(8,128)} %get-tuple-element.68.gates, bf16[128,3072]{1,0:T(8,128)(2,1)} %gout.5), custom_call_target="tpu_custom_call" | custom-call | flops 805306368 | bytes 3932160 | tf_op jit(solution)/shard_map/spread/pallas_call | solution.py:524
  125.8 8.6 %dattention.1.dout = bf16[256,1536]{1,0:T(8,128)(2,1)} custom-call(s32[11]{0:T(128)} %stack.61.table, s32[1]{0:T(128)} %bitcast.10.core.refs_9_, bf16[128,3072]{1,0:T(8,128)(2,1)} %get-tuple-element.97.own, bf16[128,3072]{1,0:T(8,128)(2,1)} %copy-done.11, bf16[12,16,3072]{2,1,0:T(8,128)(2,1)} %refs_0_.1, ...), custom_call_target="tpu_custom_call" | custom-call | flops 2415919104 | bytes 9437184 | tf_op jit(solution)/shard_map/dattention/pallas_call | solution.py:216
  134.9 6.5 %attention_grad.2 = (bf16[12,256,128]{2,1,0:T(8,128)(2,1)}, bf16[256,256]{1,0:T(8,128)(2,1)}, bf16[256,256]{1,0:T(8,128)(2,1)}, bf16[256,256]{1,0:T(8,128)(2,1)}, f32[256,256]{1,0:T(8,128)}) custom-call(bf16[12,256,128]{2,1,0:T(8,128)(2,1)} %bitcast.33, bf16[256,1536]{1,0:T(8,128)(2,1)} %dattention.1.dout, bf16[256,1536]{1,0:T(8,128)(2,1)} %get-tuple-element.56.refs_0_.attn, ...), custom_call_target="tpu_custom_call" | custom-call | flops 256 | bytes 256 | tf_op jit(solution)/shard_map/attention_grad/pallas_call | solution.py:382
  141.8 3.6 %collective-permute-start.22 = (bf16[256,256]{1,0:T(8,128)(2,1)}, bf16[256,256]{1,0:T(8,128)(2,1)S(1)}, u32[]{:S(2)}, u32[]{:S(2)}) collective-permute-start(bf16[256,256]{1,0:T(8,128)(2,1)} %get-tuple-element.77), channel_id=1, source_target_pairs={{2,0},{6,4},{8,2},{10,8},{12,6},{14,12},{3,1},{7,5},{9,3},{11,9},{... | collective-permute-start | bytes 393224 | tf_op jit(solution)/shard_map/ppermute | solution.py:50
  146.5 7.1 %attention_grad.3 = (bf16[12,256,128]{2,1,0:T(8,128)(2,1)}, bf16[256,256]{1,0:T(8,128)(2,1)}, bf16[256,256]{1,0:T(8,128)(2,1)}, bf16[256,256]{1,0:T(8,128)(2,1)}...) custom-call(bf16[12,256,128]{2,1,0:T(8,128)(2,1)} %bitcast.34, ...), custom_call_target="tpu_custom_call", output_to_operand_aliasing={{0}: (12, {})} | custom-call | flops 256 | bytes 256 | tf_op jit(solution)/shard_map/attention_grad/pallas_call | solution.py:382
  154.4 1.9 %collective-permute-start.24 = (bf16[256,256]{1,0:T(8,128)(2,1)}, bf16[256,256]{1,0:T(8,128)(2,1)S(1)}, u32[]{:S(2)}, u32[]{:S(2)}) collective-permute-start(bf16[256,256]{1,0:T(8,128)(2,1)} %get-tuple-element.82), channel_id=1, source_target_pairs={{2,0},{6,4},{8,2},{10,8},{12,6},{14,12},{3,1},{7,5},{9,3},{11,9},{... | collective-permute-start | bytes 393224 | tf_op jit(solution)/shard_map/ppermute | solution.py:50
  157.7 7.0 %collective-permute-done.24 = bf16[256,256]{1,0:T(8,128)(2,1)S(1)} collective-permute-done((bf16[256,256]{1,0:T(8,128)(2,1)}, bf16[256,256]{1,0:T(8,128)(2,1)S(1)}, u32[]{:S(2)}, u32[]{:S(2)}) %collective-permute-start.24) | collective-permute-done | bytes 131104 | tf_op jit(solution)/shard_map/ppermute | solution.py:50
  167.8 8.5 %collective-permute-done.26 = bf16[256,256]{1,0:T(8,128)(2,1)S(1)} collective-permute-done((bf16[256,256]{1,0:T(8,128)(2,1)S(1)}, bf16[256,256]{1,0:T(8,128)(2,1)S(1)}, u32[]{:S(2)}, u32[]{:S(2)}) %collective-permute-start.26) | collective-permute-done | bytes 131104 | tf_op jit(solution)/shard_map/ppermute | solution.py:39
  (95 shorter events, 24.6 us)
Async XLA Ops:
  2.6 15.4 %collective-permute-start.1 = (bf16[6,16,3072]{2,1,0:T(8,128)(2,1)}, bf16[6,16,3072]{2,1,0:T(8,128)(2,1)}, u32[]{:S(2)}, u32[]{:S(2)}) collective-permute-start(bf16[6,16,3072]{2,1,0:T(8,128)(2,1)} %constant_dynamic-slice_fusion), channel_id=1, source_target_pairs={{0,2},{2,0},{4,6},{6,4},{8,10},{10,8},{12,14},{14,12},{1,3},{3,1},... | collective-permute-start | bytes 1769480 | tf_op jit(solution)/shard_map/ppermute | solution.py:75
  2.6 17.5 %collective-permute-start = (bf16[6,16,3072]{2,1,0:T(8,128)(2,1)}, bf16[6,16,3072]{2,1,0:T(8,128)(2,1)}, u32[]{:S(2)}, u32[]{:S(2)}) collective-permute-start(bf16[6,16,3072]{2,1,0:T(8,128)(2,1)} %constant_dynamic-slice_fusion), channel_id=1, source_target_pairs={{0,4},{2,6},{4,8},{6,10},{8,12},{10,14},{12,0},{14,2},{1,5},{3,7},... | collective-permute-start | bytes 1769480 | tf_op jit(solution)/shard_map/ppermute | solution.py:74
  7.0 32.6 %copy-start.19 = (s32[128,2]{0,1:T(2,128)}, s32[128,2]{0,1:T(2,128)S(1)}, u32[]{:S(2)}) copy-start(s32[128,2]{0,1:T(2,128)S(1)} %and_select_fusion) | copy-start | bytes 3076
  11.3 72.5 %copy-start = (bf16[256,512]{1,0:T(8,128)(2,1)}, bf16[256,512]{1,0:T(8,128)(2,1)S(1)}, u32[]{:S(2)}) copy-start(bf16[256,512]{1,0:T(8,128)(2,1)S(1)} %bitcast_dynamic-update-slice_fusion.refs_3_.refs_7_) | copy-start | bytes 786436
  20.1 17.9 %collective-permute-start.3 = (bf16[1,4,2,64,3072]{4,3,2,1,0:T(8,128)(2,1)S(1)}, bf16[1,4,2,64,3072]{4,3,2,1,0:T(8,128)(2,1)S(1)}, u32[]{:S(2)}, u32[]{:S(2)}) collective-permute-start(bf16[1,4,2,64,3072]{4,3,2,1,0:T(8,128)(2,1)S(1)} %copy-done.4), channel_id=1, source_target_pairs={{0,1},{1,0},{2,3},{3,2},{4,5},{5,4},{6,7},{7,6},{8,9},{9,8},{10,11... | collective-permute-start | bytes 9437192 | tf_op jit(solution)/shard_map/ppermute | solution.py:43
  20.1 17.9 %collective-permute-start.2 = (bf16[6,16,3072]{2,1,0:T(8,128)(2,1)}, bf16[6,16,3072]{2,1,0:T(8,128)(2,1)}, u32[]{:S(2)}, u32[]{:S(2)}) collective-permute-start(bf16[6,16,3072]{2,1,0:T(8,128)(2,1)} %collective-permute-done.refs_2_.refs_1_), channel_id=1, source_target_pairs={{0,4},{2,6},{4,8},{6,10},{8,12},{10,14},{12,0},{14,2},{1,5},{3,7},... | collective-permute-start | bytes 1769480 | tf_op jit(solution)/shard_map/ppermute | solution.py:74
  20.1 28.1 %collective-permute-start.7 = (bf16[6,16,3072]{2,1,0:T(8,128)(2,1)}, bf16[6,16,3072]{2,1,0:T(8,128)(2,1)}, u32[]{:S(2)}, u32[]{:S(2)}) collective-permute-start(bf16[6,16,3072]{2,1,0:T(8,128)(2,1)} %collective-permute-done.refs_2_.refs_1_), channel_id=1, source_target_pairs={{0,2},{2,0},{4,6},{6,4},{8,10},{10,8},{12,14},{14,12},{1,3},{3,1},... | collective-permute-start | bytes 1769480 | tf_op jit(solution)/shard_map/ppermute | solution.py:75
  21.7 26.5 %collective-permute-start.6 = (bf16[6,16,3072]{2,1,0:T(8,128)(2,1)}, bf16[6,16,3072]{2,1,0:T(8,128)(2,1)}, u32[]{:S(2)}, u32[]{:S(2)}) collective-permute-start(bf16[6,16,3072]{2,1,0:T(8,128)(2,1)} %collective-permute-done.refs_2_.refs_1_), channel_id=1, source_target_pairs={{0,16},{16,0},{1,17},{17,1},{2,18},{18,2},{3,19},{19,3},{4,20},{20... | collective-permute-start | bytes 1769480 | tf_op jit(solution)/shard_map/ppermute | solution.py:43
  39.6 17.0 %collective-permute-start.5 = (bf16[6,16,3072]{2,1,0:T(8,128)(2,1)}, bf16[6,16,3072]{2,1,0:T(8,128)(2,1)S(1)}, u32[]{:S(2)}, u32[]{:S(2)}) collective-permute-start(bf16[6,16,3072]{2,1,0:T(8,128)(2,1)} %collective-permute-done.2.refs_3_.refs_2_), channel_id=1, source_target_pairs={{0,4},{2,6},{4,8},{6,10},{8,12},{10,14},{12,0},{14,2},{1,5},{3,7},... | collective-permute-start | bytes 1769480 | tf_op jit(solution)/shard_map/ppermute | solution.py:74
  40.4 19.2 %collective-permute-start.4 = (bf16[6,16,3072]{2,1,0:T(8,128)(2,1)}, bf16[6,16,3072]{2,1,0:T(8,128)(2,1)S(1)}, u32[]{:S(2)}, u32[]{:S(2)}) collective-permute-start(bf16[6,16,3072]{2,1,0:T(8,128)(2,1)} %collective-permute-done.2.refs_3_.refs_2_), channel_id=1, source_target_pairs={{0,2},{2,0},{4,6},{6,4},{8,10},{10,8},{12,14},{14,12},{1,3},{3,1},... | collective-permute-start | bytes 1769480 | tf_op jit(solution)/shard_map/ppermute | solution.py:75
  41.9 17.7 %collective-permute-start.9 = (bf16[6,16,3072]{2,1,0:T(8,128)(2,1)}, bf16[6,16,3072]{2,1,0:T(8,128)(2,1)S(1)}, u32[]{:S(2)}, u32[]{:S(2)}) collective-permute-start(bf16[6,16,3072]{2,1,0:T(8,128)(2,1)} %collective-permute-done.1.refs_5_.refs_4_), channel_id=1, source_target_pairs={{0,16},{16,0},{1,17},{17,1},{2,18},{18,2},{3,19},{19,3},{4,20},{20... | collective-permute-start | bytes 1769480 | tf_op jit(solution)/shard_map/ppermute | solution.py:43
  56.6 45.7 %copy-start.6 = (bf16[6,16,3072]{2,1,0:T(8,128)(2,1)}, bf16[6,16,3072]{2,1,0:T(8,128)(2,1)S(1)}, u32[]{:S(2)}) copy-start(bf16[6,16,3072]{2,1,0:T(8,128)(2,1)S(1)} %collective-permute-done.5.refs_4_.refs_3_) | copy-start | bytes 1769476
  56.6 16.1 %collective-permute-start.8 = (bf16[6,16,3072]{2,1,0:T(8,128)(2,1)}, bf16[6,16,3072]{2,1,0:T(8,128)(2,1)S(1)}, u32[]{:S(2)}, u32[]{:S(2)}) collective-permute-start(bf16[6,16,3072]{2,1,0:T(8,128)(2,1)} %collective-permute-done.6.refs_9_.refs_8_), channel_id=1, source_target_pairs={{0,4},{2,6},{4,8},{6,10},{8,12},{10,14},{12,0},{14,2},{1,5},{3,7},... | collective-permute-start | bytes 1769480 | tf_op jit(solution)/shard_map/ppermute | solution.py:74
  56.6 16.1 %collective-permute-start.10 = (bf16[6,16,3072]{2,1,0:T(8,128)(2,1)S(1)}, bf16[6,16,3072]{2,1,0:T(8,128)(2,1)}, u32[]{:S(2)}, u32[]{:S(2)}) collective-permute-start(bf16[6,16,3072]{2,1,0:T(8,128)(2,1)S(1)} %collective-permute-done.5.refs_4_.refs_3_), channel_id=1, source_target_pairs={{0,16},{16,0},{1,17},{17,1},{2,18},{18,2},{3,19},{19,3},{4,20},{20... | collective-permute-start | bytes 1769480 | tf_op jit(solution)/shard_map/ppermute | solution.py:43
  58.1 16.5 %collective-permute-start.14 = (bf16[6,16,3072]{2,1,0:T(8,128)(2,1)S(1)}, bf16[6,16,3072]{2,1,0:T(8,128)(2,1)}, u32[]{:S(2)}, u32[]{:S(2)}) collective-permute-start(bf16[6,16,3072]{2,1,0:T(8,128)(2,1)S(1)} %collective-permute-done.5.refs_4_.refs_3_), channel_id=1, source_target_pairs={{0,2},{2,0},{4,6},{6,4},{8,10},{10,8},{12,14},{14,12},{1,3},{3,1},... | collective-permute-start | bytes 1769480 | tf_op jit(solution)/shard_map/ppermute | solution.py:75
  59.6 42.6 %copy-start.8 = (bf16[6,16,3072]{2,1,0:T(8,128)(2,1)}, bf16[6,16,3072]{2,1,0:T(8,128)(2,1)S(1)}, u32[]{:S(2)}) copy-start(bf16[6,16,3072]{2,1,0:T(8,128)(2,1)S(1)} %collective-permute-done.9.refs_12_.refs_11_) | copy-start | bytes 1769476
  59.6 42.6 %copy-start.7 = (bf16[6,16,3072]{2,1,0:T(8,128)(2,1)}, bf16[6,16,3072]{2,1,0:T(8,128)(2,1)S(1)}, u32[]{:S(2)}) copy-start(bf16[6,16,3072]{2,1,0:T(8,128)(2,1)S(1)} %collective-permute-done.4.refs_7_.refs_6_) | copy-start | bytes 1769476
  72.7 11.1 %collective-permute-start.13 = (bf16[256,512]{1,0:T(8,128)(2,1)S(1)}, bf16[256,512]{1,0:T(8,128)(2,1)S(1)}, u32[]{:S(2)}, u32[]{:S(2)}) collective-permute-start(bf16[256,512]{1,0:T(8,128)(2,1)S(1)} %bitcast_dynamic-update-slice_fusion.refs_3_.refs_7_), channel_id=1, source_target_pairs={{0,2},{2,4},{4,6},{6,8},{8,10},{10,12},{12,14},{1,3},{3,5},{5,7},{... | collective-permute-start | bytes 786440 | tf_op jit(solution)/shard_map/ppermute | solution.py:39
  74.6 26.8 %collective-permute-start.15 = (bf16[6,16,3072]{2,1,0:T(8,128)(2,1)}, bf16[6,16,3072]{2,1,0:T(8,128)(2,1)}, u32[]{:S(2)}, u32[]{:S(2)}) collective-permute-start(bf16[6,16,3072]{2,1,0:T(8,128)(2,1)} %collective-permute-done.6.refs_9_.refs_8_), channel_id=1, source_target_pairs={{0,2},{2,0},{4,6},{6,4},{8,10},{10,8},{12,14},{14,12},{1,3},{3,1},... | collective-permute-start | bytes 1769480 | tf_op jit(solution)/shard_map/ppermute | solution.py:75
  76.7 24.7 %collective-permute-start.17 = (bf16[6,16,3072]{2,1,0:T(8,128)(2,1)}, bf16[6,16,3072]{2,1,0:T(8,128)(2,1)}, u32[]{:S(2)}, u32[]{:S(2)}) collective-permute-start(bf16[6,16,3072]{2,1,0:T(8,128)(2,1)} %collective-permute-done.14.refs_8_.refs_7_), channel_id=1, source_target_pairs={{0,16},{16,0},{1,17},{17,1},{2,18},{18,2},{3,19},{19,3},{4,20},{20... | collective-permute-start | bytes 1769480 | tf_op jit(solution)/shard_map/ppermute | solution.py:43
  78.2 24.1 %collective-permute-start.16 = (bf16[6,16,3072]{2,1,0:T(8,128)(2,1)S(1)}, bf16[6,16,3072]{2,1,0:T(8,128)(2,1)}, u32[]{:S(2)}, u32[]{:S(2)}) collective-permute-start(bf16[6,16,3072]{2,1,0:T(8,128)(2,1)S(1)} %collective-permute-done.4.refs_7_.refs_6_), channel_id=1, source_target_pairs={{0,16},{16,0},{1,17},{17,1},{2,18},{18,2},{3,19},{19,3},{4,20},{20... | collective-permute-start | bytes 1769480 | tf_op jit(solution)/shard_map/ppermute | solution.py:43
  78.7 7.9 %collective-permute-start.12 = (bf16[256,512]{1,0:T(8,128)(2,1)S(1)}, bf16[256,512]{1,0:T(8,128)(2,1)S(1)}, u32[]{:S(2)}, u32[]{:S(2)}) collective-permute-start(bf16[256,512]{1,0:T(8,128)(2,1)S(1)} %bitcast_dynamic-update-slice_fusion.refs_3_.refs_7_), channel_id=1, source_target_pairs={{0,4},{2,6},{4,8},{6,10},{8,12},{10,14},{1,5},{3,7},{5,9},{7,11},{... | collective-permute-start | bytes 786440 | tf_op jit(solution)/shard_map/ppermute | solution.py:39
  83.8 6.0 %collective-permute-start.11 = (bf16[256,512]{1,0:T(8,128)(2,1)S(1)}, bf16[256,512]{1,0:T(8,128)(2,1)S(1)}, u32[]{:S(2)}, u32[]{:S(2)}) collective-permute-start(bf16[256,512]{1,0:T(8,128)(2,1)S(1)} %bitcast_dynamic-update-slice_fusion.refs_3_.refs_7_), channel_id=1, source_target_pairs={{0,6},{2,8},{4,10},{6,12},{8,14},{1,7},{3,9},{5,11},{7,13},{9,15},... | collective-permute-start | bytes 786440 | tf_op jit(solution)/shard_map/ppermute | solution.py:39
  110.6 2.6 %collective-permute-start.18 = (bf16[128,3072]{1,0:T(8,128)(2,1)}, bf16[128,3072]{1,0:T(8,128)(2,1)S(1)}, u32[]{:S(2)}, u32[]{:S(2)}) collective-permute-start(bf16[128,3072]{1,0:T(8,128)(2,1)} %get-tuple-element.61), channel_id=1, source_target_pairs={{0,1},{1,0},{2,3},{3,2},{4,5},{5,4},{6,7},{7,6},{8,9},{9,8},{10,11... | collective-permute-start | bytes 2359304 | tf_op jit(solution)/shard_map/ppermute | solution.py:43
  120.2 4.7 %collective-permute-start.19 = (bf16[128,3072]{1,0:T(8,128)(2,1)}, bf16[128,3072]{1,0:T(8,128)(2,1)S(1)}, u32[]{:S(2)}, u32[]{:S(2)}) collective-permute-start(bf16[128,3072]{1,0:T(8,128)(2,1)} %get-tuple-element.97.own), channel_id=1, source_target_pairs={{0,1},{1,0},{2,3},{3,2},{4,5},{5,4},{6,7},{7,6},{8,9},{9,8},{10,11... | collective-permute-start | bytes 2359304 | tf_op jit(solution)/shard_map/ppermute | solution.py:43
  134.4 10.9 %collective-permute-start.20 = (bf16[256,3072]{1,0:T(8,128)(2,1)S(1)}, bf16[256,3072]{1,0:T(8,128)(2,1)S(1)}, u32[]{:S(2)}, u32[]{:S(2)}) collective-permute-start(bf16[256,3072]{1,0:T(8,128)(2,1)S(1)} %copy-done.20), channel_id=1, source_target_pairs={{0,1},{1,0},{2,3},{3,2},{4,5},{5,4},{6,7},{7,6},{8,9},{9,8},{10,11... | collective-permute-start | bytes 4718600 | tf_op jit(solution)/shard_map/ppermute | solution.py:43
  141.4 12.2 %collective-permute-start.21 = (bf16[256,256]{1,0:T(8,128)(2,1)}, bf16[256,256]{1,0:T(8,128)(2,1)S(1)}, u32[]{:S(2)}, u32[]{:S(2)}) collective-permute-start(bf16[256,256]{1,0:T(8,128)(2,1)} %get-tuple-element.76), channel_id=1, source_target_pairs={{0,2},{2,0},{4,6},{6,4},{8,10},{10,8},{12,14},{14,12},{1,3},{3,1},... | collective-permute-start | bytes 393224 | tf_op jit(solution)/shard_map/ppermute | solution.py:50
  141.8 12.6 %collective-permute-start.22 = (bf16[256,256]{1,0:T(8,128)(2,1)}, bf16[256,256]{1,0:T(8,128)(2,1)S(1)}, u32[]{:S(2)}, u32[]{:S(2)}) collective-permute-start(bf16[256,256]{1,0:T(8,128)(2,1)} %get-tuple-element.77), channel_id=1, source_target_pairs={{2,0},{6,4},{8,2},{10,8},{12,6},{14,12},{3,1},{7,5},{9,3},{11,9},{... | collective-permute-start | bytes 393224 | tf_op jit(solution)/shard_map/ppermute | solution.py:50
  154.4 10.4 %collective-permute-start.24 = (bf16[256,256]{1,0:T(8,128)(2,1)}, bf16[256,256]{1,0:T(8,128)(2,1)S(1)}, u32[]{:S(2)}, u32[]{:S(2)}) collective-permute-start(bf16[256,256]{1,0:T(8,128)(2,1)} %get-tuple-element.82), channel_id=1, source_target_pairs={{2,0},{6,4},{8,2},{10,8},{12,6},{14,12},{3,1},{7,5},{9,3},{11,9},{... | collective-permute-start | bytes 393224 | tf_op jit(solution)/shard_map/ppermute | solution.py:50
  156.3 8.4 %collective-permute-start.25 = (bf16[256,256]{1,0:T(8,128)(2,1)}, bf16[256,256]{1,0:T(8,128)(2,1)S(1)}, u32[]{:S(2)}, u32[]{:S(2)}) collective-permute-start(bf16[256,256]{1,0:T(8,128)(2,1)} %get-tuple-element.83), channel_id=1, source_target_pairs={{0,2},{2,0},{4,6},{6,4},{8,10},{10,8},{12,14},{14,12},{1,3},{3,1},... | collective-permute-start | bytes 393224 | tf_op jit(solution)/shard_map/ppermute | solution.py:50
  156.4 11.3 %collective-permute-start.23 = (bf16[256,256]{1,0:T(8,128)(2,1)S(1)}, bf16[256,256]{1,0:T(8,128)(2,1)S(1)}, u32[]{:S(2)}, u32[]{:S(2)}) collective-permute-start(bf16[256,256]{1,0:T(8,128)(2,1)S(1)} %add_convert_fusion.3), channel_id=1, source_target_pairs={{4,0},{6,2},{8,4},{10,6},{12,8},{14,10},{5,1},{7,3},{9,5},{11,7},{... | collective-permute-start | bytes 393224 | tf_op jit(solution)/shard_map/ppermute | solution.py:39
  165.7 10.6 %collective-permute-start.26 = (bf16[256,256]{1,0:T(8,128)(2,1)S(1)}, bf16[256,256]{1,0:T(8,128)(2,1)S(1)}, u32[]{:S(2)}, u32[]{:S(2)}) collective-permute-start(bf16[256,256]{1,0:T(8,128)(2,1)S(1)} %add_convert_fusion.1), channel_id=1, source_target_pairs={{4,0},{6,2},{8,4},{10,6},{12,8},{14,10},{5,1},{7,3},{9,5},{11,7},{... | collective-permute-start | bytes 393224 | tf_op jit(solution)/shard_map/ppermute | solution.py:39
  (16 other events, 139.1 us)

commit v7 on v6

--- a/solution.py
+++ b/solution.py
@@ -53,7 +53,7 @@
 def combined(two, by_one, by_three):
     even = lax.axis_index("ctx") % 2 == 0
     onward = (two.astype(F32) + jnp.where(even, by_three, by_one).astype(F32)).astype(BF16)
-    return passed_along(onward, "ctx", -2), jnp.where(even, by_one, by_three)
+    return onward, jnp.where(even, by_one, by_three)
 
 
 def after(values, *others):
@@ -240,7 +240,6 @@
 
 
 HEADS_FORWARD = 6
-HEADS_BACKWARD = 6
 
 
 def heads_a_step(most, group):
@@ -301,103 +300,126 @@
     )(place, queries, *bands, *bands)
 
 
-def attention_grad_kernel(scale, steps, last, q, dout, attn, probs, *refs):
-    refs = list(refs)
-    keys, values = refs[:BAND_BLOCKS], refs[BAND_BLOCKS : 2 * BAND_BLOCKS]
-    refs = refs[2 * BAND_BLOCKS :]
-    if last:
-        (_, core, here, back), refs, (held, sem) = refs[:4], refs[4:-2], refs[-2:]
-        joined = refs.pop(1 + BAND_BLOCKS)
-        places = core[0], 1 - core[0]
-        inward = [pltpu.make_async_copy(r, held.at[i], sem.at[0, i]) for i, r in enumerate((here, back))]
-        outward = [
-            pltpu.make_async_copy(held.at[i], joined.at[0, :, at], sem.at[1, i]) for i, at in enumerate(places)
-        ]
-
-        @pl.when(pl.program_id(0) == 0)
-        def _():
-            for copy in inward:
-                copy.start()
-
-    dq, outs, (dk, dv) = refs[0], refs[1:-2], refs[-2:]
+def score_grads(scale, q, dout, attn, probs, keys, values):
     count, tok, head_dim = q.shape
-    step = pl.program_id(0)
     grad = stacked(dout, count)
-    weight = probs[...].reshape(count * tok, BAND_BLOCKS * tok)
     delta = jnp.sum(grad.astype(F32) * stacked(attn, count).astype(F32), axis=-1, keepdims=True)
     dprob = dot_nt(grad, band_of(values))
+    weight = probs[...].reshape(dprob.shape)
     dscore = (weight.astype(F32) * (dprob - delta)).astype(BF16)
-    dq[...] = (dot_nn(dscore, band_of(keys)) * scale).astype(BF16).reshape(count, tok, head_dim)
-    if last:
-
-        @pl.when(step == 0)
+    dquery = (dot_nn(dscore, band_of(keys)) * scale).astype(BF16).reshape(count, tok, head_dim)
+    return dquery, dot_tn(dscore, q[...].reshape(count * tok, head_dim)) * scale
+
+
+def value_grads(dout, probs):
+    count, tok, span = probs.shape
+    return dot_tn(probs[...].reshape(count * tok, span), stacked(dout, count))
+
+
+def put(outs, part, value):
+    tok, head_dim = outs[0].shape[0], value.shape[1]
+    for block, out in enumerate(outs):
+        rows = value[block * tok : (block + 1) * tok]
+        out[:, part * head_dim : (part + 1) * head_dim] = rows.astype(out.dtype)
+
+
+def first_grad_kernel(scale, heads_kv, q, dout, attn, probs, *refs):
+    keys, values = refs[:BAND_BLOCKS], refs[BAND_BLOCKS : 2 * BAND_BLOCKS]
+    dq, outs = refs[2 * BAND_BLOCKS], refs[2 * BAND_BLOCKS + 1 :]
+    for head in range(heads_kv):
+
+        @pl.when(pl.program_id(0) == head)
         def _():
-            for copy in inward:
-                copy.wait()
-            for copy in outward:
-                copy.start()
-
-    dkey = dot_tn(dscore, q[...].reshape(count * tok, head_dim))
-    dvalue = dot_tn(weight, grad)
-
-    @pl.when(step == 0)
-    def _():
-        dk[...] = dkey
-        dv[...] = dvalue
-
-    @pl.when(step > 0)
-    def _():
-        dk[...] += dkey
-        dv[...] += dvalue
-
-    @pl.when(step == steps - 1)
-    def _():
-        for block, out in enumerate(outs):
-            rows = pl.ds(block * tok, tok)
-            out[:, :head_dim] = (dk[rows, :] * scale).astype(out.dtype)
-            out[:, head_dim:] = dv[rows, :].astype(out.dtype)
-        if last:
-            for copy in outward:
-                copy.wait()
-
-
-def attention_grad(queries, dout, attn, probs, bands, which, given, heads_kv, scale):
+            if head < heads_kv - 1:
+                dq[...], dkey = score_grads(scale, q, dout, attn, probs, keys, values)
+                put(outs, heads_kv + head, dkey)
+            put(outs, head, value_grads(dout, probs))
+
+
+def last_grad_kernel(scale, core, q, dout, attn, probs, *refs):
+    keys, values = refs[:BAND_BLOCKS], refs[BAND_BLOCKS : 2 * BAND_BLOCKS]
+    _, here, back, dq = refs[2 * BAND_BLOCKS : 2 * BAND_BLOCKS + 4]
+    outs, (joined, held, sem) = refs[2 * BAND_BLOCKS + 4 : -3], refs[-3:]
+    inward = [pltpu.make_async_copy(r, held.at[i], sem.at[0, i]) for i, r in enumerate((here, back))]
+    outward = [
+        pltpu.make_async_copy(held.at[i], joined.at[0, :, at], sem.at[1, i])
+        for i, at in enumerate((core[0], 1 - core[0]))
+    ]
+    for copy in inward:
+        copy.start()
+    dquery, dkey = score_grads(scale, q, dout, attn, probs, keys, values)
+    for copy in inward:
+        copy.wait()
+    for copy in outward:
+        copy.start()
+    dq[...] = dquery
+    put(outs, 0, dkey)
+    for copy in outward:
+        copy.wait()
+
+
+def grad_specs(tok, head_dim, group, heads_kv, which):
+    span = BAND_BLOCKS * tok
+    flat = pl.BlockSpec((tok, group * head_dim), lambda h, *_: (0, which(h)))
+    keys = pl.BlockSpec((tok, head_dim), lambda h, *_: (0, which(h)))
+    values = pl.BlockSpec((tok, head_dim), lambda h, *_: (0, heads_kv + which(h)))
+    return (
+        [pl.BlockSpec((group, tok, head_dim), lambda h, *_: (which(h), 0, 0)), flat, flat]
+        + [pl.BlockSpec((group, tok, span), lambda h, *_: (which(h), 0, 0))]
+        + [keys] * BAND_BLOCKS
+        + [values] * BAND_BLOCKS
+    )
+
+
+def sums_shapes(tok, lanes):
+    return [jax.ShapeDtypeStruct((tok, lanes), BF16)] * (BAND_BLOCKS - 1) + [
+        jax.ShapeDtypeStruct((tok, lanes), F32)
+    ]
+
+
+def first_grads(queries, dout, attn, probs, bands, heads_kv, scale):
     heads, tok, head_dim = queries.shape
     group = heads // heads_kv
-    count = heads_a_step(HEADS_BACKWARD, group)
-    steps = group // count
-    keys = pl.BlockSpec((tok, head_dim), lambda h: (0, which))
-    values = pl.BlockSpec((tok, head_dim), lambda h: (0, heads_kv + which))
-    by_head = pl.BlockSpec((count, tok, head_dim), lambda h: (which * steps + h, 0, 0))
-    of_all = pl.BlockSpec((tok, count * head_dim), lambda h: (0, which * steps + h))
-    span = BAND_BLOCKS * tok
-    whole = pl.BlockSpec((tok, 2 * head_dim), lambda h: (0, 0))
+    lanes = (2 * heads_kv - 1) * head_dim
+    whole = pl.BlockSpec((tok, lanes), lambda h: (0, 0))
+    return pl.pallas_call(
+        functools.partial(first_grad_kernel, scale, heads_kv),
+        grid=(heads_kv,),
+        in_specs=grad_specs(tok, head_dim, group, heads_kv, lambda h: h),
+        out_specs=[pl.BlockSpec((group, tok, head_dim), lambda h: (jnp.minimum(h, heads_kv - 2), 0, 0))]
+        + [whole] * BAND_BLOCKS,
+        out_shape=[jax.ShapeDtypeStruct((heads, tok, head_dim), BF16)] + sums_shapes(tok, lanes),
+        compiler_params=params(),
+        cost_estimate=cost(tok, tok),
+        name="first_grads",
+    )(queries, dout, attn, probs, *bands, *bands)
+
+
+def last_grads(core, queries, dout, attn, probs, bands, grad_q, here, back, heads_kv, scale):
+    heads, tok, head_dim = queries.shape
+    group = heads // heads_kv
+    held, capacity, width = here.shape
     anywhere = pl.BlockSpec(memory_space=pl.ANY)
-    last = bool(given)
-    joined, extra = [], []
-    if last:
-        held, capacity, width = given[2].shape
-        joined = [jax.ShapeDtypeStruct((1, held, 2, capacity, width), BF16)]
-        extra = [pltpu.VMEM((2, held, capacity, width), BF16), pltpu.SemaphoreType.DMA((2, 2))]
-    return pl.pallas_call(
-        functools.partial(attention_grad_kernel, scale, steps, last),
-        grid=(steps,),
-        in_specs=[by_head, of_all, of_all]
-        + [pl.BlockSpec((count, tok, span), lambda h: (which * steps + h, 0, 0))]
-        + [keys] * BAND_BLOCKS
-        + [values] * BAND_BLOCKS
-        + ([anywhere, pl.BlockSpec(memory_space=pltpu.SMEM), anywhere, anywhere] if last else []),
-        out_specs=[by_head] + [whole] * BAND_BLOCKS + [anywhere] * len(joined),
+    whole = pl.BlockSpec((tok, head_dim), lambda h, *_: (0, 0))
+    return pl.pallas_call(
+        functools.partial(last_grad_kernel, scale),
+        grid_spec=pltpu.PrefetchScalarGridSpec(
+            num_scalar_prefetch=1,
+            grid=(1,),
+            in_specs=grad_specs(tok, head_dim, group, heads_kv, lambda h: heads_kv - 1) + [anywhere] * 3,
+            out_specs=[pl.BlockSpec((group, tok, head_dim), lambda h, *_: (heads_kv - 1, 0, 0))]
+            + [whole] * BAND_BLOCKS
+            + [anywhere],
+            scratch_shapes=[pltpu.VMEM((2, held, capacity, width), BF16), pltpu.SemaphoreType.DMA((2, 2))],
+        ),
         out_shape=[jax.ShapeDtypeStruct((heads, tok, head_dim), BF16)]
-        + [jax.ShapeDtypeStruct((tok, 2 * head_dim), BF16)] * (BAND_BLOCKS - 1)
-        + [jax.ShapeDtypeStruct((tok, 2 * head_dim), F32)]
-        + joined,
-        scratch_shapes=[pltpu.VMEM((span, head_dim), F32)] * 2 + extra,
-        input_output_aliases={4 + 2 * BAND_BLOCKS: 0} if last else {},
+        + sums_shapes(tok, head_dim)
+        + [jax.ShapeDtypeStruct((1, held, 2, capacity, width), BF16)],
+        input_output_aliases={5 + 2 * BAND_BLOCKS: 0},
         compiler_params=params(),
         cost_estimate=cost(tok, tok),
-        name="attention_grad",
-    )(queries, dout, attn, probs, *bands, *bands, *given)
+        name="last_grads",
+    )(core, queries, dout, attn, probs, *bands, *bands, grad_q, here, back)
 
 
 def pick_kernel(core, slots, here_ref, there_ref, gout, first, second, dgate):
@@ -602,24 +624,22 @@
     there = after([there], dattn)[0]
     back = swapped(there, "exp").reshape(held, capacity, width)
     here = here.reshape(held, capacity, width)
-    grads, totals, given = [], [], ()
-    for i in range(heads_kv):
-        if i == heads_kv - 1:
-            given = (grads[-1][0], core_arg, here, back)
-        grad = attention_grad(queries, dattn, attn, probs, bands, i, given, heads_kv, scale)
-        if i > 0:
-            totals[-1] = after(totals[-1], grad[0])
-        totals.append(exchanged(grad[BAND_BLOCKS - 1], grad[BAND_BLOCKS - 3]))
-        grads.append(grad)
-    grad_q = jnp.transpose(grads[-1][0], (1, 0, 2))
-    grad_expert = grads[-1][1 + BAND_BLOCKS]
-    totals = [combined(grad[BAND_BLOCKS - 2], *pair) for grad, pair in zip(grads, totals)]
-    sums = [
-        (grad[BAND_BLOCKS] + (near.astype(F32) + far.astype(F32))).astype(BF16)
-        for grad, (near, far) in zip(grads, totals)
-    ]
-    grad_k = jnp.stack([t[:, :head_dim] for t in sums], axis=1)
-    grad_v = jnp.stack([t[:, head_dim:] for t in sums], axis=1)
+    early = first_grads(queries, dattn, attn, probs, bands, heads_kv, scale)
+    early_by = exchanged(early[BAND_BLOCKS - 1], early[BAND_BLOCKS - 3])
+    late = last_grads(core_arg, queries, dattn, attn, probs, bands, early[0], here, back, heads_kv, scale)
+    early_by = after(early_by, late[0])
+    late_by = exchanged(late[BAND_BLOCKS - 1], late[BAND_BLOCKS - 3])
+    early_sum, early_part = combined(early[BAND_BLOCKS - 2], *early_by)
+    late_by = after(late_by, early_sum)
+    late_sum, late_part = combined(late[BAND_BLOCKS - 2], *late_by)
+    sums = []
+    for grad, onward, part in ((early, early_sum, early_part), (late, late_sum, late_part)):
+        moved = passed_along(onward, "ctx", -2)
+        sums.append((grad[BAND_BLOCKS] + (moved.astype(F32) + part.astype(F32))).astype(BF16))
+    sums = jnp.concatenate(sums, axis=1).reshape(tok, 2, heads_kv, head_dim)
+    grad_v, grad_k = sums[:, 0], sums[:, 1]
+    grad_q = jnp.transpose(late[0], (1, 0, 2))
+    grad_expert = late[1 + BAND_BLOCKS]
     return (mixed, grad_input, grad_expert, grad_q, grad_k, grad_v)
 
 

time: 180 us -> 184 us (1.022)
  Pallas kernels: 56.9 us -> 59.2 us
  starting transfers between devices: 29.2 us -> 31.2 us
    ppermute x4, waiting for transfers between devices: 7.75 us -> 11.2 us  [exchanged(): return (lax.ppermute(one, 'ctx', pairs), lax.ppermute(three, 'ctx', others))]
    ppermute x5, waiting for transfers between devices: 16.8 us -> 13.5 us  [passed_along(): lax.ppermute(value, axis, [(source, source + steps) for source in range(i...]
    pallas_call x2, Pallas kernels: 13.6 us -> 16 us  [the longest x1 8.33 us: first_grads(): pl.pallas_call(functools.partial(first_grad_kernel, scale, heads_kv), gri...]
    ppermute x4, starting transfers between devices: 5.9 us -> 7.91 us  [exchanged(): return (lax.ppermute(one, 'ctx', pairs), lax.ppermute(three, 'ctx', others))]
    unnamed x47 -> x43, local copies, waits for them, and re-layouts: 9.78 us -> 8.19 us
  transfers between devices with their start and end apart: 27 -> 27, of which waited for: 14 -> 15; matrix products, arithmetic and copies ran while one was open for 6% -> 6% of each run, Pallas kernels for 19% -> 20%
where the time goes in v7:
time: 184 us; the launch traced here: 183 us
  waiting for transfers between devices  72 us (39%)
  Pallas kernels  59.2 us (32%)
  starting transfers between devices  31.2 us (17%)
  local copies, waits for them, and re-layouts  16 us (9%)
  other arithmetic  3.22 us (2%)
    ppermute x4, waiting for transfers between devices, gathered(): lax.ppermute(value, 'ctx', [(c, (c + 2) % count) for c in range(count)])  38.3 us
    ppermute x5, waiting for transfers between devices, passed_along(): lax.ppermute(value, axis, [(source, source + steps) for source in range(i...  13.5 us
    ppermute x4, waiting for transfers between devices, exchanged(): return (lax.ppermute(one, 'ctx', pairs), lax.ppermute(three, 'ctx', others))  11.2 us
    pallas_call x1, Pallas kernels, attention(): pl.pallas_call(functools.partial(attention_kernel, scale), grid_spec=pltp...  10.9 us
    pallas_call x1, Pallas kernels, dattention(): pl.pallas_call(functools.partial(dattn_kernel, plan, len(arrays)), grid_s...  8.63 us
    pallas_call x1, Pallas kernels, first_grads(): pl.pallas_call(functools.partial(first_grad_kernel, scale, heads_kv), gri...  8.33 us
    pallas_call x1, Pallas kernels, project(): pl.pallas_call(functools.partial(project_kernel, plan, len(arrays), len(a...  8.31 us
    unnamed x43, local copies, waits for them, and re-layouts  8.19 us
  transfers between devices with their start and end apart: 27, of which 15 were waited for; matrix products, arithmetic and copies ran while one was open for 6% of the time, Pallas kernels for 20%

profile of v7, /device:TPU:4, one launch (start us, length us, event | category | flops | bytes accessed | tf_op | source)
XLA Modules:
  0.0 182.7 jit_solution(13588519509796589149)
XLA Ops:
  0.7 1.9 %constant_dynamic-slice_fusion = bf16[6,16,3072]{2,1,0:T(8,128)(2,1)} fusion(bf16[12,16,3072]{2,1,0:T(8,128)(2,1)} %refs_0_.1, s32[]{:T(128)S(6)} %select_n.71), kind=kLoop, calls=%fused_computation.22 | loop fusion | bytes 1179652 | tf_op jit(solution)/shard_map/dynamic_slice | solution.py:77
  2.6 2.1 %collective-permute-start = (bf16[6,16,3072]{2,1,0:T(8,128)(2,1)}, bf16[6,16,3072]{2,1,0:T(8,128)(2,1)}, u32[]{:S(2)}, u32[]{:S(2)}) collective-permute-start(bf16[6,16,3072]{2,1,0:T(8,128)(2,1)} %constant_dynamic-slice_fusion), channel_id=1, source_target_pairs={{0,4},{2,6},{4,8},{6,10},{8,12},{10,14},{12,0},{14,2},{1,5},{3,7},... | collective-permute-start | bytes 1769480 | tf_op jit(solution)/shard_map/ppermute | solution.py:74
  8.2 2.3 %pad.8.router = bf16[3072,128]{1,0:T(8,128)(2,1)} pad(bf16[3072,8]{1,0:T(8,128)(2,1)} %copy.30, bf16[]{:T(256)} %constant.92.clone.1), padding=0_0x0_120 | pad | bytes 835586 | tf_op jit(solution)/shard_map/jit(_pad)/pad | solution.py:587
  12.4 5.6 %collective-permute-done.1.refs_5_.refs_4_ = bf16[6,16,3072]{2,1,0:T(8,128)(2,1)} collective-permute-done((bf16[6,16,3072]{2,1,0:T(8,128)(2,1)}, bf16[6,16,3072]{2,1,0:T(8,128)(2,1)}, u32[]{:S(2)}, u32[]{:S(2)}) %collective-permute-start.1) | collective-permute-done | bytes 589856 | tf_op jit(solution)/shard_map/ppermute | solution.py:75
  18.0 2.1 %collective-permute-done.refs_2_.refs_1_ = bf16[6,16,3072]{2,1,0:T(8,128)(2,1)} collective-permute-done((bf16[6,16,3072]{2,1,0:T(8,128)(2,1)}, bf16[6,16,3072]{2,1,0:T(8,128)(2,1)}, u32[]{:S(2)}, u32[]{:S(2)}) %collective-permute-start) | collective-permute-done | bytes 589856 | tf_op jit(solution)/shard_map/ppermute | solution.py:74
  20.1 1.6 collective-permute-start.7
  23.2 14.8 %collective-permute-done.2.refs_3_.refs_2_ = bf16[6,16,3072]{2,1,0:T(8,128)(2,1)} collective-permute-done((bf16[6,16,3072]{2,1,0:T(8,128)(2,1)}, bf16[6,16,3072]{2,1,0:T(8,128)(2,1)}, u32[]{:S(2)}, u32[]{:S(2)}) %collective-permute-start.2) | collective-permute-done | bytes 589856 | tf_op jit(solution)/shard_map/ppermute | solution.py:74
  38.0 1.7 copy-done.5
  40.4 1.5 collective-permute-start.4
  43.4 4.8 %pick.1 = (bf16[128,3072]{1,0:T(8,128)(2,1)}, bf16[128,3072]{1,0:T(8,128)(2,1)}, f32[128,128]{1,0:T(8,128)}) custom-call(s32[1]{0:T(128)} %bitcast.10.core, s32[128,2]{1,0:T(8,128)} %copy.31.slots, bf16[1,4,2,64,3072]{4,3,2,1,0:T(8,128)(2,1)} %here_ref.1, bf16[1,4,2,64,3072]{4,3,2,1,0:T(8,128)(2,1)} %copy-done.5, bf16[128,3072]{1,0:T(8,128)(2,1)} %gout.5), custom_call_target="tpu_custom_call" | custom-call | flops 805306368 | bytes 6291456 | tf_op jit(solution)/shard_map/pick/pallas_call | solution.py:460
  48.2 8.4 %collective-permute-done.5.refs_4_.refs_3_ = bf16[6,16,3072]{2,1,0:T(8,128)(2,1)S(1)} collective-permute-done((bf16[6,16,3072]{2,1,0:T(8,128)(2,1)}, bf16[6,16,3072]{2,1,0:T(8,128)(2,1)S(1)}, u32[]{:S(2)}, u32[]{:S(2)}) %collective-permute-start.5) | collective-permute-done | bytes 589856 | tf_op jit(solution)/shard_map/ppermute | solution.py:74
  56.6 1.5 collective-permute-start.10
  58.1 1.5 collective-permute-start.14
  59.6 13.0 %collective-permute-done.8.refs_10_.refs_9_ = bf16[6,16,3072]{2,1,0:T(8,128)(2,1)S(1)} collective-permute-done((bf16[6,16,3072]{2,1,0:T(8,128)(2,1)}, bf16[6,16,3072]{2,1,0:T(8,128)(2,1)S(1)}, u32[]{:S(2)}, u32[]{:S(2)}) %collective-permute-start.8) | collective-permute-done | bytes 589856 | tf_op jit(solution)/shard_map/ppermute | solution.py:74
  72.7 1.9 %collective-permute-start.13 = (bf16[256,512]{1,0:T(8,128)(2,1)S(1)}, bf16[256,512]{1,0:T(8,128)(2,1)S(1)}, u32[]{:S(2)}, u32[]{:S(2)}) collective-permute-start(bf16[256,512]{1,0:T(8,128)(2,1)S(1)} %bitcast_dynamic-update-slice_fusion.refs_3_.refs_7_), channel_id=1, source_target_pairs={{0,2},{2,4},{4,6},{6,8},{8,10},{10,12},{12,14},{1,3},{3,5},{5,7},{... | collective-permute-start | bytes 786440 | tf_op jit(solution)/shard_map/ppermute | solution.py:39
  74.6 2.1 %collective-permute-start.15 = (bf16[6,16,3072]{2,1,0:T(8,128)(2,1)}, bf16[6,16,3072]{2,1,0:T(8,128)(2,1)}, u32[]{:S(2)}, u32[]{:S(2)}) collective-permute-start(bf16[6,16,3072]{2,1,0:T(8,128)(2,1)} %collective-permute-done.6.refs_9_.refs_8_), channel_id=1, source_target_pairs={{0,2},{2,0},{4,6},{6,4},{8,10},{10,8},{12,14},{14,12},{1,3},{3,1},... | collective-permute-start | bytes 1769480 | tf_op jit(solution)/shard_map/ppermute | solution.py:75
  80.0 3.8 %collective-permute-done.13.refs_2_.refs_6_ = bf16[256,512]{1,0:T(8,128)(2,1)S(1)} collective-permute-done((bf16[256,512]{1,0:T(8,128)(2,1)S(1)}, bf16[256,512]{1,0:T(8,128)(2,1)S(1)}, u32[]{:S(2)}, u32[]{:S(2)}) %collective-permute-start.13) | collective-permute-done | bytes 262176 | tf_op jit(solution)/shard_map/ppermute | solution.py:39
  86.6 3.2 %collective-permute-done.11.refs_0_.refs_4_ = bf16[256,512]{1,0:T(8,128)(2,1)S(1)} collective-permute-done((bf16[256,512]{1,0:T(8,128)(2,1)S(1)}, bf16[256,512]{1,0:T(8,128)(2,1)S(1)}, u32[]{:S(2)}, u32[]{:S(2)}) %collective-permute-start.11) | collective-permute-done | bytes 262176 | tf_op jit(solution)/shard_map/ppermute | solution.py:39
  90.5 10.9 %attention.1 = (bf16[256,1536]{1,0:T(8,128)(2,1)}, bf16[12,256,1024]{2,1,0:T(8,128)(2,1)}) custom-call(s32[1]{0:T(128)} %bitcast.11.place, bf16[12,256,128]{2,1,0:T(8,128)(2,1)} %bitcast.32, bf16[256,512]{1,0:T(8,128)(2,1)} %copy-done.3, bf16[256,512]{1,0:T(8,128)(2,1)} %copy-done.2, bf16[256,512]{1,0:T(8,128)(2,1)} %copy-done.1, bf16[256,512]{1,0:T(8,128)(2,1)} %copy-done, ...), custom_call_target="tpu_custom_call" | custom-call | flops 1610612736 | bytes 6291456 | tf_op jit(solution)/shard_map/attention/pallas_call | solution.py:280
  102.3 8.3 %project.1 = (f32[128,3072]{1,0:T(8,128)}, bf16[128,3072]{1,0:T(8,128)(2,1)}) custom-call(s32[11]{0:T(128)} %stack.43.table, s32[1]{0:T(128)} %bitcast.10.core, bf16[256,1536]{1,0:T(8,128)(2,1)} %get-tuple-element.58.refs_0_.attn, bf16[12,16,3072]{2,1,0:T(8,128)(2,1)} %refs_0_.1, bf16[6,16,3072]{2,1,0:T(8,128)(2,1)} %collective-permute-done.refs_2_.refs_1_, ...), custom_call_target="tpu_custom_call" | custom-call | flops 2415919104 | bytes 9437184 | tf_op jit(solution)/shard_map/project/pallas_call | solution.py:160
  110.7 2.5 %collective-permute-done.18.recv = bf16[128,3072]{1,0:T(8,128)(2,1)S(1)} collective-permute-done((bf16[128,3072]{1,0:T(8,128)(2,1)}, bf16[128,3072]{1,0:T(8,128)(2,1)S(1)}, u32[]{:S(2)}, u32[]{:S(2)}) %collective-permute-start.18) | collective-permute-done | bytes 786464 | tf_op jit(solution)/shard_map/ppermute | solution.py:43
  114.0 6.2 %middle.1 = (bf16[128,3072]{1,0:T(8,128)(2,1)}, bf16[128,3072]{1,0:T(8,128)(2,1)}, f32[128,128]{1,0:T(8,128)}) custom-call(s32[128,2]{1,0:T(8,128)} %copy-done.14, f32[128,3072]{1,0:T(8,128)} %get-tuple-element.62.own, bf16[128,3072]{1,0:T(8,128)(2,1)} %copy-done.13, bf16[128,3072]{1,0:T(8,128)(2,1)} %stream.1, bf16[128,3072]{1,0:T(8,128)(2,1)} %get-tuple-element.64.first, ...), custom_call_target="tpu_custom_call" | custom-call | flops 402653184 | bytes 7864320 | tf_op jit(solution)/shard_map/middle/pallas_call | solution.py:516
  120.4 4.5 %spread.1 = (bf16[256,3072]{1,0:T(8,128)(2,1)}, bf16[256,3072]{1,0:T(8,128)(2,1)}) custom-call(s32[2,128]{1,0:T(2,128)} %bitcast.41, f32[128,128]{1,0:T(8,128)} %get-tuple-element.70.gates, bf16[128,3072]{1,0:T(8,128)(2,1)} %gout.5), custom_call_target="tpu_custom_call" | custom-call | flops 805306368 | bytes 3932160 | tf_op jit(solution)/shard_map/spread/pallas_call | solution.py:546
  125.8 8.6 %dattention.1.dout = bf16[256,1536]{1,0:T(8,128)(2,1)} custom-call(s32[11]{0:T(128)} %stack.43.table, s32[1]{0:T(128)} %bitcast.10.core, bf16[128,3072]{1,0:T(8,128)(2,1)} %get-tuple-element.42.own, bf16[128,3072]{1,0:T(8,128)(2,1)} %copy-done.12, bf16[12,16,3072]{2,1,0:T(8,128)(2,1)} %refs_0_.1, bf16[6,16,3072]{2,1,0:T(8,128)(2,1)} %collective-permute-done.refs_2_.refs_1_, ...), custom_call_target="tpu_custom_call" | custom-call | flops 2415919104 | bytes 9437184 | tf_op jit(solution)/shard_map/dattention/pallas_call | solution.py:216
  134.9 8.3 %first_grads.1 = (bf16[12,256,128]{2,1,0:T(8,128)(2,1)}, bf16[256,384]{1,0:T(8,128)(2,1)}, bf16[256,384]{1,0:T(8,128)(2,1)}, bf16[256,384]{1,0:T(8,128)(2,1)}, f32[256,384]{1,0:T(8,128)}) custom-call(bf16[12,256,128]{2,1,0:T(8,128)(2,1)} %bitcast.33, bf16[256,1536]{1,0:T(8,128)(2,1)} %dattention.1.dout, bf16[256,1536]{1,0:T(8,128)(2,1)} %get-tuple-element.58.refs_0_.attn, ...), custom_call_target="tpu_custom_call" | custom-call | flops 256 | bytes 256 | tf_op jit(solution)/shard_map/first_grads/pallas_call | solution.py:385
  143.6 3.6 %collective-permute-start.22 = (bf16[256,384]{1,0:T(8,128)(2,1)}, bf16[256,384]{1,0:T(8,128)(2,1)S(1)}, u32[]{:S(2)}, u32[]{:S(2)}) collective-permute-start(bf16[256,384]{1,0:T(8,128)(2,1)} %get-tuple-element.79), channel_id=1, source_target_pairs={{2,0},{6,4},{8,2},{10,8},{12,6},{14,12},{3,1},{7,5},{9,3},{11,9},{... | collective-permute-start | bytes 589832 | tf_op jit(solution)/shard_map/ppermute | solution.py:50
  148.4 7.6 %last_grads.1 = (bf16[12,256,128]{2,1,0:T(8,128)(2,1)}, bf16[256,128]{1,0:T(8,128)(2,1)}, bf16[256,128]{1,0:T(8,128)(2,1)}, bf16[256,128]{1,0:T(8,128)(2,1)}, f3...) custom-call(s32[1]{0:T(128)} %bitcast.10.core, ...), custom_call_target="tpu_custom_call", output_to_operand_aliasing={{0}: (13, {})} | custom-call | flops 256 | bytes 256 | tf_op jit(solution)/shard_map/last_grads/pallas_call | solution.py:404
  156.0 5.7 %collective-permute-done.22 = bf16[256,384]{1,0:T(8,128)(2,1)S(1)} collective-permute-done((bf16[256,384]{1,0:T(8,128)(2,1)}, bf16[256,384]{1,0:T(8,128)(2,1)S(1)}, u32[]{:S(2)}, u32[]{:S(2)}) %collective-permute-start.22) | collective-permute-done | bytes 196640 | tf_op jit(solution)/shard_map/ppermute | solution.py:50
  161.7 3.9 %collective-permute-start.25 = (bf16[256,128]{1,0:T(8,128)(2,1)}, bf16[256,128]{1,0:T(8,128)(2,1)S(1)}, u32[]{:S(2)}, u32[]{:S(2)}) collective-permute-start(bf16[256,128]{1,0:T(8,128)(2,1)} %get-tuple-element.85), channel_id=1, source_target_pairs={{2,0},{6,4},{8,2},{10,8},{12,6},{14,12},{3,1},{7,5},{9,3},{11,9},{... | collective-permute-start | bytes 196616 | tf_op jit(solution)/shard_map/ppermute | solution.py:50
  166.9 4.4 %collective-permute-done.25 = bf16[256,128]{1,0:T(8,128)(2,1)S(1)} collective-permute-done((bf16[256,128]{1,0:T(8,128)(2,1)}, bf16[256,128]{1,0:T(8,128)(2,1)S(1)}, u32[]{:S(2)}, u32[]{:S(2)}) %collective-permute-start.25) | collective-permute-done | bytes 65568 | tf_op jit(solution)/shard_map/ppermute | solution.py:50
  174.7 3.9 %collective-permute-done.26 = bf16[256,128]{1,0:T(8,128)(2,1)S(1)} collective-permute-done((bf16[256,128]{1,0:T(8,128)(2,1)S(1)}, bf16[256,128]{1,0:T(8,128)(2,1)S(1)}, u32[]{:S(2)}, u32[]{:S(2)}) %collective-permute-start.26) | collective-permute-done | bytes 65568 | tf_op jit(solution)/shard_map/ppermute | solution.py:39
  179.6 2.0 %collective-permute-done.23 = bf16[256,384]{1,0:T(8,128)(2,1)S(1)} collective-permute-done((bf16[256,384]{1,0:T(8,128)(2,1)S(1)}, bf16[256,384]{1,0:T(8,128)(2,1)S(1)}, u32[]{:S(2)}, u32[]{:S(2)}) %collective-permute-start.23) | collective-permute-done | bytes 196640 | tf_op jit(solution)/shard_map/ppermute | solution.py:39
  (91 shorter events, 27.4 us)
Async XLA Ops:
  2.6 15.4 %collective-permute-start.1 = (bf16[6,16,3072]{2,1,0:T(8,128)(2,1)}, bf16[6,16,3072]{2,1,0:T(8,128)(2,1)}, u32[]{:S(2)}, u32[]{:S(2)}) collective-permute-start(bf16[6,16,3072]{2,1,0:T(8,128)(2,1)} %constant_dynamic-slice_fusion), channel_id=1, source_target_pairs={{0,2},{2,0},{4,6},{6,4},{8,10},{10,8},{12,14},{14,12},{1,3},{3,1},... | collective-permute-start | bytes 1769480 | tf_op jit(solution)/shard_map/ppermute | solution.py:75
  2.6 17.5 %collective-permute-start = (bf16[6,16,3072]{2,1,0:T(8,128)(2,1)}, bf16[6,16,3072]{2,1,0:T(8,128)(2,1)}, u32[]{:S(2)}, u32[]{:S(2)}) collective-permute-start(bf16[6,16,3072]{2,1,0:T(8,128)(2,1)} %constant_dynamic-slice_fusion), channel_id=1, source_target_pairs={{0,4},{2,6},{4,8},{6,10},{8,12},{10,14},{12,0},{14,2},{1,5},{3,7},... | collective-permute-start | bytes 1769480 | tf_op jit(solution)/shard_map/ppermute | solution.py:74
  7.0 32.6 %copy-start.19 = (s32[128,2]{0,1:T(2,128)}, s32[128,2]{0,1:T(2,128)S(1)}, u32[]{:S(2)}) copy-start(s32[128,2]{0,1:T(2,128)S(1)} %and_select_fusion) | copy-start | bytes 3076
  11.3 72.5 %copy-start = (bf16[256,512]{1,0:T(8,128)(2,1)}, bf16[256,512]{1,0:T(8,128)(2,1)S(1)}, u32[]{:S(2)}) copy-start(bf16[256,512]{1,0:T(8,128)(2,1)S(1)} %bitcast_dynamic-update-slice_fusion.refs_3_.refs_7_) | copy-start | bytes 786436
  20.1 17.9 %collective-permute-start.3 = (bf16[1,4,2,64,3072]{4,3,2,1,0:T(8,128)(2,1)S(1)}, bf16[1,4,2,64,3072]{4,3,2,1,0:T(8,128)(2,1)S(1)}, u32[]{:S(2)}, u32[]{:S(2)}) collective-permute-start(bf16[1,4,2,64,3072]{4,3,2,1,0:T(8,128)(2,1)S(1)} %copy-done.4), channel_id=1, source_target_pairs={{0,1},{1,0},{2,3},{3,2},{4,5},{5,4},{6,7},{7,6},{8,9},{9,8},{10,11... | collective-permute-start | bytes 9437192 | tf_op jit(solution)/shard_map/ppermute | solution.py:43
  20.1 17.9 %collective-permute-start.2 = (bf16[6,16,3072]{2,1,0:T(8,128)(2,1)}, bf16[6,16,3072]{2,1,0:T(8,128)(2,1)}, u32[]{:S(2)}, u32[]{:S(2)}) collective-permute-start(bf16[6,16,3072]{2,1,0:T(8,128)(2,1)} %collective-permute-done.refs_2_.refs_1_), channel_id=1, source_target_pairs={{0,4},{2,6},{4,8},{6,10},{8,12},{10,14},{12,0},{14,2},{1,5},{3,7},... | collective-permute-start | bytes 1769480 | tf_op jit(solution)/shard_map/ppermute | solution.py:74
  20.1 28.1 %collective-permute-start.7 = (bf16[6,16,3072]{2,1,0:T(8,128)(2,1)}, bf16[6,16,3072]{2,1,0:T(8,128)(2,1)}, u32[]{:S(2)}, u32[]{:S(2)}) collective-permute-start(bf16[6,16,3072]{2,1,0:T(8,128)(2,1)} %collective-permute-done.refs_2_.refs_1_), channel_id=1, source_target_pairs={{0,2},{2,0},{4,6},{6,4},{8,10},{10,8},{12,14},{14,12},{1,3},{3,1},... | collective-permute-start | bytes 1769480 | tf_op jit(solution)/shard_map/ppermute | solution.py:75
  21.7 26.5 %collective-permute-start.6 = (bf16[6,16,3072]{2,1,0:T(8,128)(2,1)}, bf16[6,16,3072]{2,1,0:T(8,128)(2,1)}, u32[]{:S(2)}, u32[]{:S(2)}) collective-permute-start(bf16[6,16,3072]{2,1,0:T(8,128)(2,1)} %collective-permute-done.refs_2_.refs_1_), channel_id=1, source_target_pairs={{0,16},{16,0},{1,17},{17,1},{2,18},{18,2},{3,19},{19,3},{4,20},{20... | collective-permute-start | bytes 1769480 | tf_op jit(solution)/shard_map/ppermute | solution.py:43
  39.6 17.0 %collective-permute-start.5 = (bf16[6,16,3072]{2,1,0:T(8,128)(2,1)}, bf16[6,16,3072]{2,1,0:T(8,128)(2,1)S(1)}, u32[]{:S(2)}, u32[]{:S(2)}) collective-permute-start(bf16[6,16,3072]{2,1,0:T(8,128)(2,1)} %collective-permute-done.2.refs_3_.refs_2_), channel_id=1, source_target_pairs={{0,4},{2,6},{4,8},{6,10},{8,12},{10,14},{12,0},{14,2},{1,5},{3,7},... | collective-permute-start | bytes 1769480 | tf_op jit(solution)/shard_map/ppermute | solution.py:74
  40.4 19.2 %collective-permute-start.4 = (bf16[6,16,3072]{2,1,0:T(8,128)(2,1)}, bf16[6,16,3072]{2,1,0:T(8,128)(2,1)S(1)}, u32[]{:S(2)}, u32[]{:S(2)}) collective-permute-start(bf16[6,16,3072]{2,1,0:T(8,128)(2,1)} %collective-permute-done.2.refs_3_.refs_2_), channel_id=1, source_target_pairs={{0,2},{2,0},{4,6},{6,4},{8,10},{10,8},{12,14},{14,12},{1,3},{3,1},... | collective-permute-start | bytes 1769480 | tf_op jit(solution)/shard_map/ppermute | solution.py:75
  41.9 17.7 %collective-permute-start.9 = (bf16[6,16,3072]{2,1,0:T(8,128)(2,1)}, bf16[6,16,3072]{2,1,0:T(8,128)(2,1)S(1)}, u32[]{:S(2)}, u32[]{:S(2)}) collective-permute-start(bf16[6,16,3072]{2,1,0:T(8,128)(2,1)} %collective-permute-done.1.refs_5_.refs_4_), channel_id=1, source_target_pairs={{0,16},{16,0},{1,17},{17,1},{2,18},{18,2},{3,19},{19,3},{4,20},{20... | collective-permute-start | bytes 1769480 | tf_op jit(solution)/shard_map/ppermute | solution.py:43
  56.6 45.7 %copy-start.6 = (bf16[6,16,3072]{2,1,0:T(8,128)(2,1)}, bf16[6,16,3072]{2,1,0:T(8,128)(2,1)S(1)}, u32[]{:S(2)}) copy-start(bf16[6,16,3072]{2,1,0:T(8,128)(2,1)S(1)} %collective-permute-done.5.refs_4_.refs_3_) | copy-start | bytes 1769476
  56.6 16.1 %collective-permute-start.8 = (bf16[6,16,3072]{2,1,0:T(8,128)(2,1)}, bf16[6,16,3072]{2,1,0:T(8,128)(2,1)S(1)}, u32[]{:S(2)}, u32[]{:S(2)}) collective-permute-start(bf16[6,16,3072]{2,1,0:T(8,128)(2,1)} %collective-permute-done.6.refs_9_.refs_8_), channel_id=1, source_target_pairs={{0,4},{2,6},{4,8},{6,10},{8,12},{10,14},{12,0},{14,2},{1,5},{3,7},... | collective-permute-start | bytes 1769480 | tf_op jit(solution)/shard_map/ppermute | solution.py:74
  56.6 16.1 %collective-permute-start.10 = (bf16[6,16,3072]{2,1,0:T(8,128)(2,1)S(1)}, bf16[6,16,3072]{2,1,0:T(8,128)(2,1)S(1)}, u32[]{:S(2)}, u32[]{:S(2)}) collective-permute-start(bf16[6,16,3072]{2,1,0:T(8,128)(2,1)S(1)} %collective-permute-done.5.refs_4_.refs_3_), channel_id=1, source_target_pairs={{0,16},{16,0},{1,17},{17,1},{2,18},{18,2},{3,19},{19,3},{4,20},{20... | collective-permute-start | bytes 1769480 | tf_op jit(solution)/shard_map/ppermute | solution.py:43
  58.1 16.5 %collective-permute-start.14 = (bf16[6,16,3072]{2,1,0:T(8,128)(2,1)S(1)}, bf16[6,16,3072]{2,1,0:T(8,128)(2,1)}, u32[]{:S(2)}, u32[]{:S(2)}) collective-permute-start(bf16[6,16,3072]{2,1,0:T(8,128)(2,1)S(1)} %collective-permute-done.5.refs_4_.refs_3_), channel_id=1, source_target_pairs={{0,2},{2,0},{4,6},{6,4},{8,10},{10,8},{12,14},{14,12},{1,3},{3,1},... | collective-permute-start | bytes 1769480 | tf_op jit(solution)/shard_map/ppermute | solution.py:75
  59.6 42.6 %copy-start.8 = (bf16[6,16,3072]{2,1,0:T(8,128)(2,1)}, bf16[6,16,3072]{2,1,0:T(8,128)(2,1)S(1)}, u32[]{:S(2)}) copy-start(bf16[6,16,3072]{2,1,0:T(8,128)(2,1)S(1)} %collective-permute-done.9.refs_12_.refs_11_) | copy-start | bytes 1769476
  59.6 42.6 %copy-start.7 = (bf16[6,16,3072]{2,1,0:T(8,128)(2,1)}, bf16[6,16,3072]{2,1,0:T(8,128)(2,1)S(1)}, u32[]{:S(2)}) copy-start(bf16[6,16,3072]{2,1,0:T(8,128)(2,1)S(1)} %collective-permute-done.4.refs_7_.refs_6_) | copy-start | bytes 1769476
  72.7 11.1 %collective-permute-start.13 = (bf16[256,512]{1,0:T(8,128)(2,1)S(1)}, bf16[256,512]{1,0:T(8,128)(2,1)S(1)}, u32[]{:S(2)}, u32[]{:S(2)}) collective-permute-start(bf16[256,512]{1,0:T(8,128)(2,1)S(1)} %bitcast_dynamic-update-slice_fusion.refs_3_.refs_7_), channel_id=1, source_target_pairs={{0,2},{2,4},{4,6},{6,8},{8,10},{10,12},{12,14},{1,3},{3,5},{5,7},{... | collective-permute-start | bytes 786440 | tf_op jit(solution)/shard_map/ppermute | solution.py:39
  74.6 26.8 %collective-permute-start.15 = (bf16[6,16,3072]{2,1,0:T(8,128)(2,1)}, bf16[6,16,3072]{2,1,0:T(8,128)(2,1)}, u32[]{:S(2)}, u32[]{:S(2)}) collective-permute-start(bf16[6,16,3072]{2,1,0:T(8,128)(2,1)} %collective-permute-done.6.refs_9_.refs_8_), channel_id=1, source_target_pairs={{0,2},{2,0},{4,6},{6,4},{8,10},{10,8},{12,14},{14,12},{1,3},{3,1},... | collective-permute-start | bytes 1769480 | tf_op jit(solution)/shard_map/ppermute | solution.py:75
  76.7 24.7 %collective-permute-start.17 = (bf16[6,16,3072]{2,1,0:T(8,128)(2,1)}, bf16[6,16,3072]{2,1,0:T(8,128)(2,1)}, u32[]{:S(2)}, u32[]{:S(2)}) collective-permute-start(bf16[6,16,3072]{2,1,0:T(8,128)(2,1)} %collective-permute-done.14.refs_8_.refs_7_), channel_id=1, source_target_pairs={{0,16},{16,0},{1,17},{17,1},{2,18},{18,2},{3,19},{19,3},{4,20},{20... | collective-permute-start | bytes 1769480 | tf_op jit(solution)/shard_map/ppermute | solution.py:43
  78.2 24.1 %collective-permute-start.16 = (bf16[6,16,3072]{2,1,0:T(8,128)(2,1)S(1)}, bf16[6,16,3072]{2,1,0:T(8,128)(2,1)}, u32[]{:S(2)}, u32[]{:S(2)}) collective-permute-start(bf16[6,16,3072]{2,1,0:T(8,128)(2,1)S(1)} %collective-permute-done.4.refs_7_.refs_6_), channel_id=1, source_target_pairs={{0,16},{16,0},{1,17},{17,1},{2,18},{18,2},{3,19},{19,3},{4,20},{20... | collective-permute-start | bytes 1769480 | tf_op jit(solution)/shard_map/ppermute | solution.py:43
  78.7 7.9 %collective-permute-start.12 = (bf16[256,512]{1,0:T(8,128)(2,1)S(1)}, bf16[256,512]{1,0:T(8,128)(2,1)S(1)}, u32[]{:S(2)}, u32[]{:S(2)}) collective-permute-start(bf16[256,512]{1,0:T(8,128)(2,1)S(1)} %bitcast_dynamic-update-slice_fusion.refs_3_.refs_7_), channel_id=1, source_target_pairs={{0,4},{2,6},{4,8},{6,10},{8,12},{10,14},{1,5},{3,7},{5,9},{7,11},{... | collective-permute-start | bytes 786440 | tf_op jit(solution)/shard_map/ppermute | solution.py:39
  83.8 6.0 %collective-permute-start.11 = (bf16[256,512]{1,0:T(8,128)(2,1)S(1)}, bf16[256,512]{1,0:T(8,128)(2,1)S(1)}, u32[]{:S(2)}, u32[]{:S(2)}) collective-permute-start(bf16[256,512]{1,0:T(8,128)(2,1)S(1)} %bitcast_dynamic-update-slice_fusion.refs_3_.refs_7_), channel_id=1, source_target_pairs={{0,6},{2,8},{4,10},{6,12},{8,14},{1,7},{3,9},{5,11},{7,13},{9,15},... | collective-permute-start | bytes 786440 | tf_op jit(solution)/shard_map/ppermute | solution.py:39
  110.6 2.6 %collective-permute-start.18 = (bf16[128,3072]{1,0:T(8,128)(2,1)}, bf16[128,3072]{1,0:T(8,128)(2,1)S(1)}, u32[]{:S(2)}, u32[]{:S(2)}) collective-permute-start(bf16[128,3072]{1,0:T(8,128)(2,1)} %get-tuple-element.63), channel_id=1, source_target_pairs={{0,1},{1,0},{2,3},{3,2},{4,5},{5,4},{6,7},{7,6},{8,9},{9,8},{10,11... | collective-permute-start | bytes 2359304 | tf_op jit(solution)/shard_map/ppermute | solution.py:43
  120.2 4.7 %collective-permute-start.19 = (bf16[128,3072]{1,0:T(8,128)(2,1)}, bf16[128,3072]{1,0:T(8,128)(2,1)S(1)}, u32[]{:S(2)}, u32[]{:S(2)}) collective-permute-start(bf16[128,3072]{1,0:T(8,128)(2,1)} %get-tuple-element.42.own), channel_id=1, source_target_pairs={{0,1},{1,0},{2,3},{3,2},{4,5},{5,4},{6,7},{7,6},{8,9},{9,8},{10,11... | collective-permute-start | bytes 2359304 | tf_op jit(solution)/shard_map/ppermute | solution.py:43
  134.4 12.8 %collective-permute-start.20 = (bf16[256,3072]{1,0:T(8,128)(2,1)}, bf16[256,3072]{1,0:T(8,128)(2,1)S(1)}, u32[]{:S(2)}, u32[]{:S(2)}) collective-permute-start(bf16[256,3072]{1,0:T(8,128)(2,1)} %get-tuple-element.73), channel_id=1, source_target_pairs={{0,1},{1,0},{2,3},{3,2},{4,5},{5,4},{6,7},{7,6},{8,9},{9,8},{10,11... | collective-permute-start | bytes 4718600 | tf_op jit(solution)/shard_map/ppermute | solution.py:43
  143.2 12.8 %collective-permute-start.21 = (bf16[256,384]{1,0:T(8,128)(2,1)}, bf16[256,384]{1,0:T(8,128)(2,1)S(1)}, u32[]{:S(2)}, u32[]{:S(2)}) collective-permute-start(bf16[256,384]{1,0:T(8,128)(2,1)} %get-tuple-element.78), channel_id=1, source_target_pairs={{0,2},{2,0},{4,6},{6,4},{8,10},{10,8},{12,14},{14,12},{1,3},{3,1},... | collective-permute-start | bytes 589832 | tf_op jit(solution)/shard_map/ppermute | solution.py:50
  143.6 18.1 %collective-permute-start.22 = (bf16[256,384]{1,0:T(8,128)(2,1)}, bf16[256,384]{1,0:T(8,128)(2,1)S(1)}, u32[]{:S(2)}, u32[]{:S(2)}) collective-permute-start(bf16[256,384]{1,0:T(8,128)(2,1)} %get-tuple-element.79), channel_id=1, source_target_pairs={{2,0},{6,4},{8,2},{10,8},{12,6},{14,12},{3,1},{7,5},{9,3},{11,9},{... | collective-permute-start | bytes 589832 | tf_op jit(solution)/shard_map/ppermute | solution.py:50
  161.7 5.2 %collective-permute-start.24 = (bf16[256,128]{1,0:T(8,128)(2,1)}, bf16[256,128]{1,0:T(8,128)(2,1)S(1)}, u32[]{:S(2)}, u32[]{:S(2)}) collective-permute-start(bf16[256,128]{1,0:T(8,128)(2,1)} %get-tuple-element.84), channel_id=1, source_target_pairs={{0,2},{2,0},{4,6},{6,4},{8,10},{10,8},{12,14},{14,12},{1,3},{3,1},... | collective-permute-start | bytes 196616 | tf_op jit(solution)/shard_map/ppermute | solution.py:50
  161.7 9.5 %collective-permute-start.25 = (bf16[256,128]{1,0:T(8,128)(2,1)}, bf16[256,128]{1,0:T(8,128)(2,1)S(1)}, u32[]{:S(2)}, u32[]{:S(2)}) collective-permute-start(bf16[256,128]{1,0:T(8,128)(2,1)} %get-tuple-element.85), channel_id=1, source_target_pairs={{2,0},{6,4},{8,2},{10,8},{12,6},{14,12},{3,1},{7,5},{9,3},{11,9},{... | collective-permute-start | bytes 196616 | tf_op jit(solution)/shard_map/ppermute | solution.py:50
  172.1 6.5 %collective-permute-start.26 = (bf16[256,128]{1,0:T(8,128)(2,1)S(1)}, bf16[256,128]{1,0:T(8,128)(2,1)S(1)}, u32[]{:S(2)}, u32[]{:S(2)}) collective-permute-start(bf16[256,128]{1,0:T(8,128)(2,1)S(1)} %add_convert_fusion.3), channel_id=1, source_target_pairs={{4,0},{6,2},{8,4},{10,6},{12,8},{14,10},{5,1},{7,3},{9,5},{11,7},{... | collective-permute-start | bytes 196616 | tf_op jit(solution)/shard_map/ppermute | solution.py:39
  173.4 8.2 %collective-permute-start.23 = (bf16[256,384]{1,0:T(8,128)(2,1)S(1)}, bf16[256,384]{1,0:T(8,128)(2,1)S(1)}, u32[]{:S(2)}, u32[]{:S(2)}) collective-permute-start(bf16[256,384]{1,0:T(8,128)(2,1)S(1)} %add_convert_fusion.1), channel_id=1, source_target_pairs={{4,0},{6,2},{8,4},{10,6},{12,8},{14,10},{5,1},{7,3},{9,5},{11,7},{... | collective-permute-start | bytes 589832 | tf_op jit(solution)/shard_map/ppermute | solution.py:39
  (15 other events, 129.9 us)

commit v8 on v6

--- a/solution.py
+++ b/solution.py
@@ -171,7 +171,7 @@
             ],
         ),
         out_shape=[jax.ShapeDtypeStruct((rows, width), F32), jax.ShapeDtypeStruct((rows, width), BF16)],
-        compiler_params=params(),
+        compiler_params=params(20 << 20),
         cost_estimate=cost(2 * tok * heads * head_dim * width, 2 * heads * head_dim * width),
         name="project",
     )(table, core, *attn, *arrays)
@@ -229,7 +229,7 @@
             ],
         ),
         out_shape=jax.ShapeDtypeStruct((2 * rows, heads * head_dim), BF16),
-        compiler_params=params(),
+        compiler_params=params(20 << 20),
         cost_estimate=cost(4 * rows * heads * head_dim * width, 2 * heads * head_dim * width),
         name="dattention",
     )(table, core, own, recv, *arrays)
@@ -497,7 +497,7 @@
         in_specs=[by_row(2)] + [by_row(width)] * 6 + [by_row(128), whole(router), whole(router_t)],
         out_specs=[by_row(width), by_row(width), by_row(128)],
         out_shape=[jax.ShapeDtypeStruct((rows, width), BF16)] * 2 + [jax.ShapeDtypeStruct((rows, 128), F32)],
-        compiler_params=params(),
+        compiler_params=params(20 << 20),
         cost_estimate=cost(2 * rows * 128 * width * 4, 20 * rows * width),
         name="middle",
     )(routes, own, recv, stream, first, second, grad_out, dgate, router, router_t)
@@ -531,7 +531,7 @@
         ],
         out_specs=[by_column(room)] * 2,
         out_shape=[jax.ShapeDtypeStruct((room, width), BF16)] * 2,
-        compiler_params=params(),
+        compiler_params=params(20 << 20),
         cost_estimate=cost(8 * rows * room * width, 2 * rows * width + 4 * room * width),
         name="spread",
     )(slots_t, gates, grad_out)
@@ -618,8 +618,8 @@
         (grad[BAND_BLOCKS] + (near.astype(F32) + far.astype(F32))).astype(BF16)
         for grad, (near, far) in zip(grads, totals)
     ]
-    grad_k = jnp.stack([t[:, :head_dim] for t in sums], axis=1)
-    grad_v = jnp.stack([t[:, head_dim:] for t in sums], axis=1)
+    join = lambda lanes: jnp.concatenate([t[:, lanes] for t in sums], axis=1).reshape(tok, heads_kv, head_dim)
+    grad_k, grad_v = join(slice(0, head_dim)), join(slice(head_dim, None))
     return (mixed, grad_input, grad_expert, grad_q, grad_k, grad_v)
 
 

time: 180 us -> 171 us (0.950)
  Pallas kernels: 56.9 us -> 49.2 us
  starting transfers between devices: 29.2 us -> 31.1 us
    pallas_call x1, Pallas kernels: 6.19 us -> 3.51 us  [middle(): pl.pallas_call(functools.partial(middle_kernel, experts), grid=(rows // s...]
    ppermute x5, waiting for transfers between devices: 5.6 us -> 7.83 us  [gathered(): lax.ppermute(value, 'ctx', [(c, c ^ 1) for c in range(count)])]
    pad x1, local copies, waits for them, and re-layouts: 2.26 us -> 0.16 us  [local(): router = jnp.pad(w_router, ((0, 0), (0, 128 - experts)))]
    pallas_call x1, Pallas kernels: 8.31 us -> 6.22 us  [project(): pl.pallas_call(functools.partial(project_kernel, plan, len(arrays), len(a...]
    pallas_call x1, Pallas kernels: 8.63 us -> 6.7 us  [dattention(): pl.pallas_call(functools.partial(dattn_kernel, plan, len(arrays)), grid_s...]
  transfers between devices with their start and end apart: 27 -> 27, of which waited for: 14 -> 14; matrix products, arithmetic and copies ran while one was open for 6% -> 4% of each run, Pallas kernels for 19% -> 19%
where the time goes in v8:
time: 171 us; the launch traced here: 169 us
  waiting for transfers between devices  71.1 us (42%)
  Pallas kernels  49.2 us (29%)
  starting transfers between devices  31.1 us (18%)
  local copies, waits for them, and re-layouts  15.1 us (9%)
    ppermute x4, waiting for transfers between devices, gathered(): lax.ppermute(value, 'ctx', [(c, (c + 2) % count) for c in range(count)])  37.2 us
    ppermute x5, waiting for transfers between devices, passed_along(): lax.ppermute(value, axis, [(source, source + steps) for source in range(i...  15.6 us
    pallas_call x2, Pallas kernels, attention_grad(): pl.pallas_call(functools.partial(attention_grad_kernel, scale, steps, las...  13.6 us
    pallas_call x1, Pallas kernels, attention(): pl.pallas_call(functools.partial(attention_kernel, scale), grid_spec=pltp...  11.2 us
    unnamed x47, local copies, waits for them, and re-layouts  9.68 us
    ppermute x5, starting transfers between devices, passed_along(): lax.ppermute(value, axis, [(source, source + steps) for source in range(i...  8.52 us
    ppermute x5, waiting for transfers between devices, gathered(): lax.ppermute(value, 'ctx', [(c, c ^ 1) for c in range(count)])  7.83 us
    ppermute x5, starting transfers between devices, gathered(): lax.ppermute(value, 'ctx', [(c, c ^ 1) for c in range(count)])  7.34 us
  transfers between devices with their start and end apart: 27, of which 14 were waited for; matrix products, arithmetic and copies ran while one was open for 4% of the time, Pallas kernels for 19%

profile of v8, /device:TPU:4, one launch (start us, length us, event | category | flops | bytes accessed | tf_op | source)
XLA Modules:
  0.0 169.0 jit_solution(3791324169396198039)
XLA Ops:
  1.9 2.1 %collective-permute-start = (bf16[6,16,3072]{2,1,0:T(8,128)(2,1)S(1)}, bf16[6,16,3072]{2,1,0:T(8,128)(2,1)S(1)}, u32[]{:S(2)}, u32[]{:S(2)}) collective-permute-start(bf16[6,16,3072]{2,1,0:T(8,128)(2,1)S(1)} %constant_dynamic-slice_fusion), channel_id=1, source_target_pairs={{0,4},{2,6},{4,8},{6,10},{8,12},{10,14},{12,0},{14,2},{1,5},{3,7},... | collective-permute-start | bytes 1769480 | tf_op jit(solution)/shard_map/ppermute | solution.py:74
  5.2 1.6 bitcast_dynamic-update-slice_fusion.1
  7.4 1.6 bitcast_dynamic-update-slice_fusion.refs_3_.refs_7_
  9.1 7.8 %collective-permute-done.1.refs_5_.refs_4_ = bf16[6,16,3072]{2,1,0:T(8,128)(2,1)S(1)} collective-permute-done((bf16[6,16,3072]{2,1,0:T(8,128)(2,1)S(1)}, bf16[6,16,3072]{2,1,0:T(8,128)(2,1)S(1)}, u32[]{:S(2)}, u32[]{:S(2)}) %collective-permute-start.1) | collective-permute-done | bytes 589856 | tf_op jit(solution)/shard_map/ppermute | solution.py:75
  16.9 2.1 %collective-permute-done.refs_2_.refs_1_ = bf16[6,16,3072]{2,1,0:T(8,128)(2,1)S(1)} collective-permute-done((bf16[6,16,3072]{2,1,0:T(8,128)(2,1)S(1)}, bf16[6,16,3072]{2,1,0:T(8,128)(2,1)S(1)}, u32[]{:S(2)}, u32[]{:S(2)}) %collective-permute-start) | collective-permute-done | bytes 589856 | tf_op jit(solution)/shard_map/ppermute | solution.py:74
  19.0 1.5 collective-permute-start.7
  22.0 14.5 %collective-permute-done.2.refs_3_.refs_2_ = bf16[6,16,3072]{2,1,0:T(8,128)(2,1)S(1)} collective-permute-done((bf16[6,16,3072]{2,1,0:T(8,128)(2,1)S(1)}, bf16[6,16,3072]{2,1,0:T(8,128)(2,1)S(1)}, u32[]{:S(2)}, u32[]{:S(2)}) %collective-permute-start.2) | collective-permute-done | bytes 589856 | tf_op jit(solution)/shard_map/ppermute | solution.py:74
  37.3 1.5 collective-permute-start.4
  40.3 4.7 %pick.1 = (bf16[128,3072]{1,0:T(8,128)(2,1)}, bf16[128,3072]{1,0:T(8,128)(2,1)}, f32[128,128]{1,0:T(8,128)}) custom-call(s32[1]{0:T(128)} %bitcast.10.core.refs_9_, s32[128,2]{1,0:T(8,128)} %copy.27.slots, bf16[1,4,2,64,3072]{4,3,2,1,0:T(8,128)(2,1)} %here_ref.1, bf16[1,4,2,64,3072]{4,3,2,1,0:T(8,128)(2,1)} %collective-permute-done.3.there_ref, ...), custom_call_target="tpu_custom_call" | custom-call | flops 805306368 | bytes 6291456 | tf_op jit(solution)/shard_map/pick/pallas_call | solution.py:438
  45.0 8.4 %collective-permute-done.5.refs_4_.refs_3_ = bf16[6,16,3072]{2,1,0:T(8,128)(2,1)} collective-permute-done((bf16[6,16,3072]{2,1,0:T(8,128)(2,1)S(1)}, bf16[6,16,3072]{2,1,0:T(8,128)(2,1)}, u32[]{:S(2)}, u32[]{:S(2)}) %collective-permute-start.5) | collective-permute-done | bytes 589856 | tf_op jit(solution)/shard_map/ppermute | solution.py:74
  53.4 1.5 collective-permute-start.10
  54.9 1.5 collective-permute-start.14
  57.3 12.2 %collective-permute-done.8.refs_10_.refs_9_ = bf16[6,16,3072]{2,1,0:T(8,128)(2,1)S(1)} collective-permute-done((bf16[6,16,3072]{2,1,0:T(8,128)(2,1)}, bf16[6,16,3072]{2,1,0:T(8,128)(2,1)S(1)}, u32[]{:S(2)}, u32[]{:S(2)}) %collective-permute-start.8) | collective-permute-done | bytes 589856 | tf_op jit(solution)/shard_map/ppermute | solution.py:74
  71.1 1.9 %collective-permute-start.13 = (bf16[256,512]{1,0:T(8,128)(2,1)}, bf16[256,512]{1,0:T(8,128)(2,1)}, u32[]{:S(2)}, u32[]{:S(2)}) collective-permute-start(bf16[256,512]{1,0:T(8,128)(2,1)} %bitcast_dynamic-update-slice_fusion.refs_3_.refs_7_), channel_id=1, source_target_pairs={{0,2},{2,4},{4,6},{6,8},{8,10},{10,12},{12,14},{1,3},{3,5},{5,7},{... | collective-permute-start | bytes 786440 | tf_op jit(solution)/shard_map/ppermute | solution.py:39
  73.0 2.7 %collective-permute-start.15 = (bf16[6,16,3072]{2,1,0:T(8,128)(2,1)}, bf16[6,16,3072]{2,1,0:T(8,128)(2,1)}, u32[]{:S(2)}, u32[]{:S(2)}) collective-permute-start(bf16[6,16,3072]{2,1,0:T(8,128)(2,1)} %collective-permute-done.6.refs_9_.refs_8_), channel_id=1, source_target_pairs={{0,2},{2,0},{4,6},{6,4},{8,10},{10,8},{12,14},{14,12},{1,3},{3,1},... | collective-permute-start | bytes 1769480 | tf_op jit(solution)/shard_map/ppermute | solution.py:75
  77.8 2.0 %collective-permute-start.12 = (bf16[256,512]{1,0:T(8,128)(2,1)}, bf16[256,512]{1,0:T(8,128)(2,1)}, u32[]{:S(2)}, u32[]{:S(2)}) collective-permute-start(bf16[256,512]{1,0:T(8,128)(2,1)} %bitcast_dynamic-update-slice_fusion.refs_3_.refs_7_), channel_id=1, source_target_pairs={{0,4},{2,6},{4,8},{6,10},{8,12},{10,14},{1,5},{3,7},{5,9},{7,11},{... | collective-permute-start | bytes 786440 | tf_op jit(solution)/shard_map/ppermute | solution.py:39
  79.8 2.8 %collective-permute-done.13.refs_2_.refs_6_ = bf16[256,512]{1,0:T(8,128)(2,1)} collective-permute-done((bf16[256,512]{1,0:T(8,128)(2,1)}, bf16[256,512]{1,0:T(8,128)(2,1)}, u32[]{:S(2)}, u32[]{:S(2)}) %collective-permute-start.13) | collective-permute-done | bytes 262176 | tf_op jit(solution)/shard_map/ppermute | solution.py:39
  82.6 2.0 %collective-permute-start.11 = (bf16[256,512]{1,0:T(8,128)(2,1)}, bf16[256,512]{1,0:T(8,128)(2,1)}, u32[]{:S(2)}, u32[]{:S(2)}) collective-permute-start(bf16[256,512]{1,0:T(8,128)(2,1)} %bitcast_dynamic-update-slice_fusion.refs_3_.refs_7_), channel_id=1, source_target_pairs={{0,6},{2,8},{4,10},{6,12},{8,14},{1,7},{3,9},{5,11},{7,13},{9,15},... | collective-permute-start | bytes 786440 | tf_op jit(solution)/shard_map/ppermute | solution.py:39
  85.7 2.8 %collective-permute-done.11.refs_0_.refs_4_ = bf16[256,512]{1,0:T(8,128)(2,1)} collective-permute-done((bf16[256,512]{1,0:T(8,128)(2,1)}, bf16[256,512]{1,0:T(8,128)(2,1)}, u32[]{:S(2)}, u32[]{:S(2)}) %collective-permute-start.11) | collective-permute-done | bytes 262176 | tf_op jit(solution)/shard_map/ppermute | solution.py:39
  88.5 11.2 %attention.1 = (bf16[256,1536]{1,0:T(8,128)(2,1)}, bf16[12,256,1024]{2,1,0:T(8,128)(2,1)}) custom-call(s32[1]{0:T(128)} %bitcast.11.place, bf16[12,256,128]{2,1,0:T(8,128)(2,1)} %bitcast.26, bf16[256,512]{1,0:T(8,128)(2,1)} %collective-permute-done.11.refs_0_.refs_4_, bf16[256,512]{1,0:T(8,128)(2,1)} %collective-permute-done.12.refs_1_.refs_5_, ...), custom_call_target="tpu_custom_call" | custom-call | flops 1610612736 | bytes 6291456 | tf_op jit(solution)/shard_map/attention/pallas_call | solution.py:281
  99.7 1.6 collective-permute-done.16.refs_14_.refs_13_
  102.5 6.2 %project.1 = (f32[128,3072]{1,0:T(8,128)S(1)}, bf16[128,3072]{1,0:T(8,128)(2,1)S(1)}) custom-call(s32[11]{0:T(128)S(1)} %stack.43.table, s32[1]{0:T(128)} %bitcast.10.core.refs_9_, bf16[256,1536]{1,0:T(8,128)(2,1)S(1)} %copy-done.2, bf16[12,16,3072]{2,1,0:T(8,128)(2,1)S(1)} %copy-done, bf16[6,16,3072]{2,1,0:T(8,128)(2,1)S(1)} %collective-permute-done.refs_2_.refs_1_, ...), custom_call_target="tpu_custom_call" | custom-call | flops 2415919104 | bytes 9437184 | tf_op jit(solution)/shard_map/project/pallas_call | solution.py:160
  108.8 2.3 %collective-permute-done.18.recv = bf16[128,3072]{1,0:T(8,128)(2,1)S(1)} collective-permute-done((bf16[128,3072]{1,0:T(8,128)(2,1)S(1)}, bf16[128,3072]{1,0:T(8,128)(2,1)S(1)}, u32[]{:S(2)}, u32[]{:S(2)}) %collective-permute-start.18) | collective-permute-done | bytes 786464 | tf_op jit(solution)/shard_map/ppermute | solution.py:43
  111.1 3.5 %middle.1 = (bf16[128,3072]{1,0:T(8,128)(2,1)}, bf16[128,3072]{1,0:T(8,128)(2,1)}, f32[128,128]{1,0:T(8,128)S(1)}) custom-call(s32[128,2]{1,0:T(8,128)S(1)} %copy.28.routes, f32[128,3072]{1,0:T(8,128)S(1)} %get-tuple-element.60.own, bf16[128,3072]{1,0:T(8,128)(2,1)S(1)} %collective-permute-done.18.recv, bf16[128,3072]{1,0:T(8,128)(2,1)S(1)} %copy-done.11, ...), custom_call_target="tpu_custom_call" | custom-call | flops 402653184 | bytes 7864320 | tf_op jit(solution)/shard_map/middle/pallas_call | solution.py:494
  114.7 3.3 %spread.1 = (bf16[256,3072]{1,0:T(8,128)(2,1)S(1)}, bf16[256,3072]{1,0:T(8,128)(2,1)}) custom-call(s32[2,128]{1,0:T(2,128)S(1)} %bitcast.25, f32[128,128]{1,0:T(8,128)S(1)} %get-tuple-element.68.gates, bf16[128,3072]{1,0:T(8,128)(2,1)S(1)} %copy-done.3), custom_call_target="tpu_custom_call" | custom-call | flops 805306368 | bytes 3932160 | tf_op jit(solution)/shard_map/spread/pallas_call | solution.py:524
  119.3 6.7 %dattention.1.dout = bf16[256,1536]{1,0:T(8,128)(2,1)S(1)} custom-call(s32[11]{0:T(128)S(1)} %stack.43.table, s32[1]{0:T(128)} %bitcast.10.core.refs_9_, bf16[128,3072]{1,0:T(8,128)(2,1)S(1)} %copy-done.14, bf16[128,3072]{1,0:T(8,128)(2,1)S(1)} %collective-permute-done.19.recv, bf16[12,16,3072]{2,1,0:T(8,128)(2,1)S(1)} %copy-done, ...), custom_call_target="tpu_custom_call" | custom-call | flops 2415919104 | bytes 9437184 | tf_op jit(solution)/shard_map/dattention/pallas_call | solution.py:216
  127.2 6.5 %attention_grad.2 = (bf16[12,256,128]{2,1,0:T(8,128)(2,1)}, bf16[256,256]{1,0:T(8,128)(2,1)}, bf16[256,256]{1,0:T(8,128)(2,1)}, bf16[256,256]{1,0:T(8,128)(2,1)}, f32[256,256]{1,0:T(8,128)}) custom-call(bf16[12,256,128]{2,1,0:T(8,128)(2,1)} %bitcast.27, bf16[256,1536]{1,0:T(8,128)(2,1)} %copy-done.1, bf16[256,1536]{1,0:T(8,128)(2,1)} %get-tuple-element.56.refs_0_.attn, ...), custom_call_target="tpu_custom_call" | custom-call | flops 256 | bytes 256 | tf_op jit(solution)/shard_map/attention_grad/pallas_call | solution.py:382
  134.1 3.6 %collective-permute-start.22 = (bf16[256,256]{1,0:T(8,128)(2,1)}, bf16[256,256]{1,0:T(8,128)(2,1)S(1)}, u32[]{:S(2)}, u32[]{:S(2)}) collective-permute-start(bf16[256,256]{1,0:T(8,128)(2,1)} %get-tuple-element.77), channel_id=1, source_target_pairs={{2,0},{6,4},{8,2},{10,8},{12,6},{14,12},{3,1},{7,5},{9,3},{11,9},{... | collective-permute-start | bytes 393224 | tf_op jit(solution)/shard_map/ppermute | solution.py:50
  138.9 7.1 %attention_grad.3 = (bf16[12,256,128]{2,1,0:T(8,128)(2,1)}, bf16[256,256]{1,0:T(8,128)(2,1)}, bf16[256,256]{1,0:T(8,128)(2,1)}, bf16[256,256]{1,0:T(8,128)(2,1)}...) custom-call(bf16[12,256,128]{2,1,0:T(8,128)(2,1)} %bitcast.28, ...), custom_call_target="tpu_custom_call", output_to_operand_aliasing={{0}: (12, {})} | custom-call | flops 256 | bytes 256 | tf_op jit(solution)/shard_map/attention_grad/pallas_call | solution.py:382
  146.0 2.1 %collective-permute-start.24 = (bf16[256,256]{1,0:T(8,128)(2,1)}, bf16[256,256]{1,0:T(8,128)(2,1)S(1)}, u32[]{:S(2)}, u32[]{:S(2)}) collective-permute-start(bf16[256,256]{1,0:T(8,128)(2,1)} %get-tuple-element.82), channel_id=1, source_target_pairs={{2,0},{6,4},{8,2},{10,8},{12,6},{14,12},{3,1},{7,5},{9,3},{11,9},{... | collective-permute-start | bytes 393224 | tf_op jit(solution)/shard_map/ppermute | solution.py:50
  149.6 6.2 %collective-permute-done.24 = bf16[256,256]{1,0:T(8,128)(2,1)S(1)} collective-permute-done((bf16[256,256]{1,0:T(8,128)(2,1)}, bf16[256,256]{1,0:T(8,128)(2,1)S(1)}, u32[]{:S(2)}, u32[]{:S(2)}) %collective-permute-start.24) | collective-permute-done | bytes 131104 | tf_op jit(solution)/shard_map/ppermute | solution.py:50
  158.9 8.5 %collective-permute-done.26 = bf16[256,256]{1,0:T(8,128)(2,1)S(1)} collective-permute-done((bf16[256,256]{1,0:T(8,128)(2,1)S(1)}, bf16[256,256]{1,0:T(8,128)(2,1)S(1)}, u32[]{:S(2)}, u32[]{:S(2)}) %collective-permute-start.26) | collective-permute-done | bytes 131104 | tf_op jit(solution)/shard_map/ppermute | solution.py:39
  (97 shorter events, 23.9 us)
Async XLA Ops:
  1.8 15.1 %collective-permute-start.1 = (bf16[6,16,3072]{2,1,0:T(8,128)(2,1)S(1)}, bf16[6,16,3072]{2,1,0:T(8,128)(2,1)S(1)}, u32[]{:S(2)}, u32[]{:S(2)}) collective-permute-start(bf16[6,16,3072]{2,1,0:T(8,128)(2,1)S(1)} %constant_dynamic-slice_fusion), channel_id=1, source_target_pairs={{0,2},{2,0},{4,6},{6,4},{8,10},{10,8},{12,14},{14,12},{1,3},{3,1},... | collective-permute-start | bytes 1769480 | tf_op jit(solution)/shard_map/ppermute | solution.py:75
  1.9 17.1 %collective-permute-start = (bf16[6,16,3072]{2,1,0:T(8,128)(2,1)S(1)}, bf16[6,16,3072]{2,1,0:T(8,128)(2,1)S(1)}, u32[]{:S(2)}, u32[]{:S(2)}) collective-permute-start(bf16[6,16,3072]{2,1,0:T(8,128)(2,1)S(1)} %constant_dynamic-slice_fusion), channel_id=1, source_target_pairs={{0,4},{2,6},{4,8},{6,10},{8,12},{10,14},{12,0},{14,2},{1,5},{3,7},... | collective-permute-start | bytes 1769480 | tf_op jit(solution)/shard_map/ppermute | solution.py:74
  19.0 17.5 %collective-permute-start.3 = (bf16[1,4,2,64,3072]{4,3,2,1,0:T(8,128)(2,1)}, bf16[1,4,2,64,3072]{4,3,2,1,0:T(8,128)(2,1)}, u32[]{:S(2)}, u32[]{:S(2)}) collective-permute-start(bf16[1,4,2,64,3072]{4,3,2,1,0:T(8,128)(2,1)} %here_ref.1), channel_id=1, source_target_pairs={{0,1},{1,0},{2,3},{3,2},{4,5},{5,4},{6,7},{7,6},{8,9},{9,8},{10,11... | collective-permute-start | bytes 9437192 | tf_op jit(solution)/shard_map/ppermute | solution.py:43
  19.0 17.5 %collective-permute-start.2 = (bf16[6,16,3072]{2,1,0:T(8,128)(2,1)S(1)}, bf16[6,16,3072]{2,1,0:T(8,128)(2,1)S(1)}, u32[]{:S(2)}, u32[]{:S(2)}) collective-permute-start(bf16[6,16,3072]{2,1,0:T(8,128)(2,1)S(1)} %collective-permute-done.refs_2_.refs_1_), channel_id=1, source_target_pairs={{0,4},{2,6},{4,8},{6,10},{8,12},{10,14},{12,0},{14,2},{1,5},{3,7},... | collective-permute-start | bytes 1769480 | tf_op jit(solution)/shard_map/ppermute | solution.py:74
  19.0 26.0 %collective-permute-start.7 = (bf16[6,16,3072]{2,1,0:T(8,128)(2,1)S(1)}, bf16[6,16,3072]{2,1,0:T(8,128)(2,1)}, u32[]{:S(2)}, u32[]{:S(2)}) collective-permute-start(bf16[6,16,3072]{2,1,0:T(8,128)(2,1)S(1)} %collective-permute-done.refs_2_.refs_1_), channel_id=1, source_target_pairs={{0,2},{2,0},{4,6},{6,4},{8,10},{10,8},{12,14},{14,12},{1,3},{3,1},... | collective-permute-start | bytes 1769480 | tf_op jit(solution)/shard_map/ppermute | solution.py:75
  20.5 24.5 %collective-permute-start.6 = (bf16[6,16,3072]{2,1,0:T(8,128)(2,1)S(1)}, bf16[6,16,3072]{2,1,0:T(8,128)(2,1)}, u32[]{:S(2)}, u32[]{:S(2)}) collective-permute-start(bf16[6,16,3072]{2,1,0:T(8,128)(2,1)S(1)} %collective-permute-done.refs_2_.refs_1_), channel_id=1, source_target_pairs={{0,16},{16,0},{1,17},{17,1},{2,18},{18,2},{3,19},{19,3},{4,20},{20... | collective-permute-start | bytes 1769480 | tf_op jit(solution)/shard_map/ppermute | solution.py:43
  36.5 16.9 %collective-permute-start.5 = (bf16[6,16,3072]{2,1,0:T(8,128)(2,1)S(1)}, bf16[6,16,3072]{2,1,0:T(8,128)(2,1)}, u32[]{:S(2)}, u32[]{:S(2)}) collective-permute-start(bf16[6,16,3072]{2,1,0:T(8,128)(2,1)S(1)} %collective-permute-done.2.refs_3_.refs_2_), channel_id=1, source_target_pairs={{0,4},{2,6},{4,8},{6,10},{8,12},{10,14},{12,0},{14,2},{1,5},{3,7},... | collective-permute-start | bytes 1769480 | tf_op jit(solution)/shard_map/ppermute | solution.py:74
  37.3 20.0 %collective-permute-start.4 = (bf16[6,16,3072]{2,1,0:T(8,128)(2,1)S(1)}, bf16[6,16,3072]{2,1,0:T(8,128)(2,1)}, u32[]{:S(2)}, u32[]{:S(2)}) collective-permute-start(bf16[6,16,3072]{2,1,0:T(8,128)(2,1)S(1)} %collective-permute-done.2.refs_3_.refs_2_), channel_id=1, source_target_pairs={{0,2},{2,0},{4,6},{6,4},{8,10},{10,8},{12,14},{14,12},{1,3},{3,1},... | collective-permute-start | bytes 1769480 | tf_op jit(solution)/shard_map/ppermute | solution.py:75
  38.8 17.6 %collective-permute-start.9 = (bf16[6,16,3072]{2,1,0:T(8,128)(2,1)S(1)}, bf16[6,16,3072]{2,1,0:T(8,128)(2,1)S(1)}, u32[]{:S(2)}, u32[]{:S(2)}) collective-permute-start(bf16[6,16,3072]{2,1,0:T(8,128)(2,1)S(1)} %collective-permute-done.1.refs_5_.refs_4_), channel_id=1, source_target_pairs={{0,16},{16,0},{1,17},{17,1},{2,18},{18,2},{3,19},{19,3},{4,20},{20... | collective-permute-start | bytes 1769480 | tf_op jit(solution)/shard_map/ppermute | solution.py:43
  53.4 16.1 %collective-permute-start.8 = (bf16[6,16,3072]{2,1,0:T(8,128)(2,1)}, bf16[6,16,3072]{2,1,0:T(8,128)(2,1)S(1)}, u32[]{:S(2)}, u32[]{:S(2)}) collective-permute-start(bf16[6,16,3072]{2,1,0:T(8,128)(2,1)} %collective-permute-done.6.refs_9_.refs_8_), channel_id=1, source_target_pairs={{0,4},{2,6},{4,8},{6,10},{8,12},{10,14},{12,0},{14,2},{1,5},{3,7},... | collective-permute-start | bytes 1769480 | tf_op jit(solution)/shard_map/ppermute | solution.py:74
  53.4 16.9 %collective-permute-start.10 = (bf16[6,16,3072]{2,1,0:T(8,128)(2,1)}, bf16[6,16,3072]{2,1,0:T(8,128)(2,1)S(1)}, u32[]{:S(2)}, u32[]{:S(2)}) collective-permute-start(bf16[6,16,3072]{2,1,0:T(8,128)(2,1)} %collective-permute-done.5.refs_4_.refs_3_), channel_id=1, source_target_pairs={{0,16},{16,0},{1,17},{17,1},{2,18},{18,2},{3,19},{19,3},{4,20},{20... | collective-permute-start | bytes 1769480 | tf_op jit(solution)/shard_map/ppermute | solution.py:43
  54.9 18.1 %collective-permute-start.14 = (bf16[6,16,3072]{2,1,0:T(8,128)(2,1)}, bf16[6,16,3072]{2,1,0:T(8,128)(2,1)}, u32[]{:S(2)}, u32[]{:S(2)}) collective-permute-start(bf16[6,16,3072]{2,1,0:T(8,128)(2,1)} %collective-permute-done.5.refs_4_.refs_3_), channel_id=1, source_target_pairs={{0,2},{2,0},{4,6},{6,4},{8,10},{10,8},{12,14},{14,12},{1,3},{3,1},... | collective-permute-start | bytes 1769480 | tf_op jit(solution)/shard_map/ppermute | solution.py:75
  71.1 11.4 %collective-permute-start.13 = (bf16[256,512]{1,0:T(8,128)(2,1)}, bf16[256,512]{1,0:T(8,128)(2,1)}, u32[]{:S(2)}, u32[]{:S(2)}) collective-permute-start(bf16[256,512]{1,0:T(8,128)(2,1)} %bitcast_dynamic-update-slice_fusion.refs_3_.refs_7_), channel_id=1, source_target_pairs={{0,2},{2,4},{4,6},{6,8},{8,10},{10,12},{12,14},{1,3},{3,5},{5,7},{... | collective-permute-start | bytes 786440 | tf_op jit(solution)/shard_map/ppermute | solution.py:39
  73.0 26.7 %collective-permute-start.15 = (bf16[6,16,3072]{2,1,0:T(8,128)(2,1)}, bf16[6,16,3072]{2,1,0:T(8,128)(2,1)}, u32[]{:S(2)}, u32[]{:S(2)}) collective-permute-start(bf16[6,16,3072]{2,1,0:T(8,128)(2,1)} %collective-permute-done.6.refs_9_.refs_8_), channel_id=1, source_target_pairs={{0,2},{2,0},{4,6},{6,4},{8,10},{10,8},{12,14},{14,12},{1,3},{3,1},... | collective-permute-start | bytes 1769480 | tf_op jit(solution)/shard_map/ppermute | solution.py:75
  75.8 24.0 %collective-permute-start.17 = (bf16[6,16,3072]{2,1,0:T(8,128)(2,1)}, bf16[6,16,3072]{2,1,0:T(8,128)(2,1)}, u32[]{:S(2)}, u32[]{:S(2)}) collective-permute-start(bf16[6,16,3072]{2,1,0:T(8,128)(2,1)} %collective-permute-done.14.refs_8_.refs_7_), channel_id=1, source_target_pairs={{0,16},{16,0},{1,17},{17,1},{2,18},{18,2},{3,19},{19,3},{4,20},{20... | collective-permute-start | bytes 1769480 | tf_op jit(solution)/shard_map/ppermute | solution.py:43
  77.2 24.1 %collective-permute-start.16 = (bf16[6,16,3072]{2,1,0:T(8,128)(2,1)}, bf16[6,16,3072]{2,1,0:T(8,128)(2,1)}, u32[]{:S(2)}, u32[]{:S(2)}) collective-permute-start(bf16[6,16,3072]{2,1,0:T(8,128)(2,1)} %collective-permute-done.4.refs_7_.refs_6_), channel_id=1, source_target_pairs={{0,16},{16,0},{1,17},{17,1},{2,18},{18,2},{3,19},{19,3},{4,20},{20... | collective-permute-start | bytes 1769480 | tf_op jit(solution)/shard_map/ppermute | solution.py:43
  77.8 7.9 %collective-permute-start.12 = (bf16[256,512]{1,0:T(8,128)(2,1)}, bf16[256,512]{1,0:T(8,128)(2,1)}, u32[]{:S(2)}, u32[]{:S(2)}) collective-permute-start(bf16[256,512]{1,0:T(8,128)(2,1)} %bitcast_dynamic-update-slice_fusion.refs_3_.refs_7_), channel_id=1, source_target_pairs={{0,4},{2,6},{4,8},{6,10},{8,12},{10,14},{1,5},{3,7},{5,9},{7,11},{... | collective-permute-start | bytes 786440 | tf_op jit(solution)/shard_map/ppermute | solution.py:39
  82.6 6.0 %collective-permute-start.11 = (bf16[256,512]{1,0:T(8,128)(2,1)}, bf16[256,512]{1,0:T(8,128)(2,1)}, u32[]{:S(2)}, u32[]{:S(2)}) collective-permute-start(bf16[256,512]{1,0:T(8,128)(2,1)} %bitcast_dynamic-update-slice_fusion.refs_3_.refs_7_), channel_id=1, source_target_pairs={{0,6},{2,8},{4,10},{6,12},{8,14},{1,7},{3,9},{5,11},{7,13},{9,15},... | collective-permute-start | bytes 786440 | tf_op jit(solution)/shard_map/ppermute | solution.py:39
  88.5 12.8 %copy-start.5 = (bf16[6,16,3072]{2,1,0:T(8,128)(2,1)S(1)}, bf16[6,16,3072]{2,1,0:T(8,128)(2,1)}, u32[]{:S(2)}) copy-start(bf16[6,16,3072]{2,1,0:T(8,128)(2,1)} %copy-done.4) | copy-start | bytes 1769476
  88.5 12.8 %copy-start.7 = (bf16[6,16,3072]{2,1,0:T(8,128)(2,1)S(1)}, bf16[6,16,3072]{2,1,0:T(8,128)(2,1)}, u32[]{:S(2)}) copy-start(bf16[6,16,3072]{2,1,0:T(8,128)(2,1)} %copy-done.6) | copy-start | bytes 1769476
  88.5 12.8 %copy-start.9 = (bf16[6,16,3072]{2,1,0:T(8,128)(2,1)S(1)}, bf16[6,16,3072]{2,1,0:T(8,128)(2,1)}, u32[]{:S(2)}) copy-start(bf16[6,16,3072]{2,1,0:T(8,128)(2,1)} %copy-done.8) | copy-start | bytes 1769476
  108.7 2.4 %collective-permute-start.18 = (bf16[128,3072]{1,0:T(8,128)(2,1)S(1)}, bf16[128,3072]{1,0:T(8,128)(2,1)S(1)}, u32[]{:S(2)}, u32[]{:S(2)}) collective-permute-start(bf16[128,3072]{1,0:T(8,128)(2,1)S(1)} %get-tuple-element.61), channel_id=1, source_target_pairs={{0,1},{1,0},{2,3},{3,2},{4,5},{5,4},{6,7},{7,6},{8,9},{9,8},{10,11... | collective-permute-start | bytes 2359304 | tf_op jit(solution)/shard_map/ppermute | solution.py:43
  114.6 4.7 %collective-permute-start.19 = (bf16[128,3072]{1,0:T(8,128)(2,1)}, bf16[128,3072]{1,0:T(8,128)(2,1)S(1)}, u32[]{:S(2)}, u32[]{:S(2)}) collective-permute-start(bf16[128,3072]{1,0:T(8,128)(2,1)} %get-tuple-element.40.own), channel_id=1, source_target_pairs={{0,1},{1,0},{2,3},{3,2},{4,5},{5,4},{6,7},{7,6},{8,9},{9,8},{10,11... | collective-permute-start | bytes 2359304 | tf_op jit(solution)/shard_map/ppermute | solution.py:43
  126.9 10.9 %collective-permute-start.20 = (bf16[256,3072]{1,0:T(8,128)(2,1)}, bf16[256,3072]{1,0:T(8,128)(2,1)S(1)}, u32[]{:S(2)}, u32[]{:S(2)}) collective-permute-start(bf16[256,3072]{1,0:T(8,128)(2,1)} %get-tuple-element.71), channel_id=1, source_target_pairs={{0,1},{1,0},{2,3},{3,2},{4,5},{5,4},{6,7},{7,6},{8,9},{9,8},{10,11... | collective-permute-start | bytes 4718600 | tf_op jit(solution)/shard_map/ppermute | solution.py:43
  133.8 12.2 %collective-permute-start.21 = (bf16[256,256]{1,0:T(8,128)(2,1)}, bf16[256,256]{1,0:T(8,128)(2,1)S(1)}, u32[]{:S(2)}, u32[]{:S(2)}) collective-permute-start(bf16[256,256]{1,0:T(8,128)(2,1)} %get-tuple-element.76), channel_id=1, source_target_pairs={{0,2},{2,0},{4,6},{6,4},{8,10},{10,8},{12,14},{14,12},{1,3},{3,1},... | collective-permute-start | bytes 393224 | tf_op jit(solution)/shard_map/ppermute | solution.py:50
  134.1 12.0 %collective-permute-start.22 = (bf16[256,256]{1,0:T(8,128)(2,1)}, bf16[256,256]{1,0:T(8,128)(2,1)S(1)}, u32[]{:S(2)}, u32[]{:S(2)}) collective-permute-start(bf16[256,256]{1,0:T(8,128)(2,1)} %get-tuple-element.77), channel_id=1, source_target_pairs={{2,0},{6,4},{8,2},{10,8},{12,6},{14,12},{3,1},{7,5},{9,3},{11,9},{... | collective-permute-start | bytes 393224 | tf_op jit(solution)/shard_map/ppermute | solution.py:50
  138.9 19.9 %copy-start.17 = (f32[256,256]{1,0:T(8,128)S(1)}, f32[256,256]{1,0:T(8,128)}, u32[]{:S(2)}) copy-start(f32[256,256]{1,0:T(8,128)} %get-tuple-element.74) | copy-start | bytes 786436
  146.0 21.4 %copy-start.18 = (f32[256,256]{1,0:T(8,128)S(1)}, f32[256,256]{1,0:T(8,128)}, u32[]{:S(2)}) copy-start(f32[256,256]{1,0:T(8,128)} %get-tuple-element.80) | copy-start | bytes 786436
  146.0 9.7 %collective-permute-start.24 = (bf16[256,256]{1,0:T(8,128)(2,1)}, bf16[256,256]{1,0:T(8,128)(2,1)S(1)}, u32[]{:S(2)}, u32[]{:S(2)}) collective-permute-start(bf16[256,256]{1,0:T(8,128)(2,1)} %get-tuple-element.82), channel_id=1, source_target_pairs={{2,0},{6,4},{8,2},{10,8},{12,6},{14,12},{3,1},{7,5},{9,3},{11,9},{... | collective-permute-start | bytes 393224 | tf_op jit(solution)/shard_map/ppermute | solution.py:50
  148.1 8.1 %collective-permute-start.25 = (bf16[256,256]{1,0:T(8,128)(2,1)}, bf16[256,256]{1,0:T(8,128)(2,1)S(1)}, u32[]{:S(2)}, u32[]{:S(2)}) collective-permute-start(bf16[256,256]{1,0:T(8,128)(2,1)} %get-tuple-element.83), channel_id=1, source_target_pairs={{0,2},{2,0},{4,6},{6,4},{8,10},{10,8},{12,14},{14,12},{1,3},{3,1},... | collective-permute-start | bytes 393224 | tf_op jit(solution)/shard_map/ppermute | solution.py:50
  148.3 10.6 %collective-permute-start.23 = (bf16[256,256]{1,0:T(8,128)(2,1)S(1)}, bf16[256,256]{1,0:T(8,128)(2,1)S(1)}, u32[]{:S(2)}, u32[]{:S(2)}) collective-permute-start(bf16[256,256]{1,0:T(8,128)(2,1)S(1)} %add_convert_fusion.3), channel_id=1, source_target_pairs={{4,0},{6,2},{8,4},{10,6},{12,8},{14,10},{5,1},{7,3},{9,5},{11,7},{... | collective-permute-start | bytes 393224 | tf_op jit(solution)/shard_map/ppermute | solution.py:39
  157.1 10.3 %collective-permute-start.26 = (bf16[256,256]{1,0:T(8,128)(2,1)S(1)}, bf16[256,256]{1,0:T(8,128)(2,1)S(1)}, u32[]{:S(2)}, u32[]{:S(2)}) collective-permute-start(bf16[256,256]{1,0:T(8,128)(2,1)S(1)} %add_convert_fusion.1), channel_id=1, source_target_pairs={{4,0},{6,2},{8,4},{10,6},{12,8},{14,10},{5,1},{7,3},{9,5},{11,7},{... | collective-permute-start | bytes 393224 | tf_op jit(solution)/shard_map/ppermute | solution.py:39
  (17 other events, 89.1 us)
